TPU v7x, 128 devices: a whole 4x4x4 slice. The times are simulated.
128 devices in a mesh: rows: 32 (over x, z, core), cols: 4 (over y).
Axes of the slice: x: 4, y: 4, z: 4, core: 2. Of those that a mesh axis runs over, the one named last changes fastest.
Arguments:
- table: bfloat16 [262144, 512], P('rows', 'cols'), may hold values from -6 to 6
- item_ids: int32 [256, 256], P(('rows', 'cols')), may hold values from 0 to 262143, as said below
- cotangent: bfloat16 [256, 256, 512], P(('rows', 'cols')), may hold values from -6 to 6
- norm_gain: float32 [512], replicated, may hold values from 0.25 to 1.75
- w_in: bfloat16 [512, 2048], replicated, may hold values from -0.25 to 0.25
- bias_in: float32 [2048], replicated, may hold values from -3 to 3
- w_out: bfloat16 [2048, 512], replicated, may hold values from -0.125 to 0.125
Outputs:
- table_grad: float32 [262144, 512], P('rows', 'cols')
- w_in_grad: float32 [512, 2048], replicated
- bias_grad: float32 [2048], replicated
- w_out_grad: float32 [2048, 512], replicated
- gain_grad: float32 [512], replicated
Inputs may be any that keep to these rules, and one draw needn't show every extreme that they name: `item_ids`: within each device's 512 positions (aligned blocks of 2 sequences), at most 32 name rows of one range k * 8192 to (k + 1) * 8192 - 1; one range is named by exactly 32 positions of every device.
All inputs are finite; a program needn't handle non-finite values.
Results may differ from a plain program's by a relative error of at most 0.0051.
Values may be sent and summed in bfloat16 or wider, within the bound.
No kernel may reach another device: no remote copies, remote signals or barrier semaphores. Data moves between devices by JAX's collectives and lax.ppermute only.
A program may use at most 128 MiB of HBM per device.

v0:
```python
import math

import jax
import jax.numpy as jnp
from jax import lax
from jax.sharding import PartitionSpec as P

norm_eps = 1e-06
gelu_coef = 0.7978845608


def local_pass(embedded, d_out, norm_gain, w_in, bias_in, w_out):
    x_float = embedded.astype(jnp.float32)
    inv_rms = lax.rsqrt(jnp.mean(x_float * x_float, axis=-1, keepdims=True) + norm_eps)
    x_hat = x_float * inv_rms
    normed = (x_hat * norm_gain).astype(jnp.bfloat16)
    pre_act = jnp.dot(normed, w_in, preferred_element_type=jnp.float32) + bias_in
    tanh_part = jnp.tanh(gelu_coef * (pre_act + 0.044715 * pre_act * pre_act * pre_act))
    hidden = (0.5 * pre_act * (1.0 + tanh_part)).astype(jnp.bfloat16)
    d_act = lax.dot_general(
        d_out, w_out, (((1,), (1,)), ((), ())), preferred_element_type=jnp.float32
    )
    slope = 0.5 * (1.0 + tanh_part) + 0.5 * pre_act * (1.0 - tanh_part * tanh_part) * gelu_coef * (
        1.0 + 3.0 * 0.044715 * pre_act * pre_act
    )
    d_pre = d_act * slope
    d_pre_bf = d_pre.astype(jnp.bfloat16)
    g_out = lax.dot_general(
        hidden, d_out, (((0,), (0,)), ((), ())), preferred_element_type=jnp.float32
    )
    g_in = lax.dot_general(
        normed, d_pre_bf, (((0,), (0,)), ((), ())), preferred_element_type=jnp.float32
    )
    g_bias = jnp.sum(d_pre, axis=0)
    d_norm = lax.dot_general(
        d_pre_bf, w_in, (((1,), (1,)), ((), ())), preferred_element_type=jnp.float32
    )
    g_gain = jnp.sum(d_norm * x_hat, axis=0)
    scaled = d_norm * norm_gain
    d_embed = inv_rms * (
        scaled - x_hat * jnp.mean(scaled * x_hat, axis=-1, keepdims=True)
    ) + d_out.astype(jnp.float32)
    return (d_embed, g_in, g_bias, g_out, g_gain)


def local(table, item_ids, cotangent, norm_gain, w_in, bias_in, w_out):
    n_rows = lax.axis_size("rows")
    n_cols = lax.axis_size("cols")
    rows_dev = table.shape[0]
    col_width = table.shape[1]
    flat_ids = item_ids.reshape(-1)
    n_tokens = flat_ids.shape[0]
    capacity = max(2, 2 * n_tokens // n_rows)
    owners = flat_ids // rows_dev
    offsets = flat_ids - owners * rows_dev
    range_ids = jnp.arange(n_rows, dtype=jnp.int32)
    onehot = (owners[:, None] == range_ids[None, :]).astype(jnp.float32)
    tok_ids = jnp.arange(n_tokens, dtype=jnp.int32)
    lower = (tok_ids[:, None] >= tok_ids[None, :]).astype(jnp.float32)
    running = jnp.dot(lower, onehot, preferred_element_type=jnp.float32)
    rank_tok = (jnp.sum(running * onehot, axis=1) - 1.0).astype(jnp.int32)
    slot_of = owners * capacity + rank_tok
    n_slots = n_rows * capacity
    slot_ids = jnp.arange(n_slots, dtype=jnp.int32)
    slot_hit = slot_of[:, None] == slot_ids[None, :]
    wanted = jnp.sum(jnp.where(slot_hit, offsets[:, None], 0), axis=0).reshape(n_rows, capacity)
    requests = jnp.broadcast_to(wanted[:, None, :], (n_rows, n_cols, capacity)).reshape(
        n_rows * n_cols, capacity
    )
    looked = jnp.take(
        table,
        lax.all_to_all(requests, ("rows", "cols"), split_axis=0, concat_axis=0, tiled=True),
        axis=0,
    )
    fetched = lax.all_to_all(looked, ("rows", "cols"), split_axis=0, concat_axis=0, tiled=True)
    width = n_cols * col_width
    by_slot = jnp.transpose(
        fetched.reshape(n_rows, n_cols, capacity, col_width), (0, 2, 1, 3)
    ).reshape(n_slots, width)
    embedded = jnp.dot(
        slot_hit.astype(jnp.bfloat16), by_slot, preferred_element_type=jnp.float32
    ).astype(jnp.bfloat16)
    d_out = cotangent.reshape(n_tokens, width)
    block_rows = 512
    n_blocks = n_tokens // block_rows
    ff_width = w_in.shape[1]

    def one_block(carry, block):
        acc_in, acc_bias, acc_out, acc_gain = carry
        d_embed, g_in, g_bias, g_out, g_gain = local_pass(
            block[0], block[1], norm_gain, w_in, bias_in, w_out
        )
        return ((acc_in + g_in, acc_bias + g_bias, acc_out + g_out, acc_gain + g_gain), d_embed)

    start = (
        jnp.zeros((width, ff_width), jnp.float32),
        jnp.zeros((ff_width,), jnp.float32),
        jnp.zeros((ff_width, width), jnp.float32),
        jnp.zeros((width,), jnp.float32),
    )
    totals, d_blocks = lax.scan(
        one_block,
        start,
        (embedded.reshape(n_blocks, block_rows, width), d_out.reshape(n_blocks, block_rows, width)),
    )
    g_in, g_bias, g_out, g_gain = totals
    d_embed = d_blocks.reshape(n_tokens, width)
    slot_grad = lax.dot_general(
        slot_hit.astype(jnp.float32),
        d_embed,
        (((0,), (0,)), ((), ())),
        precision=lax.Precision.HIGHEST,
        preferred_element_type=jnp.float32,
    )
    payload = jnp.transpose(slot_grad.reshape(n_rows, capacity, n_cols, col_width), (0, 2, 1, 3))
    arrived, arrived_off = (
        lax.all_to_all(
            payload.reshape(n_rows * n_cols, capacity, col_width),
            ("rows", "cols"),
            split_axis=0,
            concat_axis=0,
            tiled=True,
        ),
        lax.all_to_all(requests, ("rows", "cols"), split_axis=0, concat_axis=0, tiled=True),
    )
    table_grad = (
        jnp.zeros((rows_dev, col_width), jnp.float32)
        .at[arrived_off.reshape(-1)]
        .add(arrived.reshape(-1, col_width))
    )
    summed = lax.psum((g_in, g_bias, g_out, g_gain), ("rows", "cols"))
    scale = 1.0 / math.sqrt(n_tokens * n_rows * n_cols)
    return (table_grad, summed[0] * scale, summed[1] * scale, summed[2] * scale, summed[3] * scale)


def solution(mesh):
    return jax.shard_map(
        local,
        mesh=mesh,
        in_specs=(
            P("rows", "cols"),
            P(("rows", "cols"), None),
            P(("rows", "cols"), None, None),
            P(),
            P(),
            P(),
            P(),
        ),
        out_specs=(P("rows", "cols"), P(), P(), P(), P()),
        check_vma=False,
    )
```

profile of v0, /device:TPU:33, one launch (start us, length us, event | category | flops | bytes accessed | tf_op | source)
XLA Modules:
  0.0 272.4 jit_solution(9714781316654998836)
XLA Ops:
  7.2 0.8 copy.22
  8.7 18.9 %all_to_all.26 = s32[128,1,32]{2,1,0:T(1,128)S(1)} all-to-all(s32[128,1,32]{2,1,0:T(1,128)S(1)} %bitcast.52), channel_id=1, replica_groups=mesh['rows'=32,'cols'=4] {'rows','cols'}, dimensions={0} | all-to-all | bytes 32768 | tf_op jit(solution)/shard_map/all_to_all | solution.py:124
  27.8 12.9 %gather_fusion = bf16[4096,128]{1,0:T(8,128)(2,1)S(1)} fusion(bf16[8192,128]{1,0:T(8,128)(2,1)} %param.7, s32[4096]{0:T(1024)S(1)} %broadcast_clamp_fusion), kind=kCustom, calls=%fused_computation | custom fusion | bytes 2113536 | tf_op jit(solution)/shard_map/jit(_take)/gather | solution.py:70
  40.7 0.8 broadcast_select_fusion
  41.5 21.9 %all_to_all.27 = bf16[128,32,128]{2,1,0:T(8,128)(2,1)S(1)} all-to-all(bf16[128,32,128]{2,1,0:T(8,128)(2,1)S(1)} %broadcast_select_fusion), channel_id=1, replica_groups=mesh['rows'=32,'cols'=4] {'rows','cols'}, dimensions={0} | all-to-all | bytes 2097152 | tf_op jit(solution)/shard_map/all_to_all | solution.py:75
  63.4 0.5 copy.18
  64.0 0.9 fusion.25
  64.9 1.4 fusion.36
  66.3 4.2 %fusion.9 = f32[2048,512]{1,0:T(8,128)} fusion(bf16[512,512]{1,0:T(8,128)(2,1)S(1)} %bitcast.50, f32[512,2048]{1,0:T(8,128)S(1)} %fusion.36, f32[2048]{0:T(1024)S(1)} %copy-done.6), kind=kOutput, calls=%fused_computation.18 | convolution fusion | flops 1084227584 | bytes 8921088 | tf_op jit(solution)/shard_map/while/body/eval_jaxpr/dot_general | solution.py:28
  70.5 3.6 %fusion.45 = (f32[2048]{0:T(1024)S(1)}, bf16[512,2048]{1,0:T(8,128)(2,1)S(1)}) fusion(f32[512,2048]{1,0:T(8,128)S(1)} %fusion.36, f32[2048]{0:T(1024)S(1)} %copy-done.6, bf16[512,512]{1,0:T(8,128)(2,1)S(1)} %bitcast.51, bf16[2048,512]{1,0:T(8,128)(2,1)S(1)} %copy-done.5), kind=kOutput, calls=%fused_computation.75 | convolution fusion | flops 1095759872 | bytes 8929280 | tf_op jit(solution)/shard_map/while/body/eval_jaxpr/dot_general | solution.py:20
  74.1 1.3 copy-done.2
  75.4 3.3 %fusion.28 = f32[512,2048]{1,0:T(8,128)} fusion(bf16[512,2048]{1,0:T(8,128)(2,1)S(1)} %get-tuple-element.53, bf16[512,512]{0,1:T(8,128)(2,1)S(1)} %get-tuple-element.50, f32[512]{0:T(512)S(1)} %copy-done.4, f32[512]{0:T(512)S(1)} %add_rsqrt_fusion), kind=kOutput, calls=%fused_computation.40 | convolution fusion | flops 1074790400 | bytes 6819840 | tf_op jit(solution)/shard_map/while/body/eval_jaxpr/dot_general | solution.py:31
  78.8 1.3 copy.21
  80.0 3.0 %fusion.24 = (f32[512]{0:T(512)S(1)}, f32[512]{0:T(512)S(1)}, f32[512,512]{0,1:T(8,128)S(1)}) fusion(bf16[512,512]{0,1:T(8,128)(2,1)S(1)} %get-tuple-element.50, f32[512]{0:T(512)S(1)} %add_rsqrt_fusion, f32[512]{0:T(512)S(1)} %copy-done.4, bf16[512,2048]{1,0:T(8,128)(2,1)S(1)} %copy-done, bf16[512,2048]{1,0:T(8,128)(2,1)} %copy-done.2), kind=kOutput, calls=%fused_computation.36 | convolution fusion | flops 1075575808 | bytes 5775360 | tf_op jit(solution)/shard_map/while/body/eval_jaxpr/dot_general | solution.py:35
  83.4 3.2 %fusion.10 = f32[32,32,4,128]{3,1,2,0:T(8,128)} fusion(f32[4,128,512,1]{2,1,0,3:T(8,128)S(1)} %bitcast.45, s32[32,32]{1,0:T(8,128)S(1)} %multiply_add_fusion.1, s32[512]{0:T(512)S(1)} %convert_add_fusion), kind=kOutput, calls=%fused_computation.19 | convolution fusion | flops 3221749760 | bytes 3151872 | tf_op jit(solution)/shard_map/dot_general | solution.py:108
  86.6 7.8 %all-to-all-start.2 = ((f32[128,32,128]{2,1,0:T(8,128)}), f32[128,32,128]{2,1,0:T(8,128)}, u32[]{:S(2)}, u32[]{:S(2)}) async-start(f32[128,32,128]{2,1,0:T(8,128)} %bitcast.42), calls=%async_computation.2 | async-start | bytes 4194304 | tf_op jit(solution)/shard_map/all_to_all | solution.py:117
  95.0 0.8 reduce.3
  95.9 84.5 %all-reduce = (f32[2048]{0:T(1024)S(1)}, f32[512]{0:T(512)S(1)}) all-reduce(f32[2048]{0:T(1024)S(1)} %get-tuple-element.52, f32[512]{0:T(512)S(1)} %get-tuple-element.29), channel_id=1, replica_groups=mesh['rows'=32,'cols'=4] {'rows','cols'}, use_global_device_ids=true, to_apply=%region_7.8 | all-reduce | flops 2560 | bytes 20480 | tf_op jit(solution)/shard_map/psum | solution.py:131
  180.4 0.6 broadcast_multiply_fusion.3
  181.0 0.6 broadcast_multiply_fusion.2
  181.6 25.4 %scatter_custom_fusion = f32[8192,128]{1,0:T(8,128)} fusion(s32[4096]{0:T(1024)S(1)} %bitcast.53, f32[4096,128]{1,0:T(8,128)} %bitcast.15, f32[]{:T(128)} %constant.40.clone.1), kind=kCustom, calls=%fused_computation.16 | custom fusion | flops 524288 | bytes 4194816 | tf_op jit(solution)/shard_map/scatter-add | solution.py:129
  207.0 51.1 %all-reduce.4.cloned.1.call-done = (f32[512,2048]{1,0:T(8,128)}, f32[2048,512]{1,0:T(8,128)}) async-done(((f32[512,2048]{1,0:T(8,128)}, f32[2048,512]{1,0:T(8,128)}), (f32[512,2048]{1,0:T(8,128)}, f32[2048,512]{1,0:T(8,128)})) %all-reduce.4.cloned.1.call-update) | async-done | bytes 8388624 | tf_op jit(solution)/shard_map/psum | solution.py:131
  258.0 4.9 %broadcast_multiply_fusion.1 = f32[512,2048]{1,0:T(8,128)} fusion(f32[512,2048]{1,0:T(8,128)} %get-tuple-element.33), kind=kLoop, calls=%fused_computation.12 | loop fusion | flops 1048576 | bytes 8388608 | tf_op jit(solution)/shard_map/mul | solution.py:133
  263.0 2.5 broadcast_multiply_fusion
  (33 shorter events, 1.8 us)
Async XLA Ops:
  7.2 57.7 %copy-start = (bf16[512,2048]{1,0:T(8,128)(2,1)S(1)}, bf16[512,2048]{1,0:T(8,128)(2,1)}, u32[]{:S(2)}) copy-start(bf16[512,2048]{1,0:T(8,128)(2,1)} %param.11) | copy-start | bytes 6291460
  7.2 250.9 %all-reduce.4.cloned.1.call-start = ((), (), s32[]{:S(2)}) async-start(), calls=%async_computation.3 | async-start | bytes 16777216 | tf_op jit(solution)/shard_map/psum | solution.py:131
  41.5 23.4 %copy-start.4 = (f32[512]{0:T(512)S(1)}, f32[512]{0:T(512)}, u32[]{:S(2)}) copy-start(f32[512]{0:T(512)} %param.10) | copy-start | bytes 6148
  64.9 1.4 copy-start.3
  64.9 1.4 copy-start.6
  66.3 4.2 %copy-start.5 = (bf16[2048,512]{1,0:T(8,128)(2,1)S(1)}, bf16[2048,512]{1,0:T(8,128)(2,1)}, u32[]{:S(2)}) copy-start(bf16[2048,512]{1,0:T(8,128)(2,1)} %param.13) | copy-start | bytes 6291460
  74.1 1.3 copy-start.2
  86.6 95.0 %all-to-all-start.2 = ((f32[128,32,128]{2,1,0:T(8,128)}), f32[128,32,128]{2,1,0:T(8,128)}, u32[]{:S(2)}, u32[]{:S(2)}) async-start(f32[128,32,128]{2,1,0:T(8,128)} %bitcast.42), calls=%async_computation.2 | async-start | bytes 4194304 | tf_op jit(solution)/shard_map/all_to_all | solution.py:117
  258.0 4.9 %copy-start.1 = (f32[2048,512]{1,0:T(8,128)S(1)}, f32[2048,512]{1,0:T(8,128)}, u32[]{:S(2)}) copy-start(f32[2048,512]{1,0:T(8,128)} %get-tuple-element.34) | copy-start | bytes 12582916
Sparse Core Ops, SparseCore 0:
  78.9 179.1 all-reduce.3
where the time goes:
time: 275 us; the launch traced here: 272 us
  blocking collectives  125 us (45%)
  waiting for transfers between devices  51.1 us (19%)
  other arithmetic  36.3 us (13%)
  matrix products  19.9 us (7%)
  local copies, waits for them, and re-layouts  17.6 us (6%)
  between operations  14.2 us (5%)
  starting transfers between devices  7.85 us (3%)
    psum x1, blocking collectives, local(): summed = lax.psum((g_in, g_bias, g_out, g_gain), ('rows', 'cols'))  84.5 us
    psum x1, waiting for transfers between devices, local(): summed = lax.psum((g_in, g_bias, g_out, g_gain), ('rows', 'cols'))  51.1 us
    scatter-add x1, other arithmetic, local(): table_grad = jnp.zeros((rows_dev, col_width), jnp.float32).at[arrived_off...  25.4 us
    all_to_all x1, blocking collectives, local(): lax.all_to_all(looked, ('rows', 'cols'), split_axis=0, concat_axis=0, til...  21.9 us
    all_to_all x1, blocking collectives, local(): lax.all_to_all(requests, ('rows', 'cols'), split_axis=0, concat_axis=0, t...  18.9 us
    gather x1, local copies, waits for them, and re-layouts, local(): jnp.take(table, lax.all_to_all(requests, ('rows', 'cols'), split_axis=0,...  12.9 us
    all_to_all x1, starting transfers between devices, local(): lax.all_to_all(payload.reshape(n_rows * n_cols, capacity, col_width), ('r...  7.81 us
  transfers between devices with their start and end apart: 2, of which 1 were waited for; matrix products, arithmetic and copies ran while one was open for 13% of the time, Pallas kernels for 0%

commit v1 on v0

v1 whole, which is shorter than its diff:
```python
import math

import jax
import jax.numpy as jnp
from jax import lax
from jax.experimental import pallas as pl
from jax.experimental.pallas import tpu as pltpu
from jax.sharding import Mesh
from jax.sharding import PartitionSpec as P

norm_eps = 1e-06
gelu_coef = 0.7978845608
bf16 = jnp.bfloat16
f32 = jnp.float32

N_X, N_Z, N_CORE, N_Y = 4, 4, 2, 4
N_XZ = N_X * N_Z
PEERS = ("x", "z", "y")
N_PEERS = N_XZ * N_Y
EVERY = ("x", "z", "core", "y")


def swap(a):
    return lax.ppermute(a, "core", [(0, 1), (1, 0)])


def exchange(a):
    return lax.all_to_all(a, PEERS, split_axis=0, concat_axis=0, tiled=True)


def by_core(core, own, other):
    return jnp.where(core == 0, jnp.stack([own, other]), jnp.stack([other, own]))


def finish_kernel(scale, core_ref, own_ref, other_ref, out_ref, in_ref):
    step = pl.program_id(0)

    def write(ref):
        for y in range(N_Y):
            out_ref[:, y * 128 : (y + 1) * 128] = ref[0, y, :64, :].astype(f32) * scale
            for part in range(2):
                lane = (y * 2 + part) * 128
                in_ref[:, lane : lane + 128] = (
                    ref[0, y, 64 + part * 32 : 96 + part * 32, :].astype(f32) * scale
                )

    @pl.when(step == 0)
    def _():
        write(own_ref)

    @pl.when(step == 1)
    def _():
        write(other_ref)


def finish(core, own, other, scale):
    n = N_XZ
    grid_spec = pltpu.PrefetchScalarGridSpec(
        num_scalar_prefetch=1,
        grid=(2, n),
        in_specs=[
            pl.BlockSpec((1, N_Y, 128, 128), lambda s, i, c: (jnp.where(s == 0, i, n - 1), 0, 0, 0)),
            pl.BlockSpec((1, N_Y, 128, 128), lambda s, i, c: (jnp.where(s == 0, 0, i), 0, 0, 0)),
        ],
        out_specs=[
            pl.BlockSpec((64, 512), lambda s, i, c: (jnp.where(s == 0, c[0], 1 - c[0]) * n + i, 0)),
            pl.BlockSpec((32, 1024), lambda s, i, c: (i, jnp.where(s == 0, c[0], 1 - c[0]))),
        ],
    )
    return pl.pallas_call(
        lambda *refs: finish_kernel(scale, *refs),
        grid_spec=grid_spec,
        out_shape=[
            jax.ShapeDtypeStruct((2048, 512), f32),
            jax.ShapeDtypeStruct((512, 2048), f32),
        ],
        name="finish",
    )(core.reshape(1), own, other)


def local(table, item_ids, cotangent, norm_gain, w_in, bias_in, w_out):
    core = lax.axis_index("core")
    rows_dev, col_width = table.shape
    width = N_Y * col_width
    own_ids = item_ids.reshape(-1)
    n_tok = own_ids.shape[0]
    n_ranges = N_XZ * N_CORE
    capacity = max(2, 2 * n_tok // n_ranges)
    n_slots = N_XZ * capacity
    half = w_in.shape[1] // 2

    ids = by_core(core, own_ids, swap(own_ids))
    own_cot = cotangent.reshape(n_tok, width)
    d_out = by_core(core, own_cot, swap(own_cot)).reshape(2 * n_tok, width)

    owners = ids // rows_dev
    offsets = ids - owners * rows_dev
    range_ids = jnp.arange(n_ranges, dtype=jnp.int32)
    onehot = (owners[:, :, None] == range_ids).astype(bf16)
    tok_ids = jnp.arange(n_tok, dtype=jnp.int32)
    lower = (tok_ids[:, None] >= tok_ids[None, :]).astype(bf16)
    running = jnp.einsum("ts,jsr->jtr", lower, onehot, preferred_element_type=f32)
    rank = (jnp.sum(running * onehot.astype(f32), axis=2) - 1.0).astype(jnp.int32)
    slot_of = jnp.where(owners % 2 == core, (owners // 2) * capacity + rank, -1)
    slot_ids = jnp.arange(n_slots, dtype=jnp.int32)
    slot_hit = slot_of[:, :, None] == slot_ids
    wanted = jnp.sum(jnp.where(slot_hit, offsets[:, :, None], 0), axis=1)
    wanted = jnp.transpose(wanted.reshape(2, N_XZ, capacity), (1, 0, 2))
    requests = jnp.broadcast_to(
        wanted.reshape(N_XZ, 1, 2 * capacity), (N_XZ, N_Y, 2 * capacity)
    ).reshape(N_PEERS, 2 * capacity)
    asked = exchange(requests)
    looked = jnp.take(table, asked, axis=0)
    fetched = exchange(looked)
    by_slot = jnp.transpose(
        fetched.reshape(N_XZ, N_Y, 2, capacity, col_width), (2, 0, 3, 1, 4)
    ).reshape(2, n_slots, width)
    hit = slot_hit.astype(bf16)
    part = (
        jnp.einsum("jts,jsw->jtw", hit, by_slot, preferred_element_type=f32)
        .astype(bf16)
        .reshape(2 * n_tok, width)
    )
    embedded = part + swap(part)

    w_in_half = lax.dynamic_slice_in_dim(w_in, core * half, half, axis=1)
    w_out_half = lax.dynamic_slice_in_dim(w_out, core * half, half, axis=0)
    bias_half = lax.dynamic_slice_in_dim(bias_in, core * half, half, axis=0)

    x_float = embedded.astype(f32)
    inv_rms = lax.rsqrt(jnp.mean(x_float * x_float, axis=-1, keepdims=True) + norm_eps)
    x_hat = x_float * inv_rms
    normed = (x_hat * norm_gain).astype(bf16)
    pre_act = jnp.dot(normed, w_in_half, preferred_element_type=f32) + bias_half
    tanh_part = jnp.tanh(gelu_coef * (pre_act + 0.044715 * pre_act * pre_act * pre_act))
    hidden = (0.5 * pre_act * (1.0 + tanh_part)).astype(bf16)
    d_act = lax.dot_general(
        d_out, w_out_half, (((1,), (1,)), ((), ())), preferred_element_type=f32
    )
    slope = 0.5 * (1.0 + tanh_part) + 0.5 * pre_act * (1.0 - tanh_part * tanh_part) * gelu_coef * (
        1.0 + 3.0 * 0.044715 * pre_act * pre_act
    )
    d_pre = d_act * slope
    d_pre_bf = d_pre.astype(bf16)
    part_norm = lax.dot_general(
        d_pre_bf, w_in_half, (((1,), (1,)), ((), ())), preferred_element_type=f32
    )
    other_norm = swap(part_norm.astype(bf16))
    g_out = lax.dot_general(hidden, d_out, (((0,), (0,)), ((), ())), preferred_element_type=f32)
    g_in = lax.dot_general(normed, d_pre_bf, (((0,), (0,)), ((), ())), preferred_element_type=f32)
    g_bias = jnp.sum(d_pre, axis=0)
    g_gain = jnp.sum(part_norm * x_hat, axis=0)
    d_norm = part_norm + other_norm.astype(f32)
    scaled = d_norm * norm_gain
    d_embed = inv_rms * (
        scaled - x_hat * jnp.mean(scaled * x_hat, axis=-1, keepdims=True)
    ) + d_out.astype(f32)

    slot_grad = jnp.einsum(
        "jts,jtw->jsw",
        hit,
        d_embed.astype(bf16).reshape(2, n_tok, width),
        preferred_element_type=f32,
    ).astype(bf16)
    to_slots = jnp.transpose(
        slot_grad.reshape(2, N_XZ, capacity, N_Y, col_width), (1, 3, 0, 2, 4)
    ).reshape(N_PEERS, 2 * capacity, col_width)
    to_out = jnp.transpose(g_out.astype(bf16).reshape(N_XZ, 64, N_Y, 128), (0, 2, 1, 3)).reshape(
        N_PEERS, 64, 128
    )
    to_in = jnp.transpose(
        g_in.astype(bf16).reshape(N_XZ, 32, N_Y, 2, 128), (0, 2, 3, 1, 4)
    ).reshape(N_PEERS, 64, 128)
    vec = jnp.concatenate([g_bias, g_gain]).astype(bf16).reshape(1, 12, 128)
    to_vec = jnp.broadcast_to(jnp.pad(vec, ((0, 0), (0, 4), (0, 0))), (N_PEERS, 16, 128))
    arrived = exchange(jnp.concatenate([to_slots, to_out, to_in, to_vec], axis=1))

    n_grad = 2 * capacity
    summed = jnp.sum(arrived[:, n_grad:].astype(f32), axis=0)
    share = summed[:128].astype(bf16)
    gathered = exchange(jnp.broadcast_to(share[None], (N_PEERS, 128, 128)))
    table_grad = (
        jnp.zeros((rows_dev, col_width), f32)
        .at[asked.reshape(-1)]
        .add(arrived[:, :n_grad].reshape(-1, col_width).astype(f32))
    )
    scale = 1.0 / math.sqrt(n_tok * N_PEERS * N_CORE)
    vec_sum = summed[128:140].reshape(-1)
    vec_other = swap(vec_sum)
    g_bias = by_core(core, vec_sum[:half], vec_other[:half]).reshape(-1)
    g_gain = vec_sum[half:] + vec_other[half:]
    own = gathered.reshape(N_XZ, N_Y, 128, 128)
    g_out, g_in = finish(core, own, swap(own), scale)
    return (table_grad, g_in, g_bias * scale, g_out, g_gain * scale)


def solution(mesh):
    pairs = Mesh(mesh.devices.reshape(N_X, N_Z, N_CORE, N_Y), EVERY)
    rows = ("x", "z", "core")
    return jax.shard_map(
        local,
        mesh=pairs,
        in_specs=(
            P(rows, "y"),
            P(EVERY, None),
            P(EVERY, None, None),
            P(),
            P(),
            P(),
            P(),
        ),
        out_specs=(P(rows, "y"), P(), P(), P(), P()),
        check_vma=False,
    )
```

time: 275 us -> 243 us (0.88)
  waiting for transfers between devices: 51.1 us -> 3.43 us
  Pallas kernels: 0 us -> 18.7 us
  local copies, waits for them, and re-layouts: 17.6 us -> 32.4 us
  between operations: 14.2 us -> 1.01 us
  blocking collectives: 125 us -> 122 us
    psum x1 -> x0, blocking collectives: 84.5 us -> none  [local(): summed = lax.psum((g_in, g_bias, g_out, g_gain), ('rows', 'cols'))]
    all_to_all x2 -> x4, blocking collectives: 40.8 us -> 122 us  [exchange(): return lax.all_to_all(a, PEERS, split_axis=0, concat_axis=0, tiled=True)]
    psum x1 -> x0, waiting for transfers between devices: 51.1 us -> none  [local(): summed = lax.psum((g_in, g_bias, g_out, g_gain), ('rows', 'cols'))]
    pallas_call x0 -> x1, Pallas kernels: none -> 18.7 us  [finish(): pl.pallas_call(lambda *refs: finish_kernel(scale, *refs), grid_spec=grid_...]
    reshape x1 -> x10, local copies, waits for them, and re-layouts: 0.09 us -> 12.9 us  [the longest x2 5.18 us: local(): g_in.astype(bf16).reshape(N_XZ, 32, N_Y, 2, 128)]
    mul x4 -> x1, other arithmetic: 8.63 us -> 0.58 us  [local(): return (table_grad, g_in, g_bias * scale, g_out, g_gain * scale)]
    all_to_all x1 -> x0, starting transfers between devices: 7.81 us -> none  [local(): lax.all_to_all(payload.reshape(n_rows * n_cols, capacity, col_width), ('r...]
    ppermute x0 -> x6, starting transfers between devices: none -> 6.32 us  [swap(): return lax.ppermute(a, 'core', [(0, 1), (1, 0)])]
  transfers between devices with their start and end apart: 2 -> 6, of which waited for: 1 -> 2; matrix products, arithmetic and copies ran while one was open for 13% -> 20% of each run, Pallas kernels for 0% -> 0%
where the time goes in v1:
time: 243 us; the launch traced here: 239 us
  blocking collectives  122 us (50%)
  other arithmetic  36.5 us (15%)
  local copies, waits for them, and re-layouts  32.4 us (13%)
  matrix products  19.5 us (8%)
  Pallas kernels  18.7 us (8%)
  starting transfers between devices  6.32 us (3%)
  waiting for transfers between devices  3.43 us (1%)
    all_to_all x4, blocking collectives, exchange(): return lax.all_to_all(a, PEERS, split_axis=0, concat_axis=0, tiled=True)  122 us
    scatter-add x1, other arithmetic, local(): table_grad = jnp.zeros((rows_dev, col_width), f32).at[asked.reshape(-1)]....  25.1 us
    pallas_call x1, Pallas kernels, finish(): pl.pallas_call(lambda *refs: finish_kernel(scale, *refs), grid_spec=grid_...  18.7 us
    gather x1, local copies, waits for them, and re-layouts, local(): looked = jnp.take(table, asked, axis=0)  12.9 us
    ppermute x6, starting transfers between devices, swap(): return lax.ppermute(a, 'core', [(0, 1), (1, 0)])  6.32 us
    reshape x2, local copies, waits for them, and re-layouts, local(): g_in.astype(bf16).reshape(N_XZ, 32, N_Y, 2, 128)  5.18 us
    dot_general x1, matrix products, local(): lax.dot_general(hidden, d_out, (((0,), (0,)), ((), ())), preferred_elemen...  5.08 us
  transfers between devices with their start and end apart: 6, of which 2 were waited for; matrix products, arithmetic and copies ran while one was open for 20% of the time, Pallas kernels for 0%

profile of v1, /device:TPU:33, one launch (start us, length us, event | category | flops | bytes accessed | tf_op | source)
XLA Modules:
  0.0 239.3 jit_solution(4170142306644749713)
XLA Ops:
  3.8 18.0 %all_to_all.30 = s32[64,1,64]{2,1,0:T(1,128)S(1)} all-to-all(s32[64,1,64]{2,1,0:T(1,128)S(1)} %bitcast.84), channel_id=1, replica_groups=mesh['x'=4,'z'=4,'core'=2,'y'=4] {'x','z','y'}, dimensions={0} | all-to-all | bytes 32768 | tf_op jit(solution)/shard_map/all_to_all | solution.py:28
  21.9 12.9 %gather_fusion = bf16[4096,128]{1,0:T(8,128)(2,1)S(1)} fusion(bf16[8192,128]{1,0:T(8,128)(2,1)} %param.7, s32[4096]{0:T(1024)S(1)} %broadcast_clamp_fusion), kind=kCustom, calls=%fused_computation | custom fusion | bytes 2113536 | tf_op jit(solution)/shard_map/jit(_take)/gather | solution.py:113
  35.5 21.0 %all_to_all.31 = bf16[64,64,128]{2,1,0:T(8,128)(2,1)S(1)} all-to-all(bf16[64,64,128]{2,1,0:T(8,128)(2,1)S(1)} %broadcast_select_fusion), channel_id=1, replica_groups=mesh['x'=4,'z'=4,'core'=2,'y'=4] {'x','z','y'}, dimensions={0} | all-to-all | bytes 2097152 | tf_op jit(solution)/shard_map/all_to_all | solution.py:28
  58.5 2.0 fusion.25
  60.5 2.9 %collective-permute-start.1 = (bf16[1024,512]{1,0:T(8,128)(2,1)S(1)}, bf16[1024,512]{1,0:T(8,128)(2,1)}, u32[]{:S(2)}, u32[]{:S(2)}) collective-permute-start(bf16[1024,512]{1,0:T(8,128)(2,1)S(1)} %bitcast.79), channel_id=1, source_target_pairs={{0,4},{4,0},{1,5},{5,1},{2,6},{6,2},{3,7},{7,3},{8,12},{12,8},{9,1... | collective-permute-start | bytes 3145736 | tf_op jit(solution)/shard_map/ppermute | solution.py:24
  63.6 3.3 %collective-permute-done.2 = bf16[512,512]{1,0:T(8,128)(2,1)} collective-permute-done((bf16[512,512]{1,0:T(8,128)(2,1)}, bf16[512,512]{1,0:T(8,128)(2,1)}, u32[]{:S(2)}, u32[]{:S(2)}) %collective-permute-start.2) | collective-permute-done | bytes 524320 | tf_op jit(solution)/shard_map/ppermute | solution.py:24
  66.8 1.8 maximum_select_fusion
  68.6 2.4 fusion.17
  72.6 3.8 %fusion.55 = (bf16[1024]{0:T(1024)(128)(2,1)S(1)}, bf16[1024,1024]{1,0:T(8,128)(2,1)S(1)}) fusion(f32[1024,1024]{1,0:T(8,128)S(1)} %fusion.38, f32[1024]{0:T(1024)S(1)} %dynamic_slice.11, bf16[1024,512]{1,0:T(8,128)(2,1)S(1)} %bitcast.74, bf16[2048,512]{1,0:T(8,128)(2,1)S(1)} %copy-done.14, s32[]{:T(128)S(6)} %select_n.134), kind=kOutput, calls=%fused_computation.98 | convolution fusion | flops 1095760896 | bytes 8394756 | tf_op jit(solution)/shard_map/dot_general | solution.py:137
  76.4 3.0 %fusion.54 = (bf16[1024,512]{1,0:T(8,128)(2,1)}, f32[1024,512]{1,0:T(8,128)}) fusion(bf16[512,2048]{1,0:T(8,128)(2,1)S(1)} %copy-done, s32[]{:T(128)S(6)} %select_n.134, bf16[1024,1024]{1,0:T(8,128)(2,1)S(1)} %get-tuple-element.18), kind=kOutput, calls=%fused_computation.97 | convolution fusion | flops 1074266112 | bytes 6291460 | tf_op jit(solution)/shard_map/dot_general | solution.py:145
  79.7 2.4 %convolution_convert_fusion = bf16[512,1024]{1,0:T(8,128)(2,1)} fusion(bf16[1024,1024]{1,0:T(8,128)(2,1)S(1)} %get-tuple-element.18, bf16[1024,512]{1,0:T(8,128)(2,1)S(1)} %get-tuple-element.12, f32[512]{0:T(512)S(1)} %copy-done.12, f32[1024]{0:T(1024)S(1)} %add_rsqrt_fusion), kind=kOutput, calls=%fused_computation.39 | convolution fusion | flops 1076363264 | bytes 4200448 | tf_op jit(solution)/shard_map/dot_general | solution.py:150
  82.2 2.6 %reshape.319 = bf16[16,32,4,2,128]{4,3,2,1,0:T(2,128)(2,1)} reshape(bf16[512,1024]{1,0:T(8,128)(2,1)} %convolution_convert_fusion) | data formatting | bytes 2097152 | tf_op jit(solution)/shard_map/reshape | solution.py:172
  84.7 2.6 %copy.29 = bf16[16,32,4,2,128]{4,1,3,2,0:T(8,128)(2,1)} copy(bf16[16,32,4,2,128]{4,3,2,1,0:T(2,128)(2,1)} %reshape.319) | data formatting | bytes 2097152 | tf_op jit(solution)/shard_map/reshape | solution.py:172
  87.3 5.1 %fusion.24 = bf16[1024,512]{1,0:T(8,128)(2,1)} fusion(bf16[1024,512]{1,0:T(8,128)(2,1)S(1)} %bitcast.75, f32[1024,1024]{1,0:T(8,128)} %copy-done.3, f32[1024]{0:T(1024)S(1)} %dynamic_slice.11), kind=kOutput, calls=%fused_computation.36 | convolution fusion | flops 1084751872 | bytes 6295552 | tf_op jit(solution)/shard_map/dot_general | solution.py:149
  92.4 2.1 reshape.317
  94.6 2.6 %copy.28 = bf16[16,64,4,128]{3,1,2,0:T(8,128)(2,1)} copy(bf16[16,64,4,128]{3,2,1,0:T(4,128)(2,1)} %reshape.317) | data formatting | bytes 2097152 | tf_op jit(solution)/shard_map/reshape | solution.py:168
  97.2 2.2 fusion.11
  99.4 2.0 fusion.15
  101.4 1.7 fusion.26
  106.2 47.4 %all_to_all.32 = bf16[64,208,128]{2,1,0:T(8,128)(2,1)S(1)} all-to-all(bf16[64,208,128]{2,1,0:T(8,128)(2,1)S(1)} %pad_maximum_fusion), channel_id=1, replica_groups=mesh['x'=4,'z'=4,'core'=2,'y'=4] {'x','z','y'}, dimensions={0} | all-to-all | bytes 6815744 | tf_op jit(solution)/shard_map/all_to_all | solution.py:28
  155.4 35.2 %all_to_all.33 = bf16[64,128,128]{2,1,0:T(8,128)(2,1)} all-to-all(bf16[64,128,128]{2,1,0:T(8,128)(2,1)S(1)} %broadcast_in_dim.69), channel_id=1, replica_groups=mesh['x'=4,'z'=4,'core'=2,'y'=4] {'x','z','y'}, dimensions={0} | all-to-all | bytes 4194304 | tf_op jit(solution)/shard_map/all_to_all | solution.py:28
  190.6 2.2 collective-permute-start.4
  194.3 25.1 %scatter_custom_fusion = f32[8192,128]{1,0:T(8,128)} fusion(s32[4096]{0:T(1024)S(1)} %bitcast.86, bf16[4096,128]{1,0:T(8,128)(2,1)S(1)} %bitcast.71, f32[]{:T(128)} %constant.71.clone.1), kind=kCustom, calls=%fused_computation.27 | custom fusion | flops 1048576 | bytes 5242884 | tf_op jit(solution)/shard_map/scatter-add | solution.py:185
  220.6 18.7 %finish.1 = (f32[2048,512]{1,0:T(8,128)}, f32[512,2048]{1,0:T(8,128)}) custom-call(s32[1]{0:T(128)} %bitcast.26.refs_0_, bf16[16,4,128,128]{3,2,1,0:T(8,128)(2,1)} %bitcast.27.refs_1_, bf16[16,4,128,128]{3,2,1,0:T(8,128)(2,1)} %collective-permute-done.4.refs_2_), custom_call_target="tpu_custom_call" | custom-call | tf_op jit(solution)/shard_map/finish/pallas_call | solution.py:70
  (82 shorter events, 15.6 us)
Async XLA Ops:
  0.6 70.4 %copy-start = (bf16[512,2048]{1,0:T(8,128)(2,1)S(1)}, bf16[512,2048]{1,0:T(8,128)(2,1)}, u32[]{:S(2)}) copy-start(bf16[512,2048]{1,0:T(8,128)(2,1)} %param.11) | copy-start | bytes 6291460
  1.5 1.5 collective-permute-start
  57.3 6.3 %copy-start.13 = (f32[2048]{0:T(1024)S(1)}, f32[2048]{0:T(1024)}, u32[]{:S(2)}) copy-start(f32[2048]{0:T(1024)} %param.12) | copy-start | bytes 24580
  60.5 8.1 %copy-start.9 = (bf16[2,512,512]{2,1,0:T(8,128)(2,1)}, bf16[2,512,512]{2,1,0:T(8,128)(2,1)S(1)}, u32[]{:S(2)}) copy-start(bf16[2,512,512]{2,1,0:T(8,128)(2,1)S(1)} %fusion.25) | copy-start | bytes 3145732
  60.5 8.1 %collective-permute-start.1 = (bf16[1024,512]{1,0:T(8,128)(2,1)S(1)}, bf16[1024,512]{1,0:T(8,128)(2,1)}, u32[]{:S(2)}, u32[]{:S(2)}) collective-permute-start(bf16[1024,512]{1,0:T(8,128)(2,1)S(1)} %bitcast.79), channel_id=1, source_target_pairs={{0,4},{4,0},{1,5},{5,1},{2,6},{6,2},{3,7},{7,3},{8,12},{12,8},{9,1... | collective-permute-start | bytes 3145736 | tf_op jit(solution)/shard_map/ppermute | solution.py:24
  63.5 3.4 %collective-permute-start.2 = (bf16[512,512]{1,0:T(8,128)(2,1)}, bf16[512,512]{1,0:T(8,128)(2,1)}, u32[]{:S(2)}, u32[]{:S(2)}) collective-permute-start(bf16[512,512]{1,0:T(8,128)(2,1)} %bitcast.13), channel_id=1, source_target_pairs={{0,4},{4,0},{1,5},{5,1},{2,6},{6,2},{3,7},{7,3},{8,12},{12,8},{9,1... | collective-permute-start | bytes 1572872 | tf_op jit(solution)/shard_map/ppermute | solution.py:24
  68.6 3.8 %copy-start.4 = (bf16[2,512,512]{2,1,0:T(8,128)(2,1)}, bf16[2,512,512]{2,1,0:T(8,128)(2,1)S(1)}, u32[]{:S(2)}) copy-start(bf16[2,512,512]{2,1,0:T(8,128)(2,1)S(1)} %maximum_select_fusion) | copy-start | bytes 3145732
  68.6 2.4 %copy-start.12 = (f32[512]{0:T(512)S(1)}, f32[512]{0:T(512)}, u32[]{:S(2)}) copy-start(f32[512]{0:T(512)} %param.10) | copy-start | bytes 6148
  71.0 1.6 copy-start.14
  72.3 4.1 %copy-start.3 = (f32[1024,1024]{1,0:T(8,128)}, f32[1024,1024]{1,0:T(8,128)S(1)}, u32[]{:S(2)}) copy-start(f32[1024,1024]{1,0:T(8,128)S(1)} %fusion.38) | copy-start | bytes 12582916
  79.4 17.8 %collective-permute-start.3 = (bf16[1024,512]{1,0:T(8,128)(2,1)}, bf16[1024,512]{1,0:T(8,128)(2,1)}, u32[]{:S(2)}, u32[]{:S(2)}) collective-permute-start(bf16[1024,512]{1,0:T(8,128)(2,1)} %get-tuple-element.15), channel_id=1, source_target_pairs={{0,4},{4,0},{1,5},{5,1},{2,6},{6,2},{3,7},{7,3},{8,12},{12,8},{9,1... | collective-permute-start | bytes 3145736 | tf_op jit(solution)/shard_map/ppermute | solution.py:24
  84.7 2.6 %copy-start.5 = (bf16[2,512,512]{2,1,0:T(8,128)(2,1)S(1)}, bf16[2,512,512]{2,1,0:T(8,128)(2,1)}, u32[]{:S(2)}) copy-start(bf16[2,512,512]{2,1,0:T(8,128)(2,1)} %copy-done.4) | copy-start | bytes 3145732
  94.5 2.6 %copy-start.2 = (f32[1024,512]{1,0:T(8,128)S(1)}, f32[1024,512]{1,0:T(8,128)}, u32[]{:S(2)}) copy-start(f32[1024,512]{1,0:T(8,128)} %get-tuple-element.16) | copy-start | bytes 6291460
  97.2 2.2 copy-start.6
  104.4 1.2 copy-start.7
  104.5 1.5 copy-start.8
  153.6 1.8 copy-start.1
  154.0 40.2 %copy-start.10 = (f32[144,128]{1,0:T(8,128)}, f32[144,128]{1,0:T(8,128)S(1)}, u32[]{:S(2)}) copy-start(f32[144,128]{1,0:T(8,128)S(1)} %convert_reduce_fusion) | copy-start | bytes 221188
  190.6 3.7 %slice-start = ((bf16[64,208,128]{2,1,0:T(8,128)(2,1)}), bf16[64,64,128]{2,1,0:T(8,128)(2,1)S(1)}, s32[]{:S(2)}) async-start(bf16[64,208,128]{2,1,0:T(8,128)(2,1)} %copy-done.1), calls=%async_computation.4 | async-start | bytes 2097152 | tf_op jit(solution)/shard_map/slice | solution.py:185
  190.6 30.0 %collective-permute-start.4 = (bf16[16,4,128,128]{3,2,1,0:T(8,128)(2,1)}, bf16[16,4,128,128]{3,2,1,0:T(8,128)(2,1)}, u32[]{:S(2)}, u32[]{:S(2)}) collective-permute-start(bf16[16,4,128,128]{3,2,1,0:T(8,128)(2,1)} %bitcast.27.refs_1_), channel_id=1, source_target_pairs={{0,4},{4,0},{1,5},{5,1},{2,6},{6,2},{3,7},{7,3},{8,12},{12,8},{9,1... | collective-permute-start | bytes 6291464 | tf_op jit(solution)/shard_map/ppermute | solution.py:24
  194.1 25.3 %collective-permute-start.5 = (f32[1536]{0:T(1024)S(1)}, f32[1536]{0:T(1024)S(1)}, u32[]{:S(2)}, u32[]{:S(2)}) collective-permute-start(f32[1536]{0:T(1024)S(1)} %slice_bitcast_fusion), channel_id=1, source_target_pairs={{0,4},{4,0},{1,5},{5,1},{2,6},{6,2},{3,7},{7,3},{8,12},{12,8},{9,1... | collective-permute-start | bytes 18440 | tf_op jit(solution)/shard_map/ppermute | solution.py:24
  194.2 25.2 %slice-start.1 = ((f32[144,128]{1,0:T(8,128)}), f32[8,128]{1,0:T(8,128)S(1)}, s32[]{:S(2)}) async-start(f32[144,128]{1,0:T(8,128)} %copy-done.10), calls=%async_computation.5 | async-start | bytes 8192 | tf_op jit(solution)/shard_map/slice | solution.py:190
  194.2 25.8 %copy-start.11 = (f32[144,128]{1,0:T(8,128)S(1)}, f32[144,128]{1,0:T(8,128)}, u32[]{:S(2)}) copy-start(f32[144,128]{1,0:T(8,128)} %copy-done.10) | copy-start | bytes 221188

commit v2 on v1

v2 whole, which is shorter than its diff:
```python
import math

import jax
import jax.numpy as jnp
from jax import lax
from jax.experimental import pallas as pl
from jax.experimental.pallas import tpu as pltpu
from jax.sharding import Mesh
from jax.sharding import PartitionSpec as P

norm_eps = 1e-06
gelu_coef = 0.7978845608
bf16 = jnp.bfloat16
f32 = jnp.float32
i32 = jnp.int32

N_X, N_Z, N_CORE, N_Y = 4, 4, 2, 4
N_XZ = N_X * N_Z
PEERS = ("x", "z", "y")
N_PEERS = N_XZ * N_Y
EVERY = ("x", "z", "core", "y")

TOK = 512
D = 512
HALF = 1024
LANES = 128
CAP = 32
PAIR_CAP = 2 * CAP
N_SLOTS = N_XZ * CAP
ROWS = 8192
N_REQ = N_PEERS * PAIR_CAP
N_W = 144


def swap(a):
    return lax.ppermute(a, "core", [(0, 1), (1, 0)])


def exchange(a):
    return lax.all_to_all(a, PEERS, split_axis=0, concat_axis=0, tiled=True)


def params(mib):
    return pltpu.CompilerParams(vmem_limit_bytes=mib << 20)


def whole(shape, space=pltpu.VMEM):
    return pl.BlockSpec(shape, lambda *_: (0,) * len(shape), memory_space=space)


def gather_kernel(asked, table_ref, out_ref, wide, picked):
    step = 1024

    def widen(i, carry):
        rows = pl.ds(pl.multiple_of(i * step, step), step)
        wide[rows, :] = table_ref[rows, :].astype(f32)
        return carry

    lax.fori_loop(0, ROWS // step, widen, 0)
    unroll = 16

    def pick(i, carry):
        base = pl.multiple_of(i * unroll, unroll)
        for u in range(unroll):
            picked[pl.ds(base + u, 1), :] = wide[pl.ds(asked[base + u], 1), :]
        return carry

    lax.fori_loop(0, N_REQ // unroll, pick, 0)

    def narrow(i, carry):
        rows = pl.ds(pl.multiple_of(i * 512, 512), 512)
        out_ref[pl.ds(i * 8, 8)] = picked[rows, :].astype(bf16).reshape(8, PAIR_CAP, LANES)
        return carry

    lax.fori_loop(0, N_REQ // 512, narrow, 0)


def gather_rows(asked, table):
    return pl.pallas_call(
        gather_kernel,
        grid_spec=pltpu.PrefetchScalarGridSpec(
            num_scalar_prefetch=1,
            grid=(1,),
            in_specs=[whole((ROWS, LANES))],
            out_specs=whole((N_PEERS, PAIR_CAP, LANES)),
            scratch_shapes=[pltpu.VMEM((ROWS, LANES), f32), pltpu.VMEM((N_REQ, LANES), f32)],
        ),
        out_shape=jax.ShapeDtypeStruct((N_PEERS, PAIR_CAP, LANES), bf16),
        compiler_params=params(24),
        name="gather_rows",
    )(asked, table)


def block_kernel(
    core,
    slot_own,
    slot_other,
    got_own,
    got_other,
    cot_own,
    cot_other,
    gain_ref,
    w_in,
    bias_ref,
    w_out,
    emb_ref,
    part_ref,
    send_ref,
    w_ref,
    by_slot,
    normed_s,
    hidden_s,
    d_pre_s,
    bias_acc,
    gain_acc,
    d_out_s,
):
    for j in range(2):
        for y in range(N_Y):
            lanes = slice(y * LANES, (y + 1) * LANES)
            by_slot[j, :N_SLOTS, lanes] = got_own[:, y, j * CAP : (j + 1) * CAP, :].reshape(
                N_SLOTS, LANES
            )
            k = 1 - j
            by_slot[j, N_SLOTS:, lanes] = got_other[:, y, k * CAP : (k + 1) * CAP, :].reshape(
                N_SLOTS, LANES
            )
    d_out_s[:TOK, :] = cot_own[...]
    d_out_s[TOK:, :] = cot_other[...]
    bias_acc[...] = jnp.zeros_like(bias_acc)
    gain_acc[...] = jnp.zeros_like(gain_acc)
    gain = gain_ref[...]
    bias = bias_ref[...]
    chunk = 256
    nt = (((1,), (1,)), ((), ()))
    tn = (((0,), (0,)), ((), ()))
    slot_ids = lax.broadcasted_iota(i32, (chunk, N_SLOTS), 1)

    def one_chunk(i, carry):
        rows = pl.ds(pl.multiple_of(i * chunk, chunk), chunk)
        hit_own = (slot_own[rows, :] == slot_ids).astype(f32).astype(bf16)
        hit_other = (slot_other[rows, :] == slot_ids).astype(f32).astype(bf16)
        j = i // (TOK // chunk)
        emb = jnp.dot(hit_own, by_slot[j, :N_SLOTS, :], preferred_element_type=f32) + jnp.dot(
            hit_other, by_slot[j, N_SLOTS:, :], preferred_element_type=f32
        )
        emb_ref[rows, :] = emb.astype(bf16)
        inv_rms = lax.rsqrt(jnp.mean(emb * emb, axis=-1, keepdims=True) + norm_eps)
        x_hat = emb * inv_rms
        normed = (x_hat * gain).astype(bf16)
        normed_s[rows, :] = normed
        pre = jnp.dot(normed, w_in[...], preferred_element_type=f32) + bias
        square = pre * pre
        tanh_part = jnp.tanh(gelu_coef * (pre + 0.044715 * (square * pre)))
        gate = 0.5 * (1.0 + tanh_part)
        hidden_s[rows, :] = (pre * gate).astype(bf16)
        slope = gate + 0.5 * pre * (1.0 - tanh_part * tanh_part) * (
            gelu_coef + (gelu_coef * 3.0 * 0.044715) * square
        )
        d_act = lax.dot_general(d_out_s[rows, :], w_out[...], nt, preferred_element_type=f32)
        d_pre = d_act * slope
        d_pre_bf = d_pre.astype(bf16)
        d_pre_s[rows, :] = d_pre_bf
        bias_acc[...] += jnp.sum(d_pre.reshape(chunk // 8, 8, HALF), axis=0)
        part = lax.dot_general(d_pre_bf, w_in[...], nt, preferred_element_type=f32)
        part_ref[rows, :] = part
        send_ref[rows, :] = part.astype(bf16)
        gain_acc[...] += jnp.sum((part * x_hat).reshape(chunk // 8, 8, D), axis=0)
        return carry

    lax.fori_loop(0, 2 * TOK // chunk, one_chunk, 0)

    def one_tile(i, carry):
        cols = pl.ds(pl.multiple_of(i * 256, 256), 256)
        g_out = lax.dot_general(
            hidden_s[:, cols], d_out_s[...], tn, preferred_element_type=f32
        ).astype(bf16)
        for y in range(N_Y):
            w_ref[pl.ds(i * 4, 4), y, 0:64, :] = g_out[:, y * LANES : (y + 1) * LANES].reshape(
                4, 64, LANES
            )
        g_in = lax.dot_general(
            normed_s[...], d_pre_s[:, cols], tn, preferred_element_type=f32
        ).astype(bf16)
        for p in range(2):
            w_ref[:, i, 64 + p * 32 : 96 + p * 32, :] = g_in[
                :, p * LANES : (p + 1) * LANES
            ].reshape(N_XZ, 32, LANES)
        return carry

    lax.fori_loop(0, HALF // 256, one_tile, 0)
    g_bias = jnp.sum(bias_acc[...], axis=0, keepdims=True)
    g_gain = jnp.sum(gain_acc[...], axis=0, keepdims=True)
    pieces = [g_bias[:, r * LANES : (r + 1) * LANES] for r in range(HALF // LANES)]
    pieces += [g_gain[:, r * LANES : (r + 1) * LANES] for r in range(D // LANES)]
    pieces += [jnp.zeros((4, LANES), f32)]
    vec = jnp.concatenate(pieces, axis=0).astype(bf16)

    def one_peer(i, carry):
        for y in range(N_Y):
            w_ref[i, y, 128:144, :] = vec
        return carry

    lax.fori_loop(0, N_XZ, one_peer, 0)


def block(core, slot_own, slot_other, got_own, got_other, cot_own, cot_other, gain, w_in, bias, w_out):
    got = (N_XZ, N_Y, PAIR_CAP, LANES)
    return pl.pallas_call(
        block_kernel,
        grid_spec=pltpu.PrefetchScalarGridSpec(
            num_scalar_prefetch=1,
            grid=(1,),
            in_specs=[
                whole((2 * TOK, 1)),
                whole((2 * TOK, 1)),
                whole(got),
                whole(got),
                whole((TOK, D)),
                whole((TOK, D)),
                whole((1, D)),
                pl.BlockSpec((D, HALF), lambda i, c: (0, c[0])),
                pl.BlockSpec((1, HALF), lambda i, c: (0, c[0])),
                pl.BlockSpec((HALF, D), lambda i, c: (c[0], 0)),
            ],
            out_specs=[
                whole((2 * TOK, D)),
                whole((2 * TOK, D)),
                whole((2 * TOK, D)),
                whole((N_XZ, N_Y, N_W, LANES)),
            ],
            scratch_shapes=[
                pltpu.VMEM((2, 2 * N_SLOTS, D), bf16),
                pltpu.VMEM((2 * TOK, D), bf16),
                pltpu.VMEM((2 * TOK, HALF), bf16),
                pltpu.VMEM((2 * TOK, HALF), bf16),
                pltpu.VMEM((8, HALF), f32),
                pltpu.VMEM((8, D), f32),
                pltpu.VMEM((2 * TOK, D), bf16),
            ],
        ),
        out_shape=[
            jax.ShapeDtypeStruct((2 * TOK, D), bf16),
            jax.ShapeDtypeStruct((2 * TOK, D), f32),
            jax.ShapeDtypeStruct((2 * TOK, D), bf16),
            jax.ShapeDtypeStruct((N_XZ, N_Y, N_W, LANES), bf16),
        ],
        compiler_params=params(48),
        name="block",
    )(core, slot_own, slot_other, got_own, got_other, cot_own, cot_other, gain, w_in, bias, w_out)


def pack_kernel(slot_ref, part_ref, other_ref, emb_ref, gain_ref, cot_own, cot_other, w_ref, out_ref):
    out_ref[:, :, PAIR_CAP:, :] = w_ref[...]
    gain = gain_ref[...]
    slot_ids = lax.broadcasted_iota(i32, (N_SLOTS, TOK), 0)
    for j in range(2):
        rows = slice(j * TOK, (j + 1) * TOK)
        theirs = slice((1 - j) * TOK, (2 - j) * TOK)
        emb = emb_ref[rows, :].astype(f32)
        inv_rms = lax.rsqrt(jnp.mean(emb * emb, axis=-1, keepdims=True) + norm_eps)
        x_hat = emb * inv_rms
        scaled = (part_ref[rows, :] + other_ref[theirs, :].astype(f32)) * gain
        d_out = (cot_own if j == 0 else cot_other)[...].astype(f32)
        d_embed = (
            inv_rms * (scaled - x_hat * jnp.mean(scaled * x_hat, axis=-1, keepdims=True)) + d_out
        ).astype(bf16)
        hit = (slot_ids == slot_ref[j : j + 1, :]).astype(f32).astype(bf16)
        grads = jnp.dot(hit, d_embed, preferred_element_type=f32).astype(bf16)
        for y in range(N_Y):
            out_ref[:, y, j * CAP : (j + 1) * CAP, :] = grads[
                :, y * LANES : (y + 1) * LANES
            ].reshape(N_XZ, CAP, LANES)


def pack(slot_row, part, other, emb, gain, cot_own, cot_other, w_part):
    return pl.pallas_call(
        pack_kernel,
        out_shape=jax.ShapeDtypeStruct((N_XZ, N_Y, PAIR_CAP + N_W, LANES), bf16),
        compiler_params=params(40),
        name="pack",
    )(slot_row, part, other, emb, gain, cot_own, cot_other, w_part)


N_ACC = 2


def scatter_kernel(asked, arrived_ref, out_ref, grads, *accs):
    zero = jnp.zeros((512, LANES), f32)

    def clear(i, carry):
        rows = pl.ds(pl.multiple_of(i * 512, 512), 512)
        for acc in (out_ref,) + accs:
            acc[rows, :] = zero
        return carry

    lax.fori_loop(0, ROWS // 512, clear, 0)

    def widen(i, carry):
        rows = pl.ds(pl.multiple_of(i * 512, 512), 512)
        grads[rows, :] = arrived_ref[pl.ds(i * 8, 8)].astype(f32).reshape(512, LANES)
        return carry

    lax.fori_loop(0, N_REQ // 512, widen, 0)
    unroll = 8
    share = N_REQ // N_ACC

    def add(i, carry):
        base = pl.multiple_of(i * unroll, unroll)
        for u in range(unroll):
            for a, acc in enumerate((out_ref,) + accs):
                row = base + (a * share + u)
                at = pl.ds(asked[row], 1)
                acc[at, :] = acc[at, :] + grads[pl.ds(row, 1), :]
        return carry

    lax.fori_loop(0, share // unroll, add, 0)

    def merge(i, carry):
        rows = pl.ds(pl.multiple_of(i * 512, 512), 512)
        total = out_ref[rows, :]
        for acc in accs:
            total = total + acc[rows, :]
        out_ref[rows, :] = total
        return carry

    lax.fori_loop(0, ROWS // 512, merge, 0)


def scatter_rows(asked, arrived):
    return pl.pallas_call(
        scatter_kernel,
        grid_spec=pltpu.PrefetchScalarGridSpec(
            num_scalar_prefetch=1,
            grid=(1,),
            in_specs=[whole((N_PEERS, PAIR_CAP, LANES))],
            out_specs=whole((ROWS, LANES)),
            scratch_shapes=[pltpu.VMEM((N_REQ, LANES), f32)]
            + [pltpu.VMEM((ROWS, LANES), f32)] * (N_ACC - 1),
        ),
        out_shape=jax.ShapeDtypeStruct((ROWS, LANES), f32),
        compiler_params=params(28),
        cost_estimate=pl.CostEstimate(flops=10**10, bytes_accessed=10**7, transcendentals=0),
        name="scatter_rows",
    )(asked, arrived)


def finish_kernel(scale, core_ref, own_ref, other_ref, out_ref, in_ref):
    n = own_ref.shape[0]

    def write(ref):
        for y in range(N_Y):
            out_ref[:, y * LANES : (y + 1) * LANES] = (
                ref[:, y, :64, :].astype(f32) * scale
            ).reshape(n * 64, LANES)
            for p in range(2):
                lane = (y * 2 + p) * LANES
                in_ref[:, lane : lane + LANES] = (
                    ref[:, y, 64 + p * 32 : 96 + p * 32, :].astype(f32) * scale
                ).reshape(n * 32, LANES)

    @pl.when(pl.program_id(0) == 0)
    def _():
        write(own_ref)

    @pl.when(pl.program_id(0) == 1)
    def _():
        write(other_ref)


def finish(core, own, other, scale):
    n, wide = 4, 4

    def half_of(s, c):
        return jnp.where(s == 0, c[0], 1 - c[0])

    return pl.pallas_call(
        lambda *refs: finish_kernel(scale, *refs),
        grid_spec=pltpu.PrefetchScalarGridSpec(
            num_scalar_prefetch=1,
            grid=(2, n),
            in_specs=[
                pl.BlockSpec(
                    (wide, N_Y, 128, LANES), lambda s, i, c: (jnp.where(s == 0, i, n - 1), 0, 0, 0)
                ),
                pl.BlockSpec(
                    (wide, N_Y, 128, LANES), lambda s, i, c: (jnp.where(s == 0, 0, i), 0, 0, 0)
                ),
            ],
            out_specs=[
                pl.BlockSpec((64 * wide, D), lambda s, i, c: (half_of(s, c) * n + i, 0)),
                pl.BlockSpec((32 * wide, HALF), lambda s, i, c: (i, half_of(s, c))),
            ],
        ),
        out_shape=[
            jax.ShapeDtypeStruct((2 * HALF, D), f32),
            jax.ShapeDtypeStruct((D, 2 * HALF), f32),
        ],
        compiler_params=params(16),
        name="finish",
    )(core, own, other)


def local(table, item_ids, cotangent, norm_gain, w_in, bias_in, w_out):
    core = lax.axis_index("core").astype(i32)
    core_arr = core.reshape(1)
    own_ids = item_ids.reshape(-1)
    cot_own = cotangent.reshape(TOK, D)
    cot_other = swap(cot_own)
    ids = jnp.stack([own_ids, swap(own_ids)])

    owners = ids // ROWS
    offsets = ids - owners * ROWS
    range_ids = jnp.arange(N_XZ * N_CORE, dtype=i32)
    onehot = (owners[:, :, None] == range_ids).astype(bf16)
    tok_ids = jnp.arange(TOK, dtype=i32)
    lower = (tok_ids[:, None] >= tok_ids[None, :]).astype(bf16)
    running = jnp.einsum("ts,jsr->jtr", lower, onehot, preferred_element_type=f32)
    rank = (jnp.sum(running * onehot.astype(f32), axis=2) - 1.0).astype(i32)
    slot = (owners // 2) * CAP + rank
    is_own = owners % 2 == core
    slot_own = jnp.where(is_own, slot, -1)
    slot_other = jnp.where(is_own, -1, slot)
    slot_ids = jnp.arange(N_SLOTS, dtype=i32)
    wanted = jnp.sum(
        jnp.where(slot_own[:, :, None] == slot_ids, offsets[:, :, None], 0), axis=1
    )
    wanted = jnp.transpose(wanted.reshape(2, N_XZ, CAP), (1, 0, 2))
    requests = jnp.broadcast_to(
        wanted.reshape(N_XZ, 1, PAIR_CAP), (N_XZ, N_Y, PAIR_CAP)
    ).reshape(N_PEERS, PAIR_CAP)
    requests, cot_other, slot_own, slot_other = lax.optimization_barrier(
        (requests, cot_other, slot_own, slot_other)
    )
    asked = exchange(requests).reshape(-1)
    fetched = exchange(gather_rows(asked, table)).reshape(N_XZ, N_Y, PAIR_CAP, LANES)
    gain_row = norm_gain.reshape(1, D)
    emb, part, send, w_part = block(
        core_arr,
        slot_own.reshape(2 * TOK, 1),
        slot_other.reshape(2 * TOK, 1),
        fetched,
        swap(fetched),
        cot_own,
        cot_other,
        gain_row,
        w_in,
        bias_in.reshape(1, 2 * HALF),
        w_out,
    )
    payload = pack(slot_own, part, swap(send), emb, gain_row, cot_own, cot_other, w_part)
    arrived = exchange(payload.reshape(N_PEERS, PAIR_CAP + N_W, LANES))

    summed = jnp.sum(arrived[:, PAIR_CAP:].astype(f32), axis=0)
    share = summed[:128].astype(bf16)
    gathered = exchange(jnp.broadcast_to(share[None], (N_PEERS, 128, LANES)))
    table_grad = scatter_rows(asked, arrived)
    scale = 1.0 / math.sqrt(TOK * N_PEERS * N_CORE)
    vec_own = summed[128:140].reshape(-1)
    vec_other = swap(vec_own)
    bias_own, bias_other = vec_own[:HALF], vec_other[:HALF]
    g_bias = jnp.where(
        core == 0, jnp.stack([bias_own, bias_other]), jnp.stack([bias_other, bias_own])
    ).reshape(-1)
    g_gain = vec_own[HALF:] + vec_other[HALF:]
    own = gathered.reshape(N_XZ, N_Y, 128, LANES)
    g_out, g_in = finish(core_arr, own, swap(own), scale)
    return (table_grad, g_in, g_bias * scale, g_out, g_gain * scale)


def solution(mesh):
    pairs = Mesh(mesh.devices.reshape(N_X, N_Z, N_CORE, N_Y), EVERY)
    rows = ("x", "z", "core")
    return jax.shard_map(
        local,
        mesh=pairs,
        in_specs=(
            P(rows, "y"),
            P(EVERY, None),
            P(EVERY, None, None),
            P(),
            P(),
            P(),
            P(),
        ),
        out_specs=(P(rows, "y"), P(), P(), P(), P()),
        check_vma=False,
    )
```

time: 243 us -> 192 us (0.79)
  other arithmetic: 36.5 us -> 2.17 us
  Pallas kernels: 18.7 us -> 45 us
  local copies, waits for them, and re-layouts: 32.4 us -> 8.56 us
  matrix products: 19.5 us -> 0.29 us
    pallas_call x1 -> x5, Pallas kernels: 18.7 us -> 45 us  [the longest x1 14.9 us: block(): pl.pallas_call(block_kernel, grid_spec=pltpu.PrefetchScalarGridSpec(num_s...]
    scatter-add x1 -> x0, other arithmetic: 25.1 us -> none  [local(): table_grad = jnp.zeros((rows_dev, col_width), f32).at[asked.reshape(-1)]....]
    dot_general x7 -> x0, matrix products: 19.2 us -> none  [the longest x1 5.08 us: local(): lax.dot_general(hidden, d_out, (((0,), (0,)), ((), ())), preferred_elemen...]
    gather x1 -> x0, local copies, waits for them, and re-layouts: 12.9 us -> none  [local(): looked = jnp.take(table, asked, axis=0)]
    reshape x10 -> x3, local copies, waits for them, and re-layouts: 12.9 us -> 0.15 us  [the longest x1 0.08 us: local(): wanted = jnp.transpose(wanted.reshape(2, N_XZ, CAP), (1, 0, 2))]
    reduce_sum x4 -> x2, other arithmetic: 5.17 us -> 0.79 us  [the longest x1 0.45 us: local(): jnp.sum(jnp.where(slot_own[:, :, None] == slot_ids, offsets[:, :, None],...]
    unnamed x33 -> x19, local copies, waits for them, and re-layouts: 4.49 us -> 7.29 us
    select_n x5 -> x2, other arithmetic: 2.52 us -> 0.03 us  [the longest x1 0.03 us: local(): slot_other = jnp.where(is_own, -1, slot)]
  transfers between devices with their start and end apart: 6 -> 6, of which waited for: 2 -> 4; matrix products, arithmetic and copies ran while one was open for 20% -> 2% of each run, Pallas kernels for 0% -> 8%
where the time goes in v2:
time: 192 us; the launch traced here: 188 us
  blocking collectives  121 us (63%)
  Pallas kernels  45 us (23%)
  local copies, waits for them, and re-layouts  8.56 us (4%)
  starting transfers between devices  5.75 us (3%)
  waiting for transfers between devices  4.67 us (2%)
  other arithmetic  2.17 us (1%)
    all_to_all x4, blocking collectives, exchange(): return lax.all_to_all(a, PEERS, split_axis=0, concat_axis=0, tiled=True)  121 us
    pallas_call x1, Pallas kernels, block(): pl.pallas_call(block_kernel, grid_spec=pltpu.PrefetchScalarGridSpec(num_s...  14.9 us
    pallas_call x1, Pallas kernels, scatter_rows(): pl.pallas_call(scatter_kernel, grid_spec=pltpu.PrefetchScalarGridSpec(num...  14.9 us
    pallas_call x1, Pallas kernels, finish(): pl.pallas_call(lambda *refs: finish_kernel(scale, *refs), grid_spec=pltpu...  7.67 us
    unnamed x19, local copies, waits for them, and re-layouts  7.29 us
    ppermute x6, starting transfers between devices, swap(): return lax.ppermute(a, 'core', [(0, 1), (1, 0)])  5.75 us
    pallas_call x1, Pallas kernels, gather_rows(): pl.pallas_call(gather_kernel, grid_spec=pltpu.PrefetchScalarGridSpec(num_...  5.68 us
    ppermute x6, waiting for transfers between devices, swap(): return lax.ppermute(a, 'core', [(0, 1), (1, 0)])  4.67 us
  transfers between devices with their start and end apart: 6, of which 4 were waited for; matrix products, arithmetic and copies ran while one was open for 2% of the time, Pallas kernels for 8%

profile of v2, /device:TPU:33, one launch (start us, length us, event | category | flops | bytes accessed | tf_op | source)
XLA Modules:
  0.0 188.3 jit_solution(17430865335524776837)
XLA Ops:
  0.6 0.7 copy.26
  1.3 0.7 collective-permute-start
  2.0 0.7 copy.25
  4.1 18.0 %all_to_all.24 = s32[64,1,64]{2,1,0:T(1,128)S(1)} all-to-all(s32[64,1,64]{2,1,0:T(1,128)S(1)} %bitcast.58), channel_id=1, replica_groups=mesh['x'=4,'z'=4,'core'=2,'y'=4] {'x','z','y'}, dimensions={0} | all-to-all | bytes 32768 | tf_op jit(solution)/shard_map/all_to_all | solution.py:40
  22.1 0.5 broadcast.182
  22.6 0.7 reduce.3
  23.4 1.6 copy-done.2
  25.0 5.7 %gather_rows.1 = bf16[64,64,128]{2,1,0:T(8,128)(2,1)S(1)} custom-call(s32[4096]{0:T(1024)S(1)} %reshape.259.asked, bf16[8192,128]{1,0:T(8,128)(2,1)S(1)} %copy-done.2), custom_call_target="tpu_custom_call" | custom-call | tf_op jit(solution)/shard_map/gather_rows/pallas_call | solution.py:79
  30.8 21.1 %all_to_all.25 = bf16[64,64,128]{2,1,0:T(8,128)(2,1)S(1)} all-to-all(bf16[64,64,128]{2,1,0:T(8,128)(2,1)S(1)} %gather_rows.1), channel_id=1, replica_groups=mesh['x'=4,'z'=4,'core'=2,'y'=4] {'x','z','y'}, dimensions={0} | all-to-all | bytes 2097152 | tf_op jit(solution)/shard_map/all_to_all | solution.py:40
  51.8 2.8 %collective-permute-start.2 = (bf16[16,4,64,128]{3,2,1,0:T(8,128)(2,1)S(1)}, bf16[16,4,64,128]{3,2,1,0:T(8,128)(2,1)}, u32[]{:S(2)}, u32[]{:S(2)}) collective-permute-start(bf16[16,4,64,128]{3,2,1,0:T(8,128)(2,1)S(1)} %bitcast.47), channel_id=1, source_target_pairs={{0,4},{4,0},{1,5},{5,1},{2,6},{6,2},{3,7},{7,3},{8,12},{12,8},{9,1... | collective-permute-start | bytes 3145736 | tf_op jit(solution)/shard_map/ppermute | solution.py:36
  55.2 1.9 %collective-permute-done.2.got_other = bf16[16,4,64,128]{3,2,1,0:T(8,128)(2,1)} collective-permute-done((bf16[16,4,64,128]{3,2,1,0:T(8,128)(2,1)S(1)}, bf16[16,4,64,128]{3,2,1,0:T(8,128)(2,1)}, u32[]{:S(2)}, u32[]{:S(2)}) %collective-permute-start.2) | collective-permute-done | bytes 1048608 | tf_op jit(solution)/shard_map/ppermute | solution.py:36
  57.1 14.9 %block.1 = (bf16[1024,512]{1,0:T(8,128)(2,1)S(1)}, f32[1024,512]{1,0:T(8,128)}, bf16[1024,512]{1,0:T(8,128)(2,1)S(1)}, bf16[16,4,144,128]{3,2,1,0:T(8,128)(2,1)}) custom-call(s32[1]{0:T(128)} %bitcast.7.core.refs_0_, s32[1024,1]{1,0:T(8,128)S(1)} %bitcast.52, s32[1024,1]{1,0:T(8,128)S(1)} %bitcast.53, bf16[16,4,64,128]{3,2,1,0:T(8,128)(2,1)S(1)} %bitcast.48, ...), custom_call_target="tpu_custom_call" | custom-call | tf_op jit(solution)/shard_map/block/pallas_call | solution.py:209
  72.4 2.3 %collective-permute-done.3.other_ref = bf16[1024,512]{1,0:T(8,128)(2,1)S(1)} collective-permute-done((bf16[1024,512]{1,0:T(8,128)(2,1)S(1)}, bf16[1024,512]{1,0:T(8,128)(2,1)S(1)}, u32[]{:S(2)}, u32[]{:S(2)}) %collective-permute-start.3) | collective-permute-done | bytes 1048608 | tf_op jit(solution)/shard_map/ppermute | solution.py:36
  74.7 1.7 copy-done
  76.4 1.6 copy-done.3
  78.0 1.8 pack.1
  79.8 47.1 %all_to_all.26.arrived_ref = bf16[64,208,128]{2,1,0:T(8,128)(2,1)S(1)} all-to-all(bf16[64,208,128]{2,1,0:T(8,128)(2,1)S(1)} %bitcast.46), channel_id=1, replica_groups=mesh['x'=4,'z'=4,'core'=2,'y'=4] {'x','z','y'}, dimensions={0} | all-to-all | bytes 6815744 | tf_op jit(solution)/shard_map/all_to_all | solution.py:40
  127.3 0.5 broadcast_in_dim.40
  127.8 34.9 %all_to_all.27 = bf16[64,128,128]{2,1,0:T(8,128)(2,1)} all-to-all(bf16[64,128,128]{2,1,0:T(8,128)(2,1)S(1)} %broadcast_in_dim.40), channel_id=1, replica_groups=mesh['x'=4,'z'=4,'core'=2,'y'=4] {'x','z','y'}, dimensions={0} | all-to-all | bytes 4194304 | tf_op jit(solution)/shard_map/all_to_all | solution.py:40
  162.6 1.8 collective-permute-start.4
  164.5 14.9 %scatter_rows.1 = f32[8192,128]{1,0:T(8,128)} custom-call(s32[4096]{0:T(1024)S(1)} %reshape.259.asked, bf16[64,208,128]{2,1,0:T(8,128)(2,1)S(1)} %all_to_all.26.arrived_ref), custom_call_target="tpu_custom_call" | custom-call | flops 10000000000 | bytes 10000000 | tf_op jit(solution)/shard_map/scatter_rows/pallas_call | solution.py:331
  179.4 0.6 copy.33
  180.0 0.6 fusion.9
  180.6 7.7 %finish.1 = (f32[2048,512]{1,0:T(8,128)}, f32[512,2048]{1,0:T(8,128)}) custom-call(s32[1]{0:T(128)} %bitcast.7.core.refs_0_, bf16[16,4,128,128]{3,2,1,0:T(8,128)(2,1)} %bitcast.12.refs_1_, bf16[16,4,128,128]{3,2,1,0:T(8,128)(2,1)} %collective-permute-done.4.refs_2_), custom_call_target="tpu_custom_call" | custom-call | tf_op jit(solution)/shard_map/finish/pallas_call | solution.py:377
  (36 shorter events, 2.7 us)
Async XLA Ops:
  1.3 1.5 collective-permute-start
  2.0 2.1 %collective-permute-start.1 = (bf16[512,512]{1,0:T(8,128)(2,1)}, bf16[512,512]{1,0:T(8,128)(2,1)S(1)}, u32[]{:S(2)}, u32[]{:S(2)}) collective-permute-start(bf16[512,512]{1,0:T(8,128)(2,1)} %bitcast.49), channel_id=1, source_target_pairs={{0,4},{4,0},{1,5},{5,1},{2,6},{6,2},{3,7},{7,3},{8,12},{12,8},{9,1... | collective-permute-start | bytes 1572872 | tf_op jit(solution)/shard_map/ppermute | solution.py:36
  23.4 1.6 copy-start.2
  30.7 26.4 %copy-start.1 = (bf16[2,256,512]{2,1,0:T(8,128)(2,1)S(1)}, bf16[2,256,512]{2,1,0:T(8,128)(2,1)}, u32[]{:S(2)}) copy-start(bf16[2,256,512]{2,1,0:T(8,128)(2,1)} %param.9) | copy-start | bytes 1572868
  30.7 26.4 %copy-start.4 = (f32[2048]{0:T(1024)S(1)}, f32[2048]{0:T(1024)}, u32[]{:S(2)}) copy-start(f32[2048]{0:T(1024)} %param.12) | copy-start | bytes 24580
  30.7 26.4 %copy-start.5 = (f32[512]{0:T(512)S(1)}, f32[512]{0:T(512)}, u32[]{:S(2)}) copy-start(f32[512]{0:T(512)} %param.10) | copy-start | bytes 6148
  51.8 5.3 %collective-permute-start.2 = (bf16[16,4,64,128]{3,2,1,0:T(8,128)(2,1)S(1)}, bf16[16,4,64,128]{3,2,1,0:T(8,128)(2,1)}, u32[]{:S(2)}, u32[]{:S(2)}) collective-permute-start(bf16[16,4,64,128]{3,2,1,0:T(8,128)(2,1)S(1)} %bitcast.47), channel_id=1, source_target_pairs={{0,4},{4,0},{1,5},{5,1},{2,6},{6,2},{3,7},{7,3},{8,12},{12,8},{9,1... | collective-permute-start | bytes 3145736 | tf_op jit(solution)/shard_map/ppermute | solution.py:36
  72.0 2.7 %collective-permute-start.3 = (bf16[1024,512]{1,0:T(8,128)(2,1)S(1)}, bf16[1024,512]{1,0:T(8,128)(2,1)S(1)}, u32[]{:S(2)}, u32[]{:S(2)}) collective-permute-start(bf16[1024,512]{1,0:T(8,128)(2,1)S(1)} %get-tuple-element.20), channel_id=1, source_target_pairs={{0,4},{4,0},{1,5},{5,1},{2,6},{6,2},{3,7},{7,3},{8,12},{12,8},{9,1... | collective-permute-start | bytes 3145736 | tf_op jit(solution)/shard_map/ppermute | solution.py:36
  74.7 1.7 copy-start
  76.4 1.6 copy-start.3
  162.6 18.0 %collective-permute-start.4 = (bf16[16,4,128,128]{3,2,1,0:T(8,128)(2,1)}, bf16[16,4,128,128]{3,2,1,0:T(8,128)(2,1)}, u32[]{:S(2)}, u32[]{:S(2)}) collective-permute-start(bf16[16,4,128,128]{3,2,1,0:T(8,128)(2,1)} %bitcast.12.refs_1_), channel_id=1, source_target_pairs={{0,4},{4,0},{1,5},{5,1},{2,6},{6,2},{3,7},{7,3},{8,12},{12,8},{9,1... | collective-permute-start | bytes 6291464 | tf_op jit(solution)/shard_map/ppermute | solution.py:36
  164.5 14.9 %collective-permute-start.5 = (f32[1536]{0:T(1024)S(1)}, f32[1536]{0:T(1024)S(1)}, u32[]{:S(2)}, u32[]{:S(2)}) collective-permute-start(f32[1536]{0:T(1024)S(1)} %slice_bitcast_fusion), channel_id=1, source_target_pairs={{0,4},{4,0},{1,5},{5,1},{2,6},{6,2},{3,7},{7,3},{8,12},{12,8},{9,1... | collective-permute-start | bytes 18440 | tf_op jit(solution)/shard_map/ppermute | solution.py:36

commit v3 on v2

--- a/solution.py
+++ b/solution.py
@@ -29,7 +29,9 @@
 N_SLOTS = N_XZ * CAP
 ROWS = 8192
 N_REQ = N_PEERS * PAIR_CAP
-N_W = 144
+N_BLOCK = 512
+N_VEC = 16
+N_RING = 4 * N_BLOCK + N_VEC
 
 
 def swap(a):
@@ -40,12 +42,38 @@
     return lax.all_to_all(a, PEERS, split_axis=0, concat_axis=0, tiled=True)
 
 
+def device(x, z, core, y):
+    return ((x * N_Z + z) * N_CORE + core) * N_Y + y
+
+
+def rings(of_core):
+    found = []
+    for core in range(N_CORE):
+        for i in range(4):
+            for j in range(4):
+                at = [{"x": (k, i, j), "y": (i, k, j), "z": (i, j, k)}[of_core[core]] for k in range(4)]
+                found.append([device(x, z, core, y) for x, y, z in at])
+    return found
+
+
+RING = (rings("xy"), rings("yz"), rings("zx"))
+
+
+def along(stage, a, shift):
+    pairs = [(ring[i], ring[(i + shift) % 4]) for ring in RING[stage] for i in range(4)]
+    return lax.ppermute(a, EVERY, pairs)
+
+
 def params(mib):
     return pltpu.CompilerParams(vmem_limit_bytes=mib << 20)
 
 
 def whole(shape, space=pltpu.VMEM):
     return pl.BlockSpec(shape, lambda *_: (0,) * len(shape), memory_space=space)
+
+
+def request_at(row):
+    return (row // PAIR_CAP) * LANES + row % PAIR_CAP
 
 
 def gather_kernel(asked, table_ref, out_ref, wide, picked):
@@ -61,8 +89,9 @@
 
     def pick(i, carry):
         base = pl.multiple_of(i * unroll, unroll)
+        at = request_at(base)
         for u in range(unroll):
-            picked[pl.ds(base + u, 1), :] = wide[pl.ds(asked[base + u], 1), :]
+            picked[pl.ds(base + u, 1), :] = wide[pl.ds(asked[at + u], 1), :]
         return carry
 
     lax.fori_loop(0, N_REQ // unroll, pick, 0)
@@ -92,7 +121,7 @@
 
 
 def block_kernel(
-    core,
+    place,
     slot_own,
     slot_other,
     got_own,
@@ -106,7 +135,10 @@
     emb_ref,
     part_ref,
     send_ref,
-    w_ref,
+    ring_0,
+    ring_1,
+    ring_2,
+    ring_3,
     by_slot,
     normed_s,
     hidden_s,
@@ -114,7 +146,10 @@
     bias_acc,
     gain_acc,
     d_out_s,
+    gin_s,
+    vec_s,
 ):
+    ring_refs = (ring_0, ring_1, ring_2, ring_3)
     for j in range(2):
         for y in range(N_Y):
             lanes = slice(y * LANES, (y + 1) * LANES)
@@ -172,39 +207,37 @@
 
     def one_tile(i, carry):
         cols = pl.ds(pl.multiple_of(i * 256, 256), 256)
+        gin_s[:, cols] = lax.dot_general(
+            normed_s[...], d_pre_s[:, cols], tn, preferred_element_type=f32
+        ).astype(bf16)
+        return carry
+
+    lax.fori_loop(0, HALF // 256, one_tile, 0)
+    g_bias = jnp.sum(bias_acc[...], axis=0, keepdims=True)
+    g_gain = jnp.sum(gain_acc[...], axis=0, keepdims=True)
+    for r in range(HALF // LANES):
+        vec_s[r : r + 1, :] = g_bias[:, r * LANES : (r + 1) * LANES]
+    for r in range(D // LANES):
+        vec_s[8 + r : 9 + r, :] = g_gain[:, r * LANES : (r + 1) * LANES]
+    for shift, ref in enumerate(ring_refs):
+        to = lax.rem(place[1] + shift, 4)
+        cols = pl.ds(pl.multiple_of(to * 256, 256), 256)
         g_out = lax.dot_general(
             hidden_s[:, cols], d_out_s[...], tn, preferred_element_type=f32
         ).astype(bf16)
-        for y in range(N_Y):
-            w_ref[pl.ds(i * 4, 4), y, 0:64, :] = g_out[:, y * LANES : (y + 1) * LANES].reshape(
-                4, 64, LANES
-            )
-        g_in = lax.dot_general(
-            normed_s[...], d_pre_s[:, cols], tn, preferred_element_type=f32
-        ).astype(bf16)
-        for p in range(2):
-            w_ref[:, i, 64 + p * 32 : 96 + p * 32, :] = g_in[
-                :, p * LANES : (p + 1) * LANES
-            ].reshape(N_XZ, 32, LANES)
-        return carry
-
-    lax.fori_loop(0, HALF // 256, one_tile, 0)
-    g_bias = jnp.sum(bias_acc[...], axis=0, keepdims=True)
-    g_gain = jnp.sum(gain_acc[...], axis=0, keepdims=True)
-    pieces = [g_bias[:, r * LANES : (r + 1) * LANES] for r in range(HALF // LANES)]
-    pieces += [g_gain[:, r * LANES : (r + 1) * LANES] for r in range(D // LANES)]
-    pieces += [jnp.zeros((4, LANES), f32)]
-    vec = jnp.concatenate(pieces, axis=0).astype(bf16)
-
-    def one_peer(i, carry):
-        for y in range(N_Y):
-            w_ref[i, y, 128:144, :] = vec
-        return carry
-
-    lax.fori_loop(0, N_XZ, one_peer, 0)
-
-
-def block(core, slot_own, slot_other, got_own, got_other, cot_own, cot_other, gain, w_in, bias, w_out):
+        for b in range(4):
+            rows = pl.ds(pl.multiple_of(to * 128 + b * 32, 32), 32)
+            for y in range(N_Y):
+                at = b * N_BLOCK + y * 128
+                ref[at : at + 64, :] = g_out[b * 64 : b * 64 + 64, y * LANES : (y + 1) * LANES]
+                for p in range(2):
+                    lane = (y * 2 + p) * LANES
+                    ref[at + 64 + p * 32 : at + 96 + p * 32, :] = gin_s[rows, lane : lane + LANES]
+        vec = [vec_s[pl.ds(to * 3 + r, 1), :] for r in range(3)] + [jnp.zeros((13, LANES), f32)]
+        ref[4 * N_BLOCK :, :] = jnp.concatenate(vec, axis=0).astype(bf16)
+
+
+def block(place, slot_own, slot_other, got_own, got_other, cot_own, cot_other, gain, w_in, bias, w_out):
     got = (N_XZ, N_Y, PAIR_CAP, LANES)
     return pl.pallas_call(
         block_kernel,
@@ -227,8 +260,8 @@
                 whole((2 * TOK, D)),
                 whole((2 * TOK, D)),
                 whole((2 * TOK, D)),
-                whole((N_XZ, N_Y, N_W, LANES)),
-            ],
+            ]
+            + [whole((N_RING, LANES))] * 4,
             scratch_shapes=[
                 pltpu.VMEM((2, 2 * N_SLOTS, D), bf16),
                 pltpu.VMEM((2 * TOK, D), bf16),
@@ -237,21 +270,22 @@
                 pltpu.VMEM((8, HALF), f32),
                 pltpu.VMEM((8, D), f32),
                 pltpu.VMEM((2 * TOK, D), bf16),
+                pltpu.VMEM((D, HALF), bf16),
+                pltpu.VMEM((16, LANES), f32),
             ],
         ),
         out_shape=[
             jax.ShapeDtypeStruct((2 * TOK, D), bf16),
             jax.ShapeDtypeStruct((2 * TOK, D), f32),
             jax.ShapeDtypeStruct((2 * TOK, D), bf16),
-            jax.ShapeDtypeStruct((N_XZ, N_Y, N_W, LANES), bf16),
-        ],
+        ]
+        + [jax.ShapeDtypeStruct((N_RING, LANES), bf16)] * 4,
         compiler_params=params(48),
         name="block",
-    )(core, slot_own, slot_other, got_own, got_other, cot_own, cot_other, gain, w_in, bias, w_out)
-
-
-def pack_kernel(slot_ref, part_ref, other_ref, emb_ref, gain_ref, cot_own, cot_other, w_ref, out_ref):
-    out_ref[:, :, PAIR_CAP:, :] = w_ref[...]
+    )(place, slot_own, slot_other, got_own, got_other, cot_own, cot_other, gain, w_in, bias, w_out)
+
+
+def pack_kernel(slot_ref, part_ref, other_ref, emb_ref, gain_ref, cot_own, cot_other, out_ref):
     gain = gain_ref[...]
     slot_ids = lax.broadcasted_iota(i32, (N_SLOTS, TOK), 0)
     for j in range(2):
@@ -273,13 +307,14 @@
             ].reshape(N_XZ, CAP, LANES)
 
 
-def pack(slot_row, part, other, emb, gain, cot_own, cot_other, w_part):
+def pack(slot_row, part, other, emb, gain, cot_own, cot_other):
     return pl.pallas_call(
         pack_kernel,
-        out_shape=jax.ShapeDtypeStruct((N_XZ, N_Y, PAIR_CAP + N_W, LANES), bf16),
-        compiler_params=params(40),
+        out_shape=jax.ShapeDtypeStruct((N_XZ, N_Y, PAIR_CAP, LANES), bf16),
+        compiler_params=params(32),
+        cost_estimate=pl.CostEstimate(flops=2 * 10**9, bytes_accessed=10**7, transcendentals=0),
         name="pack",
-    )(slot_row, part, other, emb, gain, cot_own, cot_other, w_part)
+    )(slot_row, part, other, emb, gain, cot_own, cot_other)
 
 
 N_ACC = 2
@@ -310,7 +345,7 @@
         for u in range(unroll):
             for a, acc in enumerate((out_ref,) + accs):
                 row = base + (a * share + u)
-                at = pl.ds(asked[row], 1)
+                at = pl.ds(asked[request_at(base) + (a * share * LANES // PAIR_CAP + u)], 1)
                 acc[at, :] = acc[at, :] + grads[pl.ds(row, 1), :]
         return carry
 
@@ -345,65 +380,148 @@
     )(asked, arrived)
 
 
-def finish_kernel(scale, core_ref, own_ref, other_ref, out_ref, in_ref):
-    n = own_ref.shape[0]
-
-    def write(ref):
-        for y in range(N_Y):
-            out_ref[:, y * LANES : (y + 1) * LANES] = (
-                ref[:, y, :64, :].astype(f32) * scale
-            ).reshape(n * 64, LANES)
-            for p in range(2):
-                lane = (y * 2 + p) * LANES
-                in_ref[:, lane : lane + LANES] = (
-                    ref[:, y, 64 + p * 32 : 96 + p * 32, :].astype(f32) * scale
-                ).reshape(n * 32, LANES)
-
-    @pl.when(pl.program_id(0) == 0)
+def ring_add(here, back_1, back_2, back_3, rows):
+    first = here[rows, :].astype(f32) + back_2[rows, :].astype(f32)
+    return first + (back_1[rows, :].astype(f32) + back_3[rows, :].astype(f32))
+
+
+def sum_split_kernel(place, here, back_1, back_2, back_3, *outs):
+    vec = ring_add(here, back_1, back_2, back_3, slice(4 * N_BLOCK, N_RING)).astype(bf16)
+    for shift, out in enumerate(outs):
+        to = lax.rem(place[2] + shift, 4)
+        for part in range(4):
+            step = N_BLOCK // 4
+            rows = pl.ds(pl.multiple_of(to * N_BLOCK + part * step, step), step)
+            out[part * step : (part + 1) * step, :] = ring_add(
+                here, back_1, back_2, back_3, rows
+            ).astype(bf16)
+        out[N_BLOCK:, :] = vec
+
+
+def sum_split(place, pieces):
+    return pl.pallas_call(
+        sum_split_kernel,
+        grid_spec=pltpu.PrefetchScalarGridSpec(
+            num_scalar_prefetch=1,
+            grid=(1,),
+            in_specs=[whole((N_RING, LANES))] * 4,
+            out_specs=[whole((N_BLOCK + N_VEC, LANES))] * 4,
+        ),
+        out_shape=[jax.ShapeDtypeStruct((N_BLOCK + N_VEC, LANES), bf16)] * 4,
+        compiler_params=params(8),
+        name="sum_split",
+    )(place, *pieces)
+
+
+def sum_kernel(here, back_1, back_2, back_3, out):
+    n = N_BLOCK + N_VEC
+    for at in range(0, n, 88):
+        rows = slice(at, min(at + 88, n))
+        out[rows, :] = ring_add(here, back_1, back_2, back_3, rows).astype(bf16)
+
+
+def sum_four(pieces):
+    return pl.pallas_call(
+        sum_kernel,
+        out_shape=jax.ShapeDtypeStruct((N_BLOCK + N_VEC, LANES), bf16),
+        compiler_params=params(4),
+        name="sum_four",
+    )(*pieces)
+
+
+def join_kernel(here, back_1, back_2, back_3, out):
+    for i, ref in enumerate((here, back_1, back_2, back_3)):
+        out[i * N_BLOCK : (i + 1) * N_BLOCK, :] = ref[:N_BLOCK, :]
+    out[4 * N_BLOCK :, :] = here[N_BLOCK:, :]
+
+
+def join_four(pieces):
+    return pl.pallas_call(
+        join_kernel,
+        out_shape=jax.ShapeDtypeStruct((N_RING, LANES), bf16),
+        compiler_params=params(4),
+        name="join_four",
+    )(*pieces)
+
+
+def finish_kernel(scale, place, *refs):
+    pieces, (out_ref, in_ref, bias_ref, gain_ref, vec_s) = refs[:8], refs[8:]
+
+    for s in range(8):
+
+        @pl.when(pl.program_id(0) == s)
+        def _(ref=pieces[s], s=s):
+            a = lax.rem(place[1 if s < 4 else 3] + (4 - s % 4), 4)
+            for j in range(4):
+                b = lax.rem(place[2 if s < 4 else 4] + (4 - j), 4)
+                rows_out = pl.ds(pl.multiple_of(b * 64, 64), 64)
+                rows_in = pl.ds(pl.multiple_of(b * 32, 32), 32)
+                for y in range(N_Y):
+                    at = j * N_BLOCK + y * 128
+                    out_ref[rows_out, y * LANES : (y + 1) * LANES] = (
+                        ref[at : at + 64, :].astype(f32) * scale
+                    )
+                    for p in range(2):
+                        lane = (y * 2 + p) * LANES
+                        in_ref[rows_in, lane : lane + LANES] = (
+                            ref[at + 64 + p * 32 : at + 96 + p * 32, :].astype(f32) * scale
+                        )
+            vec = ref[4 * N_BLOCK :, :].astype(f32) * scale
+            for r in range(3):
+                vec_s[s // 4, pl.ds(a * 3 + r, 1), :] = vec[r : r + 1, :]
+
+    @pl.when(pl.program_id(0) == 7)
     def _():
-        write(own_ref)
-
-    @pl.when(pl.program_id(0) == 1)
-    def _():
-        write(other_ref)
-
-
-def finish(core, own, other, scale):
-    n, wide = 4, 4
-
+        bias_ref[pl.ds(pl.multiple_of(place[0] * 8, 8), 8), :] = vec_s[0, :8, :]
+        bias_ref[pl.ds(pl.multiple_of((1 - place[0]) * 8, 8), 8), :] = vec_s[1, :8, :]
+        gain_ref[...] = vec_s[0, 8:12, :] + vec_s[1, 8:12, :]
+
+
+def finish(place, pieces, scale):
     def half_of(s, c):
-        return jnp.where(s == 0, c[0], 1 - c[0])
+        return jnp.where(s < 4, c[0], 1 - c[0])
+
+    def row_of(s, c):
+        return lax.rem(jnp.where(s < 4, c[1], c[3]) + 8 - s, 4)
 
     return pl.pallas_call(
         lambda *refs: finish_kernel(scale, *refs),
         grid_spec=pltpu.PrefetchScalarGridSpec(
             num_scalar_prefetch=1,
-            grid=(2, n),
-            in_specs=[
-                pl.BlockSpec(
-                    (wide, N_Y, 128, LANES), lambda s, i, c: (jnp.where(s == 0, i, n - 1), 0, 0, 0)
-                ),
-                pl.BlockSpec(
-                    (wide, N_Y, 128, LANES), lambda s, i, c: (jnp.where(s == 0, 0, i), 0, 0, 0)
-                ),
+            grid=(8,),
+            in_specs=[whole((N_RING, LANES))] * 8,
+            out_specs=[
+                pl.BlockSpec((256, D), lambda s, c: (half_of(s, c) * 4 + row_of(s, c), 0)),
+                pl.BlockSpec((128, HALF), lambda s, c: (row_of(s, c), half_of(s, c))),
+                whole((16, LANES)),
+                whole((4, LANES)),
             ],
-            out_specs=[
-                pl.BlockSpec((64 * wide, D), lambda s, i, c: (half_of(s, c) * n + i, 0)),
-                pl.BlockSpec((32 * wide, HALF), lambda s, i, c: (i, half_of(s, c))),
-            ],
+            scratch_shapes=[pltpu.VMEM((2, 16, LANES), f32)],
         ),
         out_shape=[
             jax.ShapeDtypeStruct((2 * HALF, D), f32),
             jax.ShapeDtypeStruct((D, 2 * HALF), f32),
+            jax.ShapeDtypeStruct((16, LANES), f32),
+            jax.ShapeDtypeStruct((4, LANES), f32),
         ],
         compiler_params=params(16),
         name="finish",
-    )(core, own, other)
+    )(place, *pieces)
 
 
 def local(table, item_ids, cotangent, norm_gain, w_in, bias_in, w_out):
     core = lax.axis_index("core").astype(i32)
-    core_arr = core.reshape(1)
+    x, y, z = (lax.axis_index(name).astype(i32) for name in "xyz")
+    is_first = core == 0
+    place = jnp.stack(
+        [
+            core,
+            jnp.where(is_first, x, y),
+            jnp.where(is_first, y, z),
+            jnp.where(is_first, y, x),
+            jnp.where(is_first, z, y),
+        ]
+    )
     own_ids = item_ids.reshape(-1)
     cot_own = cotangent.reshape(TOK, D)
     cot_other = swap(cot_own)
@@ -426,17 +544,16 @@
         jnp.where(slot_own[:, :, None] == slot_ids, offsets[:, :, None], 0), axis=1
     )
     wanted = jnp.transpose(wanted.reshape(2, N_XZ, CAP), (1, 0, 2))
-    requests = jnp.broadcast_to(
-        wanted.reshape(N_XZ, 1, PAIR_CAP), (N_XZ, N_Y, PAIR_CAP)
-    ).reshape(N_PEERS, PAIR_CAP)
+    wanted = jnp.pad(wanted.reshape(N_XZ, 1, PAIR_CAP), ((0, 0), (0, 0), (0, LANES - PAIR_CAP)))
+    requests = jnp.broadcast_to(wanted, (N_XZ, N_Y, LANES)).reshape(N_PEERS, 1, LANES)
     requests, cot_other, slot_own, slot_other = lax.optimization_barrier(
         (requests, cot_other, slot_own, slot_other)
     )
     asked = exchange(requests).reshape(-1)
     fetched = exchange(gather_rows(asked, table)).reshape(N_XZ, N_Y, PAIR_CAP, LANES)
     gain_row = norm_gain.reshape(1, D)
-    emb, part, send, w_part = block(
-        core_arr,
+    emb, part, send, *ring = block(
+        place,
         slot_own.reshape(2 * TOK, 1),
         slot_other.reshape(2 * TOK, 1),
         fetched,
@@ -448,24 +565,19 @@
         bias_in.reshape(1, 2 * HALF),
         w_out,
     )
-    payload = pack(slot_own, part, swap(send), emb, gain_row, cot_own, cot_other, w_part)
-    arrived = exchange(payload.reshape(N_PEERS, PAIR_CAP + N_W, LANES))
-
-    summed = jnp.sum(arrived[:, PAIR_CAP:].astype(f32), axis=0)
-    share = summed[:128].astype(bf16)
-    gathered = exchange(jnp.broadcast_to(share[None], (N_PEERS, 128, LANES)))
+    other = swap(send)
+    split = list(sum_split(place, ring[:1] + [along(0, ring[s], s) for s in (1, 2, 3)]))
+    payload = pack(slot_own, part, other, emb, gain_row, cot_own, cot_other)
+    arrived = exchange(payload.reshape(N_PEERS, PAIR_CAP, LANES))
+    mine = sum_four(split[:1] + [along(1, split[s], s) for s in (1, 2, 3)])
+    total = sum_four([mine] + [along(2, mine, s) for s in (1, 2, 3)])
+    joined = join_four([total] + [along(1, total, s) for s in (1, 2, 3)])
+    pieces = [joined] + [along(0, joined, s) for s in (1, 2, 3)]
     table_grad = scatter_rows(asked, arrived)
+    pieces += [swap(p) for p in pieces]
     scale = 1.0 / math.sqrt(TOK * N_PEERS * N_CORE)
-    vec_own = summed[128:140].reshape(-1)
-    vec_other = swap(vec_own)
-    bias_own, bias_other = vec_own[:HALF], vec_other[:HALF]
-    g_bias = jnp.where(
-        core == 0, jnp.stack([bias_own, bias_other]), jnp.stack([bias_other, bias_own])
-    ).reshape(-1)
-    g_gain = vec_own[HALF:] + vec_other[HALF:]
-    own = gathered.reshape(N_XZ, N_Y, 128, LANES)
-    g_out, g_in = finish(core_arr, own, swap(own), scale)
-    return (table_grad, g_in, g_bias * scale, g_out, g_gain * scale)
+    g_out, g_in, g_bias, g_gain = finish(place, pieces, scale)
+    return (table_grad, g_in, g_bias.reshape(-1), g_out, g_gain.reshape(-1))
 
 
 def solution(mesh):

time: 192 us -> 173 us (0.901)
  blocking collectives: 121 us -> 39.1 us
  starting transfers between devices: 5.75 us -> 48.9 us
  waiting for transfers between devices: 4.67 us -> 30.4 us
  local copies, waits for them, and re-layouts: 8.56 us -> 3.72 us
  Pallas kernels: 45 us -> 47.1 us
    all_to_all x4 -> x2, blocking collectives: 121 us -> 39.1 us  [exchange(): return lax.all_to_all(a, PEERS, split_axis=0, concat_axis=0, tiled=True)]
    ppermute x0 -> x15, waiting for transfers between devices: none -> 25.8 us  [along(): return lax.ppermute(a, EVERY, pairs)]
    ppermute x6 -> x8, starting transfers between devices: 5.75 us -> 24.9 us  [swap(): return lax.ppermute(a, 'core', [(0, 1), (1, 0)])]
    ppermute x0 -> x15, starting transfers between devices: none -> 16.2 us  [along(): return lax.ppermute(a, EVERY, pairs)]
    all_to_all x0 -> x1, starting transfers between devices: none -> 7.79 us  [exchange(): return lax.all_to_all(a, PEERS, split_axis=0, concat_axis=0, tiled=True)]
    unnamed x19 -> x22, local copies, waits for them, and re-layouts: 7.29 us -> 3.45 us
    pallas_call x1, Pallas kernels: 7.67 us -> 5.23 us  [finish(): pl.pallas_call(lambda *refs: finish_kernel(scale, *refs), grid_spec=pltpu...]
    ppermute x6 -> x8, waiting for transfers between devices: 4.67 us -> 4.65 us  [swap(): return lax.ppermute(a, 'core', [(0, 1), (1, 0)])]
  transfers between devices with their start and end apart: 6 -> 24, of which waited for: 4 -> 16; matrix products, arithmetic and copies ran while one was open for 2% -> 1% of each run, Pallas kernels for 8% -> 5%
where the time goes in v3:
time: 173 us; the launch traced here: 171 us
  starting transfers between devices  48.9 us (28%)
  Pallas kernels  47.1 us (27%)
  blocking collectives  39.1 us (23%)
  waiting for transfers between devices  30.4 us (18%)
  local copies, waits for them, and re-layouts  3.72 us (2%)
    all_to_all x2, blocking collectives, exchange(): return lax.all_to_all(a, PEERS, split_axis=0, concat_axis=0, tiled=True)  39.1 us
    ppermute x15, waiting for transfers between devices, along(): return lax.ppermute(a, EVERY, pairs)  25.8 us
    ppermute x8, starting transfers between devices, swap(): return lax.ppermute(a, 'core', [(0, 1), (1, 0)])  24.9 us
    ppermute x15, starting transfers between devices, along(): return lax.ppermute(a, EVERY, pairs)  16.2 us
    pallas_call x1, Pallas kernels, scatter_rows(): pl.pallas_call(scatter_kernel, grid_spec=pltpu.PrefetchScalarGridSpec(num...  15.8 us
    pallas_call x1, Pallas kernels, block(): pl.pallas_call(block_kernel, grid_spec=pltpu.PrefetchScalarGridSpec(num_s...  15.1 us
    all_to_all x1, starting transfers between devices, exchange(): return lax.all_to_all(a, PEERS, split_axis=0, concat_axis=0, tiled=True)  7.79 us
    pallas_call x1, Pallas kernels, gather_rows(): pl.pallas_call(gather_kernel, grid_spec=pltpu.PrefetchScalarGridSpec(num_...  7.43 us
  transfers between devices with their start and end apart: 24, of which 16 were waited for; matrix products, arithmetic and copies ran while one was open for 1% of the time, Pallas kernels for 5%

profile of v3, /device:TPU:33, one launch (start us, length us, event | category | flops | bytes accessed | tf_op | source)
XLA Modules:
  0.0 170.9 jit_solution(6124800635487394248)
XLA Ops:
  4.1 18.0 %all_to_all.15 = s32[64,1,128]{2,1,0:T(1,128)S(1)} all-to-all(s32[64,1,128]{2,1,0:T(1,128)S(1)} %bitcast.53), channel_id=1, replica_groups=mesh['x'=4,'z'=4,'core'=2,'y'=4] {'x','z','y'}, dimensions={0} | all-to-all | bytes 65536 | tf_op jit(solution)/shard_map/all_to_all | solution.py:42
  22.1 1.6 copy-done
  23.7 7.4 %gather_rows.1 = bf16[64,64,128]{2,1,0:T(8,128)(2,1)S(1)} custom-call(s32[8192]{0:T(1024)S(1)} %bitcast.45, bf16[8192,128]{1,0:T(8,128)(2,1)S(1)} %copy-done), custom_call_target="tpu_custom_call" | custom-call | tf_op jit(solution)/shard_map/gather_rows/pallas_call | solution.py:108
  31.2 21.1 %all_to_all.16 = bf16[64,64,128]{2,1,0:T(8,128)(2,1)S(1)} all-to-all(bf16[64,64,128]{2,1,0:T(8,128)(2,1)S(1)} %gather_rows.1), channel_id=1, replica_groups=mesh['x'=4,'z'=4,'core'=2,'y'=4] {'x','z','y'}, dimensions={0} | all-to-all | bytes 2097152 | tf_op jit(solution)/shard_map/all_to_all | solution.py:42
  52.3 2.8 %collective-permute-start.2 = (bf16[16,4,64,128]{3,2,1,0:T(8,128)(2,1)S(1)}, bf16[16,4,64,128]{3,2,1,0:T(8,128)(2,1)}, u32[]{:S(2)}, u32[]{:S(2)}) collective-permute-start(bf16[16,4,64,128]{3,2,1,0:T(8,128)(2,1)S(1)} %bitcast.51), channel_id=1, source_target_pairs={{0,4},{4,0},{1,5},{5,1},{2,6},{6,2},{3,7},{7,3},{8,12},{12,8},{9,1... | collective-permute-start | bytes 3145736 | tf_op jit(solution)/shard_map/ppermute | solution.py:38
  55.7 1.9 %collective-permute-done.2.got_other = bf16[16,4,64,128]{3,2,1,0:T(8,128)(2,1)} collective-permute-done((bf16[16,4,64,128]{3,2,1,0:T(8,128)(2,1)S(1)}, bf16[16,4,64,128]{3,2,1,0:T(8,128)(2,1)}, u32[]{:S(2)}, u32[]{:S(2)}) %collective-permute-start.2) | collective-permute-done | bytes 1048608 | tf_op jit(solution)/shard_map/ppermute | solution.py:38
  57.6 15.1 %block.1 = (bf16[1024,512]{1,0:T(8,128)(2,1)S(1)}, f32[1024,512]{1,0:T(8,128)}, bf16[1024,512]{1,0:T(8,128)(2,1)}, bf16[2064,128]{1,0:T(8,128)(2,1)S(1)}, bf16[2...) custom-call(s32[5]{0:T(128)S(1)} %stack.34.place.refs_0_, ...), custom_call_target="tpu_custom_call" | custom-call | tf_op jit(solution)/shard_map/block/pallas_call | solution.py:242
  75.9 12.4 %collective-permute-done.4.back_1 = bf16[2064,128]{1,0:T(8,128)(2,1)S(1)} collective-permute-done((bf16[2064,128]{1,0:T(8,128)(2,1)S(1)}, bf16[2064,128]{1,0:T(8,128)(2,1)S(1)}, u32[]{:S(2)}, u32[]{:S(2)}) %collective-permute-start.4) | collective-permute-done | bytes 528416 | tf_op jit(solution)/shard_map/ppermute | solution.py:64
  89.8 3.1 %collective-permute-start.8 = (bf16[528,128]{1,0:T(8,128)(2,1)S(1)}, bf16[528,128]{1,0:T(8,128)(2,1)S(1)}, u32[]{:S(2)}, u32[]{:S(2)}) collective-permute-start(bf16[528,128]{1,0:T(8,128)(2,1)S(1)} %get-tuple-element.37), channel_id=1, source_target_pairs={{0,2},{1,3},{2,0},{3,1},{8,10},{9,11},{10,8},{11,9},{16,18},{17,19... | collective-permute-start | bytes 405512 | tf_op jit(solution)/shard_map/ppermute | solution.py:64
  93.7 1.9 %collective-permute-done.8.back_2 = bf16[528,128]{1,0:T(8,128)(2,1)S(1)} collective-permute-done((bf16[528,128]{1,0:T(8,128)(2,1)S(1)}, bf16[528,128]{1,0:T(8,128)(2,1)S(1)}, u32[]{:S(2)}, u32[]{:S(2)}) %collective-permute-start.8) | collective-permute-done | bytes 135200 | tf_op jit(solution)/shard_map/ppermute | solution.py:64
  95.6 1.5 collective-permute-done.9.back_3
  99.2 1.9 %collective-permute-done.12.back_3 = bf16[528,128]{1,0:T(8,128)(2,1)S(1)} collective-permute-done((bf16[528,128]{1,0:T(8,128)(2,1)S(1)}, bf16[528,128]{1,0:T(8,128)(2,1)S(1)}, u32[]{:S(2)}, u32[]{:S(2)}) %collective-permute-start.12) | collective-permute-done | bytes 135200 | tf_op jit(solution)/shard_map/ppermute | solution.py:64
  101.1 2.3 %collective-permute-done.11.back_2 = bf16[528,128]{1,0:T(8,128)(2,1)S(1)} collective-permute-done((bf16[528,128]{1,0:T(8,128)(2,1)S(1)}, bf16[528,128]{1,0:T(8,128)(2,1)S(1)}, u32[]{:S(2)}, u32[]{:S(2)}) %collective-permute-start.11) | collective-permute-done | bytes 135200 | tf_op jit(solution)/shard_map/ppermute | solution.py:64
  103.4 1.4 collective-permute-done.10.back_1
  104.9 1.8 %collective-permute-start.15 = (bf16[528,128]{1,0:T(8,128)(2,1)S(1)}, bf16[528,128]{1,0:T(8,128)(2,1)S(1)}, u32[]{:S(2)}, u32[]{:S(2)}) collective-permute-start(bf16[528,128]{1,0:T(8,128)(2,1)S(1)} %sum_four.3.here), channel_id=1, source_target_pairs={{0,3},{1,0},{2,1},{3,2},{8,11},{9,8},{10,9},{11,10},{16,19},{17,16... | collective-permute-start | bytes 405512 | tf_op jit(solution)/shard_map/ppermute | solution.py:64
  108.0 2.0 %collective-permute-start.13 = (bf16[528,128]{1,0:T(8,128)(2,1)S(1)}, bf16[528,128]{1,0:T(8,128)(2,1)S(1)}, u32[]{:S(2)}, u32[]{:S(2)}) collective-permute-start(bf16[528,128]{1,0:T(8,128)(2,1)S(1)} %sum_four.3.here), channel_id=1, source_target_pairs={{0,1},{1,2},{2,3},{3,0},{8,9},{9,10},{10,11},{11,8},{16,17},{17,18... | collective-permute-start | bytes 405512 | tf_op jit(solution)/shard_map/ppermute | solution.py:64
  110.0 2.1 %collective-permute-done.14.back_2 = bf16[528,128]{1,0:T(8,128)(2,1)S(1)} collective-permute-done((bf16[528,128]{1,0:T(8,128)(2,1)S(1)}, bf16[528,128]{1,0:T(8,128)(2,1)S(1)}, u32[]{:S(2)}, u32[]{:S(2)}) %collective-permute-start.14) | collective-permute-done | bytes 135200 | tf_op jit(solution)/shard_map/ppermute | solution.py:64
  113.0 2.4 %collective-permute-start.18 = (bf16[2064,128]{1,0:T(8,128)(2,1)S(1)}, bf16[2064,128]{1,0:T(8,128)(2,1)S(1)}, u32[]{:S(2)}, u32[]{:S(2)}) collective-permute-start(bf16[2064,128]{1,0:T(8,128)(2,1)S(1)} %join_four.1.refs_1_), channel_id=1, source_target_pairs={{0,96},{32,0},{64,32},{96,64},{8,104},{40,8},{72,40},{104,72},{16,... | collective-permute-start | bytes 1585160 | tf_op jit(solution)/shard_map/ppermute | solution.py:64
  116.0 2.5 %pack.1 = bf16[16,4,64,128]{3,2,1,0:T(8,128)(2,1)} custom-call(s32[2,512]{1,0:T(2,128)S(1)} %broadcast_select_fusion.1.slot_ref, f32[1024,512]{1,0:T(8,128)S(1)} %copy-done.6, bf16[1024,512]{1,0:T(8,128)(2,1)S(1)} %collective-permute-done.3.other_ref, bf16[1024,512]{1,0:T(8,128)(2,1)S(1)} %get-tuple-element.30.emb_ref, f32[1,512]{1,0:T(1,128)S(1)} %bitcast.50, ...), custom_call_target="tpu_custom_call" | custom-call | flops 2000000000 | bytes 10000000 | tf_op jit(solution)/shard_map/pack/pallas_call | solution.py:311
  118.6 7.8 %all-to-all-start.2 = ((bf16[64,64,128]{2,1,0:T(8,128)(2,1)}), bf16[64,64,128]{2,1,0:T(8,128)(2,1)S(1)}, u32[]{:S(2)}, u32[]{:S(2)}) async-start(bf16[64,64,128]{2,1,0:T(8,128)(2,1)} %bitcast.16), calls=%async_computation.2 | async-start | bytes 2097152 | tf_op jit(solution)/shard_map/all_to_all | solution.py:42
  126.4 13.0 %collective-permute-start.19 = (bf16[2064,128]{1,0:T(8,128)(2,1)S(1)}, bf16[2064,128]{1,0:T(8,128)(2,1)S(1)}, u32[]{:S(2)}, u32[]{:S(2)}) collective-permute-start(bf16[2064,128]{1,0:T(8,128)(2,1)S(1)} %join_four.1.refs_1_), channel_id=1, source_target_pairs={{0,4},{4,0},{1,5},{5,1},{2,6},{6,2},{3,7},{7,3},{8,12},{12,8},{9,1... | collective-permute-start | bytes 1585160 | tf_op jit(solution)/shard_map/ppermute | solution.py:38
  139.4 7.3 %collective-permute-start.22 = (bf16[2064,128]{1,0:T(8,128)(2,1)S(1)}, bf16[2064,128]{1,0:T(8,128)(2,1)S(1)}, u32[]{:S(2)}, u32[]{:S(2)}) collective-permute-start(bf16[2064,128]{1,0:T(8,128)(2,1)S(1)} %collective-permute-done.18.refs_4_), channel_id=1, source_target_pairs={{0,4},{4,0},{1,5},{5,1},{2,6},{6,2},{3,7},{7,3},{8,12},{12,8},{9,1... | collective-permute-start | bytes 1585160 | tf_op jit(solution)/shard_map/ppermute | solution.py:38
  149.8 5.2 %finish.1 = (f32[2048,512]{1,0:T(8,128)}, f32[512,2048]{1,0:T(8,128)}, f32[16,128]{1,0:T(8,128)}, f32[4,128]{1,0:T(4,128)}) custom-call(s32[5]{0:T(128)S(1)} %stack.34.place.refs_0_, bf16[2064,128]{1,0:T(8,128)(2,1)S(1)} %join_four.1.refs_1_, bf16[2064,128]{1,0:T(8,128)(2,1)S(1)} %collective-permute-done.16.refs_2_, ...), custom_call_target="tpu_custom_call" | custom-call | tf_op jit(solution)/shard_map/finish/pallas_call | solution.py:487
  155.0 15.8 %scatter_rows.1 = f32[8192,128]{1,0:T(8,128)} custom-call(s32[8192]{0:T(1024)S(1)} %bitcast.46, bf16[64,64,128]{2,1,0:T(8,128)(2,1)S(1)} %all-to-all-done.2.arrived_ref), custom_call_target="tpu_custom_call" | custom-call | flops 10000000000 | bytes 10000000 | tf_op jit(solution)/shard_map/scatter_rows/pallas_call | solution.py:366
  (68 shorter events, 17.7 us)
Async XLA Ops:
  1.3 1.5 collective-permute-start
  2.0 2.1 %collective-permute-start.1 = (bf16[512,512]{1,0:T(8,128)(2,1)}, bf16[512,512]{1,0:T(8,128)(2,1)S(1)}, u32[]{:S(2)}, u32[]{:S(2)}) collective-permute-start(bf16[512,512]{1,0:T(8,128)(2,1)} %bitcast.42), channel_id=1, source_target_pairs={{0,4},{4,0},{1,5},{5,1},{2,6},{6,2},{3,7},{7,3},{8,12},{12,8},{9,1... | collective-permute-start | bytes 1572872 | tf_op jit(solution)/shard_map/ppermute | solution.py:38
  52.3 5.3 %collective-permute-start.2 = (bf16[16,4,64,128]{3,2,1,0:T(8,128)(2,1)S(1)}, bf16[16,4,64,128]{3,2,1,0:T(8,128)(2,1)}, u32[]{:S(2)}, u32[]{:S(2)}) collective-permute-start(bf16[16,4,64,128]{3,2,1,0:T(8,128)(2,1)S(1)} %bitcast.51), channel_id=1, source_target_pairs={{0,4},{4,0},{1,5},{5,1},{2,6},{6,2},{3,7},{7,3},{8,12},{12,8},{9,1... | collective-permute-start | bytes 3145736 | tf_op jit(solution)/shard_map/ppermute | solution.py:38
  72.7 43.4 %collective-permute-start.3 = (bf16[1024,512]{1,0:T(8,128)(2,1)}, bf16[1024,512]{1,0:T(8,128)(2,1)S(1)}, u32[]{:S(2)}, u32[]{:S(2)}) collective-permute-start(bf16[1024,512]{1,0:T(8,128)(2,1)} %get-tuple-element.29), channel_id=1, source_target_pairs={{0,4},{4,0},{1,5},{5,1},{2,6},{6,2},{3,7},{7,3},{8,12},{12,8},{9,1... | collective-permute-start | bytes 3145736 | tf_op jit(solution)/shard_map/ppermute | solution.py:38
  73.0 15.2 %collective-permute-start.4 = (bf16[2064,128]{1,0:T(8,128)(2,1)S(1)}, bf16[2064,128]{1,0:T(8,128)(2,1)S(1)}, u32[]{:S(2)}, u32[]{:S(2)}) collective-permute-start(bf16[2064,128]{1,0:T(8,128)(2,1)S(1)} %get-tuple-element.32), channel_id=1, source_target_pairs={{0,32},{32,64},{64,96},{96,0},{8,40},{40,72},{72,104},{104,8},{16,... | collective-permute-start | bytes 1585160 | tf_op jit(solution)/shard_map/ppermute | solution.py:64
  73.5 14.8 %collective-permute-start.5 = (bf16[2064,128]{1,0:T(8,128)(2,1)S(1)}, bf16[2064,128]{1,0:T(8,128)(2,1)S(1)}, u32[]{:S(2)}, u32[]{:S(2)}) collective-permute-start(bf16[2064,128]{1,0:T(8,128)(2,1)S(1)} %get-tuple-element.33), channel_id=1, source_target_pairs={{0,64},{32,96},{64,0},{96,32},{8,72},{40,104},{72,8},{104,40},{16,... | collective-permute-start | bytes 1585160 | tf_op jit(solution)/shard_map/ppermute | solution.py:64
  74.7 14.2 %collective-permute-start.6 = (bf16[2064,128]{1,0:T(8,128)(2,1)S(1)}, bf16[2064,128]{1,0:T(8,128)(2,1)S(1)}, u32[]{:S(2)}, u32[]{:S(2)}) collective-permute-start(bf16[2064,128]{1,0:T(8,128)(2,1)S(1)} %get-tuple-element.34), channel_id=1, source_target_pairs={{0,96},{32,0},{64,32},{96,64},{8,104},{40,8},{72,40},{104,72},{16,... | collective-permute-start | bytes 1585160 | tf_op jit(solution)/shard_map/ppermute | solution.py:64
  89.7 3.9 %collective-permute-start.7 = (bf16[528,128]{1,0:T(8,128)(2,1)S(1)}, bf16[528,128]{1,0:T(8,128)(2,1)S(1)}, u32[]{:S(2)}, u32[]{:S(2)}) collective-permute-start(bf16[528,128]{1,0:T(8,128)(2,1)S(1)} %get-tuple-element.36), channel_id=1, source_target_pairs={{0,1},{1,2},{2,3},{3,0},{8,9},{9,10},{10,11},{11,8},{16,17},{17,18... | collective-permute-start | bytes 405512 | tf_op jit(solution)/shard_map/ppermute | solution.py:64
  89.8 5.8 %collective-permute-start.8 = (bf16[528,128]{1,0:T(8,128)(2,1)S(1)}, bf16[528,128]{1,0:T(8,128)(2,1)S(1)}, u32[]{:S(2)}, u32[]{:S(2)}) collective-permute-start(bf16[528,128]{1,0:T(8,128)(2,1)S(1)} %get-tuple-element.37), channel_id=1, source_target_pairs={{0,2},{1,3},{2,0},{3,1},{8,10},{9,11},{10,8},{11,9},{16,18},{17,19... | collective-permute-start | bytes 405512 | tf_op jit(solution)/shard_map/ppermute | solution.py:64
  92.9 4.2 %collective-permute-start.9 = (bf16[528,128]{1,0:T(8,128)(2,1)S(1)}, bf16[528,128]{1,0:T(8,128)(2,1)S(1)}, u32[]{:S(2)}, u32[]{:S(2)}) collective-permute-start(bf16[528,128]{1,0:T(8,128)(2,1)S(1)} %get-tuple-element.38), channel_id=1, source_target_pairs={{0,3},{1,0},{2,1},{3,2},{8,11},{9,8},{10,9},{11,10},{16,19},{17,16... | collective-permute-start | bytes 405512 | tf_op jit(solution)/shard_map/ppermute | solution.py:64
  97.2 3.9 %collective-permute-start.12 = (bf16[528,128]{1,0:T(8,128)(2,1)S(1)}, bf16[528,128]{1,0:T(8,128)(2,1)S(1)}, u32[]{:S(2)}, u32[]{:S(2)}) collective-permute-start(bf16[528,128]{1,0:T(8,128)(2,1)S(1)} %sum_four.2.here), channel_id=1, source_target_pairs={{0,24},{8,0},{16,8},{24,16},{1,25},{9,1},{17,9},{25,17},{2,26},{10... | collective-permute-start | bytes 405512 | tf_op jit(solution)/shard_map/ppermute | solution.py:64
  98.0 5.4 %collective-permute-start.11 = (bf16[528,128]{1,0:T(8,128)(2,1)S(1)}, bf16[528,128]{1,0:T(8,128)(2,1)S(1)}, u32[]{:S(2)}, u32[]{:S(2)}) collective-permute-start(bf16[528,128]{1,0:T(8,128)(2,1)S(1)} %sum_four.2.here), channel_id=1, source_target_pairs={{0,16},{8,24},{16,0},{24,8},{1,17},{9,25},{17,1},{25,9},{2,18},{10... | collective-permute-start | bytes 405512 | tf_op jit(solution)/shard_map/ppermute | solution.py:64
  99.2 5.6 %collective-permute-start.10 = (bf16[528,128]{1,0:T(8,128)(2,1)S(1)}, bf16[528,128]{1,0:T(8,128)(2,1)S(1)}, u32[]{:S(2)}, u32[]{:S(2)}) collective-permute-start(bf16[528,128]{1,0:T(8,128)(2,1)S(1)} %sum_four.2.here), channel_id=1, source_target_pairs={{0,8},{8,16},{16,24},{24,0},{1,9},{9,17},{17,25},{25,1},{2,10},{10... | collective-permute-start | bytes 405512 | tf_op jit(solution)/shard_map/ppermute | solution.py:64
  104.9 5.1 %collective-permute-start.15 = (bf16[528,128]{1,0:T(8,128)(2,1)S(1)}, bf16[528,128]{1,0:T(8,128)(2,1)S(1)}, u32[]{:S(2)}, u32[]{:S(2)}) collective-permute-start(bf16[528,128]{1,0:T(8,128)(2,1)S(1)} %sum_four.3.here), channel_id=1, source_target_pairs={{0,3},{1,0},{2,1},{3,2},{8,11},{9,8},{10,9},{11,10},{16,19},{17,16... | collective-permute-start | bytes 405512 | tf_op jit(solution)/shard_map/ppermute | solution.py:64
  106.7 5.4 %collective-permute-start.14 = (bf16[528,128]{1,0:T(8,128)(2,1)S(1)}, bf16[528,128]{1,0:T(8,128)(2,1)S(1)}, u32[]{:S(2)}, u32[]{:S(2)}) collective-permute-start(bf16[528,128]{1,0:T(8,128)(2,1)S(1)} %sum_four.3.here), channel_id=1, source_target_pairs={{0,2},{1,3},{2,0},{3,1},{8,10},{9,11},{10,8},{11,9},{16,18},{17,19... | collective-permute-start | bytes 405512 | tf_op jit(solution)/shard_map/ppermute | solution.py:64
  108.0 4.9 %collective-permute-start.13 = (bf16[528,128]{1,0:T(8,128)(2,1)S(1)}, bf16[528,128]{1,0:T(8,128)(2,1)S(1)}, u32[]{:S(2)}, u32[]{:S(2)}) collective-permute-start(bf16[528,128]{1,0:T(8,128)(2,1)S(1)} %sum_four.3.here), channel_id=1, source_target_pairs={{0,1},{1,2},{2,3},{3,0},{8,9},{9,10},{10,11},{11,8},{16,17},{17,18... | collective-permute-start | bytes 405512 | tf_op jit(solution)/shard_map/ppermute | solution.py:64
  113.0 26.4 %collective-permute-start.18 = (bf16[2064,128]{1,0:T(8,128)(2,1)S(1)}, bf16[2064,128]{1,0:T(8,128)(2,1)S(1)}, u32[]{:S(2)}, u32[]{:S(2)}) collective-permute-start(bf16[2064,128]{1,0:T(8,128)(2,1)S(1)} %join_four.1.refs_1_), channel_id=1, source_target_pairs={{0,96},{32,0},{64,32},{96,64},{8,104},{40,8},{72,40},{104,72},{16,... | collective-permute-start | bytes 1585160 | tf_op jit(solution)/shard_map/ppermute | solution.py:64
  115.4 31.4 %collective-permute-start.17 = (bf16[2064,128]{1,0:T(8,128)(2,1)S(1)}, bf16[2064,128]{1,0:T(8,128)(2,1)S(1)}, u32[]{:S(2)}, u32[]{:S(2)}) collective-permute-start(bf16[2064,128]{1,0:T(8,128)(2,1)S(1)} %join_four.1.refs_1_), channel_id=1, source_target_pairs={{0,64},{32,96},{64,0},{96,32},{8,72},{40,104},{72,8},{104,40},{16,... | collective-permute-start | bytes 1585160 | tf_op jit(solution)/shard_map/ppermute | solution.py:64
  115.4 31.4 %collective-permute-start.16 = (bf16[2064,128]{1,0:T(8,128)(2,1)S(1)}, bf16[2064,128]{1,0:T(8,128)(2,1)S(1)}, u32[]{:S(2)}, u32[]{:S(2)}) collective-permute-start(bf16[2064,128]{1,0:T(8,128)(2,1)S(1)} %join_four.1.refs_1_), channel_id=1, source_target_pairs={{0,32},{32,64},{64,96},{96,0},{8,40},{40,72},{72,104},{104,8},{16,... | collective-permute-start | bytes 1585160 | tf_op jit(solution)/shard_map/ppermute | solution.py:64
  118.6 36.4 %all-to-all-start.2 = ((bf16[64,64,128]{2,1,0:T(8,128)(2,1)}), bf16[64,64,128]{2,1,0:T(8,128)(2,1)S(1)}, u32[]{:S(2)}, u32[]{:S(2)}) async-start(bf16[64,64,128]{2,1,0:T(8,128)(2,1)} %bitcast.16), calls=%async_computation.2 | async-start | bytes 2097152 | tf_op jit(solution)/shard_map/all_to_all | solution.py:42
  126.4 21.1 %collective-permute-start.19 = (bf16[2064,128]{1,0:T(8,128)(2,1)S(1)}, bf16[2064,128]{1,0:T(8,128)(2,1)S(1)}, u32[]{:S(2)}, u32[]{:S(2)}) collective-permute-start(bf16[2064,128]{1,0:T(8,128)(2,1)S(1)} %join_four.1.refs_1_), channel_id=1, source_target_pairs={{0,4},{4,0},{1,5},{5,1},{2,6},{6,2},{3,7},{7,3},{8,12},{12,8},{9,1... | collective-permute-start | bytes 1585160 | tf_op jit(solution)/shard_map/ppermute | solution.py:38
  139.4 8.9 %collective-permute-start.22 = (bf16[2064,128]{1,0:T(8,128)(2,1)S(1)}, bf16[2064,128]{1,0:T(8,128)(2,1)S(1)}, u32[]{:S(2)}, u32[]{:S(2)}) collective-permute-start(bf16[2064,128]{1,0:T(8,128)(2,1)S(1)} %collective-permute-done.18.refs_4_), channel_id=1, source_target_pairs={{0,4},{4,0},{1,5},{5,1},{2,6},{6,2},{3,7},{7,3},{8,12},{12,8},{9,1... | collective-permute-start | bytes 1585160 | tf_op jit(solution)/shard_map/ppermute | solution.py:38
  146.7 2.3 %collective-permute-start.21 = (bf16[2064,128]{1,0:T(8,128)(2,1)S(1)}, bf16[2064,128]{1,0:T(8,128)(2,1)S(1)}, u32[]{:S(2)}, u32[]{:S(2)}) collective-permute-start(bf16[2064,128]{1,0:T(8,128)(2,1)S(1)} %collective-permute-done.17.refs_3_), channel_id=1, source_target_pairs={{0,4},{4,0},{1,5},{5,1},{2,6},{6,2},{3,7},{7,3},{8,12},{12,8},{9,1... | collective-permute-start | bytes 1585160 | tf_op jit(solution)/shard_map/ppermute | solution.py:38
  146.7 3.0 %collective-permute-start.20 = (bf16[2064,128]{1,0:T(8,128)(2,1)S(1)}, bf16[2064,128]{1,0:T(8,128)(2,1)S(1)}, u32[]{:S(2)}, u32[]{:S(2)}) collective-permute-start(bf16[2064,128]{1,0:T(8,128)(2,1)S(1)} %collective-permute-done.16.refs_2_), channel_id=1, source_target_pairs={{0,4},{4,0},{1,5},{5,1},{2,6},{6,2},{3,7},{7,3},{8,12},{12,8},{9,1... | collective-permute-start | bytes 1585160 | tf_op jit(solution)/shard_map/ppermute | solution.py:38
  (8 other events, 193.7 us)

commit v4 on v3

--- a/solution.py
+++ b/solution.py
@@ -73,18 +73,23 @@
 
 
 def request_at(row):
-    return (row // PAIR_CAP) * LANES + row % PAIR_CAP
-
-
-def gather_kernel(asked, table_ref, out_ref, wide, picked):
-    step = 1024
-
-    def widen(i, carry):
-        rows = pl.ds(pl.multiple_of(i * step, step), step)
-        wide[rows, :] = table_ref[rows, :].astype(f32)
-        return carry
-
-    lax.fori_loop(0, ROWS // step, widen, 0)
+    return lax.shift_left(lax.shift_right_logical(row, 6), 7) + lax.bitwise_and(row, 63)
+
+
+def gather_kernel(asked, table_ref, out_ref, near, sems, wide, picked):
+    step = ROWS // 8
+    copies = [
+        pltpu.make_async_copy(
+            table_ref.at[pl.ds(i * step, step)], near.at[pl.ds(i * step, step)], sems.at[i]
+        )
+        for i in range(8)
+    ]
+    for copy in copies:
+        copy.start()
+    for i, copy in enumerate(copies):
+        copy.wait()
+        rows = slice(i * step, (i + 1) * step)
+        wide[rows, :] = near[rows, :].astype(f32)
     unroll = 16
 
     def pick(i, carry):
@@ -110,12 +115,17 @@
         grid_spec=pltpu.PrefetchScalarGridSpec(
             num_scalar_prefetch=1,
             grid=(1,),
-            in_specs=[whole((ROWS, LANES))],
+            in_specs=[pl.BlockSpec(memory_space=pltpu.HBM)],
             out_specs=whole((N_PEERS, PAIR_CAP, LANES)),
-            scratch_shapes=[pltpu.VMEM((ROWS, LANES), f32), pltpu.VMEM((N_REQ, LANES), f32)],
+            scratch_shapes=[
+                pltpu.VMEM((ROWS, LANES), bf16),
+                pltpu.SemaphoreType.DMA((8,)),
+                pltpu.VMEM((ROWS, LANES), f32),
+                pltpu.VMEM((N_REQ, LANES), f32),
+            ],
         ),
         out_shape=jax.ShapeDtypeStruct((N_PEERS, PAIR_CAP, LANES), bf16),
-        compiler_params=params(24),
+        compiler_params=params(58),
         name="gather_rows",
     )(asked, table)
 
@@ -566,15 +576,18 @@
         w_out,
     )
     other = swap(send)
-    split = list(sum_split(place, ring[:1] + [along(0, ring[s], s) for s in (1, 2, 3)]))
+    ring_got = [along(0, ring[s], s) for s in (1, 2, 3)]
     payload = pack(slot_own, part, other, emb, gain_row, cot_own, cot_other)
+    place_late, payload, *ring_got = lax.optimization_barrier((place, payload, *ring_got))
+    split = list(sum_split(place_late, ring[:1] + ring_got))
     arrived = exchange(payload.reshape(N_PEERS, PAIR_CAP, LANES))
     mine = sum_four(split[:1] + [along(1, split[s], s) for s in (1, 2, 3)])
     total = sum_four([mine] + [along(2, mine, s) for s in (1, 2, 3)])
     joined = join_four([total] + [along(1, total, s) for s in (1, 2, 3)])
     pieces = [joined] + [along(0, joined, s) for s in (1, 2, 3)]
     table_grad = scatter_rows(asked, arrived)
-    pieces += [swap(p) for p in pieces]
+    *late, table_grad = lax.optimization_barrier((*pieces, table_grad))
+    pieces += [swap(p) for p in late]
     scale = 1.0 / math.sqrt(TOK * N_PEERS * N_CORE)
     g_out, g_in, g_bias, g_gain = finish(place, pieces, scale)
     return (table_grad, g_in, g_bias.reshape(-1), g_out, g_gain.reshape(-1))

time: 173 us -> 165 us (0.954)
  the two profiles are of different devices: /device:TPU:33 before, /device:TPU:1 now
where the time goes in v4:
time: 165 us; the launch traced here: 164 us
  Pallas kernels  47.6 us (29%)
  blocking collectives  41.3 us (25%)
  waiting for transfers between devices  37.7 us (23%)
  starting transfers between devices  31.2 us (19%)
  local copies, waits for them, and re-layouts  4.75 us (3%)
    all_to_all x2, blocking collectives, exchange(): return lax.all_to_all(a, PEERS, split_axis=0, concat_axis=0, tiled=True)  41.3 us
    ppermute x15, waiting for transfers between devices, along(): return lax.ppermute(a, EVERY, pairs)  32 us
    ppermute x15, starting transfers between devices, along(): return lax.ppermute(a, EVERY, pairs)  16.1 us
    pallas_call x1, Pallas kernels, scatter_rows(): pl.pallas_call(scatter_kernel, grid_spec=pltpu.PrefetchScalarGridSpec(num...  15.3 us
    pallas_call x1, Pallas kernels, block(): pl.pallas_call(block_kernel, grid_spec=pltpu.PrefetchScalarGridSpec(num_s...  15.2 us
    ppermute x8, starting transfers between devices, swap(): return lax.ppermute(a, 'core', [(0, 1), (1, 0)])  9.62 us
    pallas_call x1, Pallas kernels, gather_rows(): pl.pallas_call(gather_kernel, grid_spec=pltpu.PrefetchScalarGridSpec(num_...  8.35 us
    ppermute x8, waiting for transfers between devices, swap(): return lax.ppermute(a, 'core', [(0, 1), (1, 0)])  5.71 us
  transfers between devices with their start and end apart: 24, of which 17 were waited for; matrix products, arithmetic and copies ran while one was open for 1% of the time, Pallas kernels for 11%

profile of v4, /device:TPU:1, one launch (start us, length us, event | category | flops | bytes accessed | tf_op | source)
XLA Modules:
  0.0 164.1 jit_solution(4664151045845208965)
XLA Ops:
  4.9 19.5 %all_to_all.15 = s32[64,1,128]{2,1,0:T(1,128)} all-to-all(s32[64,1,128]{2,1,0:T(1,128)S(1)} %bitcast.51), channel_id=1, replica_groups=mesh['x'=4,'z'=4,'core'=2,'y'=4] {'x','z','y'}, dimensions={0} | all-to-all | bytes 65536 | tf_op jit(solution)/shard_map/all_to_all | solution.py:42
  24.4 8.4 %gather_rows.1 = bf16[64,64,128]{2,1,0:T(8,128)(2,1)} custom-call(s32[8192]{0:T(1024)} %bitcast.45, bf16[8192,128]{1,0:T(8,128)(2,1)} %table_ref.1), custom_call_target="tpu_custom_call" | custom-call | tf_op jit(solution)/shard_map/gather_rows/pallas_call | solution.py:113
  32.8 21.8 %all_to_all.16 = bf16[64,64,128]{2,1,0:T(8,128)(2,1)} all-to-all(bf16[64,64,128]{2,1,0:T(8,128)(2,1)} %gather_rows.1), channel_id=1, replica_groups=mesh['x'=4,'z'=4,'core'=2,'y'=4] {'x','z','y'}, dimensions={0} | all-to-all | bytes 2097152 | tf_op jit(solution)/shard_map/all_to_all | solution.py:42
  54.6 3.3 %collective-permute-start.2 = (bf16[16,4,64,128]{3,2,1,0:T(8,128)(2,1)}, bf16[16,4,64,128]{3,2,1,0:T(8,128)(2,1)}, u32[]{:S(2)}, u32[]{:S(2)}) collective-permute-start(bf16[16,4,64,128]{3,2,1,0:T(8,128)(2,1)} %bitcast.13.got_own), channel_id=1, source_target_pairs={{0,4},{4,0},{1,5},{5,1},{2,6},{6,2},{3,7},{7,3},{8,12},{12,8},{9,1... | collective-permute-start | bytes 3145736 | tf_op jit(solution)/shard_map/ppermute | solution.py:38
  58.4 2.1 %collective-permute-done.2.got_other = bf16[16,4,64,128]{3,2,1,0:T(8,128)(2,1)} collective-permute-done((bf16[16,4,64,128]{3,2,1,0:T(8,128)(2,1)}, bf16[16,4,64,128]{3,2,1,0:T(8,128)(2,1)}, u32[]{:S(2)}, u32[]{:S(2)}) %collective-permute-start.2) | collective-permute-done | bytes 1048608 | tf_op jit(solution)/shard_map/ppermute | solution.py:38
  60.5 15.2 %block.1 = (bf16[1024,512]{1,0:T(8,128)(2,1)S(1)}, f32[1024,512]{1,0:T(8,128)}, bf16[1024,512]{1,0:T(8,128)(2,1)}, bf16[2064,128]{1,0:T(8,128)(2,1)S(1)}, bf16[2...) custom-call(s32[5]{0:T(128)S(1)} %stack.31.place.refs_0_, ...), custom_call_target="tpu_custom_call" | custom-call | tf_op jit(solution)/shard_map/block/pallas_call | solution.py:252
  80.4 1.6 copy-done.6
  81.9 2.5 %pack.1 = bf16[16,4,64,128]{3,2,1,0:T(8,128)(2,1)} custom-call(s32[2,512]{1,0:T(2,128)S(1)} %broadcast_select_fusion.1.slot_ref, f32[1024,512]{1,0:T(8,128)S(1)} %copy-done.6, bf16[1024,512]{1,0:T(8,128)(2,1)S(1)} %collective-permute-done.3.other_ref, bf16[1024,512]{1,0:T(8,128)(2,1)S(1)} %get-tuple-element.40.emb_ref, f32[1,512]{1,0:T(1,128)S(1)} %bitcast.50, ...), custom_call_target="tpu_custom_call" | custom-call | flops 2000000000 | bytes 10000000 | tf_op jit(solution)/shard_map/pack/pallas_call | solution.py:321
  84.5 6.9 %collective-permute-done.4.back_1 = bf16[2064,128]{1,0:T(8,128)(2,1)S(1)} collective-permute-done((bf16[2064,128]{1,0:T(8,128)(2,1)S(1)}, bf16[2064,128]{1,0:T(8,128)(2,1)S(1)}, u32[]{:S(2)}, u32[]{:S(2)}) %collective-permute-start.4) | collective-permute-done | bytes 528416 | tf_op jit(solution)/shard_map/ppermute | solution.py:64
  91.9 5.5 %all-to-all-start.2 = ((bf16[64,64,128]{2,1,0:T(8,128)(2,1)}), bf16[64,64,128]{2,1,0:T(8,128)(2,1)S(1)}, u32[]{:S(2)}, u32[]{:S(2)}) async-start(bf16[64,64,128]{2,1,0:T(8,128)(2,1)} %bitcast.16), calls=%async_computation.2 | async-start | bytes 2097152 | tf_op jit(solution)/shard_map/all_to_all | solution.py:42
  99.5 2.4 %collective-permute-start.8 = (bf16[528,128]{1,0:T(8,128)(2,1)S(1)}, bf16[528,128]{1,0:T(8,128)(2,1)S(1)}, u32[]{:S(2)}, u32[]{:S(2)}) collective-permute-start(bf16[528,128]{1,0:T(8,128)(2,1)S(1)} %get-tuple-element.51), channel_id=1, source_target_pairs={{0,2},{1,3},{2,0},{3,1},{8,10},{9,11},{10,8},{11,9},{16,18},{17,19... | collective-permute-start | bytes 405512 | tf_op jit(solution)/shard_map/ppermute | solution.py:64
  103.1 8.2 %collective-permute-done.7.back_1 = bf16[528,128]{1,0:T(8,128)(2,1)S(1)} collective-permute-done((bf16[528,128]{1,0:T(8,128)(2,1)S(1)}, bf16[528,128]{1,0:T(8,128)(2,1)S(1)}, u32[]{:S(2)}, u32[]{:S(2)}) %collective-permute-start.7) | collective-permute-done | bytes 135200 | tf_op jit(solution)/shard_map/ppermute | solution.py:64
  111.2 5.3 %collective-permute-done.8.back_2 = bf16[528,128]{1,0:T(8,128)(2,1)S(1)} collective-permute-done((bf16[528,128]{1,0:T(8,128)(2,1)S(1)}, bf16[528,128]{1,0:T(8,128)(2,1)S(1)}, u32[]{:S(2)}, u32[]{:S(2)}) %collective-permute-start.8) | collective-permute-done | bytes 135200 | tf_op jit(solution)/shard_map/ppermute | solution.py:64
  116.6 1.8 %collective-permute-start.12 = (bf16[528,128]{1,0:T(8,128)(2,1)S(1)}, bf16[528,128]{1,0:T(8,128)(2,1)S(1)}, u32[]{:S(2)}, u32[]{:S(2)}) collective-permute-start(bf16[528,128]{1,0:T(8,128)(2,1)S(1)} %sum_four.2.here), channel_id=1, source_target_pairs={{0,24},{8,0},{16,8},{24,16},{1,25},{9,1},{17,9},{25,17},{2,26},{10... | collective-permute-start | bytes 405512 | tf_op jit(solution)/shard_map/ppermute | solution.py:64
  119.6 2.2 %collective-permute-done.12.back_3 = bf16[528,128]{1,0:T(8,128)(2,1)S(1)} collective-permute-done((bf16[528,128]{1,0:T(8,128)(2,1)S(1)}, bf16[528,128]{1,0:T(8,128)(2,1)S(1)}, u32[]{:S(2)}, u32[]{:S(2)}) %collective-permute-start.12) | collective-permute-done | bytes 135200 | tf_op jit(solution)/shard_map/ppermute | solution.py:64
  121.8 2.3 %collective-permute-done.11.back_2 = bf16[528,128]{1,0:T(8,128)(2,1)S(1)} collective-permute-done((bf16[528,128]{1,0:T(8,128)(2,1)S(1)}, bf16[528,128]{1,0:T(8,128)(2,1)S(1)}, u32[]{:S(2)}, u32[]{:S(2)}) %collective-permute-start.11) | collective-permute-done | bytes 135200 | tf_op jit(solution)/shard_map/ppermute | solution.py:64
  124.1 1.4 collective-permute-done.10.back_1
  126.2 1.7 %collective-permute-start.14 = (bf16[528,128]{1,0:T(8,128)(2,1)S(1)}, bf16[528,128]{1,0:T(8,128)(2,1)S(1)}, u32[]{:S(2)}, u32[]{:S(2)}) collective-permute-start(bf16[528,128]{1,0:T(8,128)(2,1)S(1)} %sum_four.3.here), channel_id=1, source_target_pairs={{0,2},{1,3},{2,0},{3,1},{8,10},{9,11},{10,8},{11,9},{16,18},{17,19... | collective-permute-start | bytes 405512 | tf_op jit(solution)/shard_map/ppermute | solution.py:64
  129.5 2.1 %collective-permute-done.14.back_2 = bf16[528,128]{1,0:T(8,128)(2,1)S(1)} collective-permute-done((bf16[528,128]{1,0:T(8,128)(2,1)S(1)}, bf16[528,128]{1,0:T(8,128)(2,1)S(1)}, u32[]{:S(2)}, u32[]{:S(2)}) %collective-permute-start.14) | collective-permute-done | bytes 135200 | tf_op jit(solution)/shard_map/ppermute | solution.py:64
  131.6 1.7 %collective-permute-done.13.back_1 = bf16[528,128]{1,0:T(8,128)(2,1)S(1)} collective-permute-done((bf16[528,128]{1,0:T(8,128)(2,1)S(1)}, bf16[528,128]{1,0:T(8,128)(2,1)S(1)}, u32[]{:S(2)}, u32[]{:S(2)}) %collective-permute-start.13) | collective-permute-done | bytes 135200 | tf_op jit(solution)/shard_map/ppermute | solution.py:64
  133.4 1.7 %collective-permute-start.18 = (bf16[2064,128]{1,0:T(8,128)(2,1)S(1)}, bf16[2064,128]{1,0:T(8,128)(2,1)S(1)}, u32[]{:S(2)}, u32[]{:S(2)}) collective-permute-start(bf16[2064,128]{1,0:T(8,128)(2,1)S(1)} %join_four.1.refs_1_), channel_id=1, source_target_pairs={{0,96},{32,0},{64,32},{96,64},{8,104},{40,8},{72,40},{104,72},{16,... | collective-permute-start | bytes 1585160 | tf_op jit(solution)/shard_map/ppermute | solution.py:64
  135.8 15.3 %scatter_rows.1 = f32[8192,128]{1,0:T(8,128)} custom-call(s32[8192]{0:T(1024)S(1)} %bitcast.46, bf16[64,64,128]{2,1,0:T(8,128)(2,1)S(1)} %all-to-all-done.2.arrived_ref), custom_call_target="tpu_custom_call" | custom-call | flops 10000000000 | bytes 10000000 | tf_op jit(solution)/shard_map/scatter_rows/pallas_call | solution.py:376
  151.1 4.0 %collective-permute-start.19 = (bf16[2064,128]{1,0:T(8,128)(2,1)S(1)}, bf16[2064,128]{1,0:T(8,128)(2,1)S(1)}, u32[]{:S(2)}, u32[]{:S(2)}) collective-permute-start(bf16[2064,128]{1,0:T(8,128)(2,1)S(1)} %join_four.1.refs_1_), channel_id=1, source_target_pairs={{0,4},{4,0},{1,5},{5,1},{2,6},{6,2},{3,7},{7,3},{8,12},{12,8},{9,1... | collective-permute-start | bytes 1585160 | tf_op jit(solution)/shard_map/ppermute | solution.py:38
  158.9 5.2 %finish.1 = (f32[2048,512]{1,0:T(8,128)}, f32[512,2048]{1,0:T(8,128)}, f32[16,128]{1,0:T(8,128)}, f32[4,128]{1,0:T(4,128)}) custom-call(s32[5]{0:T(128)S(1)} %stack.31.place.refs_0_, bf16[2064,128]{1,0:T(8,128)(2,1)S(1)} %join_four.1.refs_1_, bf16[2064,128]{1,0:T(8,128)(2,1)S(1)} %collective-permute-done.16.refs_2_, ...), custom_call_target="tpu_custom_call" | custom-call | tf_op jit(solution)/shard_map/finish/pallas_call | solution.py:497
  (66 shorter events, 21.6 us)
Async XLA Ops:
  1.3 2.2 %collective-permute-start = (s32[512]{0:T(512)S(1)}, s32[512]{0:T(512)S(1)}, u32[]{:S(2)}, u32[]{:S(2)}) collective-permute-start(s32[512]{0:T(512)S(1)} %bitcast.59), channel_id=1, source_target_pairs={{0,4},{4,0},{1,5},{5,1},{2,6},{6,2},{3,7},{7,3},{8,12},{12,8},{9,1... | collective-permute-start | bytes 6152 | tf_op jit(solution)/shard_map/ppermute | solution.py:38
  2.7 2.1 %collective-permute-start.1 = (bf16[512,512]{1,0:T(8,128)(2,1)}, bf16[512,512]{1,0:T(8,128)(2,1)S(1)}, u32[]{:S(2)}, u32[]{:S(2)}) collective-permute-start(bf16[512,512]{1,0:T(8,128)(2,1)} %bitcast.42), channel_id=1, source_target_pairs={{0,4},{4,0},{1,5},{5,1},{2,6},{6,2},{3,7},{7,3},{8,12},{12,8},{9,1... | collective-permute-start | bytes 1572872 | tf_op jit(solution)/shard_map/ppermute | solution.py:38
  54.6 5.9 %collective-permute-start.2 = (bf16[16,4,64,128]{3,2,1,0:T(8,128)(2,1)}, bf16[16,4,64,128]{3,2,1,0:T(8,128)(2,1)}, u32[]{:S(2)}, u32[]{:S(2)}) collective-permute-start(bf16[16,4,64,128]{3,2,1,0:T(8,128)(2,1)} %bitcast.13.got_own), channel_id=1, source_target_pairs={{0,4},{4,0},{1,5},{5,1},{2,6},{6,2},{3,7},{7,3},{8,12},{12,8},{9,1... | collective-permute-start | bytes 3145736 | tf_op jit(solution)/shard_map/ppermute | solution.py:38
  75.7 3.6 %collective-permute-start.3 = (bf16[1024,512]{1,0:T(8,128)(2,1)}, bf16[1024,512]{1,0:T(8,128)(2,1)S(1)}, u32[]{:S(2)}, u32[]{:S(2)}) collective-permute-start(bf16[1024,512]{1,0:T(8,128)(2,1)} %get-tuple-element.39), channel_id=1, source_target_pairs={{0,4},{4,0},{1,5},{5,1},{2,6},{6,2},{3,7},{7,3},{8,12},{12,8},{9,1... | collective-permute-start | bytes 3145736 | tf_op jit(solution)/shard_map/ppermute | solution.py:38
  76.1 15.2 %collective-permute-start.4 = (bf16[2064,128]{1,0:T(8,128)(2,1)S(1)}, bf16[2064,128]{1,0:T(8,128)(2,1)S(1)}, u32[]{:S(2)}, u32[]{:S(2)}) collective-permute-start(bf16[2064,128]{1,0:T(8,128)(2,1)S(1)} %get-tuple-element.41), channel_id=1, source_target_pairs={{0,32},{32,64},{64,96},{96,0},{8,40},{40,72},{72,104},{104,8},{16,... | collective-permute-start | bytes 1585160 | tf_op jit(solution)/shard_map/ppermute | solution.py:64
  76.6 14.7 %collective-permute-start.5 = (bf16[2064,128]{1,0:T(8,128)(2,1)S(1)}, bf16[2064,128]{1,0:T(8,128)(2,1)S(1)}, u32[]{:S(2)}, u32[]{:S(2)}) collective-permute-start(bf16[2064,128]{1,0:T(8,128)(2,1)S(1)} %get-tuple-element.42), channel_id=1, source_target_pairs={{0,64},{32,96},{64,0},{96,32},{8,72},{40,104},{72,8},{104,40},{16,... | collective-permute-start | bytes 1585160 | tf_op jit(solution)/shard_map/ppermute | solution.py:64
  77.9 14.1 %collective-permute-start.6 = (bf16[2064,128]{1,0:T(8,128)(2,1)S(1)}, bf16[2064,128]{1,0:T(8,128)(2,1)S(1)}, u32[]{:S(2)}, u32[]{:S(2)}) collective-permute-start(bf16[2064,128]{1,0:T(8,128)(2,1)S(1)} %get-tuple-element.43), channel_id=1, source_target_pairs={{0,96},{32,0},{64,32},{96,64},{8,104},{40,8},{72,40},{104,72},{16,... | collective-permute-start | bytes 1585160 | tf_op jit(solution)/shard_map/ppermute | solution.py:64
  91.9 43.9 %all-to-all-start.2 = ((bf16[64,64,128]{2,1,0:T(8,128)(2,1)}), bf16[64,64,128]{2,1,0:T(8,128)(2,1)S(1)}, u32[]{:S(2)}, u32[]{:S(2)}) async-start(bf16[64,64,128]{2,1,0:T(8,128)(2,1)} %bitcast.16), calls=%async_computation.2 | async-start | bytes 2097152 | tf_op jit(solution)/shard_map/all_to_all | solution.py:42
  98.2 13.0 %collective-permute-start.7 = (bf16[528,128]{1,0:T(8,128)(2,1)S(1)}, bf16[528,128]{1,0:T(8,128)(2,1)S(1)}, u32[]{:S(2)}, u32[]{:S(2)}) collective-permute-start(bf16[528,128]{1,0:T(8,128)(2,1)S(1)} %get-tuple-element.50), channel_id=1, source_target_pairs={{0,1},{1,2},{2,3},{3,0},{8,9},{9,10},{10,11},{11,8},{16,17},{17,18... | collective-permute-start | bytes 405512 | tf_op jit(solution)/shard_map/ppermute | solution.py:64
  99.5 17.0 %collective-permute-start.8 = (bf16[528,128]{1,0:T(8,128)(2,1)S(1)}, bf16[528,128]{1,0:T(8,128)(2,1)S(1)}, u32[]{:S(2)}, u32[]{:S(2)}) collective-permute-start(bf16[528,128]{1,0:T(8,128)(2,1)S(1)} %get-tuple-element.51), channel_id=1, source_target_pairs={{0,2},{1,3},{2,0},{3,1},{8,10},{9,11},{10,8},{11,9},{16,18},{17,19... | collective-permute-start | bytes 405512 | tf_op jit(solution)/shard_map/ppermute | solution.py:64
  101.9 14.6 %collective-permute-start.9 = (bf16[528,128]{1,0:T(8,128)(2,1)S(1)}, bf16[528,128]{1,0:T(8,128)(2,1)S(1)}, u32[]{:S(2)}, u32[]{:S(2)}) collective-permute-start(bf16[528,128]{1,0:T(8,128)(2,1)S(1)} %get-tuple-element.52), channel_id=1, source_target_pairs={{0,3},{1,0},{2,1},{3,2},{8,11},{9,8},{10,9},{11,10},{16,19},{17,16... | collective-permute-start | bytes 405512 | tf_op jit(solution)/shard_map/ppermute | solution.py:64
  116.6 5.2 %collective-permute-start.12 = (bf16[528,128]{1,0:T(8,128)(2,1)S(1)}, bf16[528,128]{1,0:T(8,128)(2,1)S(1)}, u32[]{:S(2)}, u32[]{:S(2)}) collective-permute-start(bf16[528,128]{1,0:T(8,128)(2,1)S(1)} %sum_four.2.here), channel_id=1, source_target_pairs={{0,24},{8,0},{16,8},{24,16},{1,25},{9,1},{17,9},{25,17},{2,26},{10... | collective-permute-start | bytes 405512 | tf_op jit(solution)/shard_map/ppermute | solution.py:64
  118.4 5.7 %collective-permute-start.11 = (bf16[528,128]{1,0:T(8,128)(2,1)S(1)}, bf16[528,128]{1,0:T(8,128)(2,1)S(1)}, u32[]{:S(2)}, u32[]{:S(2)}) collective-permute-start(bf16[528,128]{1,0:T(8,128)(2,1)S(1)} %sum_four.2.here), channel_id=1, source_target_pairs={{0,16},{8,24},{16,0},{24,8},{1,17},{9,25},{17,1},{25,9},{2,18},{10... | collective-permute-start | bytes 405512 | tf_op jit(solution)/shard_map/ppermute | solution.py:64
  119.3 6.2 %collective-permute-start.10 = (bf16[528,128]{1,0:T(8,128)(2,1)S(1)}, bf16[528,128]{1,0:T(8,128)(2,1)S(1)}, u32[]{:S(2)}, u32[]{:S(2)}) collective-permute-start(bf16[528,128]{1,0:T(8,128)(2,1)S(1)} %sum_four.2.here), channel_id=1, source_target_pairs={{0,8},{8,16},{16,24},{24,0},{1,9},{9,17},{17,25},{25,1},{2,10},{10... | collective-permute-start | bytes 405512 | tf_op jit(solution)/shard_map/ppermute | solution.py:64
  125.6 3.9 %collective-permute-start.15 = (bf16[528,128]{1,0:T(8,128)(2,1)S(1)}, bf16[528,128]{1,0:T(8,128)(2,1)S(1)}, u32[]{:S(2)}, u32[]{:S(2)}) collective-permute-start(bf16[528,128]{1,0:T(8,128)(2,1)S(1)} %sum_four.3.here), channel_id=1, source_target_pairs={{0,3},{1,0},{2,1},{3,2},{8,11},{9,8},{10,9},{11,10},{16,19},{17,16... | collective-permute-start | bytes 405512 | tf_op jit(solution)/shard_map/ppermute | solution.py:64
  126.2 5.4 %collective-permute-start.14 = (bf16[528,128]{1,0:T(8,128)(2,1)S(1)}, bf16[528,128]{1,0:T(8,128)(2,1)S(1)}, u32[]{:S(2)}, u32[]{:S(2)}) collective-permute-start(bf16[528,128]{1,0:T(8,128)(2,1)S(1)} %sum_four.3.here), channel_id=1, source_target_pairs={{0,2},{1,3},{2,0},{3,1},{8,10},{9,11},{10,8},{11,9},{16,18},{17,19... | collective-permute-start | bytes 405512 | tf_op jit(solution)/shard_map/ppermute | solution.py:64
  127.9 5.4 %collective-permute-start.13 = (bf16[528,128]{1,0:T(8,128)(2,1)S(1)}, bf16[528,128]{1,0:T(8,128)(2,1)S(1)}, u32[]{:S(2)}, u32[]{:S(2)}) collective-permute-start(bf16[528,128]{1,0:T(8,128)(2,1)S(1)} %sum_four.3.here), channel_id=1, source_target_pairs={{0,1},{1,2},{2,3},{3,0},{8,9},{9,10},{10,11},{11,8},{16,17},{17,18... | collective-permute-start | bytes 405512 | tf_op jit(solution)/shard_map/ppermute | solution.py:64
  133.4 17.7 %collective-permute-start.18 = (bf16[2064,128]{1,0:T(8,128)(2,1)S(1)}, bf16[2064,128]{1,0:T(8,128)(2,1)S(1)}, u32[]{:S(2)}, u32[]{:S(2)}) collective-permute-start(bf16[2064,128]{1,0:T(8,128)(2,1)S(1)} %join_four.1.refs_1_), channel_id=1, source_target_pairs={{0,96},{32,0},{64,32},{96,64},{8,104},{40,8},{72,40},{104,72},{16,... | collective-permute-start | bytes 1585160 | tf_op jit(solution)/shard_map/ppermute | solution.py:64
  135.0 16.1 %collective-permute-start.17 = (bf16[2064,128]{1,0:T(8,128)(2,1)S(1)}, bf16[2064,128]{1,0:T(8,128)(2,1)S(1)}, u32[]{:S(2)}, u32[]{:S(2)}) collective-permute-start(bf16[2064,128]{1,0:T(8,128)(2,1)S(1)} %join_four.1.refs_1_), channel_id=1, source_target_pairs={{0,64},{32,96},{64,0},{96,32},{8,72},{40,104},{72,8},{104,40},{16,... | collective-permute-start | bytes 1585160 | tf_op jit(solution)/shard_map/ppermute | solution.py:64
  135.4 15.8 %collective-permute-start.16 = (bf16[2064,128]{1,0:T(8,128)(2,1)S(1)}, bf16[2064,128]{1,0:T(8,128)(2,1)S(1)}, u32[]{:S(2)}, u32[]{:S(2)}) collective-permute-start(bf16[2064,128]{1,0:T(8,128)(2,1)S(1)} %join_four.1.refs_1_), channel_id=1, source_target_pairs={{0,32},{32,64},{64,96},{96,0},{8,40},{40,72},{72,104},{104,8},{16,... | collective-permute-start | bytes 1585160 | tf_op jit(solution)/shard_map/ppermute | solution.py:64
  151.1 5.5 %collective-permute-start.19 = (bf16[2064,128]{1,0:T(8,128)(2,1)S(1)}, bf16[2064,128]{1,0:T(8,128)(2,1)S(1)}, u32[]{:S(2)}, u32[]{:S(2)}) collective-permute-start(bf16[2064,128]{1,0:T(8,128)(2,1)S(1)} %join_four.1.refs_1_), channel_id=1, source_target_pairs={{0,4},{4,0},{1,5},{5,1},{2,6},{6,2},{3,7},{7,3},{8,12},{12,8},{9,1... | collective-permute-start | bytes 1585160 | tf_op jit(solution)/shard_map/ppermute | solution.py:38
  155.1 2.3 %collective-permute-start.20 = (bf16[2064,128]{1,0:T(8,128)(2,1)S(1)}, bf16[2064,128]{1,0:T(8,128)(2,1)S(1)}, u32[]{:S(2)}, u32[]{:S(2)}) collective-permute-start(bf16[2064,128]{1,0:T(8,128)(2,1)S(1)} %collective-permute-done.16.refs_2_), channel_id=1, source_target_pairs={{0,4},{4,0},{1,5},{5,1},{2,6},{6,2},{3,7},{7,3},{8,12},{12,8},{9,1... | collective-permute-start | bytes 1585160 | tf_op jit(solution)/shard_map/ppermute | solution.py:38
  155.2 3.0 %collective-permute-start.21 = (bf16[2064,128]{1,0:T(8,128)(2,1)S(1)}, bf16[2064,128]{1,0:T(8,128)(2,1)S(1)}, u32[]{:S(2)}, u32[]{:S(2)}) collective-permute-start(bf16[2064,128]{1,0:T(8,128)(2,1)S(1)} %collective-permute-done.17.refs_3_), channel_id=1, source_target_pairs={{0,4},{4,0},{1,5},{5,1},{2,6},{6,2},{3,7},{7,3},{8,12},{12,8},{9,1... | collective-permute-start | bytes 1585160 | tf_op jit(solution)/shard_map/ppermute | solution.py:38
  155.6 3.3 %collective-permute-start.22 = (bf16[2064,128]{1,0:T(8,128)(2,1)S(1)}, bf16[2064,128]{1,0:T(8,128)(2,1)S(1)}, u32[]{:S(2)}, u32[]{:S(2)}) collective-permute-start(bf16[2064,128]{1,0:T(8,128)(2,1)S(1)} %collective-permute-done.18.refs_4_), channel_id=1, source_target_pairs={{0,4},{4,0},{1,5},{5,1},{2,6},{6,2},{3,7},{7,3},{8,12},{12,8},{9,1... | collective-permute-start | bytes 1585160 | tf_op jit(solution)/shard_map/ppermute | solution.py:38
  (7 other events, 179.8 us)

commit v5 on v4

--- a/solution.py
+++ b/solution.py
@@ -419,6 +419,7 @@
         ),
         out_shape=[jax.ShapeDtypeStruct((N_BLOCK + N_VEC, LANES), bf16)] * 4,
         compiler_params=params(8),
+        cost_estimate=pl.CostEstimate(flops=2*10**9, bytes_accessed=10**6, transcendentals=0),
         name="sum_split",
     )(place, *pieces)
 
@@ -435,6 +436,7 @@
         sum_kernel,
         out_shape=jax.ShapeDtypeStruct((N_BLOCK + N_VEC, LANES), bf16),
         compiler_params=params(4),
+        cost_estimate=pl.CostEstimate(flops=2*10**9, bytes_accessed=10**6, transcendentals=0),
         name="sum_four",
     )(*pieces)
 
@@ -450,6 +452,7 @@
         join_kernel,
         out_shape=jax.ShapeDtypeStruct((N_RING, LANES), bf16),
         compiler_params=params(4),
+        cost_estimate=pl.CostEstimate(flops=2*10**9, bytes_accessed=10**6, transcendentals=0),
         name="join_four",
     )(*pieces)
 
@@ -578,7 +581,7 @@
     other = swap(send)
     ring_got = [along(0, ring[s], s) for s in (1, 2, 3)]
     payload = pack(slot_own, part, other, emb, gain_row, cot_own, cot_other)
-    place_late, payload, *ring_got = lax.optimization_barrier((place, payload, *ring_got))
+    place_late, payload = lax.optimization_barrier((place, payload))
     split = list(sum_split(place_late, ring[:1] + ring_got))
     arrived = exchange(payload.reshape(N_PEERS, PAIR_CAP, LANES))
     mine = sum_four(split[:1] + [along(1, split[s], s) for s in (1, 2, 3)])

time: 165 us -> 161 us (0.976)
  the two profiles are of different devices: /device:TPU:1 before, /device:TPU:99 now
where the time goes in v5:
time: 161 us; the launch traced here: 160 us
  Pallas kernels  49.2 us (31%)
  starting transfers between devices  45.2 us (28%)
  blocking collectives  37.5 us (23%)
  waiting for transfers between devices  23.1 us (14%)
  local copies, waits for them, and re-layouts  3.72 us (2%)
    all_to_all x2, blocking collectives, exchange(): return lax.all_to_all(a, PEERS, split_axis=0, concat_axis=0, tiled=True)  37.5 us
    ppermute x8, starting transfers between devices, swap(): return lax.ppermute(a, 'core', [(0, 1), (1, 0)])  18.5 us
    ppermute x15, starting transfers between devices, along(): return lax.ppermute(a, EVERY, pairs)  18.4 us
    ppermute x15, waiting for transfers between devices, along(): return lax.ppermute(a, EVERY, pairs)  17.7 us
    pallas_call x1, Pallas kernels, block(): pl.pallas_call(block_kernel, grid_spec=pltpu.PrefetchScalarGridSpec(num_s...  15.5 us
    pallas_call x1, Pallas kernels, scatter_rows(): pl.pallas_call(scatter_kernel, grid_spec=pltpu.PrefetchScalarGridSpec(num...  15.3 us
    pallas_call x1, Pallas kernels, gather_rows(): pl.pallas_call(gather_kernel, grid_spec=pltpu.PrefetchScalarGridSpec(num_...  8.35 us
    all_to_all x1, starting transfers between devices, exchange(): return lax.all_to_all(a, PEERS, split_axis=0, concat_axis=0, tiled=True)  8.33 us
  transfers between devices with their start and end apart: 24, of which 16 were waited for; matrix products, arithmetic and copies ran while one was open for 1% of the time, Pallas kernels for 13%

profile of v5, /device:TPU:99, one launch (start us, length us, event | category | flops | bytes accessed | tf_op | source)
XLA Modules:
  0.0 160.4 jit_solution(11209303964588677893)
XLA Ops:
  4.1 15.7 %all_to_all.15 = s32[64,1,128]{2,1,0:T(1,128)} all-to-all(s32[64,1,128]{2,1,0:T(1,128)S(1)} %bitcast.53), channel_id=1, replica_groups=mesh['x'=4,'z'=4,'core'=2,'y'=4] {'x','z','y'}, dimensions={0} | all-to-all | bytes 65536 | tf_op jit(solution)/shard_map/all_to_all | solution.py:42
  19.8 8.4 %gather_rows.1 = bf16[64,64,128]{2,1,0:T(8,128)(2,1)} custom-call(s32[8192]{0:T(1024)} %bitcast.45, bf16[8192,128]{1,0:T(8,128)(2,1)} %table_ref.1), custom_call_target="tpu_custom_call" | custom-call | tf_op jit(solution)/shard_map/gather_rows/pallas_call | solution.py:113
  28.2 21.7 %all_to_all.16 = bf16[64,64,128]{2,1,0:T(8,128)(2,1)S(1)} all-to-all(bf16[64,64,128]{2,1,0:T(8,128)(2,1)} %gather_rows.1), channel_id=1, replica_groups=mesh['x'=4,'z'=4,'core'=2,'y'=4] {'x','z','y'}, dimensions={0} | all-to-all | bytes 2097152 | tf_op jit(solution)/shard_map/all_to_all | solution.py:42
  50.0 1.6 %collective-permute-start.2 = (bf16[16,4,64,128]{3,2,1,0:T(8,128)(2,1)S(1)}, bf16[16,4,64,128]{3,2,1,0:T(8,128)(2,1)}, u32[]{:S(2)}, u32[]{:S(2)}) collective-permute-start(bf16[16,4,64,128]{3,2,1,0:T(8,128)(2,1)S(1)} %bitcast.51), channel_id=1, source_target_pairs={{0,4},{4,0},{1,5},{5,1},{2,6},{6,2},{3,7},{7,3},{8,12},{12,8},{9,1... | collective-permute-start | bytes 3145736 | tf_op jit(solution)/shard_map/ppermute | solution.py:38
  52.2 1.9 %collective-permute-done.2.got_other = bf16[16,4,64,128]{3,2,1,0:T(8,128)(2,1)} collective-permute-done((bf16[16,4,64,128]{3,2,1,0:T(8,128)(2,1)S(1)}, bf16[16,4,64,128]{3,2,1,0:T(8,128)(2,1)}, u32[]{:S(2)}, u32[]{:S(2)}) %collective-permute-start.2) | collective-permute-done | bytes 1048608 | tf_op jit(solution)/shard_map/ppermute | solution.py:38
  54.0 15.5 %block.1 = (bf16[1024,512]{1,0:T(8,128)(2,1)S(1)}, f32[1024,512]{1,0:T(8,128)}, bf16[1024,512]{1,0:T(8,128)(2,1)}, bf16[2064,128]{1,0:T(8,128)(2,1)S(1)}, bf16[2...) custom-call(s32[5]{0:T(128)S(1)} %stack.31.place.refs_0_, s32[1024,1]{1,0:T(8,128)S(1)} %bitcast.40, ...), custom_call_target="tpu_custom_call" | custom-call | tf_op jit(solution)/shard_map/block/pallas_call | solution.py:252
  70.3 2.3 %collective-permute-start.5 = (bf16[2064,128]{1,0:T(8,128)(2,1)}, bf16[2064,128]{1,0:T(8,128)(2,1)}, u32[]{:S(2)}, u32[]{:S(2)}) collective-permute-start(bf16[2064,128]{1,0:T(8,128)(2,1)} %get-tuple-element.41), channel_id=1, source_target_pairs={{0,64},{32,96},{64,0},{96,32},{8,72},{40,104},{72,8},{104,40},{16,... | collective-permute-start | bytes 1585160 | tf_op jit(solution)/shard_map/ppermute | solution.py:64
  73.5 1.6 copy-done.4
  75.1 2.5 %pack.1 = bf16[16,4,64,128]{3,2,1,0:T(8,128)(2,1)} custom-call(s32[2,512]{1,0:T(2,128)S(1)} %broadcast_select_fusion.1.slot_ref, f32[1024,512]{1,0:T(8,128)S(1)} %copy-done.4, bf16[1024,512]{1,0:T(8,128)(2,1)S(1)} %collective-permute-done.3.other_ref, bf16[1024,512]{1,0:T(8,128)(2,1)S(1)} %get-tuple-element.37.emb_ref, f32[1,512]{1,0:T(1,128)S(1)} %bitcast.50, ...), custom_call_target="tpu_custom_call" | custom-call | flops 2000000000 | bytes 10000000 | tf_op jit(solution)/shard_map/pack/pallas_call | solution.py:321
  77.6 8.3 %all-to-all-start.2 = ((bf16[64,64,128]{2,1,0:T(8,128)(2,1)}), bf16[64,64,128]{2,1,0:T(8,128)(2,1)S(1)}, u32[]{:S(2)}, u32[]{:S(2)}) async-start(bf16[64,64,128]{2,1,0:T(8,128)(2,1)} %bitcast.16), calls=%async_computation.2 | async-start | bytes 2097152 | tf_op jit(solution)/shard_map/all_to_all | solution.py:42
  86.1 2.2 %sum_split.1 = (bf16[528,128]{1,0:T(8,128)(2,1)S(1)}, bf16[528,128]{1,0:T(8,128)(2,1)S(1)}, bf16[528,128]{1,0:T(8,128)(2,1)S(1)}, bf16[528,128]{1,0:T(8,128)(2,1)S(1)}) custom-call(s32[5]{0:T(128)S(1)} %stack.31.place.refs_0_, bf16[2064,128]{1,0:T(8,128)(2,1)S(1)} %copy-done.6, bf16[2064,128]{1,0:T(8,128)(2,1)} %collective-permute-done.4.back_1, ...), custom_call_target="tpu_custom_call" | custom-call | flops 2000000000 | bytes 1000000 | tf_op jit(solution)/shard_map/sum_split/pallas_call | solution.py:412
  88.3 2.9 %collective-permute-start.7 = (bf16[528,128]{1,0:T(8,128)(2,1)S(1)}, bf16[528,128]{1,0:T(8,128)(2,1)S(1)}, u32[]{:S(2)}, u32[]{:S(2)}) collective-permute-start(bf16[528,128]{1,0:T(8,128)(2,1)S(1)} %get-tuple-element.44), channel_id=1, source_target_pairs={{0,1},{1,2},{2,3},{3,0},{8,9},{9,10},{10,11},{11,8},{16,17},{17,18... | collective-permute-start | bytes 405512 | tf_op jit(solution)/shard_map/ppermute | solution.py:64
  91.9 9.3 %collective-permute-done.7.back_1 = bf16[528,128]{1,0:T(8,128)(2,1)S(1)} collective-permute-done((bf16[528,128]{1,0:T(8,128)(2,1)S(1)}, bf16[528,128]{1,0:T(8,128)(2,1)S(1)}, u32[]{:S(2)}, u32[]{:S(2)}) %collective-permute-start.7) | collective-permute-done | bytes 135200 | tf_op jit(solution)/shard_map/ppermute | solution.py:64
  101.2 1.4 collective-permute-done.8.back_2
  103.3 1.2 collective-permute-start.12
  104.5 1.4 collective-permute-start.11
  105.9 1.6 %collective-permute-start.10 = (bf16[528,128]{1,0:T(8,128)(2,1)S(1)}, bf16[528,128]{1,0:T(8,128)(2,1)S(1)}, u32[]{:S(2)}, u32[]{:S(2)}) collective-permute-start(bf16[528,128]{1,0:T(8,128)(2,1)S(1)} %sum_four.2.here), channel_id=1, source_target_pairs={{0,8},{8,16},{16,24},{24,0},{1,9},{9,17},{17,25},{25,1},{2,10},{10... | collective-permute-start | bytes 405512 | tf_op jit(solution)/shard_map/ppermute | solution.py:64
  107.6 2.6 %collective-permute-done.11.back_2 = bf16[528,128]{1,0:T(8,128)(2,1)S(1)} collective-permute-done((bf16[528,128]{1,0:T(8,128)(2,1)S(1)}, bf16[528,128]{1,0:T(8,128)(2,1)S(1)}, u32[]{:S(2)}, u32[]{:S(2)}) %collective-permute-start.11) | collective-permute-done | bytes 135200 | tf_op jit(solution)/shard_map/ppermute | solution.py:64
  111.8 2.2 %collective-permute-start.14 = (bf16[528,128]{1,0:T(8,128)(2,1)S(1)}, bf16[528,128]{1,0:T(8,128)(2,1)S(1)}, u32[]{:S(2)}, u32[]{:S(2)}) collective-permute-start(bf16[528,128]{1,0:T(8,128)(2,1)S(1)} %sum_four.3.here), channel_id=1, source_target_pairs={{0,2},{1,3},{2,0},{3,1},{8,10},{9,11},{10,8},{11,9},{16,18},{17,19... | collective-permute-start | bytes 405512 | tf_op jit(solution)/shard_map/ppermute | solution.py:64
  116.0 1.8 %collective-permute-done.14.back_2 = bf16[528,128]{1,0:T(8,128)(2,1)S(1)} collective-permute-done((bf16[528,128]{1,0:T(8,128)(2,1)S(1)}, bf16[528,128]{1,0:T(8,128)(2,1)S(1)}, u32[]{:S(2)}, u32[]{:S(2)}) %collective-permute-start.14) | collective-permute-done | bytes 135200 | tf_op jit(solution)/shard_map/ppermute | solution.py:64
  118.1 1.8 %collective-permute-start.18 = (bf16[2064,128]{1,0:T(8,128)(2,1)S(1)}, bf16[2064,128]{1,0:T(8,128)(2,1)S(1)}, u32[]{:S(2)}, u32[]{:S(2)}) collective-permute-start(bf16[2064,128]{1,0:T(8,128)(2,1)S(1)} %join_four.1.refs_1_), channel_id=1, source_target_pairs={{0,96},{32,0},{64,32},{96,64},{8,104},{40,8},{72,40},{104,72},{16,... | collective-permute-start | bytes 1585160 | tf_op jit(solution)/shard_map/ppermute | solution.py:64
  120.9 15.3 %scatter_rows.1 = f32[8192,128]{1,0:T(8,128)} custom-call(s32[8192]{0:T(1024)S(1)} %bitcast.46, bf16[64,64,128]{2,1,0:T(8,128)(2,1)S(1)} %all-to-all-done.2.arrived_ref), custom_call_target="tpu_custom_call" | custom-call | flops 10000000000 | bytes 10000000 | tf_op jit(solution)/shard_map/scatter_rows/pallas_call | solution.py:376
  136.2 15.2 %collective-permute-start.19 = (bf16[2064,128]{1,0:T(8,128)(2,1)S(1)}, bf16[2064,128]{1,0:T(8,128)(2,1)S(1)}, u32[]{:S(2)}, u32[]{:S(2)}) collective-permute-start(bf16[2064,128]{1,0:T(8,128)(2,1)S(1)} %join_four.1.refs_1_), channel_id=1, source_target_pairs={{0,4},{4,0},{1,5},{5,1},{2,6},{6,2},{3,7},{7,3},{8,12},{12,8},{9,1... | collective-permute-start | bytes 1585160 | tf_op jit(solution)/shard_map/ppermute | solution.py:38
  155.1 5.2 %finish.1 = (f32[2048,512]{1,0:T(8,128)}, f32[512,2048]{1,0:T(8,128)}, f32[16,128]{1,0:T(8,128)}, f32[4,128]{1,0:T(4,128)}) custom-call(s32[5]{0:T(128)S(1)} %stack.31.place.refs_0_, bf16[2064,128]{1,0:T(8,128)(2,1)S(1)} %join_four.1.refs_1_, bf16[2064,128]{1,0:T(8,128)(2,1)S(1)} %collective-permute-done.16.refs_2_, ...), custom_call_target="tpu_custom_call" | custom-call | tf_op jit(solution)/shard_map/finish/pallas_call | solution.py:500
  (68 shorter events, 16.0 us)
Async XLA Ops:
  1.3 1.5 collective-permute-start
  2.0 2.1 %collective-permute-start.1 = (bf16[512,512]{1,0:T(8,128)(2,1)}, bf16[512,512]{1,0:T(8,128)(2,1)S(1)}, u32[]{:S(2)}, u32[]{:S(2)}) collective-permute-start(bf16[512,512]{1,0:T(8,128)(2,1)} %bitcast.42), channel_id=1, source_target_pairs={{0,4},{4,0},{1,5},{5,1},{2,6},{6,2},{3,7},{7,3},{8,12},{12,8},{9,1... | collective-permute-start | bytes 1572872 | tf_op jit(solution)/shard_map/ppermute | solution.py:38
  50.0 4.0 %collective-permute-start.2 = (bf16[16,4,64,128]{3,2,1,0:T(8,128)(2,1)S(1)}, bf16[16,4,64,128]{3,2,1,0:T(8,128)(2,1)}, u32[]{:S(2)}, u32[]{:S(2)}) collective-permute-start(bf16[16,4,64,128]{3,2,1,0:T(8,128)(2,1)S(1)} %bitcast.51), channel_id=1, source_target_pairs={{0,4},{4,0},{1,5},{5,1},{2,6},{6,2},{3,7},{7,3},{8,12},{12,8},{9,1... | collective-permute-start | bytes 3145736 | tf_op jit(solution)/shard_map/ppermute | solution.py:38
  69.5 4.0 %collective-permute-start.3 = (bf16[1024,512]{1,0:T(8,128)(2,1)}, bf16[1024,512]{1,0:T(8,128)(2,1)S(1)}, u32[]{:S(2)}, u32[]{:S(2)}) collective-permute-start(bf16[1024,512]{1,0:T(8,128)(2,1)} %get-tuple-element.36), channel_id=1, source_target_pairs={{0,4},{4,0},{1,5},{5,1},{2,6},{6,2},{3,7},{7,3},{8,12},{12,8},{9,1... | collective-permute-start | bytes 3145736 | tf_op jit(solution)/shard_map/ppermute | solution.py:38
  69.9 16.0 %collective-permute-start.4 = (bf16[2064,128]{1,0:T(8,128)(2,1)}, bf16[2064,128]{1,0:T(8,128)(2,1)}, u32[]{:S(2)}, u32[]{:S(2)}) collective-permute-start(bf16[2064,128]{1,0:T(8,128)(2,1)} %get-tuple-element.40), channel_id=1, source_target_pairs={{0,32},{32,64},{64,96},{96,0},{8,40},{40,72},{72,104},{104,8},{16,... | collective-permute-start | bytes 1585160 | tf_op jit(solution)/shard_map/ppermute | solution.py:64
  70.3 15.7 %collective-permute-start.5 = (bf16[2064,128]{1,0:T(8,128)(2,1)}, bf16[2064,128]{1,0:T(8,128)(2,1)}, u32[]{:S(2)}, u32[]{:S(2)}) collective-permute-start(bf16[2064,128]{1,0:T(8,128)(2,1)} %get-tuple-element.41), channel_id=1, source_target_pairs={{0,64},{32,96},{64,0},{96,32},{8,72},{40,104},{72,8},{104,40},{16,... | collective-permute-start | bytes 1585160 | tf_op jit(solution)/shard_map/ppermute | solution.py:64
  72.6 13.5 %collective-permute-start.6 = (bf16[2064,128]{1,0:T(8,128)(2,1)}, bf16[2064,128]{1,0:T(8,128)(2,1)}, u32[]{:S(2)}, u32[]{:S(2)}) collective-permute-start(bf16[2064,128]{1,0:T(8,128)(2,1)} %get-tuple-element.42), channel_id=1, source_target_pairs={{0,96},{32,0},{64,32},{96,64},{8,104},{40,8},{72,40},{104,72},{16,... | collective-permute-start | bytes 1585160 | tf_op jit(solution)/shard_map/ppermute | solution.py:64
  77.6 43.3 %all-to-all-start.2 = ((bf16[64,64,128]{2,1,0:T(8,128)(2,1)}), bf16[64,64,128]{2,1,0:T(8,128)(2,1)S(1)}, u32[]{:S(2)}, u32[]{:S(2)}) async-start(bf16[64,64,128]{2,1,0:T(8,128)(2,1)} %bitcast.16), calls=%async_computation.2 | async-start | bytes 2097152 | tf_op jit(solution)/shard_map/all_to_all | solution.py:42
  88.3 12.9 %collective-permute-start.7 = (bf16[528,128]{1,0:T(8,128)(2,1)S(1)}, bf16[528,128]{1,0:T(8,128)(2,1)S(1)}, u32[]{:S(2)}, u32[]{:S(2)}) collective-permute-start(bf16[528,128]{1,0:T(8,128)(2,1)S(1)} %get-tuple-element.44), channel_id=1, source_target_pairs={{0,1},{1,2},{2,3},{3,0},{8,9},{9,10},{10,11},{11,8},{16,17},{17,18... | collective-permute-start | bytes 405512 | tf_op jit(solution)/shard_map/ppermute | solution.py:64
  91.3 11.3 %collective-permute-start.8 = (bf16[528,128]{1,0:T(8,128)(2,1)S(1)}, bf16[528,128]{1,0:T(8,128)(2,1)S(1)}, u32[]{:S(2)}, u32[]{:S(2)}) collective-permute-start(bf16[528,128]{1,0:T(8,128)(2,1)S(1)} %get-tuple-element.45), channel_id=1, source_target_pairs={{0,2},{1,3},{2,0},{3,1},{8,10},{9,11},{10,8},{11,9},{16,18},{17,19... | collective-permute-start | bytes 405512 | tf_op jit(solution)/shard_map/ppermute | solution.py:64
  91.3 12.0 %collective-permute-start.9 = (bf16[528,128]{1,0:T(8,128)(2,1)S(1)}, bf16[528,128]{1,0:T(8,128)(2,1)S(1)}, u32[]{:S(2)}, u32[]{:S(2)}) collective-permute-start(bf16[528,128]{1,0:T(8,128)(2,1)S(1)} %get-tuple-element.46), channel_id=1, source_target_pairs={{0,3},{1,0},{2,1},{3,2},{8,11},{9,8},{10,9},{11,10},{16,19},{17,16... | collective-permute-start | bytes 405512 | tf_op jit(solution)/shard_map/ppermute | solution.py:64
  103.3 4.2 %collective-permute-start.12 = (bf16[528,128]{1,0:T(8,128)(2,1)S(1)}, bf16[528,128]{1,0:T(8,128)(2,1)S(1)}, u32[]{:S(2)}, u32[]{:S(2)}) collective-permute-start(bf16[528,128]{1,0:T(8,128)(2,1)S(1)} %sum_four.2.here), channel_id=1, source_target_pairs={{0,24},{8,0},{16,8},{24,16},{1,25},{9,1},{17,9},{25,17},{2,26},{10... | collective-permute-start | bytes 405512 | tf_op jit(solution)/shard_map/ppermute | solution.py:64
  104.5 5.7 %collective-permute-start.11 = (bf16[528,128]{1,0:T(8,128)(2,1)S(1)}, bf16[528,128]{1,0:T(8,128)(2,1)S(1)}, u32[]{:S(2)}, u32[]{:S(2)}) collective-permute-start(bf16[528,128]{1,0:T(8,128)(2,1)S(1)} %sum_four.2.here), channel_id=1, source_target_pairs={{0,16},{8,24},{16,0},{24,8},{1,17},{9,25},{17,1},{25,9},{2,18},{10... | collective-permute-start | bytes 405512 | tf_op jit(solution)/shard_map/ppermute | solution.py:64
  105.9 4.8 %collective-permute-start.10 = (bf16[528,128]{1,0:T(8,128)(2,1)S(1)}, bf16[528,128]{1,0:T(8,128)(2,1)S(1)}, u32[]{:S(2)}, u32[]{:S(2)}) collective-permute-start(bf16[528,128]{1,0:T(8,128)(2,1)S(1)} %sum_four.2.here), channel_id=1, source_target_pairs={{0,8},{8,16},{16,24},{24,0},{1,9},{9,17},{17,25},{25,1},{2,10},{10... | collective-permute-start | bytes 405512 | tf_op jit(solution)/shard_map/ppermute | solution.py:64
  110.9 5.1 %collective-permute-start.15 = (bf16[528,128]{1,0:T(8,128)(2,1)S(1)}, bf16[528,128]{1,0:T(8,128)(2,1)S(1)}, u32[]{:S(2)}, u32[]{:S(2)}) collective-permute-start(bf16[528,128]{1,0:T(8,128)(2,1)S(1)} %sum_four.3.here), channel_id=1, source_target_pairs={{0,3},{1,0},{2,1},{3,2},{8,11},{9,8},{10,9},{11,10},{16,19},{17,16... | collective-permute-start | bytes 405512 | tf_op jit(solution)/shard_map/ppermute | solution.py:64
  111.8 6.0 %collective-permute-start.14 = (bf16[528,128]{1,0:T(8,128)(2,1)S(1)}, bf16[528,128]{1,0:T(8,128)(2,1)S(1)}, u32[]{:S(2)}, u32[]{:S(2)}) collective-permute-start(bf16[528,128]{1,0:T(8,128)(2,1)S(1)} %sum_four.3.here), channel_id=1, source_target_pairs={{0,2},{1,3},{2,0},{3,1},{8,10},{9,11},{10,8},{11,9},{16,18},{17,19... | collective-permute-start | bytes 405512 | tf_op jit(solution)/shard_map/ppermute | solution.py:64
  114.0 4.1 %collective-permute-start.13 = (bf16[528,128]{1,0:T(8,128)(2,1)S(1)}, bf16[528,128]{1,0:T(8,128)(2,1)S(1)}, u32[]{:S(2)}, u32[]{:S(2)}) collective-permute-start(bf16[528,128]{1,0:T(8,128)(2,1)S(1)} %sum_four.3.here), channel_id=1, source_target_pairs={{0,1},{1,2},{2,3},{3,0},{8,9},{9,10},{10,11},{11,8},{16,17},{17,18... | collective-permute-start | bytes 405512 | tf_op jit(solution)/shard_map/ppermute | solution.py:64
  118.1 18.1 %collective-permute-start.18 = (bf16[2064,128]{1,0:T(8,128)(2,1)S(1)}, bf16[2064,128]{1,0:T(8,128)(2,1)S(1)}, u32[]{:S(2)}, u32[]{:S(2)}) collective-permute-start(bf16[2064,128]{1,0:T(8,128)(2,1)S(1)} %join_four.1.refs_1_), channel_id=1, source_target_pairs={{0,96},{32,0},{64,32},{96,64},{8,104},{40,8},{72,40},{104,72},{16,... | collective-permute-start | bytes 1585160 | tf_op jit(solution)/shard_map/ppermute | solution.py:64
  119.8 16.3 %collective-permute-start.17 = (bf16[2064,128]{1,0:T(8,128)(2,1)S(1)}, bf16[2064,128]{1,0:T(8,128)(2,1)S(1)}, u32[]{:S(2)}, u32[]{:S(2)}) collective-permute-start(bf16[2064,128]{1,0:T(8,128)(2,1)S(1)} %join_four.1.refs_1_), channel_id=1, source_target_pairs={{0,64},{32,96},{64,0},{96,32},{8,72},{40,104},{72,8},{104,40},{16,... | collective-permute-start | bytes 1585160 | tf_op jit(solution)/shard_map/ppermute | solution.py:64
  120.4 15.8 %collective-permute-start.16 = (bf16[2064,128]{1,0:T(8,128)(2,1)S(1)}, bf16[2064,128]{1,0:T(8,128)(2,1)S(1)}, u32[]{:S(2)}, u32[]{:S(2)}) collective-permute-start(bf16[2064,128]{1,0:T(8,128)(2,1)S(1)} %join_four.1.refs_1_), channel_id=1, source_target_pairs={{0,32},{32,64},{64,96},{96,0},{8,40},{40,72},{72,104},{104,8},{16,... | collective-permute-start | bytes 1585160 | tf_op jit(solution)/shard_map/ppermute | solution.py:64
  136.2 16.7 %collective-permute-start.19 = (bf16[2064,128]{1,0:T(8,128)(2,1)S(1)}, bf16[2064,128]{1,0:T(8,128)(2,1)S(1)}, u32[]{:S(2)}, u32[]{:S(2)}) collective-permute-start(bf16[2064,128]{1,0:T(8,128)(2,1)S(1)} %join_four.1.refs_1_), channel_id=1, source_target_pairs={{0,4},{4,0},{1,5},{5,1},{2,6},{6,2},{3,7},{7,3},{8,12},{12,8},{9,1... | collective-permute-start | bytes 1585160 | tf_op jit(solution)/shard_map/ppermute | solution.py:38
  151.3 2.3 %collective-permute-start.20 = (bf16[2064,128]{1,0:T(8,128)(2,1)S(1)}, bf16[2064,128]{1,0:T(8,128)(2,1)S(1)}, u32[]{:S(2)}, u32[]{:S(2)}) collective-permute-start(bf16[2064,128]{1,0:T(8,128)(2,1)S(1)} %collective-permute-done.16.refs_2_), channel_id=1, source_target_pairs={{0,4},{4,0},{1,5},{5,1},{2,6},{6,2},{3,7},{7,3},{8,12},{12,8},{9,1... | collective-permute-start | bytes 1585160 | tf_op jit(solution)/shard_map/ppermute | solution.py:38
  151.4 3.0 %collective-permute-start.21 = (bf16[2064,128]{1,0:T(8,128)(2,1)S(1)}, bf16[2064,128]{1,0:T(8,128)(2,1)S(1)}, u32[]{:S(2)}, u32[]{:S(2)}) collective-permute-start(bf16[2064,128]{1,0:T(8,128)(2,1)S(1)} %collective-permute-done.17.refs_3_), channel_id=1, source_target_pairs={{0,4},{4,0},{1,5},{5,1},{2,6},{6,2},{3,7},{7,3},{8,12},{12,8},{9,1... | collective-permute-start | bytes 1585160 | tf_op jit(solution)/shard_map/ppermute | solution.py:38
  151.8 3.3 %collective-permute-start.22 = (bf16[2064,128]{1,0:T(8,128)(2,1)S(1)}, bf16[2064,128]{1,0:T(8,128)(2,1)S(1)}, u32[]{:S(2)}, u32[]{:S(2)}) collective-permute-start(bf16[2064,128]{1,0:T(8,128)(2,1)S(1)} %collective-permute-done.18.refs_4_), channel_id=1, source_target_pairs={{0,4},{4,0},{1,5},{5,1},{2,6},{6,2},{3,7},{7,3},{8,12},{12,8},{9,1... | collective-permute-start | bytes 1585160 | tf_op jit(solution)/shard_map/ppermute | solution.py:38
  (8 other events, 109.7 us)

commit v6 on v5

--- a/solution.py
+++ b/solution.py
@@ -72,12 +72,26 @@
     return pl.BlockSpec(shape, lambda *_: (0,) * len(shape), memory_space=space)
 
 
+SCALARS = pl.BlockSpec(memory_space=pltpu.SMEM)
+NEAR = pl.BlockSpec(memory_space=pltpu.VMEM)
+
+
+GATHER_MIB = 50
+
+
 def request_at(row):
     return lax.shift_left(lax.shift_right_logical(row, 6), 7) + lax.bitwise_and(row, 63)
 
 
-def gather_kernel(asked, table_ref, out_ref, near, sems, wide, picked):
+def gather_kernel(
+    asked, core, table_ref, w_in_ref, w_out_ref, out_ref, w_in_near, w_out_near, near, sems, wide, picked,
+):
     step = ROWS // 8
+    half = pl.ds(pl.multiple_of(core[0] * HALF, HALF), HALF)
+    staged = [
+        pltpu.make_async_copy(w_in_ref.at[:, half], w_in_near, sems.at[8]),
+        pltpu.make_async_copy(w_out_ref.at[half, :], w_out_near, sems.at[9]),
+    ]
     copies = [
         pltpu.make_async_copy(
             table_ref.at[pl.ds(i * step, step)], near.at[pl.ds(i * step, step)], sems.at[i]
@@ -86,48 +100,50 @@
     ]
     for copy in copies:
         copy.start()
+    for copy in staged:
+        copy.start()
     for i, copy in enumerate(copies):
         copy.wait()
         rows = slice(i * step, (i + 1) * step)
         wide[rows, :] = near[rows, :].astype(f32)
-    unroll = 16
 
     def pick(i, carry):
-        base = pl.multiple_of(i * unroll, unroll)
-        at = request_at(base)
-        for u in range(unroll):
-            picked[pl.ds(base + u, 1), :] = wide[pl.ds(asked[at + u], 1), :]
+        for u in range(PAIR_CAP):
+            picked[pl.ds(i * PAIR_CAP + u, 1), :] = wide[pl.ds(asked[i * LANES + u], 1), :]
+        rows = pl.ds(pl.multiple_of(i * PAIR_CAP, PAIR_CAP), PAIR_CAP)
+        out_ref[i] = picked[rows, :].astype(bf16)
         return carry
 
-    lax.fori_loop(0, N_REQ // unroll, pick, 0)
-
-    def narrow(i, carry):
-        rows = pl.ds(pl.multiple_of(i * 512, 512), 512)
-        out_ref[pl.ds(i * 8, 8)] = picked[rows, :].astype(bf16).reshape(8, PAIR_CAP, LANES)
-        return carry
-
-    lax.fori_loop(0, N_REQ // 512, narrow, 0)
-
-
-def gather_rows(asked, table):
+    lax.fori_loop(0, N_PEERS, pick, 0)
+    for copy in staged:
+        copy.wait()
+
+
+def gather_rows(asked, core, table, w_in, w_out):
     return pl.pallas_call(
         gather_kernel,
-        grid_spec=pltpu.PrefetchScalarGridSpec(
-            num_scalar_prefetch=1,
-            grid=(1,),
-            in_specs=[pl.BlockSpec(memory_space=pltpu.HBM)],
-            out_specs=whole((N_PEERS, PAIR_CAP, LANES)),
-            scratch_shapes=[
-                pltpu.VMEM((ROWS, LANES), bf16),
-                pltpu.SemaphoreType.DMA((8,)),
-                pltpu.VMEM((ROWS, LANES), f32),
-                pltpu.VMEM((N_REQ, LANES), f32),
-            ],
-        ),
-        out_shape=jax.ShapeDtypeStruct((N_PEERS, PAIR_CAP, LANES), bf16),
-        compiler_params=params(58),
+        in_specs=[SCALARS] * 2 + [pl.BlockSpec(memory_space=pltpu.HBM)] * 3,
+        out_specs=[NEAR] * 3,
+        scratch_shapes=[
+            pltpu.VMEM((ROWS, LANES), bf16),
+            pltpu.SemaphoreType.DMA((10,)),
+            pltpu.VMEM((ROWS, LANES), f32),
+            pltpu.VMEM((N_REQ, LANES), f32),
+        ],
+        out_shape=[
+            jax.ShapeDtypeStruct((N_PEERS, PAIR_CAP, LANES), bf16),
+            jax.ShapeDtypeStruct((D, HALF), bf16),
+            jax.ShapeDtypeStruct((HALF, D), bf16),
+        ],
+        compiler_params=params(GATHER_MIB),
         name="gather_rows",
-    )(asked, table)
+    )(asked, core, table, w_in, w_out)
+
+
+CHUNK = 512
+UNROLL = 1
+GIN = 1024
+BLOCK_MIB = 40
 
 
 def block_kernel(
@@ -143,7 +159,6 @@
     bias_ref,
     w_out,
     emb_ref,
-    part_ref,
     send_ref,
     ring_0,
     ring_1,
@@ -160,6 +175,7 @@
     vec_s,
 ):
     ring_refs = (ring_0, ring_1, ring_2, ring_3)
+    own_half = pl.ds(pl.multiple_of(place[0] * HALF, HALF), HALF)
     for j in range(2):
         for y in range(N_Y):
             lanes = slice(y * LANES, (y + 1) * LANES)
@@ -175,8 +191,8 @@
     bias_acc[...] = jnp.zeros_like(bias_acc)
     gain_acc[...] = jnp.zeros_like(gain_acc)
     gain = gain_ref[...]
-    bias = bias_ref[...]
-    chunk = 256
+    bias = bias_ref[:, own_half]
+    chunk = CHUNK
     nt = (((1,), (1,)), ((), ()))
     tn = (((0,), (0,)), ((), ()))
     slot_ids = lax.broadcasted_iota(i32, (chunk, N_SLOTS), 1)
@@ -208,21 +224,20 @@
         d_pre_s[rows, :] = d_pre_bf
         bias_acc[...] += jnp.sum(d_pre.reshape(chunk // 8, 8, HALF), axis=0)
         part = lax.dot_general(d_pre_bf, w_in[...], nt, preferred_element_type=f32)
-        part_ref[rows, :] = part
         send_ref[rows, :] = part.astype(bf16)
         gain_acc[...] += jnp.sum((part * x_hat).reshape(chunk // 8, 8, D), axis=0)
         return carry
 
-    lax.fori_loop(0, 2 * TOK // chunk, one_chunk, 0)
+    lax.fori_loop(0, 2 * TOK // chunk, one_chunk, 0, unroll=UNROLL)
 
     def one_tile(i, carry):
-        cols = pl.ds(pl.multiple_of(i * 256, 256), 256)
+        cols = pl.ds(pl.multiple_of(i * GIN, GIN), GIN)
         gin_s[:, cols] = lax.dot_general(
             normed_s[...], d_pre_s[:, cols], tn, preferred_element_type=f32
         ).astype(bf16)
         return carry
 
-    lax.fori_loop(0, HALF // 256, one_tile, 0)
+    lax.fori_loop(0, HALF // GIN, one_tile, 0)
     g_bias = jnp.sum(bias_acc[...], axis=0, keepdims=True)
     g_gain = jnp.sum(gain_acc[...], axis=0, keepdims=True)
     for r in range(HALF // LANES):
@@ -248,49 +263,24 @@
 
 
 def block(place, slot_own, slot_other, got_own, got_other, cot_own, cot_other, gain, w_in, bias, w_out):
-    got = (N_XZ, N_Y, PAIR_CAP, LANES)
     return pl.pallas_call(
         block_kernel,
-        grid_spec=pltpu.PrefetchScalarGridSpec(
-            num_scalar_prefetch=1,
-            grid=(1,),
-            in_specs=[
-                whole((2 * TOK, 1)),
-                whole((2 * TOK, 1)),
-                whole(got),
-                whole(got),
-                whole((TOK, D)),
-                whole((TOK, D)),
-                whole((1, D)),
-                pl.BlockSpec((D, HALF), lambda i, c: (0, c[0])),
-                pl.BlockSpec((1, HALF), lambda i, c: (0, c[0])),
-                pl.BlockSpec((HALF, D), lambda i, c: (c[0], 0)),
-            ],
-            out_specs=[
-                whole((2 * TOK, D)),
-                whole((2 * TOK, D)),
-                whole((2 * TOK, D)),
-            ]
-            + [whole((N_RING, LANES))] * 4,
-            scratch_shapes=[
-                pltpu.VMEM((2, 2 * N_SLOTS, D), bf16),
-                pltpu.VMEM((2 * TOK, D), bf16),
-                pltpu.VMEM((2 * TOK, HALF), bf16),
-                pltpu.VMEM((2 * TOK, HALF), bf16),
-                pltpu.VMEM((8, HALF), f32),
-                pltpu.VMEM((8, D), f32),
-                pltpu.VMEM((2 * TOK, D), bf16),
-                pltpu.VMEM((D, HALF), bf16),
-                pltpu.VMEM((16, LANES), f32),
-            ],
-        ),
-        out_shape=[
-            jax.ShapeDtypeStruct((2 * TOK, D), bf16),
-            jax.ShapeDtypeStruct((2 * TOK, D), f32),
-            jax.ShapeDtypeStruct((2 * TOK, D), bf16),
-        ]
+        in_specs=[SCALARS] + [NEAR] * 10,
+        out_specs=[NEAR] * 6,
+        scratch_shapes=[
+            pltpu.VMEM((2, 2 * N_SLOTS, D), bf16),
+            pltpu.VMEM((2 * TOK, D), bf16),
+            pltpu.VMEM((2 * TOK, HALF), bf16),
+            pltpu.VMEM((2 * TOK, HALF), bf16),
+            pltpu.VMEM((8, HALF), f32),
+            pltpu.VMEM((8, D), f32),
+            pltpu.VMEM((2 * TOK, D), bf16),
+            pltpu.VMEM((D, HALF), bf16),
+            pltpu.VMEM((16, LANES), f32),
+        ],
+        out_shape=[jax.ShapeDtypeStruct((2 * TOK, D), bf16)] * 2
         + [jax.ShapeDtypeStruct((N_RING, LANES), bf16)] * 4,
-        compiler_params=params(48),
+        compiler_params=params(BLOCK_MIB),
         name="block",
     )(place, slot_own, slot_other, got_own, got_other, cot_own, cot_other, gain, w_in, bias, w_out)
 
@@ -304,7 +294,7 @@
         emb = emb_ref[rows, :].astype(f32)
         inv_rms = lax.rsqrt(jnp.mean(emb * emb, axis=-1, keepdims=True) + norm_eps)
         x_hat = emb * inv_rms
-        scaled = (part_ref[rows, :] + other_ref[theirs, :].astype(f32)) * gain
+        scaled = (part_ref[rows, :].astype(f32) + other_ref[theirs, :].astype(f32)) * gain
         d_out = (cot_own if j == 0 else cot_other)[...].astype(f32)
         d_embed = (
             inv_rms * (scaled - x_hat * jnp.mean(scaled * x_hat, axis=-1, keepdims=True)) + d_out
@@ -327,7 +317,8 @@
     )(slot_row, part, other, emb, gain, cot_own, cot_other)
 
 
-N_ACC = 2
+N_ACC = 8
+SCATTER_MIB = 48
 
 
 def scatter_kernel(asked, arrived_ref, out_ref, grads, *accs):
@@ -375,16 +366,12 @@
 def scatter_rows(asked, arrived):
     return pl.pallas_call(
         scatter_kernel,
-        grid_spec=pltpu.PrefetchScalarGridSpec(
-            num_scalar_prefetch=1,
-            grid=(1,),
-            in_specs=[whole((N_PEERS, PAIR_CAP, LANES))],
-            out_specs=whole((ROWS, LANES)),
-            scratch_shapes=[pltpu.VMEM((N_REQ, LANES), f32)]
-            + [pltpu.VMEM((ROWS, LANES), f32)] * (N_ACC - 1),
-        ),
+        in_specs=[SCALARS, NEAR],
+        out_specs=NEAR,
+        scratch_shapes=[pltpu.VMEM((N_REQ, LANES), f32)]
+        + [pltpu.VMEM((ROWS, LANES), f32)] * (N_ACC - 1),
         out_shape=jax.ShapeDtypeStruct((ROWS, LANES), f32),
-        compiler_params=params(28),
+        compiler_params=params(SCATTER_MIB),
         cost_estimate=pl.CostEstimate(flops=10**10, bytes_accessed=10**7, transcendentals=0),
         name="scatter_rows",
     )(asked, arrived)
@@ -411,12 +398,8 @@
 def sum_split(place, pieces):
     return pl.pallas_call(
         sum_split_kernel,
-        grid_spec=pltpu.PrefetchScalarGridSpec(
-            num_scalar_prefetch=1,
-            grid=(1,),
-            in_specs=[whole((N_RING, LANES))] * 4,
-            out_specs=[whole((N_BLOCK + N_VEC, LANES))] * 4,
-        ),
+        in_specs=[SCALARS] + [NEAR] * 4,
+        out_specs=[NEAR] * 4,
         out_shape=[jax.ShapeDtypeStruct((N_BLOCK + N_VEC, LANES), bf16)] * 4,
         compiler_params=params(8),
         cost_estimate=pl.CostEstimate(flops=2*10**9, bytes_accessed=10**6, transcendentals=0),
@@ -563,9 +546,10 @@
         (requests, cot_other, slot_own, slot_other)
     )
     asked = exchange(requests).reshape(-1)
-    fetched = exchange(gather_rows(asked, table)).reshape(N_XZ, N_Y, PAIR_CAP, LANES)
+    looked, w_in_half, w_out_half = gather_rows(asked, place, table, w_in, w_out)
+    fetched = exchange(looked).reshape(N_XZ, N_Y, PAIR_CAP, LANES)
     gain_row = norm_gain.reshape(1, D)
-    emb, part, send, *ring = block(
+    emb, send, *ring = block(
         place,
         slot_own.reshape(2 * TOK, 1),
         slot_other.reshape(2 * TOK, 1),
@@ -574,13 +558,13 @@
         cot_own,
         cot_other,
         gain_row,
-        w_in,
+        w_in_half,
         bias_in.reshape(1, 2 * HALF),
-        w_out,
+        w_out_half,
     )
     other = swap(send)
     ring_got = [along(0, ring[s], s) for s in (1, 2, 3)]
-    payload = pack(slot_own, part, other, emb, gain_row, cot_own, cot_other)
+    payload = pack(slot_own, send, other, emb, gain_row, cot_own, cot_other)
     place_late, payload = lax.optimization_barrier((place, payload))
     split = list(sum_split(place_late, ring[:1] + ring_got))
     arrived = exchange(payload.reshape(N_PEERS, PAIR_CAP, LANES))

time: 161 us -> 157 us (0.975)
  the two profiles are of different devices: /device:TPU:99 before, /device:TPU:97 now
where the time goes in v6:
time: 157 us; the launch traced here: 156 us
  starting transfers between devices  54 us (34%)
  Pallas kernels  38.7 us (25%)
  waiting for transfers between devices  36.2 us (23%)
  blocking collectives  19.7 us (13%)
  local copies, waits for them, and re-layouts  6.09 us (4%)
    ppermute x15, waiting for transfers between devices, along(): return lax.ppermute(a, EVERY, pairs)  23.7 us
    all_to_all x1, blocking collectives, exchange(): return lax.all_to_all(a, PEERS, split_axis=0, concat_axis=0, tiled=True)  19.7 us
    ppermute x15, starting transfers between devices, along(): return lax.ppermute(a, EVERY, pairs)  19.5 us
    ppermute x8, starting transfers between devices, swap(): return lax.ppermute(a, 'core', [(0, 1), (1, 0)])  17.9 us
    all_to_all x2, starting transfers between devices, exchange(): return lax.all_to_all(a, PEERS, split_axis=0, concat_axis=0, tiled=True)  16.7 us
    pallas_call x1, Pallas kernels, block(): pl.pallas_call(block_kernel, in_specs=[SCALARS] + [NEAR] * 10, out_specs=...  11.5 us
    pallas_call x1, Pallas kernels, scatter_rows(): pl.pallas_call(scatter_kernel, in_specs=[SCALARS, NEAR], out_specs=NEAR,...  11 us
    pallas_call x1, Pallas kernels, gather_rows(): pl.pallas_call(gather_kernel, in_specs=[SCALARS] * 2 + [pl.BlockSpec(memo...  6.92 us
  transfers between devices with their start and end apart: 25, of which 21 were waited for; matrix products, arithmetic and copies ran while one was open for 1% of the time, Pallas kernels for 10%

profile of v6, /device:TPU:97, one launch (start us, length us, event | category | flops | bytes accessed | tf_op | source)
XLA Modules:
  0.0 156.3 jit_solution(2018965079828647559)
XLA Ops:
  4.8 9.6 %all-to-all-start = ((s32[64,1,128]{2,1,0:T(1,128)}), s32[64,1,128]{2,1,0:T(1,128)S(1)}, u32[]{:S(2)}, u32[]{:S(2)}) async-start(s32[64,1,128]{2,1,0:T(1,128)} %bitcast.10), calls=%async_computation | async-start | bytes 65536 | tf_op jit(solution)/shard_map/all_to_all | solution.py:42
  14.5 6.8 %all-to-all-done = s32[64,1,128]{2,1,0:T(1,128)S(1)} async-done(((s32[64,1,128]{2,1,0:T(1,128)}), s32[64,1,128]{2,1,0:T(1,128)S(1)}, u32[]{:S(2)}, u32[]{:S(2)}) %all-to-all-start) | async-done | bytes 32800 | tf_op jit(solution)/shard_map/all_to_all | solution.py:42
  21.3 6.9 %gather_rows.1 = (bf16[64,64,128]{2,1,0:T(8,128)(2,1)S(1)}, bf16[512,1024]{1,0:T(8,128)(2,1)S(1)}, bf16[1024,512]{1,0:T(8,128)(2,1)S(1)}) custom-call(s32[8192]{0:T(1024)S(1)} %bitcast.47, s32[5]{0:T(128)S(1)} %stack.31.core.place.refs_0_, bf16[8192,128]{1,0:T(8,128)(2,1)} %table_ref.1, bf16[512,2048]{1,0:T(8,128)(2,1)} %w_in_ref.1, bf16[2048,512]{1,0:T(8,128)(2,1)} %w_out_ref.1), custom_call_target="tpu_custom_call" | custom-call | tf_op jit(solution)/shard_map/gather_rows/pallas_call | solution.py:123
  28.3 19.7 %all_to_all.15 = bf16[64,64,128]{2,1,0:T(8,128)(2,1)S(1)} all-to-all(bf16[64,64,128]{2,1,0:T(8,128)(2,1)S(1)} %get-tuple-element.36), channel_id=1, replica_groups=mesh['x'=4,'z'=4,'core'=2,'y'=4] {'x','z','y'}, dimensions={0} | all-to-all | bytes 2097152 | tf_op jit(solution)/shard_map/all_to_all | solution.py:42
  48.0 3.5 %collective-permute-start.2 = (bf16[16,4,64,128]{3,2,1,0:T(8,128)(2,1)S(1)}, bf16[16,4,64,128]{3,2,1,0:T(8,128)(2,1)}, u32[]{:S(2)}, u32[]{:S(2)}) collective-permute-start(bf16[16,4,64,128]{3,2,1,0:T(8,128)(2,1)S(1)} %bitcast.40), channel_id=1, source_target_pairs={{0,4},{4,0},{1,5},{5,1},{2,6},{6,2},{3,7},{7,3},{8,12},{12,8},{9,1... | collective-permute-start | bytes 3145736 | tf_op jit(solution)/shard_map/ppermute | solution.py:38
  52.0 1.9 %collective-permute-done.2.got_other = bf16[16,4,64,128]{3,2,1,0:T(8,128)(2,1)} collective-permute-done((bf16[16,4,64,128]{3,2,1,0:T(8,128)(2,1)S(1)}, bf16[16,4,64,128]{3,2,1,0:T(8,128)(2,1)}, u32[]{:S(2)}, u32[]{:S(2)}) %collective-permute-start.2) | collective-permute-done | bytes 1048608 | tf_op jit(solution)/shard_map/ppermute | solution.py:38
  57.2 11.5 %block.1 = (bf16[1024,512]{1,0:T(8,128)(2,1)S(1)}, bf16[1024,512]{1,0:T(8,128)(2,1)S(1)}, bf16[2064,128]{1,0:T(8,128)(2,1)S(1)}, bf16[2064,128]{1,0:T(8,128)(2,1...) custom-call(s32[5]{0:T(128)S(1)} %stack.31.core.place.refs_0_, s32[1024,1]{1,0:T(8,128)S(1)} %bitcast.42, ...), custom_call_target="tpu_custom_call" | custom-call | tf_op jit(solution)/shard_map/block/pallas_call | solution.py:266
  69.8 1.9 %collective-permute-start.5 = (bf16[2064,128]{1,0:T(8,128)(2,1)}, bf16[2064,128]{1,0:T(8,128)(2,1)S(1)}, u32[]{:S(2)}, u32[]{:S(2)}) collective-permute-start(bf16[2064,128]{1,0:T(8,128)(2,1)} %get-tuple-element.45), channel_id=1, source_target_pairs={{0,64},{32,96},{64,0},{96,32},{8,72},{40,104},{72,8},{104,40},{16,... | collective-permute-start | bytes 1585160 | tf_op jit(solution)/shard_map/ppermute | solution.py:64
  72.8 2.6 %pack.1 = bf16[16,4,64,128]{3,2,1,0:T(8,128)(2,1)} custom-call(s32[2,512]{1,0:T(2,128)S(1)} %broadcast_select_fusion.1.slot_ref, bf16[1024,512]{1,0:T(8,128)(2,1)S(1)} %get-tuple-element.40.part_ref, bf16[1024,512]{1,0:T(8,128)(2,1)S(1)} %collective-permute-done.3.other_ref, bf16[1024,512]{1,0:T(8,128)(2,1)S(1)} %get-tuple-element.41.emb_ref, ...), custom_call_target="tpu_custom_call" | custom-call | flops 2000000000 | bytes 10000000 | tf_op jit(solution)/shard_map/pack/pallas_call | solution.py:311
  75.4 7.1 %all-to-all-start.2 = ((bf16[64,64,128]{2,1,0:T(8,128)(2,1)}), bf16[64,64,128]{2,1,0:T(8,128)(2,1)S(1)}, u32[]{:S(2)}, u32[]{:S(2)}) async-start(bf16[64,64,128]{2,1,0:T(8,128)(2,1)} %bitcast.16), calls=%async_computation.2 | async-start | bytes 2097152 | tf_op jit(solution)/shard_map/all_to_all | solution.py:42
  82.6 1.9 %collective-permute-done.5.back_2 = bf16[2064,128]{1,0:T(8,128)(2,1)S(1)} collective-permute-done((bf16[2064,128]{1,0:T(8,128)(2,1)}, bf16[2064,128]{1,0:T(8,128)(2,1)S(1)}, u32[]{:S(2)}, u32[]{:S(2)}) %collective-permute-start.5) | collective-permute-done | bytes 528416 | tf_op jit(solution)/shard_map/ppermute | solution.py:64
  86.6 6.0 %collective-permute-start.7 = (bf16[528,128]{1,0:T(8,128)(2,1)S(1)}, bf16[528,128]{1,0:T(8,128)(2,1)S(1)}, u32[]{:S(2)}, u32[]{:S(2)}) collective-permute-start(bf16[528,128]{1,0:T(8,128)(2,1)S(1)} %get-tuple-element.48), channel_id=1, source_target_pairs={{0,1},{1,2},{2,3},{3,0},{8,9},{9,10},{10,11},{11,8},{16,17},{17,18... | collective-permute-start | bytes 405512 | tf_op jit(solution)/shard_map/ppermute | solution.py:64
  93.2 4.5 %collective-permute-done.7.back_1 = bf16[528,128]{1,0:T(8,128)(2,1)S(1)} collective-permute-done((bf16[528,128]{1,0:T(8,128)(2,1)S(1)}, bf16[528,128]{1,0:T(8,128)(2,1)S(1)}, u32[]{:S(2)}, u32[]{:S(2)}) %collective-permute-start.7) | collective-permute-done | bytes 135200 | tf_op jit(solution)/shard_map/ppermute | solution.py:64
  97.7 2.8 %collective-permute-done.8.back_2 = bf16[528,128]{1,0:T(8,128)(2,1)S(1)} collective-permute-done((bf16[528,128]{1,0:T(8,128)(2,1)S(1)}, bf16[528,128]{1,0:T(8,128)(2,1)S(1)}, u32[]{:S(2)}, u32[]{:S(2)}) %collective-permute-start.8) | collective-permute-done | bytes 135200 | tf_op jit(solution)/shard_map/ppermute | solution.py:64
  101.7 1.5 collective-permute-start.12
  103.9 1.7 %collective-permute-done.12.back_3 = bf16[528,128]{1,0:T(8,128)(2,1)S(1)} collective-permute-done((bf16[528,128]{1,0:T(8,128)(2,1)S(1)}, bf16[528,128]{1,0:T(8,128)(2,1)S(1)}, u32[]{:S(2)}, u32[]{:S(2)}) %collective-permute-start.12) | collective-permute-done | bytes 135200 | tf_op jit(solution)/shard_map/ppermute | solution.py:64
  105.6 3.3 %collective-permute-done.11.back_2 = bf16[528,128]{1,0:T(8,128)(2,1)S(1)} collective-permute-done((bf16[528,128]{1,0:T(8,128)(2,1)S(1)}, bf16[528,128]{1,0:T(8,128)(2,1)S(1)}, u32[]{:S(2)}, u32[]{:S(2)}) %collective-permute-start.11) | collective-permute-done | bytes 135200 | tf_op jit(solution)/shard_map/ppermute | solution.py:64
  110.8 2.3 %collective-permute-start.14 = (bf16[528,128]{1,0:T(8,128)(2,1)S(1)}, bf16[528,128]{1,0:T(8,128)(2,1)S(1)}, u32[]{:S(2)}, u32[]{:S(2)}) collective-permute-start(bf16[528,128]{1,0:T(8,128)(2,1)S(1)} %sum_four.3.here), channel_id=1, source_target_pairs={{0,2},{1,3},{2,0},{3,1},{8,10},{9,11},{10,8},{11,9},{16,18},{17,19... | collective-permute-start | bytes 405512 | tf_op jit(solution)/shard_map/ppermute | solution.py:64
  115.2 1.6 %collective-permute-done.14.back_2 = bf16[528,128]{1,0:T(8,128)(2,1)S(1)} collective-permute-done((bf16[528,128]{1,0:T(8,128)(2,1)S(1)}, bf16[528,128]{1,0:T(8,128)(2,1)S(1)}, u32[]{:S(2)}, u32[]{:S(2)}) %collective-permute-start.14) | collective-permute-done | bytes 135200 | tf_op jit(solution)/shard_map/ppermute | solution.py:64
  117.3 2.3 %collective-permute-start.18 = (bf16[2064,128]{1,0:T(8,128)(2,1)S(1)}, bf16[2064,128]{1,0:T(8,128)(2,1)S(1)}, u32[]{:S(2)}, u32[]{:S(2)}) collective-permute-start(bf16[2064,128]{1,0:T(8,128)(2,1)S(1)} %join_four.1.refs_1_), channel_id=1, source_target_pairs={{0,96},{32,0},{64,32},{96,64},{8,104},{40,8},{72,40},{104,72},{16,... | collective-permute-start | bytes 1585160 | tf_op jit(solution)/shard_map/ppermute | solution.py:64
  120.2 11.0 %scatter_rows.1 = f32[8192,128]{1,0:T(8,128)} custom-call(s32[8192]{0:T(1024)S(1)} %bitcast.48, bf16[64,64,128]{2,1,0:T(8,128)(2,1)S(1)} %all-to-all-done.2.arrived_ref), custom_call_target="tpu_custom_call" | custom-call | flops 10000000000 | bytes 10000000 | tf_op jit(solution)/shard_map/scatter_rows/pallas_call | solution.py:367
  131.4 3.1 %collective-permute-done.16.refs_2_ = bf16[2064,128]{1,0:T(8,128)(2,1)S(1)} collective-permute-done((bf16[2064,128]{1,0:T(8,128)(2,1)S(1)}, bf16[2064,128]{1,0:T(8,128)(2,1)S(1)}, u32[]{:S(2)}, u32[]{:S(2)}) %collective-permute-start.16) | collective-permute-done | bytes 528416 | tf_op jit(solution)/shard_map/ppermute | solution.py:64
  134.5 12.8 %collective-permute-start.19 = (bf16[2064,128]{1,0:T(8,128)(2,1)S(1)}, bf16[2064,128]{1,0:T(8,128)(2,1)S(1)}, u32[]{:S(2)}, u32[]{:S(2)}) collective-permute-start(bf16[2064,128]{1,0:T(8,128)(2,1)S(1)} %join_four.1.refs_1_), channel_id=1, source_target_pairs={{0,4},{4,0},{1,5},{5,1},{2,6},{6,2},{3,7},{7,3},{8,12},{12,8},{9,1... | collective-permute-start | bytes 1585160 | tf_op jit(solution)/shard_map/ppermute | solution.py:38
  151.1 5.2 %finish.1 = (f32[2048,512]{1,0:T(8,128)}, f32[512,2048]{1,0:T(8,128)}, f32[16,128]{1,0:T(8,128)}, f32[4,128]{1,0:T(4,128)}) custom-call(s32[5]{0:T(128)S(1)} %stack.31.core.place.refs_0_, bf16[2064,128]{1,0:T(8,128)(2,1)S(1)} %join_four.1.refs_1_, bf16[2064,128]{1,0:T(8,128)(2,1)S(1)} %collective-permute-done.16.refs_2_, ...), custom_call_target="tpu_custom_call" | custom-call | tf_op jit(solution)/shard_map/finish/pallas_call | solution.py:483
  (71 shorter events, 24.0 us)
Async XLA Ops:
  2.0 2.1 %collective-permute-start.1 = (bf16[512,512]{1,0:T(8,128)(2,1)}, bf16[512,512]{1,0:T(8,128)(2,1)S(1)}, u32[]{:S(2)}, u32[]{:S(2)}) collective-permute-start(bf16[512,512]{1,0:T(8,128)(2,1)} %bitcast.44), channel_id=1, source_target_pairs={{0,4},{4,0},{1,5},{5,1},{2,6},{6,2},{3,7},{7,3},{8,12},{12,8},{9,1... | collective-permute-start | bytes 1572872 | tf_op jit(solution)/shard_map/ppermute | solution.py:38
  4.8 16.5 %all-to-all-start = ((s32[64,1,128]{2,1,0:T(1,128)}), s32[64,1,128]{2,1,0:T(1,128)S(1)}, u32[]{:S(2)}, u32[]{:S(2)}) async-start(s32[64,1,128]{2,1,0:T(1,128)} %bitcast.10), calls=%async_computation | async-start | bytes 65536 | tf_op jit(solution)/shard_map/all_to_all | solution.py:42
  48.0 6.0 %collective-permute-start.2 = (bf16[16,4,64,128]{3,2,1,0:T(8,128)(2,1)S(1)}, bf16[16,4,64,128]{3,2,1,0:T(8,128)(2,1)}, u32[]{:S(2)}, u32[]{:S(2)}) collective-permute-start(bf16[16,4,64,128]{3,2,1,0:T(8,128)(2,1)S(1)} %bitcast.40), channel_id=1, source_target_pairs={{0,4},{4,0},{1,5},{5,1},{2,6},{6,2},{3,7},{7,3},{8,12},{12,8},{9,1... | collective-permute-start | bytes 3145736 | tf_op jit(solution)/shard_map/ppermute | solution.py:38
  68.7 4.1 %collective-permute-start.3 = (bf16[1024,512]{1,0:T(8,128)(2,1)S(1)}, bf16[1024,512]{1,0:T(8,128)(2,1)S(1)}, u32[]{:S(2)}, u32[]{:S(2)}) collective-permute-start(bf16[1024,512]{1,0:T(8,128)(2,1)S(1)} %get-tuple-element.40.part_ref), channel_id=1, source_target_pairs={{0,4},{4,0},{1,5},{5,1},{2,6},{6,2},{3,7},{7,3},{8,12},{12,8},{9,1... | collective-permute-start | bytes 3145736 | tf_op jit(solution)/shard_map/ppermute | solution.py:38
  69.1 13.5 %collective-permute-start.4 = (bf16[2064,128]{1,0:T(8,128)(2,1)}, bf16[2064,128]{1,0:T(8,128)(2,1)S(1)}, u32[]{:S(2)}, u32[]{:S(2)}) collective-permute-start(bf16[2064,128]{1,0:T(8,128)(2,1)} %get-tuple-element.44), channel_id=1, source_target_pairs={{0,32},{32,64},{64,96},{96,0},{8,40},{40,72},{72,104},{104,8},{16,... | collective-permute-start | bytes 1585160 | tf_op jit(solution)/shard_map/ppermute | solution.py:64
  69.8 14.7 %collective-permute-start.5 = (bf16[2064,128]{1,0:T(8,128)(2,1)}, bf16[2064,128]{1,0:T(8,128)(2,1)S(1)}, u32[]{:S(2)}, u32[]{:S(2)}) collective-permute-start(bf16[2064,128]{1,0:T(8,128)(2,1)} %get-tuple-element.45), channel_id=1, source_target_pairs={{0,64},{32,96},{64,0},{96,32},{8,72},{40,104},{72,8},{104,40},{16,... | collective-permute-start | bytes 1585160 | tf_op jit(solution)/shard_map/ppermute | solution.py:64
  71.7 13.5 %collective-permute-start.6 = (bf16[2064,128]{1,0:T(8,128)(2,1)}, bf16[2064,128]{1,0:T(8,128)(2,1)}, u32[]{:S(2)}, u32[]{:S(2)}) collective-permute-start(bf16[2064,128]{1,0:T(8,128)(2,1)} %get-tuple-element.46), channel_id=1, source_target_pairs={{0,96},{32,0},{64,32},{96,64},{8,104},{40,8},{72,40},{104,72},{16,... | collective-permute-start | bytes 1585160 | tf_op jit(solution)/shard_map/ppermute | solution.py:64
  75.4 44.8 %all-to-all-start.2 = ((bf16[64,64,128]{2,1,0:T(8,128)(2,1)}), bf16[64,64,128]{2,1,0:T(8,128)(2,1)S(1)}, u32[]{:S(2)}, u32[]{:S(2)}) async-start(bf16[64,64,128]{2,1,0:T(8,128)(2,1)} %bitcast.16), calls=%async_computation.2 | async-start | bytes 2097152 | tf_op jit(solution)/shard_map/all_to_all | solution.py:42
  86.6 11.1 %collective-permute-start.7 = (bf16[528,128]{1,0:T(8,128)(2,1)S(1)}, bf16[528,128]{1,0:T(8,128)(2,1)S(1)}, u32[]{:S(2)}, u32[]{:S(2)}) collective-permute-start(bf16[528,128]{1,0:T(8,128)(2,1)S(1)} %get-tuple-element.48), channel_id=1, source_target_pairs={{0,1},{1,2},{2,3},{3,0},{8,9},{9,10},{10,11},{11,8},{16,17},{17,18... | collective-permute-start | bytes 405512 | tf_op jit(solution)/shard_map/ppermute | solution.py:64
  92.5 7.9 %collective-permute-start.8 = (bf16[528,128]{1,0:T(8,128)(2,1)S(1)}, bf16[528,128]{1,0:T(8,128)(2,1)S(1)}, u32[]{:S(2)}, u32[]{:S(2)}) collective-permute-start(bf16[528,128]{1,0:T(8,128)(2,1)S(1)} %get-tuple-element.49), channel_id=1, source_target_pairs={{0,2},{1,3},{2,0},{3,1},{8,10},{9,11},{10,8},{11,9},{16,18},{17,19... | collective-permute-start | bytes 405512 | tf_op jit(solution)/shard_map/ppermute | solution.py:64
  92.5 9.1 %collective-permute-start.9 = (bf16[528,128]{1,0:T(8,128)(2,1)S(1)}, bf16[528,128]{1,0:T(8,128)(2,1)S(1)}, u32[]{:S(2)}, u32[]{:S(2)}) collective-permute-start(bf16[528,128]{1,0:T(8,128)(2,1)S(1)} %get-tuple-element.50), channel_id=1, source_target_pairs={{0,3},{1,0},{2,1},{3,2},{8,11},{9,8},{10,9},{11,10},{16,19},{17,16... | collective-permute-start | bytes 405512 | tf_op jit(solution)/shard_map/ppermute | solution.py:64
  101.7 3.9 %collective-permute-start.12 = (bf16[528,128]{1,0:T(8,128)(2,1)S(1)}, bf16[528,128]{1,0:T(8,128)(2,1)S(1)}, u32[]{:S(2)}, u32[]{:S(2)}) collective-permute-start(bf16[528,128]{1,0:T(8,128)(2,1)S(1)} %sum_four.2.here), channel_id=1, source_target_pairs={{0,24},{8,0},{16,8},{24,16},{1,25},{9,1},{17,9},{25,17},{2,26},{10... | collective-permute-start | bytes 405512 | tf_op jit(solution)/shard_map/ppermute | solution.py:64
  103.2 5.7 %collective-permute-start.11 = (bf16[528,128]{1,0:T(8,128)(2,1)S(1)}, bf16[528,128]{1,0:T(8,128)(2,1)S(1)}, u32[]{:S(2)}, u32[]{:S(2)}) collective-permute-start(bf16[528,128]{1,0:T(8,128)(2,1)S(1)} %sum_four.2.here), channel_id=1, source_target_pairs={{0,16},{8,24},{16,0},{24,8},{1,17},{9,25},{17,1},{25,9},{2,18},{10... | collective-permute-start | bytes 405512 | tf_op jit(solution)/shard_map/ppermute | solution.py:64
  103.6 6.4 %collective-permute-start.10 = (bf16[528,128]{1,0:T(8,128)(2,1)S(1)}, bf16[528,128]{1,0:T(8,128)(2,1)S(1)}, u32[]{:S(2)}, u32[]{:S(2)}) collective-permute-start(bf16[528,128]{1,0:T(8,128)(2,1)S(1)} %sum_four.2.here), channel_id=1, source_target_pairs={{0,8},{8,16},{16,24},{24,0},{1,9},{9,17},{17,25},{25,1},{2,10},{10... | collective-permute-start | bytes 405512 | tf_op jit(solution)/shard_map/ppermute | solution.py:64
  110.1 5.1 %collective-permute-start.15 = (bf16[528,128]{1,0:T(8,128)(2,1)S(1)}, bf16[528,128]{1,0:T(8,128)(2,1)S(1)}, u32[]{:S(2)}, u32[]{:S(2)}) collective-permute-start(bf16[528,128]{1,0:T(8,128)(2,1)S(1)} %sum_four.3.here), channel_id=1, source_target_pairs={{0,3},{1,0},{2,1},{3,2},{8,11},{9,8},{10,9},{11,10},{16,19},{17,16... | collective-permute-start | bytes 405512 | tf_op jit(solution)/shard_map/ppermute | solution.py:64
  110.8 6.1 %collective-permute-start.14 = (bf16[528,128]{1,0:T(8,128)(2,1)S(1)}, bf16[528,128]{1,0:T(8,128)(2,1)S(1)}, u32[]{:S(2)}, u32[]{:S(2)}) collective-permute-start(bf16[528,128]{1,0:T(8,128)(2,1)S(1)} %sum_four.3.here), channel_id=1, source_target_pairs={{0,2},{1,3},{2,0},{3,1},{8,10},{9,11},{10,8},{11,9},{16,18},{17,19... | collective-permute-start | bytes 405512 | tf_op jit(solution)/shard_map/ppermute | solution.py:64
  113.0 4.2 %collective-permute-start.13 = (bf16[528,128]{1,0:T(8,128)(2,1)S(1)}, bf16[528,128]{1,0:T(8,128)(2,1)S(1)}, u32[]{:S(2)}, u32[]{:S(2)}) collective-permute-start(bf16[528,128]{1,0:T(8,128)(2,1)S(1)} %sum_four.3.here), channel_id=1, source_target_pairs={{0,1},{1,2},{2,3},{3,0},{8,9},{9,10},{10,11},{11,8},{16,17},{17,18... | collective-permute-start | bytes 405512 | tf_op jit(solution)/shard_map/ppermute | solution.py:64
  117.3 14.1 %collective-permute-start.18 = (bf16[2064,128]{1,0:T(8,128)(2,1)S(1)}, bf16[2064,128]{1,0:T(8,128)(2,1)S(1)}, u32[]{:S(2)}, u32[]{:S(2)}) collective-permute-start(bf16[2064,128]{1,0:T(8,128)(2,1)S(1)} %join_four.1.refs_1_), channel_id=1, source_target_pairs={{0,96},{32,0},{64,32},{96,64},{8,104},{40,8},{72,40},{104,72},{16,... | collective-permute-start | bytes 1585160 | tf_op jit(solution)/shard_map/ppermute | solution.py:64
  119.6 11.8 %collective-permute-start.17 = (bf16[2064,128]{1,0:T(8,128)(2,1)S(1)}, bf16[2064,128]{1,0:T(8,128)(2,1)S(1)}, u32[]{:S(2)}, u32[]{:S(2)}) collective-permute-start(bf16[2064,128]{1,0:T(8,128)(2,1)S(1)} %join_four.1.refs_1_), channel_id=1, source_target_pairs={{0,64},{32,96},{64,0},{96,32},{8,72},{40,104},{72,8},{104,40},{16,... | collective-permute-start | bytes 1585160 | tf_op jit(solution)/shard_map/ppermute | solution.py:64
  119.6 14.9 %collective-permute-start.16 = (bf16[2064,128]{1,0:T(8,128)(2,1)S(1)}, bf16[2064,128]{1,0:T(8,128)(2,1)S(1)}, u32[]{:S(2)}, u32[]{:S(2)}) collective-permute-start(bf16[2064,128]{1,0:T(8,128)(2,1)S(1)} %join_four.1.refs_1_), channel_id=1, source_target_pairs={{0,32},{32,64},{64,96},{96,0},{8,40},{40,72},{72,104},{104,8},{16,... | collective-permute-start | bytes 1585160 | tf_op jit(solution)/shard_map/ppermute | solution.py:64
  134.5 14.3 %collective-permute-start.19 = (bf16[2064,128]{1,0:T(8,128)(2,1)S(1)}, bf16[2064,128]{1,0:T(8,128)(2,1)S(1)}, u32[]{:S(2)}, u32[]{:S(2)}) collective-permute-start(bf16[2064,128]{1,0:T(8,128)(2,1)S(1)} %join_four.1.refs_1_), channel_id=1, source_target_pairs={{0,4},{4,0},{1,5},{5,1},{2,6},{6,2},{3,7},{7,3},{8,12},{12,8},{9,1... | collective-permute-start | bytes 1585160 | tf_op jit(solution)/shard_map/ppermute | solution.py:38
  147.3 2.3 %collective-permute-start.20 = (bf16[2064,128]{1,0:T(8,128)(2,1)S(1)}, bf16[2064,128]{1,0:T(8,128)(2,1)S(1)}, u32[]{:S(2)}, u32[]{:S(2)}) collective-permute-start(bf16[2064,128]{1,0:T(8,128)(2,1)S(1)} %collective-permute-done.16.refs_2_), channel_id=1, source_target_pairs={{0,4},{4,0},{1,5},{5,1},{2,6},{6,2},{3,7},{7,3},{8,12},{12,8},{9,1... | collective-permute-start | bytes 1585160 | tf_op jit(solution)/shard_map/ppermute | solution.py:38
  147.3 3.1 %collective-permute-start.21 = (bf16[2064,128]{1,0:T(8,128)(2,1)S(1)}, bf16[2064,128]{1,0:T(8,128)(2,1)S(1)}, u32[]{:S(2)}, u32[]{:S(2)}) collective-permute-start(bf16[2064,128]{1,0:T(8,128)(2,1)S(1)} %collective-permute-done.17.refs_3_), channel_id=1, source_target_pairs={{0,4},{4,0},{1,5},{5,1},{2,6},{6,2},{3,7},{7,3},{8,12},{12,8},{9,1... | collective-permute-start | bytes 1585160 | tf_op jit(solution)/shard_map/ppermute | solution.py:38
  147.8 3.3 %collective-permute-start.22 = (bf16[2064,128]{1,0:T(8,128)(2,1)S(1)}, bf16[2064,128]{1,0:T(8,128)(2,1)S(1)}, u32[]{:S(2)}, u32[]{:S(2)}) collective-permute-start(bf16[2064,128]{1,0:T(8,128)(2,1)S(1)} %collective-permute-done.18.refs_4_), channel_id=1, source_target_pairs={{0,4},{4,0},{1,5},{5,1},{2,6},{6,2},{3,7},{7,3},{8,12},{12,8},{9,1... | collective-permute-start | bytes 1585160 | tf_op jit(solution)/shard_map/ppermute | solution.py:38
  (10 other events, 120.1 us)

commit v7 on v6

--- a/solution.py
+++ b/solution.py
@@ -74,24 +74,18 @@
 
 SCALARS = pl.BlockSpec(memory_space=pltpu.SMEM)
 NEAR = pl.BlockSpec(memory_space=pltpu.VMEM)
-
-
-GATHER_MIB = 50
+FAR = pl.BlockSpec(memory_space=pltpu.HBM)
+
+
+GATHER_MIB = 54
 
 
 def request_at(row):
     return lax.shift_left(lax.shift_right_logical(row, 6), 7) + lax.bitwise_and(row, 63)
 
 
-def gather_kernel(
-    asked, core, table_ref, w_in_ref, w_out_ref, out_ref, w_in_near, w_out_near, near, sems, wide, picked,
-):
+def gather_kernel(asked, table_ref, out_ref, near, sems, wide, picked):
     step = ROWS // 8
-    half = pl.ds(pl.multiple_of(core[0] * HALF, HALF), HALF)
-    staged = [
-        pltpu.make_async_copy(w_in_ref.at[:, half], w_in_near, sems.at[8]),
-        pltpu.make_async_copy(w_out_ref.at[half, :], w_out_near, sems.at[9]),
-    ]
     copies = [
         pltpu.make_async_copy(
             table_ref.at[pl.ds(i * step, step)], near.at[pl.ds(i * step, step)], sems.at[i]
@@ -100,8 +94,6 @@
     ]
     for copy in copies:
         copy.start()
-    for copy in staged:
-        copy.start()
     for i, copy in enumerate(copies):
         copy.wait()
         rows = slice(i * step, (i + 1) * step)
@@ -115,35 +107,28 @@
         return carry
 
     lax.fori_loop(0, N_PEERS, pick, 0)
-    for copy in staged:
-        copy.wait()
-
-
-def gather_rows(asked, core, table, w_in, w_out):
+
+
+def gather_rows(asked, table):
     return pl.pallas_call(
         gather_kernel,
-        in_specs=[SCALARS] * 2 + [pl.BlockSpec(memory_space=pltpu.HBM)] * 3,
-        out_specs=[NEAR] * 3,
+        in_specs=[SCALARS, FAR],
+        out_specs=NEAR,
         scratch_shapes=[
             pltpu.VMEM((ROWS, LANES), bf16),
-            pltpu.SemaphoreType.DMA((10,)),
+            pltpu.SemaphoreType.DMA((8,)),
             pltpu.VMEM((ROWS, LANES), f32),
             pltpu.VMEM((N_REQ, LANES), f32),
         ],
-        out_shape=[
-            jax.ShapeDtypeStruct((N_PEERS, PAIR_CAP, LANES), bf16),
-            jax.ShapeDtypeStruct((D, HALF), bf16),
-            jax.ShapeDtypeStruct((HALF, D), bf16),
-        ],
+        out_shape=jax.ShapeDtypeStruct((N_PEERS, PAIR_CAP, LANES), bf16),
         compiler_params=params(GATHER_MIB),
         name="gather_rows",
-    )(asked, core, table, w_in, w_out)
+    )(asked, table)
 
 
 CHUNK = 512
-UNROLL = 1
 GIN = 1024
-BLOCK_MIB = 40
+BLOCK_MIB = 46
 
 
 def block_kernel(
@@ -155,9 +140,9 @@
     cot_own,
     cot_other,
     gain_ref,
-    w_in,
+    w_in_far,
     bias_ref,
-    w_out,
+    w_out_far,
     emb_ref,
     send_ref,
     ring_0,
@@ -173,9 +158,21 @@
     d_out_s,
     gin_s,
     vec_s,
+    w_in,
+    w_out,
+    sems,
 ):
     ring_refs = (ring_0, ring_1, ring_2, ring_3)
     own_half = pl.ds(pl.multiple_of(place[0] * HALF, HALF), HALF)
+    w_in_copy = pltpu.make_async_copy(w_in_far.at[:, own_half], w_in, sems.at[0])
+    late_copies = [
+        pltpu.make_async_copy(w_out_far.at[own_half, :], w_out, sems.at[1]),
+        pltpu.make_async_copy(cot_own, d_out_s.at[pl.ds(0, TOK)], sems.at[2]),
+        pltpu.make_async_copy(cot_other, d_out_s.at[pl.ds(TOK, TOK)], sems.at[3]),
+    ]
+    w_in_copy.start()
+    for copy in late_copies:
+        copy.start()
     for j in range(2):
         for y in range(N_Y):
             lanes = slice(y * LANES, (y + 1) * LANES)
@@ -186,8 +183,6 @@
             by_slot[j, N_SLOTS:, lanes] = got_other[:, y, k * CAP : (k + 1) * CAP, :].reshape(
                 N_SLOTS, LANES
             )
-    d_out_s[:TOK, :] = cot_own[...]
-    d_out_s[TOK:, :] = cot_other[...]
     bias_acc[...] = jnp.zeros_like(bias_acc)
     gain_acc[...] = jnp.zeros_like(gain_acc)
     gain = gain_ref[...]
@@ -197,8 +192,8 @@
     tn = (((0,), (0,)), ((), ()))
     slot_ids = lax.broadcasted_iota(i32, (chunk, N_SLOTS), 1)
 
-    def one_chunk(i, carry):
-        rows = pl.ds(pl.multiple_of(i * chunk, chunk), chunk)
+    for i in range(2 * TOK // chunk):
+        rows = slice(i * chunk, (i + 1) * chunk)
         hit_own = (slot_own[rows, :] == slot_ids).astype(f32).astype(bf16)
         hit_other = (slot_other[rows, :] == slot_ids).astype(f32).astype(bf16)
         j = i // (TOK // chunk)
@@ -210,6 +205,8 @@
         x_hat = emb * inv_rms
         normed = (x_hat * gain).astype(bf16)
         normed_s[rows, :] = normed
+        if i == 0:
+            w_in_copy.wait()
         pre = jnp.dot(normed, w_in[...], preferred_element_type=f32) + bias
         square = pre * pre
         tanh_part = jnp.tanh(gelu_coef * (pre + 0.044715 * (square * pre)))
@@ -218,6 +215,9 @@
         slope = gate + 0.5 * pre * (1.0 - tanh_part * tanh_part) * (
             gelu_coef + (gelu_coef * 3.0 * 0.044715) * square
         )
+        if i == 0:
+            for copy in late_copies:
+                copy.wait()
         d_act = lax.dot_general(d_out_s[rows, :], w_out[...], nt, preferred_element_type=f32)
         d_pre = d_act * slope
         d_pre_bf = d_pre.astype(bf16)
@@ -226,9 +226,6 @@
         part = lax.dot_general(d_pre_bf, w_in[...], nt, preferred_element_type=f32)
         send_ref[rows, :] = part.astype(bf16)
         gain_acc[...] += jnp.sum((part * x_hat).reshape(chunk // 8, 8, D), axis=0)
-        return carry
-
-    lax.fori_loop(0, 2 * TOK // chunk, one_chunk, 0, unroll=UNROLL)
 
     def one_tile(i, carry):
         cols = pl.ds(pl.multiple_of(i * GIN, GIN), GIN)
@@ -265,7 +262,7 @@
 def block(place, slot_own, slot_other, got_own, got_other, cot_own, cot_other, gain, w_in, bias, w_out):
     return pl.pallas_call(
         block_kernel,
-        in_specs=[SCALARS] + [NEAR] * 10,
+        in_specs=[SCALARS] + [NEAR] * 4 + [FAR] * 2 + [NEAR, FAR, NEAR, FAR],
         out_specs=[NEAR] * 6,
         scratch_shapes=[
             pltpu.VMEM((2, 2 * N_SLOTS, D), bf16),
@@ -277,6 +274,9 @@
             pltpu.VMEM((2 * TOK, D), bf16),
             pltpu.VMEM((D, HALF), bf16),
             pltpu.VMEM((16, LANES), f32),
+            pltpu.VMEM((D, HALF), bf16),
+            pltpu.VMEM((HALF, D), bf16),
+            pltpu.SemaphoreType.DMA((4,)),
         ],
         out_shape=[jax.ShapeDtypeStruct((2 * TOK, D), bf16)] * 2
         + [jax.ShapeDtypeStruct((N_RING, LANES), bf16)] * 4,
@@ -440,16 +440,14 @@
     )(*pieces)
 
 
-def finish_kernel(scale, place, *refs):
-    pieces, (out_ref, in_ref, bias_ref, gain_ref, vec_s) = refs[:8], refs[8:]
-
-    for s in range(8):
+def write_pieces(scale, place, a_at, b_at, pieces, out_ref, in_ref, vec_s):
+    for s in range(4):
 
         @pl.when(pl.program_id(0) == s)
         def _(ref=pieces[s], s=s):
-            a = lax.rem(place[1 if s < 4 else 3] + (4 - s % 4), 4)
+            a = lax.rem(place[a_at] + (4 - s), 4)
             for j in range(4):
-                b = lax.rem(place[2 if s < 4 else 4] + (4 - j), 4)
+                b = lax.rem(place[b_at] + (4 - j), 4)
                 rows_out = pl.ds(pl.multiple_of(b * 64, 64), 64)
                 rows_in = pl.ds(pl.multiple_of(b * 32, 32), 32)
                 for y in range(N_Y):
@@ -464,45 +462,68 @@
                         )
             vec = ref[4 * N_BLOCK :, :].astype(f32) * scale
             for r in range(3):
-                vec_s[s // 4, pl.ds(a * 3 + r, 1), :] = vec[r : r + 1, :]
-
-    @pl.when(pl.program_id(0) == 7)
+                vec_s[pl.ds(a * 3 + r, 1), :] = vec[r : r + 1, :]
+
+
+def finish_own_kernel(scale, place, *refs):
+    write_pieces(scale, place, 1, 2, refs[:4], *refs[4:])
+
+
+def finish_other_kernel(scale, place, *refs):
+    own_vec, out_ref, in_ref, bias_ref, gain_ref, vec_s = refs[4:5] + refs[7:]
+    write_pieces(scale, place, 3, 4, refs[:4], out_ref, in_ref, vec_s)
+
+    @pl.when(pl.program_id(0) == 3)
     def _():
-        bias_ref[pl.ds(pl.multiple_of(place[0] * 8, 8), 8), :] = vec_s[0, :8, :]
-        bias_ref[pl.ds(pl.multiple_of((1 - place[0]) * 8, 8), 8), :] = vec_s[1, :8, :]
-        gain_ref[...] = vec_s[0, 8:12, :] + vec_s[1, 8:12, :]
-
-
-def finish(place, pieces, scale):
-    def half_of(s, c):
-        return jnp.where(s < 4, c[0], 1 - c[0])
-
-    def row_of(s, c):
-        return lax.rem(jnp.where(s < 4, c[1], c[3]) + 8 - s, 4)
-
-    return pl.pallas_call(
-        lambda *refs: finish_kernel(scale, *refs),
+        bias_ref[pl.ds(pl.multiple_of(place[0] * 8, 8), 8), :] = own_vec[:8, :]
+        bias_ref[pl.ds(pl.multiple_of((1 - place[0]) * 8, 8), 8), :] = vec_s[:8, :]
+        gain_ref[...] = own_vec[8:12, :] + vec_s[8:12, :]
+
+
+def finish(place, own, other, scale):
+    results = [
+        jax.ShapeDtypeStruct((2 * HALF, D), f32),
+        jax.ShapeDtypeStruct((D, 2 * HALF), f32),
+    ]
+    piece_specs = [whole((N_RING, LANES))] * 4
+
+    def blocks(half_of, a_at):
+        def row_of(s, c):
+            return lax.rem(c[a_at] + 4 - s, 4)
+
+        return [
+            pl.BlockSpec((256, D), lambda s, c: (half_of(c) * 4 + row_of(s, c), 0)),
+            pl.BlockSpec((128, HALF), lambda s, c: (row_of(s, c), half_of(c))),
+        ]
+
+    g_out, g_in, vec = pl.pallas_call(
+        lambda *refs: finish_own_kernel(scale, *refs),
         grid_spec=pltpu.PrefetchScalarGridSpec(
             num_scalar_prefetch=1,
-            grid=(8,),
-            in_specs=[whole((N_RING, LANES))] * 8,
-            out_specs=[
-                pl.BlockSpec((256, D), lambda s, c: (half_of(s, c) * 4 + row_of(s, c), 0)),
-                pl.BlockSpec((128, HALF), lambda s, c: (row_of(s, c), half_of(s, c))),
-                whole((16, LANES)),
-                whole((4, LANES)),
-            ],
-            scratch_shapes=[pltpu.VMEM((2, 16, LANES), f32)],
+            grid=(4,),
+            in_specs=piece_specs,
+            out_specs=blocks(lambda c: c[0], 1) + [whole((16, LANES))],
         ),
-        out_shape=[
-            jax.ShapeDtypeStruct((2 * HALF, D), f32),
-            jax.ShapeDtypeStruct((D, 2 * HALF), f32),
-            jax.ShapeDtypeStruct((16, LANES), f32),
-            jax.ShapeDtypeStruct((4, LANES), f32),
-        ],
-        compiler_params=params(16),
-        name="finish",
-    )(place, *pieces)
+        out_shape=results + [jax.ShapeDtypeStruct((16, LANES), f32)],
+        compiler_params=params(12),
+        cost_estimate=pl.CostEstimate(flops=6 * 10**9, bytes_accessed=10**7, transcendentals=0),
+        name="finish_own",
+    )(place, *own)
+    return pl.pallas_call(
+        lambda *refs: finish_other_kernel(scale, *refs),
+        grid_spec=pltpu.PrefetchScalarGridSpec(
+            num_scalar_prefetch=1,
+            grid=(4,),
+            in_specs=piece_specs + [whole((16, LANES))] + [pl.BlockSpec(memory_space=pl.ANY)] * 2,
+            out_specs=blocks(lambda c: 1 - c[0], 3) + [whole((16, LANES)), whole((4, LANES))],
+            scratch_shapes=[pltpu.VMEM((16, LANES), f32)],
+        ),
+        out_shape=results
+        + [jax.ShapeDtypeStruct((16, LANES), f32), jax.ShapeDtypeStruct((4, LANES), f32)],
+        input_output_aliases={6: 0, 7: 1},
+        compiler_params=params(12),
+        name="finish_other",
+    )(place, *other, vec, g_out, g_in)
 
 
 def local(table, item_ids, cotangent, norm_gain, w_in, bias_in, w_out):
@@ -546,8 +567,7 @@
         (requests, cot_other, slot_own, slot_other)
     )
     asked = exchange(requests).reshape(-1)
-    looked, w_in_half, w_out_half = gather_rows(asked, place, table, w_in, w_out)
-    fetched = exchange(looked).reshape(N_XZ, N_Y, PAIR_CAP, LANES)
+    fetched = exchange(gather_rows(asked, table)).reshape(N_XZ, N_Y, PAIR_CAP, LANES)
     gain_row = norm_gain.reshape(1, D)
     emb, send, *ring = block(
         place,
@@ -558,9 +578,9 @@
         cot_own,
         cot_other,
         gain_row,
-        w_in_half,
+        w_in,
         bias_in.reshape(1, 2 * HALF),
-        w_out_half,
+        w_out,
     )
     other = swap(send)
     ring_got = [along(0, ring[s], s) for s in (1, 2, 3)]
@@ -574,9 +594,9 @@
     pieces = [joined] + [along(0, joined, s) for s in (1, 2, 3)]
     table_grad = scatter_rows(asked, arrived)
     *late, table_grad = lax.optimization_barrier((*pieces, table_grad))
-    pieces += [swap(p) for p in late]
+    others = [swap(p) for p in late]
     scale = 1.0 / math.sqrt(TOK * N_PEERS * N_CORE)
-    g_out, g_in, g_bias, g_gain = finish(place, pieces, scale)
+    g_out, g_in, g_bias, g_gain = finish(place, late, others, scale)
     return (table_grad, g_in, g_bias.reshape(-1), g_out, g_gain.reshape(-1))
 
 

time: 157 us -> 156 us (level)
  the two profiles are of different devices: /device:TPU:97 before, /device:TPU:33 now
where the time goes in v7:
time: 156 us; the launch traced here: 155 us
  Pallas kernels  42.6 us (27%)
  starting transfers between devices  40.1 us (26%)
  blocking collectives  40 us (26%)
  waiting for transfers between devices  28.9 us (19%)
  local copies, waits for them, and re-layouts  2.13 us (1%)
    all_to_all x2, blocking collectives, exchange(): return lax.all_to_all(a, PEERS, split_axis=0, concat_axis=0, tiled=True)  40 us
    ppermute x15, waiting for transfers between devices, along(): return lax.ppermute(a, EVERY, pairs)  26.6 us
    ppermute x8, starting transfers between devices, swap(): return lax.ppermute(a, 'core', [(0, 1), (1, 0)])  17.4 us
    ppermute x15, starting transfers between devices, along(): return lax.ppermute(a, EVERY, pairs)  16.2 us
    pallas_call x1, Pallas kernels, block(): pl.pallas_call(block_kernel, in_specs=[SCALARS] + [NEAR] * 4 + [FAR] * 2...  12 us
    pallas_call x1, Pallas kernels, scatter_rows(): pl.pallas_call(scatter_kernel, in_specs=[SCALARS, NEAR], out_specs=NEAR,...  11 us
    pallas_call x1, Pallas kernels, gather_rows(): pl.pallas_call(gather_kernel, in_specs=[SCALARS, FAR], out_specs=NEAR, sc...  7.99 us
    all_to_all x1, starting transfers between devices, exchange(): return lax.all_to_all(a, PEERS, split_axis=0, concat_axis=0, tiled=True)  6.63 us
  transfers between devices with their start and end apart: 24, of which 16 were waited for; matrix products, arithmetic and copies ran while one was open for 1% of the time, Pallas kernels for 13%

profile of v7, /device:TPU:33, one launch (start us, length us, event | category | flops | bytes accessed | tf_op | source)
XLA Modules:
  0.0 155.4 jit_solution(12006439870858138769)
XLA Ops:
  4.1 18.1 %all_to_all.15 = s32[64,1,128]{2,1,0:T(1,128)} all-to-all(s32[64,1,128]{2,1,0:T(1,128)S(1)} %bitcast.53), channel_id=1, replica_groups=mesh['x'=4,'z'=4,'core'=2,'y'=4] {'x','z','y'}, dimensions={0} | all-to-all | bytes 65536 | tf_op jit(solution)/shard_map/all_to_all | solution.py:42
  22.2 8.0 %gather_rows.1 = bf16[64,64,128]{2,1,0:T(8,128)(2,1)} custom-call(s32[8192]{0:T(1024)} %bitcast.47, bf16[8192,128]{1,0:T(8,128)(2,1)} %table_ref.1), custom_call_target="tpu_custom_call" | custom-call | tf_op jit(solution)/shard_map/gather_rows/pallas_call | solution.py:113
  30.3 21.9 %all_to_all.16 = bf16[64,64,128]{2,1,0:T(8,128)(2,1)S(1)} all-to-all(bf16[64,64,128]{2,1,0:T(8,128)(2,1)} %gather_rows.1), channel_id=1, replica_groups=mesh['x'=4,'z'=4,'core'=2,'y'=4] {'x','z','y'}, dimensions={0} | all-to-all | bytes 2097152 | tf_op jit(solution)/shard_map/all_to_all | solution.py:42
  52.1 2.5 %collective-permute-start.2 = (bf16[16,4,64,128]{3,2,1,0:T(8,128)(2,1)S(1)}, bf16[16,4,64,128]{3,2,1,0:T(8,128)(2,1)}, u32[]{:S(2)}, u32[]{:S(2)}) collective-permute-start(bf16[16,4,64,128]{3,2,1,0:T(8,128)(2,1)S(1)} %bitcast.40), channel_id=1, source_target_pairs={{0,4},{4,0},{1,5},{5,1},{2,6},{6,2},{3,7},{7,3},{8,12},{12,8},{9,1... | collective-permute-start | bytes 3145736 | tf_op jit(solution)/shard_map/ppermute | solution.py:38
  55.1 1.9 %collective-permute-done.2.got_other = bf16[16,4,64,128]{3,2,1,0:T(8,128)(2,1)} collective-permute-done((bf16[16,4,64,128]{3,2,1,0:T(8,128)(2,1)S(1)}, bf16[16,4,64,128]{3,2,1,0:T(8,128)(2,1)}, u32[]{:S(2)}, u32[]{:S(2)}) %collective-permute-start.2) | collective-permute-done | bytes 1048608 | tf_op jit(solution)/shard_map/ppermute | solution.py:38
  57.0 12.0 %block.1 = (bf16[1024,512]{1,0:T(8,128)(2,1)S(1)}, bf16[1024,512]{1,0:T(8,128)(2,1)S(1)}, bf16[2064,128]{1,0:T(8,128)(2,1)S(1)}, bf16[2064,128]{1,0:T(8,128)(2,1...) custom-call(s32[5]{0:T(128)S(1)} %stack.31.place.refs_0_, s32[1024,1]{1,0:T(8,128)S(1)} %bitcast.42, ...), custom_call_target="tpu_custom_call" | custom-call | tf_op jit(solution)/shard_map/block/pallas_call | solution.py:263
  72.4 2.6 %pack.1 = bf16[16,4,64,128]{3,2,1,0:T(8,128)(2,1)} custom-call(s32[2,512]{1,0:T(2,128)S(1)} %broadcast_select_fusion.1.slot_ref, bf16[1024,512]{1,0:T(8,128)(2,1)S(1)} %get-tuple-element.37.part_ref, bf16[1024,512]{1,0:T(8,128)(2,1)S(1)} %collective-permute-done.3.other_ref, bf16[1024,512]{1,0:T(8,128)(2,1)S(1)} %get-tuple-element.38.emb_ref, ...), custom_call_target="tpu_custom_call" | custom-call | flops 2000000000 | bytes 10000000 | tf_op jit(solution)/shard_map/pack/pallas_call | solution.py:311
  75.0 6.6 %all-to-all-start.2 = ((bf16[64,64,128]{2,1,0:T(8,128)(2,1)}), bf16[64,64,128]{2,1,0:T(8,128)(2,1)S(1)}, u32[]{:S(2)}, u32[]{:S(2)}) async-start(bf16[64,64,128]{2,1,0:T(8,128)(2,1)} %bitcast.16), calls=%async_computation.2 | async-start | bytes 2097152 | tf_op jit(solution)/shard_map/all_to_all | solution.py:42
  81.6 3.5 %collective-permute-done.4.back_1 = bf16[2064,128]{1,0:T(8,128)(2,1)} collective-permute-done((bf16[2064,128]{1,0:T(8,128)(2,1)}, bf16[2064,128]{1,0:T(8,128)(2,1)}, u32[]{:S(2)}, u32[]{:S(2)}) %collective-permute-start.4) | collective-permute-done | bytes 528416 | tf_op jit(solution)/shard_map/ppermute | solution.py:64
  85.1 1.4 collective-permute-done.6.back_3
  86.5 1.6 %sum_split.1 = (bf16[528,128]{1,0:T(8,128)(2,1)S(1)}, bf16[528,128]{1,0:T(8,128)(2,1)S(1)}, bf16[528,128]{1,0:T(8,128)(2,1)S(1)}, bf16[528,128]{1,0:T(8,128)(2,1)S(1)}) custom-call(s32[5]{0:T(128)S(1)} %stack.31.place.refs_0_, bf16[2064,128]{1,0:T(8,128)(2,1)S(1)} %copy-done.5, bf16[2064,128]{1,0:T(8,128)(2,1)} %collective-permute-done.4.back_1, ...), custom_call_target="tpu_custom_call" | custom-call | flops 2000000000 | bytes 1000000 | tf_op jit(solution)/shard_map/sum_split/pallas_call | solution.py:399
  88.3 4.8 %collective-permute-start.8 = (bf16[528,128]{1,0:T(8,128)(2,1)S(1)}, bf16[528,128]{1,0:T(8,128)(2,1)S(1)}, u32[]{:S(2)}, u32[]{:S(2)}) collective-permute-start(bf16[528,128]{1,0:T(8,128)(2,1)S(1)} %get-tuple-element.46), channel_id=1, source_target_pairs={{0,2},{1,3},{2,0},{3,1},{8,10},{9,11},{10,8},{11,9},{16,18},{17,19... | collective-permute-start | bytes 405512 | tf_op jit(solution)/shard_map/ppermute | solution.py:64
  93.1 6.0 %collective-permute-done.7.back_1 = bf16[528,128]{1,0:T(8,128)(2,1)S(1)} collective-permute-done((bf16[528,128]{1,0:T(8,128)(2,1)S(1)}, bf16[528,128]{1,0:T(8,128)(2,1)S(1)}, u32[]{:S(2)}, u32[]{:S(2)}) %collective-permute-start.7) | collective-permute-done | bytes 135200 | tf_op jit(solution)/shard_map/ppermute | solution.py:64
  101.3 1.9 %collective-permute-start.12 = (bf16[528,128]{1,0:T(8,128)(2,1)S(1)}, bf16[528,128]{1,0:T(8,128)(2,1)S(1)}, u32[]{:S(2)}, u32[]{:S(2)}) collective-permute-start(bf16[528,128]{1,0:T(8,128)(2,1)S(1)} %sum_four.2.here), channel_id=1, source_target_pairs={{0,24},{8,0},{16,8},{24,16},{1,25},{9,1},{17,9},{25,17},{2,26},{10... | collective-permute-start | bytes 405512 | tf_op jit(solution)/shard_map/ppermute | solution.py:64
  103.8 2.7 %collective-permute-done.12.back_3 = bf16[528,128]{1,0:T(8,128)(2,1)S(1)} collective-permute-done((bf16[528,128]{1,0:T(8,128)(2,1)S(1)}, bf16[528,128]{1,0:T(8,128)(2,1)S(1)}, u32[]{:S(2)}, u32[]{:S(2)}) %collective-permute-start.12) | collective-permute-done | bytes 135200 | tf_op jit(solution)/shard_map/ppermute | solution.py:64
  106.6 2.1 %collective-permute-done.11.back_2 = bf16[528,128]{1,0:T(8,128)(2,1)S(1)} collective-permute-done((bf16[528,128]{1,0:T(8,128)(2,1)S(1)}, bf16[528,128]{1,0:T(8,128)(2,1)S(1)}, u32[]{:S(2)}, u32[]{:S(2)}) %collective-permute-start.11) | collective-permute-done | bytes 135200 | tf_op jit(solution)/shard_map/ppermute | solution.py:64
  111.6 1.5 collective-permute-start.13
  114.0 2.4 %collective-permute-done.14.back_2 = bf16[528,128]{1,0:T(8,128)(2,1)S(1)} collective-permute-done((bf16[528,128]{1,0:T(8,128)(2,1)S(1)}, bf16[528,128]{1,0:T(8,128)(2,1)S(1)}, u32[]{:S(2)}, u32[]{:S(2)}) %collective-permute-start.14) | collective-permute-done | bytes 135200 | tf_op jit(solution)/shard_map/ppermute | solution.py:64
  117.3 1.9 %collective-permute-start.18 = (bf16[2064,128]{1,0:T(8,128)(2,1)S(1)}, bf16[2064,128]{1,0:T(8,128)(2,1)S(1)}, u32[]{:S(2)}, u32[]{:S(2)}) collective-permute-start(bf16[2064,128]{1,0:T(8,128)(2,1)S(1)} %join_four.1.refs_1_), channel_id=1, source_target_pairs={{0,96},{32,0},{64,32},{96,64},{8,104},{40,8},{72,40},{104,72},{16,... | collective-permute-start | bytes 1585160 | tf_op jit(solution)/shard_map/ppermute | solution.py:64
  119.8 11.0 %scatter_rows.1 = f32[8192,128]{1,0:T(8,128)} custom-call(s32[8192]{0:T(1024)S(1)} %bitcast.48, bf16[64,64,128]{2,1,0:T(8,128)(2,1)S(1)} %all-to-all-done.2.arrived_ref), custom_call_target="tpu_custom_call" | custom-call | flops 10000000000 | bytes 10000000 | tf_op jit(solution)/shard_map/scatter_rows/pallas_call | solution.py:367
  131.0 3.4 %collective-permute-done.16.refs_2_ = bf16[2064,128]{1,0:T(8,128)(2,1)} collective-permute-done((bf16[2064,128]{1,0:T(8,128)(2,1)S(1)}, bf16[2064,128]{1,0:T(8,128)(2,1)}, u32[]{:S(2)}, u32[]{:S(2)}) %collective-permute-start.16) | collective-permute-done | bytes 528416 | tf_op jit(solution)/shard_map/ppermute | solution.py:64
  134.4 13.2 %collective-permute-start.19 = (bf16[2064,128]{1,0:T(8,128)(2,1)S(1)}, bf16[2064,128]{1,0:T(8,128)(2,1)S(1)}, u32[]{:S(2)}, u32[]{:S(2)}) collective-permute-start(bf16[2064,128]{1,0:T(8,128)(2,1)S(1)} %join_four.1.refs_1_), channel_id=1, source_target_pairs={{0,4},{4,0},{1,5},{5,1},{2,6},{6,2},{3,7},{7,3},{8,12},{12,8},{9,1... | collective-permute-start | bytes 1585160 | tf_op jit(solution)/shard_map/ppermute | solution.py:38
  148.1 4.1 %finish_own.1 = (f32[2048,512]{1,0:T(8,128)}, f32[512,2048]{1,0:T(8,128)}, f32[16,128]{1,0:T(8,128)S(1)}) custom-call(s32[5]{0:T(128)S(1)} %stack.31.place.refs_0_, bf16[2064,128]{1,0:T(8,128)(2,1)S(1)} %join_four.1.refs_1_, bf16[2064,128]{1,0:T(8,128)(2,1)} %collective-permute-done.16.refs_2_, bf16[2064,128]{1,0:T(8,128)(2,1)S(1)} %collective-permute-done.17.refs_3_, ...), custom_call_target="tpu_custom_call" | custom-call | flops 6000000000 | bytes 10000000 | tf_op jit(solution)/shard_map/finish_own/pallas_call | solution.py:499
  152.3 3.1 %finish_other.1 = (f32[2048,512]{1,0:T(8,128)}, f32[512,2048]{1,0:T(8,128)}, f32[16,128]{1,0:T(8,128)}, f32[4,128]{1,0:T(4,128)}) custom-call(s32[5]{0:T(128)S(1)} %stack.31.place.refs_0_, bf16[2064,128]{1,0:T(8,128)(2,1)S(1)} %collective-permute-done.19.refs_1_, ...), custom_call_target="tpu_custom_call", output_to_operand_aliasing={{0}: (6, {}), {1}: (7, {})} | custom-call | tf_op jit(solution)/shard_map/finish_other/pallas_call | solution.py:512
  (65 shorter events, 16.4 us)
Async XLA Ops:
  1.3 1.5 collective-permute-start
  2.0 2.1 %collective-permute-start.1 = (bf16[512,512]{1,0:T(8,128)(2,1)}, bf16[512,512]{1,0:T(8,128)(2,1)S(1)}, u32[]{:S(2)}, u32[]{:S(2)}) collective-permute-start(bf16[512,512]{1,0:T(8,128)(2,1)} %bitcast.44), channel_id=1, source_target_pairs={{0,4},{4,0},{1,5},{5,1},{2,6},{6,2},{3,7},{7,3},{8,12},{12,8},{9,1... | collective-permute-start | bytes 1572872 | tf_op jit(solution)/shard_map/ppermute | solution.py:38
  52.1 4.9 %collective-permute-start.2 = (bf16[16,4,64,128]{3,2,1,0:T(8,128)(2,1)S(1)}, bf16[16,4,64,128]{3,2,1,0:T(8,128)(2,1)}, u32[]{:S(2)}, u32[]{:S(2)}) collective-permute-start(bf16[16,4,64,128]{3,2,1,0:T(8,128)(2,1)S(1)} %bitcast.40), channel_id=1, source_target_pairs={{0,4},{4,0},{1,5},{5,1},{2,6},{6,2},{3,7},{7,3},{8,12},{12,8},{9,1... | collective-permute-start | bytes 3145736 | tf_op jit(solution)/shard_map/ppermute | solution.py:38
  69.1 3.3 %collective-permute-start.3 = (bf16[1024,512]{1,0:T(8,128)(2,1)S(1)}, bf16[1024,512]{1,0:T(8,128)(2,1)S(1)}, u32[]{:S(2)}, u32[]{:S(2)}) collective-permute-start(bf16[1024,512]{1,0:T(8,128)(2,1)S(1)} %get-tuple-element.37.part_ref), channel_id=1, source_target_pairs={{0,4},{4,0},{1,5},{5,1},{2,6},{6,2},{3,7},{7,3},{8,12},{12,8},{9,1... | collective-permute-start | bytes 3145736 | tf_op jit(solution)/shard_map/ppermute | solution.py:38
  69.5 15.6 %collective-permute-start.4 = (bf16[2064,128]{1,0:T(8,128)(2,1)}, bf16[2064,128]{1,0:T(8,128)(2,1)}, u32[]{:S(2)}, u32[]{:S(2)}) collective-permute-start(bf16[2064,128]{1,0:T(8,128)(2,1)} %get-tuple-element.41), channel_id=1, source_target_pairs={{0,32},{32,64},{64,96},{96,0},{8,40},{40,72},{72,104},{104,8},{16,... | collective-permute-start | bytes 1585160 | tf_op jit(solution)/shard_map/ppermute | solution.py:64
  70.0 15.1 %collective-permute-start.5 = (bf16[2064,128]{1,0:T(8,128)(2,1)}, bf16[2064,128]{1,0:T(8,128)(2,1)}, u32[]{:S(2)}, u32[]{:S(2)}) collective-permute-start(bf16[2064,128]{1,0:T(8,128)(2,1)} %get-tuple-element.42), channel_id=1, source_target_pairs={{0,64},{32,96},{64,0},{96,32},{8,72},{40,104},{72,8},{104,40},{16,... | collective-permute-start | bytes 1585160 | tf_op jit(solution)/shard_map/ppermute | solution.py:64
  71.1 15.4 %collective-permute-start.6 = (bf16[2064,128]{1,0:T(8,128)(2,1)}, bf16[2064,128]{1,0:T(8,128)(2,1)}, u32[]{:S(2)}, u32[]{:S(2)}) collective-permute-start(bf16[2064,128]{1,0:T(8,128)(2,1)} %get-tuple-element.43), channel_id=1, source_target_pairs={{0,96},{32,0},{64,32},{96,64},{8,104},{40,8},{72,40},{104,72},{16,... | collective-permute-start | bytes 1585160 | tf_op jit(solution)/shard_map/ppermute | solution.py:64
  75.0 44.9 %all-to-all-start.2 = ((bf16[64,64,128]{2,1,0:T(8,128)(2,1)}), bf16[64,64,128]{2,1,0:T(8,128)(2,1)S(1)}, u32[]{:S(2)}, u32[]{:S(2)}) async-start(bf16[64,64,128]{2,1,0:T(8,128)(2,1)} %bitcast.16), calls=%async_computation.2 | async-start | bytes 2097152 | tf_op jit(solution)/shard_map/all_to_all | solution.py:42
  88.2 10.9 %collective-permute-start.7 = (bf16[528,128]{1,0:T(8,128)(2,1)S(1)}, bf16[528,128]{1,0:T(8,128)(2,1)S(1)}, u32[]{:S(2)}, u32[]{:S(2)}) collective-permute-start(bf16[528,128]{1,0:T(8,128)(2,1)S(1)} %get-tuple-element.45), channel_id=1, source_target_pairs={{0,1},{1,2},{2,3},{3,0},{8,9},{9,10},{10,11},{11,8},{16,17},{17,18... | collective-permute-start | bytes 405512 | tf_op jit(solution)/shard_map/ppermute | solution.py:64
  88.3 11.8 %collective-permute-start.8 = (bf16[528,128]{1,0:T(8,128)(2,1)S(1)}, bf16[528,128]{1,0:T(8,128)(2,1)S(1)}, u32[]{:S(2)}, u32[]{:S(2)}) collective-permute-start(bf16[528,128]{1,0:T(8,128)(2,1)S(1)} %get-tuple-element.46), channel_id=1, source_target_pairs={{0,2},{1,3},{2,0},{3,1},{8,10},{9,11},{10,8},{11,9},{16,18},{17,19... | collective-permute-start | bytes 405512 | tf_op jit(solution)/shard_map/ppermute | solution.py:64
  93.1 8.1 %collective-permute-start.9 = (bf16[528,128]{1,0:T(8,128)(2,1)S(1)}, bf16[528,128]{1,0:T(8,128)(2,1)S(1)}, u32[]{:S(2)}, u32[]{:S(2)}) collective-permute-start(bf16[528,128]{1,0:T(8,128)(2,1)S(1)} %get-tuple-element.47), channel_id=1, source_target_pairs={{0,3},{1,0},{2,1},{3,2},{8,11},{9,8},{10,9},{11,10},{16,19},{17,16... | collective-permute-start | bytes 405512 | tf_op jit(solution)/shard_map/ppermute | solution.py:64
  101.3 5.3 %collective-permute-start.12 = (bf16[528,128]{1,0:T(8,128)(2,1)S(1)}, bf16[528,128]{1,0:T(8,128)(2,1)S(1)}, u32[]{:S(2)}, u32[]{:S(2)}) collective-permute-start(bf16[528,128]{1,0:T(8,128)(2,1)S(1)} %sum_four.2.here), channel_id=1, source_target_pairs={{0,24},{8,0},{16,8},{24,16},{1,25},{9,1},{17,9},{25,17},{2,26},{10... | collective-permute-start | bytes 405512 | tf_op jit(solution)/shard_map/ppermute | solution.py:64
  103.1 5.5 %collective-permute-start.11 = (bf16[528,128]{1,0:T(8,128)(2,1)S(1)}, bf16[528,128]{1,0:T(8,128)(2,1)S(1)}, u32[]{:S(2)}, u32[]{:S(2)}) collective-permute-start(bf16[528,128]{1,0:T(8,128)(2,1)S(1)} %sum_four.2.here), channel_id=1, source_target_pairs={{0,16},{8,24},{16,0},{24,8},{1,17},{9,25},{17,1},{25,9},{2,18},{10... | collective-permute-start | bytes 405512 | tf_op jit(solution)/shard_map/ppermute | solution.py:64
  103.2 6.5 %collective-permute-start.10 = (bf16[528,128]{1,0:T(8,128)(2,1)S(1)}, bf16[528,128]{1,0:T(8,128)(2,1)S(1)}, u32[]{:S(2)}, u32[]{:S(2)}) collective-permute-start(bf16[528,128]{1,0:T(8,128)(2,1)S(1)} %sum_four.2.here), channel_id=1, source_target_pairs={{0,8},{8,16},{16,24},{24,0},{1,9},{9,17},{17,25},{25,1},{2,10},{10... | collective-permute-start | bytes 405512 | tf_op jit(solution)/shard_map/ppermute | solution.py:64
  109.8 4.2 %collective-permute-start.15 = (bf16[528,128]{1,0:T(8,128)(2,1)S(1)}, bf16[528,128]{1,0:T(8,128)(2,1)S(1)}, u32[]{:S(2)}, u32[]{:S(2)}) collective-permute-start(bf16[528,128]{1,0:T(8,128)(2,1)S(1)} %sum_four.3.here), channel_id=1, source_target_pairs={{0,3},{1,0},{2,1},{3,2},{8,11},{9,8},{10,9},{11,10},{16,19},{17,16... | collective-permute-start | bytes 405512 | tf_op jit(solution)/shard_map/ppermute | solution.py:64
  111.0 5.4 %collective-permute-start.14 = (bf16[528,128]{1,0:T(8,128)(2,1)S(1)}, bf16[528,128]{1,0:T(8,128)(2,1)S(1)}, u32[]{:S(2)}, u32[]{:S(2)}) collective-permute-start(bf16[528,128]{1,0:T(8,128)(2,1)S(1)} %sum_four.3.here), channel_id=1, source_target_pairs={{0,2},{1,3},{2,0},{3,1},{8,10},{9,11},{10,8},{11,9},{16,18},{17,19... | collective-permute-start | bytes 405512 | tf_op jit(solution)/shard_map/ppermute | solution.py:64
  111.6 5.6 %collective-permute-start.13 = (bf16[528,128]{1,0:T(8,128)(2,1)S(1)}, bf16[528,128]{1,0:T(8,128)(2,1)S(1)}, u32[]{:S(2)}, u32[]{:S(2)}) collective-permute-start(bf16[528,128]{1,0:T(8,128)(2,1)S(1)} %sum_four.3.here), channel_id=1, source_target_pairs={{0,1},{1,2},{2,3},{3,0},{8,9},{9,10},{10,11},{11,8},{16,17},{17,18... | collective-permute-start | bytes 405512 | tf_op jit(solution)/shard_map/ppermute | solution.py:64
  117.3 13.7 %collective-permute-start.18 = (bf16[2064,128]{1,0:T(8,128)(2,1)S(1)}, bf16[2064,128]{1,0:T(8,128)(2,1)S(1)}, u32[]{:S(2)}, u32[]{:S(2)}) collective-permute-start(bf16[2064,128]{1,0:T(8,128)(2,1)S(1)} %join_four.1.refs_1_), channel_id=1, source_target_pairs={{0,96},{32,0},{64,32},{96,64},{8,104},{40,8},{72,40},{104,72},{16,... | collective-permute-start | bytes 1585160 | tf_op jit(solution)/shard_map/ppermute | solution.py:64
  119.2 11.8 %collective-permute-start.17 = (bf16[2064,128]{1,0:T(8,128)(2,1)S(1)}, bf16[2064,128]{1,0:T(8,128)(2,1)S(1)}, u32[]{:S(2)}, u32[]{:S(2)}) collective-permute-start(bf16[2064,128]{1,0:T(8,128)(2,1)S(1)} %join_four.1.refs_1_), channel_id=1, source_target_pairs={{0,64},{32,96},{64,0},{96,32},{8,72},{40,104},{72,8},{104,40},{16,... | collective-permute-start | bytes 1585160 | tf_op jit(solution)/shard_map/ppermute | solution.py:64
  119.4 15.1 %collective-permute-start.16 = (bf16[2064,128]{1,0:T(8,128)(2,1)S(1)}, bf16[2064,128]{1,0:T(8,128)(2,1)}, u32[]{:S(2)}, u32[]{:S(2)}) collective-permute-start(bf16[2064,128]{1,0:T(8,128)(2,1)S(1)} %join_four.1.refs_1_), channel_id=1, source_target_pairs={{0,32},{32,64},{64,96},{96,0},{8,40},{40,72},{72,104},{104,8},{16,... | collective-permute-start | bytes 1585160 | tf_op jit(solution)/shard_map/ppermute | solution.py:64
  134.4 17.9 %collective-permute-start.19 = (bf16[2064,128]{1,0:T(8,128)(2,1)S(1)}, bf16[2064,128]{1,0:T(8,128)(2,1)S(1)}, u32[]{:S(2)}, u32[]{:S(2)}) collective-permute-start(bf16[2064,128]{1,0:T(8,128)(2,1)S(1)} %join_four.1.refs_1_), channel_id=1, source_target_pairs={{0,4},{4,0},{1,5},{5,1},{2,6},{6,2},{3,7},{7,3},{8,12},{12,8},{9,1... | collective-permute-start | bytes 1585160 | tf_op jit(solution)/shard_map/ppermute | solution.py:38
  147.6 4.6 %collective-permute-start.20 = (bf16[2064,128]{1,0:T(8,128)(2,1)}, bf16[2064,128]{1,0:T(8,128)(2,1)S(1)}, u32[]{:S(2)}, u32[]{:S(2)}) collective-permute-start(bf16[2064,128]{1,0:T(8,128)(2,1)} %collective-permute-done.16.refs_2_), channel_id=1, source_target_pairs={{0,4},{4,0},{1,5},{5,1},{2,6},{6,2},{3,7},{7,3},{8,12},{12,8},{9,1... | collective-permute-start | bytes 1585160 | tf_op jit(solution)/shard_map/ppermute | solution.py:38
  147.6 4.6 %collective-permute-start.21 = (bf16[2064,128]{1,0:T(8,128)(2,1)S(1)}, bf16[2064,128]{1,0:T(8,128)(2,1)S(1)}, u32[]{:S(2)}, u32[]{:S(2)}) collective-permute-start(bf16[2064,128]{1,0:T(8,128)(2,1)S(1)} %collective-permute-done.17.refs_3_), channel_id=1, source_target_pairs={{0,4},{4,0},{1,5},{5,1},{2,6},{6,2},{3,7},{7,3},{8,12},{12,8},{9,1... | collective-permute-start | bytes 1585160 | tf_op jit(solution)/shard_map/ppermute | solution.py:38
  148.1 4.1 %collective-permute-start.22 = (bf16[2064,128]{1,0:T(8,128)(2,1)S(1)}, bf16[2064,128]{1,0:T(8,128)(2,1)S(1)}, u32[]{:S(2)}, u32[]{:S(2)}) collective-permute-start(bf16[2064,128]{1,0:T(8,128)(2,1)S(1)} %collective-permute-done.18.refs_4_), channel_id=1, source_target_pairs={{0,4},{4,0},{1,5},{5,1},{2,6},{6,2},{3,7},{7,3},{8,12},{12,8},{9,1... | collective-permute-start | bytes 1585160 | tf_op jit(solution)/shard_map/ppermute | solution.py:38
  (6 other events, 107.9 us)

commit v8 on v7

--- a/solution.py
+++ b/solution.py
@@ -402,7 +402,7 @@
         out_specs=[NEAR] * 4,
         out_shape=[jax.ShapeDtypeStruct((N_BLOCK + N_VEC, LANES), bf16)] * 4,
         compiler_params=params(8),
-        cost_estimate=pl.CostEstimate(flops=2*10**9, bytes_accessed=10**6, transcendentals=0),
+        cost_estimate=pl.CostEstimate(flops=4 * 10**9, bytes_accessed=10**6, transcendentals=0),
         name="sum_split",
     )(place, *pieces)
 
@@ -419,7 +419,7 @@
         sum_kernel,
         out_shape=jax.ShapeDtypeStruct((N_BLOCK + N_VEC, LANES), bf16),
         compiler_params=params(4),
-        cost_estimate=pl.CostEstimate(flops=2*10**9, bytes_accessed=10**6, transcendentals=0),
+        cost_estimate=pl.CostEstimate(flops=4 * 10**9, bytes_accessed=10**6, transcendentals=0),
         name="sum_four",
     )(*pieces)
 
@@ -435,7 +435,7 @@
         join_kernel,
         out_shape=jax.ShapeDtypeStruct((N_RING, LANES), bf16),
         compiler_params=params(4),
-        cost_estimate=pl.CostEstimate(flops=2*10**9, bytes_accessed=10**6, transcendentals=0),
+        cost_estimate=pl.CostEstimate(flops=4 * 10**9, bytes_accessed=10**6, transcendentals=0),
         name="join_four",
     )(*pieces)
 

time: 156 us -> 155 us (level); the launches traced: 155 us -> 152 us
  starting transfers between devices: 40.1 us -> 34.1 us
  waiting for transfers between devices: 28.9 us -> 33.3 us
  Pallas kernels: 42.6 us -> 41 us
    ppermute x8, starting transfers between devices: 17.4 us -> 8.81 us  [swap(): return lax.ppermute(a, 'core', [(0, 1), (1, 0)])]
    ppermute x15, waiting for transfers between devices: 26.6 us -> 30.9 us  [along(): return lax.ppermute(a, EVERY, pairs)]
  transfers between devices with their start and end apart: 24 -> 24, of which waited for: 16 -> 12; matrix products, arithmetic and copies ran while one was open for 1% -> 1% of each run, Pallas kernels for 13% -> 12%
where the time goes in v8:
time: 155 us; the launch traced here: 152 us
  Pallas kernels  41 us (26%)
  blocking collectives  39.8 us (26%)
  starting transfers between devices  34.1 us (22%)
  waiting for transfers between devices  33.3 us (21%)
  local copies, waits for them, and re-layouts  2.12 us (1%)
    all_to_all x2, blocking collectives, exchange(): return lax.all_to_all(a, PEERS, split_axis=0, concat_axis=0, tiled=True)  39.8 us
    ppermute x15, waiting for transfers between devices, along(): return lax.ppermute(a, EVERY, pairs)  30.9 us
    ppermute x15, starting transfers between devices, along(): return lax.ppermute(a, EVERY, pairs)  17.7 us
    pallas_call x1, Pallas kernels, block(): pl.pallas_call(block_kernel, in_specs=[SCALARS] + [NEAR] * 4 + [FAR] * 2...  11.2 us
    pallas_call x1, Pallas kernels, scatter_rows(): pl.pallas_call(scatter_kernel, in_specs=[SCALARS, NEAR], out_specs=NEAR,...  11 us
    ppermute x8, starting transfers between devices, swap(): return lax.ppermute(a, 'core', [(0, 1), (1, 0)])  8.81 us
    pallas_call x1, Pallas kernels, gather_rows(): pl.pallas_call(gather_kernel, in_specs=[SCALARS, FAR], out_specs=NEAR, sc...  7.99 us
    all_to_all x1, starting transfers between devices, exchange(): return lax.all_to_all(a, PEERS, split_axis=0, concat_axis=0, tiled=True)  7.65 us
  transfers between devices with their start and end apart: 24, of which 12 were waited for; matrix products, arithmetic and copies ran while one was open for 1% of the time, Pallas kernels for 12%

profile of v8, /device:TPU:33, one launch (start us, length us, event | category | flops | bytes accessed | tf_op | source)
XLA Modules:
  0.0 151.9 jit_solution(3028899113266791152)
XLA Ops:
  4.1 18.1 %all_to_all.15 = s32[64,1,128]{2,1,0:T(1,128)} all-to-all(s32[64,1,128]{2,1,0:T(1,128)S(1)} %bitcast.53), channel_id=1, replica_groups=mesh['x'=4,'z'=4,'core'=2,'y'=4] {'x','z','y'}, dimensions={0} | all-to-all | bytes 65536 | tf_op jit(solution)/shard_map/all_to_all | solution.py:42
  22.2 8.0 %gather_rows.1 = bf16[64,64,128]{2,1,0:T(8,128)(2,1)} custom-call(s32[8192]{0:T(1024)} %bitcast.47, bf16[8192,128]{1,0:T(8,128)(2,1)} %table_ref.1), custom_call_target="tpu_custom_call" | custom-call | tf_op jit(solution)/shard_map/gather_rows/pallas_call | solution.py:113
  30.3 21.6 %all_to_all.16 = bf16[64,64,128]{2,1,0:T(8,128)(2,1)S(1)} all-to-all(bf16[64,64,128]{2,1,0:T(8,128)(2,1)} %gather_rows.1), channel_id=1, replica_groups=mesh['x'=4,'z'=4,'core'=2,'y'=4] {'x','z','y'}, dimensions={0} | all-to-all | bytes 2097152 | tf_op jit(solution)/shard_map/all_to_all | solution.py:42
  51.9 2.7 %collective-permute-start.2 = (bf16[16,4,64,128]{3,2,1,0:T(8,128)(2,1)S(1)}, bf16[16,4,64,128]{3,2,1,0:T(8,128)(2,1)}, u32[]{:S(2)}, u32[]{:S(2)}) collective-permute-start(bf16[16,4,64,128]{3,2,1,0:T(8,128)(2,1)S(1)} %bitcast.40), channel_id=1, source_target_pairs={{0,4},{4,0},{1,5},{5,1},{2,6},{6,2},{3,7},{7,3},{8,12},{12,8},{9,1... | collective-permute-start | bytes 3145736 | tf_op jit(solution)/shard_map/ppermute | solution.py:38
  55.1 1.9 %collective-permute-done.2.got_other = bf16[16,4,64,128]{3,2,1,0:T(8,128)(2,1)} collective-permute-done((bf16[16,4,64,128]{3,2,1,0:T(8,128)(2,1)S(1)}, bf16[16,4,64,128]{3,2,1,0:T(8,128)(2,1)}, u32[]{:S(2)}, u32[]{:S(2)}) %collective-permute-start.2) | collective-permute-done | bytes 1048608 | tf_op jit(solution)/shard_map/ppermute | solution.py:38
  57.0 11.2 %block.1 = (bf16[1024,512]{1,0:T(8,128)(2,1)S(1)}, bf16[1024,512]{1,0:T(8,128)(2,1)S(1)}, bf16[2064,128]{1,0:T(8,128)(2,1)S(1)}, bf16[2064,128]{1,0:T(8,128)(2,1...) custom-call(s32[5]{0:T(128)S(1)} %stack.31.place.refs_0_, s32[1024,1]{1,0:T(8,128)S(1)} %bitcast.42, ...), custom_call_target="tpu_custom_call" | custom-call | tf_op jit(solution)/shard_map/block/pallas_call | solution.py:263
  70.3 1.2 collective-permute-start.6
  71.5 2.6 %pack.1 = bf16[16,4,64,128]{3,2,1,0:T(8,128)(2,1)} custom-call(s32[2,512]{1,0:T(2,128)S(1)} %broadcast_select_fusion.1.slot_ref, bf16[1024,512]{1,0:T(8,128)(2,1)S(1)} %get-tuple-element.37.part_ref, bf16[1024,512]{1,0:T(8,128)(2,1)S(1)} %collective-permute-done.3.other_ref, bf16[1024,512]{1,0:T(8,128)(2,1)S(1)} %get-tuple-element.38.emb_ref, ...), custom_call_target="tpu_custom_call" | custom-call | flops 2000000000 | bytes 10000000 | tf_op jit(solution)/shard_map/pack/pallas_call | solution.py:311
  74.2 9.8 %collective-permute-done.4.back_1 = bf16[2064,128]{1,0:T(8,128)(2,1)S(1)} collective-permute-done((bf16[2064,128]{1,0:T(8,128)(2,1)S(1)}, bf16[2064,128]{1,0:T(8,128)(2,1)S(1)}, u32[]{:S(2)}, u32[]{:S(2)}) %collective-permute-start.4) | collective-permute-done | bytes 528416 | tf_op jit(solution)/shard_map/ppermute | solution.py:64
  85.5 3.1 %collective-permute-start.8 = (bf16[528,128]{1,0:T(8,128)(2,1)S(1)}, bf16[528,128]{1,0:T(8,128)(2,1)S(1)}, u32[]{:S(2)}, u32[]{:S(2)}) collective-permute-start(bf16[528,128]{1,0:T(8,128)(2,1)S(1)} %get-tuple-element.46), channel_id=1, source_target_pairs={{0,2},{1,3},{2,0},{3,1},{8,10},{9,11},{10,8},{11,9},{16,18},{17,19... | collective-permute-start | bytes 405512 | tf_op jit(solution)/shard_map/ppermute | solution.py:64
  88.6 7.7 %all-to-all-start.2 = ((bf16[64,64,128]{2,1,0:T(8,128)(2,1)}), bf16[64,64,128]{2,1,0:T(8,128)(2,1)S(1)}, u32[]{:S(2)}, u32[]{:S(2)}) async-start(bf16[64,64,128]{2,1,0:T(8,128)(2,1)} %bitcast.16), calls=%async_computation.2 | async-start | bytes 2097152 | tf_op jit(solution)/shard_map/all_to_all | solution.py:42
  96.3 2.7 %collective-permute-start.12 = (bf16[528,128]{1,0:T(8,128)(2,1)S(1)}, bf16[528,128]{1,0:T(8,128)(2,1)S(1)}, u32[]{:S(2)}, u32[]{:S(2)}) collective-permute-start(bf16[528,128]{1,0:T(8,128)(2,1)S(1)} %sum_four.2.here), channel_id=1, source_target_pairs={{0,24},{8,0},{16,8},{24,16},{1,25},{9,1},{17,9},{25,17},{2,26},{10... | collective-permute-start | bytes 405512 | tf_op jit(solution)/shard_map/ppermute | solution.py:64
  100.1 10.2 %collective-permute-done.12.back_3 = bf16[528,128]{1,0:T(8,128)(2,1)S(1)} collective-permute-done((bf16[528,128]{1,0:T(8,128)(2,1)S(1)}, bf16[528,128]{1,0:T(8,128)(2,1)S(1)}, u32[]{:S(2)}, u32[]{:S(2)}) %collective-permute-start.12) | collective-permute-done | bytes 135200 | tf_op jit(solution)/shard_map/ppermute | solution.py:64
  110.2 1.6 %collective-permute-done.11.back_2 = bf16[528,128]{1,0:T(8,128)(2,1)S(1)} collective-permute-done((bf16[528,128]{1,0:T(8,128)(2,1)S(1)}, bf16[528,128]{1,0:T(8,128)(2,1)S(1)}, u32[]{:S(2)}, u32[]{:S(2)}) %collective-permute-start.11) | collective-permute-done | bytes 135200 | tf_op jit(solution)/shard_map/ppermute | solution.py:64
  111.9 2.2 %collective-permute-done.10.back_1 = bf16[528,128]{1,0:T(8,128)(2,1)S(1)} collective-permute-done((bf16[528,128]{1,0:T(8,128)(2,1)S(1)}, bf16[528,128]{1,0:T(8,128)(2,1)S(1)}, u32[]{:S(2)}, u32[]{:S(2)}) %collective-permute-start.10) | collective-permute-done | bytes 135200 | tf_op jit(solution)/shard_map/ppermute | solution.py:64
  114.5 1.9 %collective-permute-start.14 = (bf16[528,128]{1,0:T(8,128)(2,1)S(1)}, bf16[528,128]{1,0:T(8,128)(2,1)S(1)}, u32[]{:S(2)}, u32[]{:S(2)}) collective-permute-start(bf16[528,128]{1,0:T(8,128)(2,1)S(1)} %sum_four.3.here), channel_id=1, source_target_pairs={{0,2},{1,3},{2,0},{3,1},{8,10},{9,11},{10,8},{11,9},{16,18},{17,19... | collective-permute-start | bytes 405512 | tf_op jit(solution)/shard_map/ppermute | solution.py:64
  116.4 1.7 %collective-permute-start.13 = (bf16[528,128]{1,0:T(8,128)(2,1)S(1)}, bf16[528,128]{1,0:T(8,128)(2,1)S(1)}, u32[]{:S(2)}, u32[]{:S(2)}) collective-permute-start(bf16[528,128]{1,0:T(8,128)(2,1)S(1)} %sum_four.3.here), channel_id=1, source_target_pairs={{0,1},{1,2},{2,3},{3,0},{8,9},{9,10},{10,11},{11,8},{16,17},{17,18... | collective-permute-start | bytes 405512 | tf_op jit(solution)/shard_map/ppermute | solution.py:64
  118.6 1.8 %collective-permute-done.14.back_2 = bf16[528,128]{1,0:T(8,128)(2,1)S(1)} collective-permute-done((bf16[528,128]{1,0:T(8,128)(2,1)S(1)}, bf16[528,128]{1,0:T(8,128)(2,1)S(1)}, u32[]{:S(2)}, u32[]{:S(2)}) %collective-permute-start.14) | collective-permute-done | bytes 135200 | tf_op jit(solution)/shard_map/ppermute | solution.py:64
  121.3 2.6 %collective-permute-start.18 = (bf16[2064,128]{1,0:T(8,128)(2,1)S(1)}, bf16[2064,128]{1,0:T(8,128)(2,1)S(1)}, u32[]{:S(2)}, u32[]{:S(2)}) collective-permute-start(bf16[2064,128]{1,0:T(8,128)(2,1)S(1)} %join_four.1.refs_1_), channel_id=1, source_target_pairs={{0,96},{32,0},{64,32},{96,64},{8,104},{40,8},{72,40},{104,72},{16,... | collective-permute-start | bytes 1585160 | tf_op jit(solution)/shard_map/ppermute | solution.py:64
  125.2 11.0 %scatter_rows.1 = f32[8192,128]{1,0:T(8,128)} custom-call(s32[8192]{0:T(1024)S(1)} %bitcast.48, bf16[64,64,128]{2,1,0:T(8,128)(2,1)S(1)} %all-to-all-done.2.arrived_ref), custom_call_target="tpu_custom_call" | custom-call | flops 10000000000 | bytes 10000000 | tf_op jit(solution)/shard_map/scatter_rows/pallas_call | solution.py:367
  136.2 3.4 %collective-permute-done.16.refs_2_ = bf16[2064,128]{1,0:T(8,128)(2,1)} collective-permute-done((bf16[2064,128]{1,0:T(8,128)(2,1)S(1)}, bf16[2064,128]{1,0:T(8,128)(2,1)}, u32[]{:S(2)}, u32[]{:S(2)}) %collective-permute-start.16) | collective-permute-done | bytes 528416 | tf_op jit(solution)/shard_map/ppermute | solution.py:64
  139.6 4.5 %collective-permute-start.19 = (bf16[2064,128]{1,0:T(8,128)(2,1)S(1)}, bf16[2064,128]{1,0:T(8,128)(2,1)S(1)}, u32[]{:S(2)}, u32[]{:S(2)}) collective-permute-start(bf16[2064,128]{1,0:T(8,128)(2,1)S(1)} %join_four.1.refs_1_), channel_id=1, source_target_pairs={{0,4},{4,0},{1,5},{5,1},{2,6},{6,2},{3,7},{7,3},{8,12},{12,8},{9,1... | collective-permute-start | bytes 1585160 | tf_op jit(solution)/shard_map/ppermute | solution.py:38
  144.6 4.1 %finish_own.1 = (f32[2048,512]{1,0:T(8,128)}, f32[512,2048]{1,0:T(8,128)}, f32[16,128]{1,0:T(8,128)S(1)}) custom-call(s32[5]{0:T(128)S(1)} %stack.31.place.refs_0_, bf16[2064,128]{1,0:T(8,128)(2,1)S(1)} %join_four.1.refs_1_, bf16[2064,128]{1,0:T(8,128)(2,1)} %collective-permute-done.16.refs_2_, bf16[2064,128]{1,0:T(8,128)(2,1)S(1)} %collective-permute-done.17.refs_3_, ...), custom_call_target="tpu_custom_call" | custom-call | flops 6000000000 | bytes 10000000 | tf_op jit(solution)/shard_map/finish_own/pallas_call | solution.py:499
  148.8 3.1 %finish_other.1 = (f32[2048,512]{1,0:T(8,128)}, f32[512,2048]{1,0:T(8,128)}, f32[16,128]{1,0:T(8,128)}, f32[4,128]{1,0:T(4,128)}) custom-call(s32[5]{0:T(128)S(1)} %stack.31.place.refs_0_, bf16[2064,128]{1,0:T(8,128)(2,1)S(1)} %collective-permute-done.19.refs_1_, ...), custom_call_target="tpu_custom_call", output_to_operand_aliasing={{0}: (6, {}), {1}: (7, {})} | custom-call | tf_op jit(solution)/shard_map/finish_other/pallas_call | solution.py:512
  (61 shorter events, 12.4 us)
Async XLA Ops:
  1.3 1.5 collective-permute-start
  2.0 2.1 %collective-permute-start.1 = (bf16[512,512]{1,0:T(8,128)(2,1)}, bf16[512,512]{1,0:T(8,128)(2,1)S(1)}, u32[]{:S(2)}, u32[]{:S(2)}) collective-permute-start(bf16[512,512]{1,0:T(8,128)(2,1)} %bitcast.44), channel_id=1, source_target_pairs={{0,4},{4,0},{1,5},{5,1},{2,6},{6,2},{3,7},{7,3},{8,12},{12,8},{9,1... | collective-permute-start | bytes 1572872 | tf_op jit(solution)/shard_map/ppermute | solution.py:38
  51.9 5.1 %collective-permute-start.2 = (bf16[16,4,64,128]{3,2,1,0:T(8,128)(2,1)S(1)}, bf16[16,4,64,128]{3,2,1,0:T(8,128)(2,1)}, u32[]{:S(2)}, u32[]{:S(2)}) collective-permute-start(bf16[16,4,64,128]{3,2,1,0:T(8,128)(2,1)S(1)} %bitcast.40), channel_id=1, source_target_pairs={{0,4},{4,0},{1,5},{5,1},{2,6},{6,2},{3,7},{7,3},{8,12},{12,8},{9,1... | collective-permute-start | bytes 3145736 | tf_op jit(solution)/shard_map/ppermute | solution.py:38
  68.2 3.3 %collective-permute-start.3 = (bf16[1024,512]{1,0:T(8,128)(2,1)S(1)}, bf16[1024,512]{1,0:T(8,128)(2,1)S(1)}, u32[]{:S(2)}, u32[]{:S(2)}) collective-permute-start(bf16[1024,512]{1,0:T(8,128)(2,1)S(1)} %get-tuple-element.37.part_ref), channel_id=1, source_target_pairs={{0,4},{4,0},{1,5},{5,1},{2,6},{6,2},{3,7},{7,3},{8,12},{12,8},{9,1... | collective-permute-start | bytes 3145736 | tf_op jit(solution)/shard_map/ppermute | solution.py:38
  68.7 15.2 %collective-permute-start.4 = (bf16[2064,128]{1,0:T(8,128)(2,1)S(1)}, bf16[2064,128]{1,0:T(8,128)(2,1)S(1)}, u32[]{:S(2)}, u32[]{:S(2)}) collective-permute-start(bf16[2064,128]{1,0:T(8,128)(2,1)S(1)} %get-tuple-element.41), channel_id=1, source_target_pairs={{0,32},{32,64},{64,96},{96,0},{8,40},{40,72},{72,104},{104,8},{16,... | collective-permute-start | bytes 1585160 | tf_op jit(solution)/shard_map/ppermute | solution.py:64
  69.1 14.8 %collective-permute-start.5 = (bf16[2064,128]{1,0:T(8,128)(2,1)S(1)}, bf16[2064,128]{1,0:T(8,128)(2,1)S(1)}, u32[]{:S(2)}, u32[]{:S(2)}) collective-permute-start(bf16[2064,128]{1,0:T(8,128)(2,1)S(1)} %get-tuple-element.42), channel_id=1, source_target_pairs={{0,64},{32,96},{64,0},{96,32},{8,72},{40,104},{72,8},{104,40},{16,... | collective-permute-start | bytes 1585160 | tf_op jit(solution)/shard_map/ppermute | solution.py:64
  70.3 14.2 %collective-permute-start.6 = (bf16[2064,128]{1,0:T(8,128)(2,1)S(1)}, bf16[2064,128]{1,0:T(8,128)(2,1)S(1)}, u32[]{:S(2)}, u32[]{:S(2)}) collective-permute-start(bf16[2064,128]{1,0:T(8,128)(2,1)S(1)} %get-tuple-element.43), channel_id=1, source_target_pairs={{0,96},{32,0},{64,32},{96,64},{8,104},{40,8},{72,40},{104,72},{16,... | collective-permute-start | bytes 1585160 | tf_op jit(solution)/shard_map/ppermute | solution.py:64
  85.4 10.9 %collective-permute-start.7 = (bf16[528,128]{1,0:T(8,128)(2,1)S(1)}, bf16[528,128]{1,0:T(8,128)(2,1)S(1)}, u32[]{:S(2)}, u32[]{:S(2)}) collective-permute-start(bf16[528,128]{1,0:T(8,128)(2,1)S(1)} %get-tuple-element.45), channel_id=1, source_target_pairs={{0,1},{1,2},{2,3},{3,0},{8,9},{9,10},{10,11},{11,8},{16,17},{17,18... | collective-permute-start | bytes 405512 | tf_op jit(solution)/shard_map/ppermute | solution.py:64
  85.5 10.8 %collective-permute-start.8 = (bf16[528,128]{1,0:T(8,128)(2,1)S(1)}, bf16[528,128]{1,0:T(8,128)(2,1)S(1)}, u32[]{:S(2)}, u32[]{:S(2)}) collective-permute-start(bf16[528,128]{1,0:T(8,128)(2,1)S(1)} %get-tuple-element.46), channel_id=1, source_target_pairs={{0,2},{1,3},{2,0},{3,1},{8,10},{9,11},{10,8},{11,9},{16,18},{17,19... | collective-permute-start | bytes 405512 | tf_op jit(solution)/shard_map/ppermute | solution.py:64
  88.6 7.7 %collective-permute-start.9 = (bf16[528,128]{1,0:T(8,128)(2,1)S(1)}, bf16[528,128]{1,0:T(8,128)(2,1)S(1)}, u32[]{:S(2)}, u32[]{:S(2)}) collective-permute-start(bf16[528,128]{1,0:T(8,128)(2,1)S(1)} %get-tuple-element.47), channel_id=1, source_target_pairs={{0,3},{1,0},{2,1},{3,2},{8,11},{9,8},{10,9},{11,10},{16,19},{17,16... | collective-permute-start | bytes 405512 | tf_op jit(solution)/shard_map/ppermute | solution.py:64
  88.6 36.6 %all-to-all-start.2 = ((bf16[64,64,128]{2,1,0:T(8,128)(2,1)}), bf16[64,64,128]{2,1,0:T(8,128)(2,1)S(1)}, u32[]{:S(2)}, u32[]{:S(2)}) async-start(bf16[64,64,128]{2,1,0:T(8,128)(2,1)} %bitcast.16), calls=%async_computation.2 | async-start | bytes 2097152 | tf_op jit(solution)/shard_map/all_to_all | solution.py:42
  96.3 13.9 %collective-permute-start.12 = (bf16[528,128]{1,0:T(8,128)(2,1)S(1)}, bf16[528,128]{1,0:T(8,128)(2,1)S(1)}, u32[]{:S(2)}, u32[]{:S(2)}) collective-permute-start(bf16[528,128]{1,0:T(8,128)(2,1)S(1)} %sum_four.2.here), channel_id=1, source_target_pairs={{0,24},{8,0},{16,8},{24,16},{1,25},{9,1},{17,9},{25,17},{2,26},{10... | collective-permute-start | bytes 405512 | tf_op jit(solution)/shard_map/ppermute | solution.py:64
  99.0 12.8 %collective-permute-start.11 = (bf16[528,128]{1,0:T(8,128)(2,1)S(1)}, bf16[528,128]{1,0:T(8,128)(2,1)S(1)}, u32[]{:S(2)}, u32[]{:S(2)}) collective-permute-start(bf16[528,128]{1,0:T(8,128)(2,1)S(1)} %sum_four.2.here), channel_id=1, source_target_pairs={{0,16},{8,24},{16,0},{24,8},{1,17},{9,25},{17,1},{25,9},{2,18},{10... | collective-permute-start | bytes 405512 | tf_op jit(solution)/shard_map/ppermute | solution.py:64
  99.4 14.6 %collective-permute-start.10 = (bf16[528,128]{1,0:T(8,128)(2,1)S(1)}, bf16[528,128]{1,0:T(8,128)(2,1)S(1)}, u32[]{:S(2)}, u32[]{:S(2)}) collective-permute-start(bf16[528,128]{1,0:T(8,128)(2,1)S(1)} %sum_four.2.here), channel_id=1, source_target_pairs={{0,8},{8,16},{16,24},{24,0},{1,9},{9,17},{17,25},{25,1},{2,10},{10... | collective-permute-start | bytes 405512 | tf_op jit(solution)/shard_map/ppermute | solution.py:64
  114.1 4.5 %collective-permute-start.15 = (bf16[528,128]{1,0:T(8,128)(2,1)S(1)}, bf16[528,128]{1,0:T(8,128)(2,1)S(1)}, u32[]{:S(2)}, u32[]{:S(2)}) collective-permute-start(bf16[528,128]{1,0:T(8,128)(2,1)S(1)} %sum_four.3.here), channel_id=1, source_target_pairs={{0,3},{1,0},{2,1},{3,2},{8,11},{9,8},{10,9},{11,10},{16,19},{17,16... | collective-permute-start | bytes 405512 | tf_op jit(solution)/shard_map/ppermute | solution.py:64
  114.5 5.9 %collective-permute-start.14 = (bf16[528,128]{1,0:T(8,128)(2,1)S(1)}, bf16[528,128]{1,0:T(8,128)(2,1)S(1)}, u32[]{:S(2)}, u32[]{:S(2)}) collective-permute-start(bf16[528,128]{1,0:T(8,128)(2,1)S(1)} %sum_four.3.here), channel_id=1, source_target_pairs={{0,2},{1,3},{2,0},{3,1},{8,10},{9,11},{10,8},{11,9},{16,18},{17,19... | collective-permute-start | bytes 405512 | tf_op jit(solution)/shard_map/ppermute | solution.py:64
  116.4 4.9 %collective-permute-start.13 = (bf16[528,128]{1,0:T(8,128)(2,1)S(1)}, bf16[528,128]{1,0:T(8,128)(2,1)S(1)}, u32[]{:S(2)}, u32[]{:S(2)}) collective-permute-start(bf16[528,128]{1,0:T(8,128)(2,1)S(1)} %sum_four.3.here), channel_id=1, source_target_pairs={{0,1},{1,2},{2,3},{3,0},{8,9},{9,10},{10,11},{11,8},{16,17},{17,18... | collective-permute-start | bytes 405512 | tf_op jit(solution)/shard_map/ppermute | solution.py:64
  121.3 14.8 %collective-permute-start.18 = (bf16[2064,128]{1,0:T(8,128)(2,1)S(1)}, bf16[2064,128]{1,0:T(8,128)(2,1)S(1)}, u32[]{:S(2)}, u32[]{:S(2)}) collective-permute-start(bf16[2064,128]{1,0:T(8,128)(2,1)S(1)} %join_four.1.refs_1_), channel_id=1, source_target_pairs={{0,96},{32,0},{64,32},{96,64},{8,104},{40,8},{72,40},{104,72},{16,... | collective-permute-start | bytes 1585160 | tf_op jit(solution)/shard_map/ppermute | solution.py:64
  124.0 12.2 %collective-permute-start.17 = (bf16[2064,128]{1,0:T(8,128)(2,1)S(1)}, bf16[2064,128]{1,0:T(8,128)(2,1)S(1)}, u32[]{:S(2)}, u32[]{:S(2)}) collective-permute-start(bf16[2064,128]{1,0:T(8,128)(2,1)S(1)} %join_four.1.refs_1_), channel_id=1, source_target_pairs={{0,64},{32,96},{64,0},{96,32},{8,72},{40,104},{72,8},{104,40},{16,... | collective-permute-start | bytes 1585160 | tf_op jit(solution)/shard_map/ppermute | solution.py:64
  124.6 15.0 %collective-permute-start.16 = (bf16[2064,128]{1,0:T(8,128)(2,1)S(1)}, bf16[2064,128]{1,0:T(8,128)(2,1)}, u32[]{:S(2)}, u32[]{:S(2)}) collective-permute-start(bf16[2064,128]{1,0:T(8,128)(2,1)S(1)} %join_four.1.refs_1_), channel_id=1, source_target_pairs={{0,32},{32,64},{64,96},{96,0},{8,40},{40,72},{72,104},{104,8},{16,... | collective-permute-start | bytes 1585160 | tf_op jit(solution)/shard_map/ppermute | solution.py:64
  139.6 9.1 %collective-permute-start.19 = (bf16[2064,128]{1,0:T(8,128)(2,1)S(1)}, bf16[2064,128]{1,0:T(8,128)(2,1)S(1)}, u32[]{:S(2)}, u32[]{:S(2)}) collective-permute-start(bf16[2064,128]{1,0:T(8,128)(2,1)S(1)} %join_four.1.refs_1_), channel_id=1, source_target_pairs={{0,4},{4,0},{1,5},{5,1},{2,6},{6,2},{3,7},{7,3},{8,12},{12,8},{9,1... | collective-permute-start | bytes 1585160 | tf_op jit(solution)/shard_map/ppermute | solution.py:38
  144.1 4.6 %collective-permute-start.20 = (bf16[2064,128]{1,0:T(8,128)(2,1)}, bf16[2064,128]{1,0:T(8,128)(2,1)S(1)}, u32[]{:S(2)}, u32[]{:S(2)}) collective-permute-start(bf16[2064,128]{1,0:T(8,128)(2,1)} %collective-permute-done.16.refs_2_), channel_id=1, source_target_pairs={{0,4},{4,0},{1,5},{5,1},{2,6},{6,2},{3,7},{7,3},{8,12},{12,8},{9,1... | collective-permute-start | bytes 1585160 | tf_op jit(solution)/shard_map/ppermute | solution.py:38
  144.1 4.6 %collective-permute-start.21 = (bf16[2064,128]{1,0:T(8,128)(2,1)S(1)}, bf16[2064,128]{1,0:T(8,128)(2,1)S(1)}, u32[]{:S(2)}, u32[]{:S(2)}) collective-permute-start(bf16[2064,128]{1,0:T(8,128)(2,1)S(1)} %collective-permute-done.17.refs_3_), channel_id=1, source_target_pairs={{0,4},{4,0},{1,5},{5,1},{2,6},{6,2},{3,7},{7,3},{8,12},{12,8},{9,1... | collective-permute-start | bytes 1585160 | tf_op jit(solution)/shard_map/ppermute | solution.py:38
  144.6 4.1 %collective-permute-start.22 = (bf16[2064,128]{1,0:T(8,128)(2,1)S(1)}, bf16[2064,128]{1,0:T(8,128)(2,1)S(1)}, u32[]{:S(2)}, u32[]{:S(2)}) collective-permute-start(bf16[2064,128]{1,0:T(8,128)(2,1)S(1)} %collective-permute-done.18.refs_4_), channel_id=1, source_target_pairs={{0,4},{4,0},{1,5},{5,1},{2,6},{6,2},{3,7},{7,3},{8,12},{12,8},{9,1... | collective-permute-start | bytes 1585160 | tf_op jit(solution)/shard_map/ppermute | solution.py:38
  (4 other events, 91.4 us)

commit v9 on v7

--- a/solution.py
+++ b/solution.py
@@ -16,7 +16,7 @@
 
 N_X, N_Z, N_CORE, N_Y = 4, 4, 2, 4
 N_XZ = N_X * N_Z
-PEERS = ("x", "z", "y")
+PEERS = ("z", "x", "y")
 N_PEERS = N_XZ * N_Y
 EVERY = ("x", "z", "core", "y")
 
@@ -552,7 +552,8 @@
     lower = (tok_ids[:, None] >= tok_ids[None, :]).astype(bf16)
     running = jnp.einsum("ts,jsr->jtr", lower, onehot, preferred_element_type=f32)
     rank = (jnp.sum(running * onehot.astype(f32), axis=2) - 1.0).astype(i32)
-    slot = (owners // 2) * CAP + rank
+    column = owners // 2
+    slot = (column % N_Z * N_X + column // N_Z) * CAP + rank
     is_own = owners % 2 == core
     slot_own = jnp.where(is_own, slot, -1)
     slot_other = jnp.where(is_own, -1, slot)

time: 156 us -> 156 us (level)
  starting transfers between devices: 40.1 us -> 41.8 us
where the time goes in v9:
time: 156 us; the launch traced here: 155 us
  Pallas kernels  42.6 us (27%)
  starting transfers between devices  41.8 us (27%)
  blocking collectives  39.4 us (25%)
  waiting for transfers between devices  27.8 us (18%)
  local copies, waits for them, and re-layouts  2.13 us (1%)
    all_to_all x2, blocking collectives, exchange(): return lax.all_to_all(a, PEERS, split_axis=0, concat_axis=0, tiled=True)  39.4 us
    ppermute x15, waiting for transfers between devices, along(): return lax.ppermute(a, EVERY, pairs)  25.5 us
    ppermute x8, starting transfers between devices, swap(): return lax.ppermute(a, 'core', [(0, 1), (1, 0)])  17.8 us
    ppermute x15, starting transfers between devices, along(): return lax.ppermute(a, EVERY, pairs)  17.7 us
    pallas_call x1, Pallas kernels, block(): pl.pallas_call(block_kernel, in_specs=[SCALARS] + [NEAR] * 4 + [FAR] * 2...  12 us
    pallas_call x1, Pallas kernels, scatter_rows(): pl.pallas_call(scatter_kernel, in_specs=[SCALARS, NEAR], out_specs=NEAR,...  10.9 us
    pallas_call x1, Pallas kernels, gather_rows(): pl.pallas_call(gather_kernel, in_specs=[SCALARS, FAR], out_specs=NEAR, sc...  7.99 us
    all_to_all x1, starting transfers between devices, exchange(): return lax.all_to_all(a, PEERS, split_axis=0, concat_axis=0, tiled=True)  6.28 us
  transfers between devices with their start and end apart: 24, of which 16 were waited for; matrix products, arithmetic and copies ran while one was open for 1% of the time, Pallas kernels for 13%

profile of v9, /device:TPU:33, one launch (start us, length us, event | category | flops | bytes accessed | tf_op | source)
XLA Modules:
  0.0 155.2 jit_solution(13556268294610073642)
XLA Ops:
  4.1 18.1 %all_to_all.15 = s32[64,1,128]{2,1,0:T(1,128)} all-to-all(s32[64,1,128]{2,1,0:T(1,128)S(1)} %bitcast.53), channel_id=1, replica_groups=mesh['x'=4,'z'=4,'core'=2,'y'=4] {'z','x','y'}, dimensions={0} | all-to-all | bytes 65536 | tf_op jit(solution)/shard_map/all_to_all | solution.py:42
  22.2 8.0 %gather_rows.1 = bf16[64,64,128]{2,1,0:T(8,128)(2,1)} custom-call(s32[8192]{0:T(1024)} %bitcast.47, bf16[8192,128]{1,0:T(8,128)(2,1)} %table_ref.1), custom_call_target="tpu_custom_call" | custom-call | tf_op jit(solution)/shard_map/gather_rows/pallas_call | solution.py:113
  30.2 21.3 %all_to_all.16 = bf16[64,64,128]{2,1,0:T(8,128)(2,1)S(1)} all-to-all(bf16[64,64,128]{2,1,0:T(8,128)(2,1)} %gather_rows.1), channel_id=1, replica_groups=mesh['x'=4,'z'=4,'core'=2,'y'=4] {'z','x','y'}, dimensions={0} | all-to-all | bytes 2097152 | tf_op jit(solution)/shard_map/all_to_all | solution.py:42
  51.5 3.1 %collective-permute-start.2 = (bf16[16,4,64,128]{3,2,1,0:T(8,128)(2,1)S(1)}, bf16[16,4,64,128]{3,2,1,0:T(8,128)(2,1)}, u32[]{:S(2)}, u32[]{:S(2)}) collective-permute-start(bf16[16,4,64,128]{3,2,1,0:T(8,128)(2,1)S(1)} %bitcast.40), channel_id=1, source_target_pairs={{0,4},{4,0},{1,5},{5,1},{2,6},{6,2},{3,7},{7,3},{8,12},{12,8},{9,1... | collective-permute-start | bytes 3145736 | tf_op jit(solution)/shard_map/ppermute | solution.py:38
  55.2 1.9 %collective-permute-done.2.got_other = bf16[16,4,64,128]{3,2,1,0:T(8,128)(2,1)} collective-permute-done((bf16[16,4,64,128]{3,2,1,0:T(8,128)(2,1)S(1)}, bf16[16,4,64,128]{3,2,1,0:T(8,128)(2,1)}, u32[]{:S(2)}, u32[]{:S(2)}) %collective-permute-start.2) | collective-permute-done | bytes 1048608 | tf_op jit(solution)/shard_map/ppermute | solution.py:38
  57.1 12.0 %block.1 = (bf16[1024,512]{1,0:T(8,128)(2,1)S(1)}, bf16[1024,512]{1,0:T(8,128)(2,1)S(1)}, bf16[2064,128]{1,0:T(8,128)(2,1)S(1)}, bf16[2064,128]{1,0:T(8,128)(2,1...) custom-call(s32[5]{0:T(128)S(1)} %stack.31.place.refs_0_, s32[1024,1]{1,0:T(8,128)S(1)} %bitcast.42, ...), custom_call_target="tpu_custom_call" | custom-call | tf_op jit(solution)/shard_map/block/pallas_call | solution.py:263
  70.8 2.0 %collective-permute-start.6 = (bf16[2064,128]{1,0:T(8,128)(2,1)}, bf16[2064,128]{1,0:T(8,128)(2,1)}, u32[]{:S(2)}, u32[]{:S(2)}) collective-permute-start(bf16[2064,128]{1,0:T(8,128)(2,1)} %get-tuple-element.43), channel_id=1, source_target_pairs={{0,96},{32,0},{64,32},{96,64},{8,104},{40,8},{72,40},{104,72},{16,... | collective-permute-start | bytes 1585160 | tf_op jit(solution)/shard_map/ppermute | solution.py:64
  72.8 2.6 %pack.1 = bf16[16,4,64,128]{3,2,1,0:T(8,128)(2,1)} custom-call(s32[2,512]{1,0:T(2,128)S(1)} %broadcast_select_fusion.slot_ref, bf16[1024,512]{1,0:T(8,128)(2,1)S(1)} %get-tuple-element.37.part_ref, bf16[1024,512]{1,0:T(8,128)(2,1)S(1)} %collective-permute-done.3.other_ref, bf16[1024,512]{1,0:T(8,128)(2,1)S(1)} %get-tuple-element.38.emb_ref, ...), custom_call_target="tpu_custom_call" | custom-call | flops 2000000000 | bytes 10000000 | tf_op jit(solution)/shard_map/pack/pallas_call | solution.py:311
  75.4 6.3 %all-to-all-start.2 = ((bf16[64,64,128]{2,1,0:T(8,128)(2,1)}), bf16[64,64,128]{2,1,0:T(8,128)(2,1)S(1)}, u32[]{:S(2)}, u32[]{:S(2)}) async-start(bf16[64,64,128]{2,1,0:T(8,128)(2,1)} %bitcast.16), calls=%async_computation.2 | async-start | bytes 2097152 | tf_op jit(solution)/shard_map/all_to_all | solution.py:42
  81.7 3.4 %collective-permute-done.4.back_1 = bf16[2064,128]{1,0:T(8,128)(2,1)} collective-permute-done((bf16[2064,128]{1,0:T(8,128)(2,1)}, bf16[2064,128]{1,0:T(8,128)(2,1)}, u32[]{:S(2)}, u32[]{:S(2)}) %collective-permute-start.4) | collective-permute-done | bytes 528416 | tf_op jit(solution)/shard_map/ppermute | solution.py:64
  85.1 2.6 %collective-permute-done.6.back_3 = bf16[2064,128]{1,0:T(8,128)(2,1)} collective-permute-done((bf16[2064,128]{1,0:T(8,128)(2,1)}, bf16[2064,128]{1,0:T(8,128)(2,1)}, u32[]{:S(2)}, u32[]{:S(2)}) %collective-permute-start.6) | collective-permute-done | bytes 528416 | tf_op jit(solution)/shard_map/ppermute | solution.py:64
  87.7 1.6 %sum_split.1 = (bf16[528,128]{1,0:T(8,128)(2,1)S(1)}, bf16[528,128]{1,0:T(8,128)(2,1)S(1)}, bf16[528,128]{1,0:T(8,128)(2,1)S(1)}, bf16[528,128]{1,0:T(8,128)(2,1)S(1)}) custom-call(s32[5]{0:T(128)S(1)} %stack.31.place.refs_0_, bf16[2064,128]{1,0:T(8,128)(2,1)S(1)} %copy-done.5, bf16[2064,128]{1,0:T(8,128)(2,1)} %collective-permute-done.4.back_1, ...), custom_call_target="tpu_custom_call" | custom-call | flops 2000000000 | bytes 1000000 | tf_op jit(solution)/shard_map/sum_split/pallas_call | solution.py:399
  89.5 5.2 %collective-permute-start.8 = (bf16[528,128]{1,0:T(8,128)(2,1)S(1)}, bf16[528,128]{1,0:T(8,128)(2,1)S(1)}, u32[]{:S(2)}, u32[]{:S(2)}) collective-permute-start(bf16[528,128]{1,0:T(8,128)(2,1)S(1)} %get-tuple-element.46), channel_id=1, source_target_pairs={{0,2},{1,3},{2,0},{3,1},{8,10},{9,11},{10,8},{11,9},{16,18},{17,19... | collective-permute-start | bytes 405512 | tf_op jit(solution)/shard_map/ppermute | solution.py:64
  94.7 4.9 %collective-permute-done.7.back_1 = bf16[528,128]{1,0:T(8,128)(2,1)S(1)} collective-permute-done((bf16[528,128]{1,0:T(8,128)(2,1)S(1)}, bf16[528,128]{1,0:T(8,128)(2,1)S(1)}, u32[]{:S(2)}, u32[]{:S(2)}) %collective-permute-start.7) | collective-permute-done | bytes 135200 | tf_op jit(solution)/shard_map/ppermute | solution.py:64
  104.4 2.0 %collective-permute-done.12.back_3 = bf16[528,128]{1,0:T(8,128)(2,1)S(1)} collective-permute-done((bf16[528,128]{1,0:T(8,128)(2,1)S(1)}, bf16[528,128]{1,0:T(8,128)(2,1)S(1)}, u32[]{:S(2)}, u32[]{:S(2)}) %collective-permute-start.12) | collective-permute-done | bytes 135200 | tf_op jit(solution)/shard_map/ppermute | solution.py:64
  106.5 2.1 %collective-permute-done.11.back_2 = bf16[528,128]{1,0:T(8,128)(2,1)S(1)} collective-permute-done((bf16[528,128]{1,0:T(8,128)(2,1)S(1)}, bf16[528,128]{1,0:T(8,128)(2,1)S(1)}, u32[]{:S(2)}, u32[]{:S(2)}) %collective-permute-start.11) | collective-permute-done | bytes 135200 | tf_op jit(solution)/shard_map/ppermute | solution.py:64
  111.6 1.9 %collective-permute-start.13 = (bf16[528,128]{1,0:T(8,128)(2,1)S(1)}, bf16[528,128]{1,0:T(8,128)(2,1)S(1)}, u32[]{:S(2)}, u32[]{:S(2)}) collective-permute-start(bf16[528,128]{1,0:T(8,128)(2,1)S(1)} %sum_four.3.here), channel_id=1, source_target_pairs={{0,1},{1,2},{2,3},{3,0},{8,9},{9,10},{10,11},{11,8},{16,17},{17,18... | collective-permute-start | bytes 405512 | tf_op jit(solution)/shard_map/ppermute | solution.py:64
  114.2 2.7 %collective-permute-done.14.back_2 = bf16[528,128]{1,0:T(8,128)(2,1)S(1)} collective-permute-done((bf16[528,128]{1,0:T(8,128)(2,1)S(1)}, bf16[528,128]{1,0:T(8,128)(2,1)S(1)}, u32[]{:S(2)}, u32[]{:S(2)}) %collective-permute-start.14) | collective-permute-done | bytes 135200 | tf_op jit(solution)/shard_map/ppermute | solution.py:64
  117.2 1.9 %collective-permute-start.18 = (bf16[2064,128]{1,0:T(8,128)(2,1)S(1)}, bf16[2064,128]{1,0:T(8,128)(2,1)S(1)}, u32[]{:S(2)}, u32[]{:S(2)}) collective-permute-start(bf16[2064,128]{1,0:T(8,128)(2,1)S(1)} %join_four.1.refs_1_), channel_id=1, source_target_pairs={{0,96},{32,0},{64,32},{96,64},{8,104},{40,8},{72,40},{104,72},{16,... | collective-permute-start | bytes 1585160 | tf_op jit(solution)/shard_map/ppermute | solution.py:64
  119.8 10.9 %scatter_rows.1 = f32[8192,128]{1,0:T(8,128)} custom-call(s32[8192]{0:T(1024)S(1)} %bitcast.48, bf16[64,64,128]{2,1,0:T(8,128)(2,1)S(1)} %all-to-all-done.2.arrived_ref), custom_call_target="tpu_custom_call" | custom-call | flops 10000000000 | bytes 10000000 | tf_op jit(solution)/shard_map/scatter_rows/pallas_call | solution.py:367
  130.9 3.5 %collective-permute-done.16.refs_2_ = bf16[2064,128]{1,0:T(8,128)(2,1)} collective-permute-done((bf16[2064,128]{1,0:T(8,128)(2,1)S(1)}, bf16[2064,128]{1,0:T(8,128)(2,1)}, u32[]{:S(2)}, u32[]{:S(2)}) %collective-permute-start.16) | collective-permute-done | bytes 528416 | tf_op jit(solution)/shard_map/ppermute | solution.py:64
  134.4 13.1 %collective-permute-start.19 = (bf16[2064,128]{1,0:T(8,128)(2,1)S(1)}, bf16[2064,128]{1,0:T(8,128)(2,1)S(1)}, u32[]{:S(2)}, u32[]{:S(2)}) collective-permute-start(bf16[2064,128]{1,0:T(8,128)(2,1)S(1)} %join_four.1.refs_1_), channel_id=1, source_target_pairs={{0,4},{4,0},{1,5},{5,1},{2,6},{6,2},{3,7},{7,3},{8,12},{12,8},{9,1... | collective-permute-start | bytes 1585160 | tf_op jit(solution)/shard_map/ppermute | solution.py:38
  148.0 4.1 %finish_own.1 = (f32[2048,512]{1,0:T(8,128)}, f32[512,2048]{1,0:T(8,128)}, f32[16,128]{1,0:T(8,128)S(1)}) custom-call(s32[5]{0:T(128)S(1)} %stack.31.place.refs_0_, bf16[2064,128]{1,0:T(8,128)(2,1)S(1)} %join_four.1.refs_1_, bf16[2064,128]{1,0:T(8,128)(2,1)} %collective-permute-done.16.refs_2_, bf16[2064,128]{1,0:T(8,128)(2,1)S(1)} %collective-permute-done.17.refs_3_, ...), custom_call_target="tpu_custom_call" | custom-call | flops 6000000000 | bytes 10000000 | tf_op jit(solution)/shard_map/finish_own/pallas_call | solution.py:499
  152.2 3.1 %finish_other.1 = (f32[2048,512]{1,0:T(8,128)}, f32[512,2048]{1,0:T(8,128)}, f32[16,128]{1,0:T(8,128)}, f32[4,128]{1,0:T(4,128)}) custom-call(s32[5]{0:T(128)S(1)} %stack.31.place.refs_0_, bf16[2064,128]{1,0:T(8,128)(2,1)S(1)} %collective-permute-done.19.refs_1_, ...), custom_call_target="tpu_custom_call", output_to_operand_aliasing={{0}: (6, {}), {1}: (7, {})} | custom-call | tf_op jit(solution)/shard_map/finish_other/pallas_call | solution.py:512
  (65 shorter events, 16.0 us)
Async XLA Ops:
  1.3 1.5 collective-permute-start
  2.0 2.1 %collective-permute-start.1 = (bf16[512,512]{1,0:T(8,128)(2,1)}, bf16[512,512]{1,0:T(8,128)(2,1)S(1)}, u32[]{:S(2)}, u32[]{:S(2)}) collective-permute-start(bf16[512,512]{1,0:T(8,128)(2,1)} %bitcast.44), channel_id=1, source_target_pairs={{0,4},{4,0},{1,5},{5,1},{2,6},{6,2},{3,7},{7,3},{8,12},{12,8},{9,1... | collective-permute-start | bytes 1572872 | tf_op jit(solution)/shard_map/ppermute | solution.py:38
  51.5 5.5 %collective-permute-start.2 = (bf16[16,4,64,128]{3,2,1,0:T(8,128)(2,1)S(1)}, bf16[16,4,64,128]{3,2,1,0:T(8,128)(2,1)}, u32[]{:S(2)}, u32[]{:S(2)}) collective-permute-start(bf16[16,4,64,128]{3,2,1,0:T(8,128)(2,1)S(1)} %bitcast.40), channel_id=1, source_target_pairs={{0,4},{4,0},{1,5},{5,1},{2,6},{6,2},{3,7},{7,3},{8,12},{12,8},{9,1... | collective-permute-start | bytes 3145736 | tf_op jit(solution)/shard_map/ppermute | solution.py:38
  69.1 3.7 %collective-permute-start.3 = (bf16[1024,512]{1,0:T(8,128)(2,1)S(1)}, bf16[1024,512]{1,0:T(8,128)(2,1)S(1)}, u32[]{:S(2)}, u32[]{:S(2)}) collective-permute-start(bf16[1024,512]{1,0:T(8,128)(2,1)S(1)} %get-tuple-element.37.part_ref), channel_id=1, source_target_pairs={{0,4},{4,0},{1,5},{5,1},{2,6},{6,2},{3,7},{7,3},{8,12},{12,8},{9,1... | collective-permute-start | bytes 3145736 | tf_op jit(solution)/shard_map/ppermute | solution.py:38
  69.6 15.6 %collective-permute-start.4 = (bf16[2064,128]{1,0:T(8,128)(2,1)}, bf16[2064,128]{1,0:T(8,128)(2,1)}, u32[]{:S(2)}, u32[]{:S(2)}) collective-permute-start(bf16[2064,128]{1,0:T(8,128)(2,1)} %get-tuple-element.41), channel_id=1, source_target_pairs={{0,32},{32,64},{64,96},{96,0},{8,40},{40,72},{72,104},{104,8},{16,... | collective-permute-start | bytes 1585160 | tf_op jit(solution)/shard_map/ppermute | solution.py:64
  69.7 15.4 %collective-permute-start.5 = (bf16[2064,128]{1,0:T(8,128)(2,1)}, bf16[2064,128]{1,0:T(8,128)(2,1)}, u32[]{:S(2)}, u32[]{:S(2)}) collective-permute-start(bf16[2064,128]{1,0:T(8,128)(2,1)} %get-tuple-element.42), channel_id=1, source_target_pairs={{0,64},{32,96},{64,0},{96,32},{8,72},{40,104},{72,8},{104,40},{16,... | collective-permute-start | bytes 1585160 | tf_op jit(solution)/shard_map/ppermute | solution.py:64
  70.8 16.9 %collective-permute-start.6 = (bf16[2064,128]{1,0:T(8,128)(2,1)}, bf16[2064,128]{1,0:T(8,128)(2,1)}, u32[]{:S(2)}, u32[]{:S(2)}) collective-permute-start(bf16[2064,128]{1,0:T(8,128)(2,1)} %get-tuple-element.43), channel_id=1, source_target_pairs={{0,96},{32,0},{64,32},{96,64},{8,104},{40,8},{72,40},{104,72},{16,... | collective-permute-start | bytes 1585160 | tf_op jit(solution)/shard_map/ppermute | solution.py:64
  75.4 44.3 %all-to-all-start.2 = ((bf16[64,64,128]{2,1,0:T(8,128)(2,1)}), bf16[64,64,128]{2,1,0:T(8,128)(2,1)S(1)}, u32[]{:S(2)}, u32[]{:S(2)}) async-start(bf16[64,64,128]{2,1,0:T(8,128)(2,1)} %bitcast.16), calls=%async_computation.2 | async-start | bytes 2097152 | tf_op jit(solution)/shard_map/all_to_all | solution.py:42
  89.4 10.2 %collective-permute-start.7 = (bf16[528,128]{1,0:T(8,128)(2,1)S(1)}, bf16[528,128]{1,0:T(8,128)(2,1)S(1)}, u32[]{:S(2)}, u32[]{:S(2)}) collective-permute-start(bf16[528,128]{1,0:T(8,128)(2,1)S(1)} %get-tuple-element.45), channel_id=1, source_target_pairs={{0,1},{1,2},{2,3},{3,0},{8,9},{9,10},{10,11},{11,8},{16,17},{17,18... | collective-permute-start | bytes 405512 | tf_op jit(solution)/shard_map/ppermute | solution.py:64
  89.5 10.9 %collective-permute-start.8 = (bf16[528,128]{1,0:T(8,128)(2,1)S(1)}, bf16[528,128]{1,0:T(8,128)(2,1)S(1)}, u32[]{:S(2)}, u32[]{:S(2)}) collective-permute-start(bf16[528,128]{1,0:T(8,128)(2,1)S(1)} %get-tuple-element.46), channel_id=1, source_target_pairs={{0,2},{1,3},{2,0},{3,1},{8,10},{9,11},{10,8},{11,9},{16,18},{17,19... | collective-permute-start | bytes 405512 | tf_op jit(solution)/shard_map/ppermute | solution.py:64
  94.7 6.7 %collective-permute-start.9 = (bf16[528,128]{1,0:T(8,128)(2,1)S(1)}, bf16[528,128]{1,0:T(8,128)(2,1)S(1)}, u32[]{:S(2)}, u32[]{:S(2)}) collective-permute-start(bf16[528,128]{1,0:T(8,128)(2,1)S(1)} %get-tuple-element.47), channel_id=1, source_target_pairs={{0,3},{1,0},{2,1},{3,2},{8,11},{9,8},{10,9},{11,10},{16,19},{17,16... | collective-permute-start | bytes 405512 | tf_op jit(solution)/shard_map/ppermute | solution.py:64
  101.4 5.0 %collective-permute-start.12 = (bf16[528,128]{1,0:T(8,128)(2,1)S(1)}, bf16[528,128]{1,0:T(8,128)(2,1)S(1)}, u32[]{:S(2)}, u32[]{:S(2)}) collective-permute-start(bf16[528,128]{1,0:T(8,128)(2,1)S(1)} %sum_four.2.here), channel_id=1, source_target_pairs={{0,24},{8,0},{16,8},{24,16},{1,25},{9,1},{17,9},{25,17},{2,26},{10... | collective-permute-start | bytes 405512 | tf_op jit(solution)/shard_map/ppermute | solution.py:64
  103.1 5.5 %collective-permute-start.11 = (bf16[528,128]{1,0:T(8,128)(2,1)S(1)}, bf16[528,128]{1,0:T(8,128)(2,1)S(1)}, u32[]{:S(2)}, u32[]{:S(2)}) collective-permute-start(bf16[528,128]{1,0:T(8,128)(2,1)S(1)} %sum_four.2.here), channel_id=1, source_target_pairs={{0,16},{8,24},{16,0},{24,8},{1,17},{9,25},{17,1},{25,9},{2,18},{10... | collective-permute-start | bytes 405512 | tf_op jit(solution)/shard_map/ppermute | solution.py:64
  103.7 6.2 %collective-permute-start.10 = (bf16[528,128]{1,0:T(8,128)(2,1)S(1)}, bf16[528,128]{1,0:T(8,128)(2,1)S(1)}, u32[]{:S(2)}, u32[]{:S(2)}) collective-permute-start(bf16[528,128]{1,0:T(8,128)(2,1)S(1)} %sum_four.2.here), channel_id=1, source_target_pairs={{0,8},{8,16},{16,24},{24,0},{1,9},{9,17},{17,25},{25,1},{2,10},{10... | collective-permute-start | bytes 405512 | tf_op jit(solution)/shard_map/ppermute | solution.py:64
  110.0 4.2 %collective-permute-start.15 = (bf16[528,128]{1,0:T(8,128)(2,1)S(1)}, bf16[528,128]{1,0:T(8,128)(2,1)S(1)}, u32[]{:S(2)}, u32[]{:S(2)}) collective-permute-start(bf16[528,128]{1,0:T(8,128)(2,1)S(1)} %sum_four.3.here), channel_id=1, source_target_pairs={{0,3},{1,0},{2,1},{3,2},{8,11},{9,8},{10,9},{11,10},{16,19},{17,16... | collective-permute-start | bytes 405512 | tf_op jit(solution)/shard_map/ppermute | solution.py:64
  111.5 5.4 %collective-permute-start.14 = (bf16[528,128]{1,0:T(8,128)(2,1)S(1)}, bf16[528,128]{1,0:T(8,128)(2,1)S(1)}, u32[]{:S(2)}, u32[]{:S(2)}) collective-permute-start(bf16[528,128]{1,0:T(8,128)(2,1)S(1)} %sum_four.3.here), channel_id=1, source_target_pairs={{0,2},{1,3},{2,0},{3,1},{8,10},{9,11},{10,8},{11,9},{16,18},{17,19... | collective-permute-start | bytes 405512 | tf_op jit(solution)/shard_map/ppermute | solution.py:64
  111.6 5.5 %collective-permute-start.13 = (bf16[528,128]{1,0:T(8,128)(2,1)S(1)}, bf16[528,128]{1,0:T(8,128)(2,1)S(1)}, u32[]{:S(2)}, u32[]{:S(2)}) collective-permute-start(bf16[528,128]{1,0:T(8,128)(2,1)S(1)} %sum_four.3.here), channel_id=1, source_target_pairs={{0,1},{1,2},{2,3},{3,0},{8,9},{9,10},{10,11},{11,8},{16,17},{17,18... | collective-permute-start | bytes 405512 | tf_op jit(solution)/shard_map/ppermute | solution.py:64
  117.2 13.7 %collective-permute-start.18 = (bf16[2064,128]{1,0:T(8,128)(2,1)S(1)}, bf16[2064,128]{1,0:T(8,128)(2,1)S(1)}, u32[]{:S(2)}, u32[]{:S(2)}) collective-permute-start(bf16[2064,128]{1,0:T(8,128)(2,1)S(1)} %join_four.1.refs_1_), channel_id=1, source_target_pairs={{0,96},{32,0},{64,32},{96,64},{8,104},{40,8},{72,40},{104,72},{16,... | collective-permute-start | bytes 1585160 | tf_op jit(solution)/shard_map/ppermute | solution.py:64
  119.1 11.8 %collective-permute-start.17 = (bf16[2064,128]{1,0:T(8,128)(2,1)S(1)}, bf16[2064,128]{1,0:T(8,128)(2,1)S(1)}, u32[]{:S(2)}, u32[]{:S(2)}) collective-permute-start(bf16[2064,128]{1,0:T(8,128)(2,1)S(1)} %join_four.1.refs_1_), channel_id=1, source_target_pairs={{0,64},{32,96},{64,0},{96,32},{8,72},{40,104},{72,8},{104,40},{16,... | collective-permute-start | bytes 1585160 | tf_op jit(solution)/shard_map/ppermute | solution.py:64
  119.5 15.0 %collective-permute-start.16 = (bf16[2064,128]{1,0:T(8,128)(2,1)S(1)}, bf16[2064,128]{1,0:T(8,128)(2,1)}, u32[]{:S(2)}, u32[]{:S(2)}) collective-permute-start(bf16[2064,128]{1,0:T(8,128)(2,1)S(1)} %join_four.1.refs_1_), channel_id=1, source_target_pairs={{0,32},{32,64},{64,96},{96,0},{8,40},{40,72},{72,104},{104,8},{16,... | collective-permute-start | bytes 1585160 | tf_op jit(solution)/shard_map/ppermute | solution.py:64
  134.4 17.7 %collective-permute-start.19 = (bf16[2064,128]{1,0:T(8,128)(2,1)S(1)}, bf16[2064,128]{1,0:T(8,128)(2,1)S(1)}, u32[]{:S(2)}, u32[]{:S(2)}) collective-permute-start(bf16[2064,128]{1,0:T(8,128)(2,1)S(1)} %join_four.1.refs_1_), channel_id=1, source_target_pairs={{0,4},{4,0},{1,5},{5,1},{2,6},{6,2},{3,7},{7,3},{8,12},{12,8},{9,1... | collective-permute-start | bytes 1585160 | tf_op jit(solution)/shard_map/ppermute | solution.py:38
  147.5 4.6 %collective-permute-start.20 = (bf16[2064,128]{1,0:T(8,128)(2,1)}, bf16[2064,128]{1,0:T(8,128)(2,1)S(1)}, u32[]{:S(2)}, u32[]{:S(2)}) collective-permute-start(bf16[2064,128]{1,0:T(8,128)(2,1)} %collective-permute-done.16.refs_2_), channel_id=1, source_target_pairs={{0,4},{4,0},{1,5},{5,1},{2,6},{6,2},{3,7},{7,3},{8,12},{12,8},{9,1... | collective-permute-start | bytes 1585160 | tf_op jit(solution)/shard_map/ppermute | solution.py:38
  147.5 4.6 %collective-permute-start.21 = (bf16[2064,128]{1,0:T(8,128)(2,1)S(1)}, bf16[2064,128]{1,0:T(8,128)(2,1)S(1)}, u32[]{:S(2)}, u32[]{:S(2)}) collective-permute-start(bf16[2064,128]{1,0:T(8,128)(2,1)S(1)} %collective-permute-done.17.refs_3_), channel_id=1, source_target_pairs={{0,4},{4,0},{1,5},{5,1},{2,6},{6,2},{3,7},{7,3},{8,12},{12,8},{9,1... | collective-permute-start | bytes 1585160 | tf_op jit(solution)/shard_map/ppermute | solution.py:38
  148.0 4.1 %collective-permute-start.22 = (bf16[2064,128]{1,0:T(8,128)(2,1)S(1)}, bf16[2064,128]{1,0:T(8,128)(2,1)S(1)}, u32[]{:S(2)}, u32[]{:S(2)}) collective-permute-start(bf16[2064,128]{1,0:T(8,128)(2,1)S(1)} %collective-permute-done.18.refs_4_), channel_id=1, source_target_pairs={{0,4},{4,0},{1,5},{5,1},{2,6},{6,2},{3,7},{7,3},{8,12},{12,8},{9,1... | collective-permute-start | bytes 1585160 | tf_op jit(solution)/shard_map/ppermute | solution.py:38
  (6 other events, 109.1 us)

commit v10 on v8

--- a/solution.py
+++ b/solution.py
@@ -402,7 +402,7 @@
         out_specs=[NEAR] * 4,
         out_shape=[jax.ShapeDtypeStruct((N_BLOCK + N_VEC, LANES), bf16)] * 4,
         compiler_params=params(8),
-        cost_estimate=pl.CostEstimate(flops=4 * 10**9, bytes_accessed=10**6, transcendentals=0),
+        cost_estimate=pl.CostEstimate(flops=6 * 10**9, bytes_accessed=10**6, transcendentals=0),
         name="sum_split",
     )(place, *pieces)
 
@@ -419,7 +419,7 @@
         sum_kernel,
         out_shape=jax.ShapeDtypeStruct((N_BLOCK + N_VEC, LANES), bf16),
         compiler_params=params(4),
-        cost_estimate=pl.CostEstimate(flops=4 * 10**9, bytes_accessed=10**6, transcendentals=0),
+        cost_estimate=pl.CostEstimate(flops=6 * 10**9, bytes_accessed=10**6, transcendentals=0),
         name="sum_four",
     )(*pieces)
 
@@ -435,7 +435,7 @@
         join_kernel,
         out_shape=jax.ShapeDtypeStruct((N_RING, LANES), bf16),
         compiler_params=params(4),
-        cost_estimate=pl.CostEstimate(flops=4 * 10**9, bytes_accessed=10**6, transcendentals=0),
+        cost_estimate=pl.CostEstimate(flops=6 * 10**9, bytes_accessed=10**6, transcendentals=0),
         name="join_four",
     )(*pieces)
 

time: 155 us -> 152 us (0.981)
  starting transfers between devices: 34.1 us -> 31.1 us
    ppermute x15, starting transfers between devices: 17.7 us -> 14.8 us  [along(): return lax.ppermute(a, EVERY, pairs)]
    ppermute x8, starting transfers between devices: 8.81 us -> 6.52 us  [swap(): return lax.ppermute(a, 'core', [(0, 1), (1, 0)])]
    all_to_all x1, starting transfers between devices: 7.65 us -> 9.84 us  [exchange(): return lax.all_to_all(a, PEERS, split_axis=0, concat_axis=0, tiled=True)]
where the time goes in v10:
time: 152 us; the launch traced here: 150 us
  Pallas kernels  41 us (27%)
  blocking collectives  39.8 us (26%)
  waiting for transfers between devices  34.3 us (23%)
  starting transfers between devices  31.1 us (20%)
  local copies, waits for them, and re-layouts  2.12 us (1%)
    all_to_all x2, blocking collectives, exchange(): return lax.all_to_all(a, PEERS, split_axis=0, concat_axis=0, tiled=True)  39.8 us
    ppermute x15, waiting for transfers between devices, along(): return lax.ppermute(a, EVERY, pairs)  32 us
    ppermute x15, starting transfers between devices, along(): return lax.ppermute(a, EVERY, pairs)  14.8 us
    pallas_call x1, Pallas kernels, block(): pl.pallas_call(block_kernel, in_specs=[SCALARS] + [NEAR] * 4 + [FAR] * 2...  11.2 us
    pallas_call x1, Pallas kernels, scatter_rows(): pl.pallas_call(scatter_kernel, in_specs=[SCALARS, NEAR], out_specs=NEAR,...  10.9 us
    all_to_all x1, starting transfers between devices, exchange(): return lax.all_to_all(a, PEERS, split_axis=0, concat_axis=0, tiled=True)  9.84 us
    pallas_call x1, Pallas kernels, gather_rows(): pl.pallas_call(gather_kernel, in_specs=[SCALARS, FAR], out_specs=NEAR, sc...  7.99 us
    ppermute x8, starting transfers between devices, swap(): return lax.ppermute(a, 'core', [(0, 1), (1, 0)])  6.52 us
  transfers between devices with their start and end apart: 24, of which 12 were waited for; matrix products, arithmetic and copies ran while one was open for 1% of the time, Pallas kernels for 12%

profile of v10, /device:TPU:33, one launch (start us, length us, event | category | flops | bytes accessed | tf_op | source)
XLA Modules:
  0.0 150.0 jit_solution(3161973274548012578)
XLA Ops:
  4.1 18.1 %all_to_all.15 = s32[64,1,128]{2,1,0:T(1,128)} all-to-all(s32[64,1,128]{2,1,0:T(1,128)S(1)} %bitcast.53), channel_id=1, replica_groups=mesh['x'=4,'z'=4,'core'=2,'y'=4] {'x','z','y'}, dimensions={0} | all-to-all | bytes 65536 | tf_op jit(solution)/shard_map/all_to_all | solution.py:42
  22.2 8.0 %gather_rows.1 = bf16[64,64,128]{2,1,0:T(8,128)(2,1)} custom-call(s32[8192]{0:T(1024)} %bitcast.47, bf16[8192,128]{1,0:T(8,128)(2,1)} %table_ref.1), custom_call_target="tpu_custom_call" | custom-call | tf_op jit(solution)/shard_map/gather_rows/pallas_call | solution.py:113
  30.3 21.6 %all_to_all.16 = bf16[64,64,128]{2,1,0:T(8,128)(2,1)S(1)} all-to-all(bf16[64,64,128]{2,1,0:T(8,128)(2,1)} %gather_rows.1), channel_id=1, replica_groups=mesh['x'=4,'z'=4,'core'=2,'y'=4] {'x','z','y'}, dimensions={0} | all-to-all | bytes 2097152 | tf_op jit(solution)/shard_map/all_to_all | solution.py:42
  51.9 2.7 %collective-permute-start.2 = (bf16[16,4,64,128]{3,2,1,0:T(8,128)(2,1)S(1)}, bf16[16,4,64,128]{3,2,1,0:T(8,128)(2,1)}, u32[]{:S(2)}, u32[]{:S(2)}) collective-permute-start(bf16[16,4,64,128]{3,2,1,0:T(8,128)(2,1)S(1)} %bitcast.40), channel_id=1, source_target_pairs={{0,4},{4,0},{1,5},{5,1},{2,6},{6,2},{3,7},{7,3},{8,12},{12,8},{9,1... | collective-permute-start | bytes 3145736 | tf_op jit(solution)/shard_map/ppermute | solution.py:38
  55.1 1.9 %collective-permute-done.2.got_other = bf16[16,4,64,128]{3,2,1,0:T(8,128)(2,1)} collective-permute-done((bf16[16,4,64,128]{3,2,1,0:T(8,128)(2,1)S(1)}, bf16[16,4,64,128]{3,2,1,0:T(8,128)(2,1)}, u32[]{:S(2)}, u32[]{:S(2)}) %collective-permute-start.2) | collective-permute-done | bytes 1048608 | tf_op jit(solution)/shard_map/ppermute | solution.py:38
  57.0 11.2 %block.1 = (bf16[1024,512]{1,0:T(8,128)(2,1)S(1)}, bf16[1024,512]{1,0:T(8,128)(2,1)S(1)}, bf16[2064,128]{1,0:T(8,128)(2,1)S(1)}, bf16[2064,128]{1,0:T(8,128)(2,1...) custom-call(s32[5]{0:T(128)S(1)} %stack.31.place.refs_0_, s32[1024,1]{1,0:T(8,128)S(1)} %bitcast.42, ...), custom_call_target="tpu_custom_call" | custom-call | tf_op jit(solution)/shard_map/block/pallas_call | solution.py:263
  69.1 1.2 collective-permute-start.5
  70.3 1.2 collective-permute-start.6
  71.5 2.6 %pack.1 = bf16[16,4,64,128]{3,2,1,0:T(8,128)(2,1)} custom-call(s32[2,512]{1,0:T(2,128)S(1)} %broadcast_select_fusion.1.slot_ref, bf16[1024,512]{1,0:T(8,128)(2,1)S(1)} %get-tuple-element.37.part_ref, bf16[1024,512]{1,0:T(8,128)(2,1)S(1)} %collective-permute-done.3.other_ref, bf16[1024,512]{1,0:T(8,128)(2,1)S(1)} %get-tuple-element.38.emb_ref, ...), custom_call_target="tpu_custom_call" | custom-call | flops 2000000000 | bytes 10000000 | tf_op jit(solution)/shard_map/pack/pallas_call | solution.py:311
  74.2 9.8 %collective-permute-done.4.back_1 = bf16[2064,128]{1,0:T(8,128)(2,1)S(1)} collective-permute-done((bf16[2064,128]{1,0:T(8,128)(2,1)S(1)}, bf16[2064,128]{1,0:T(8,128)(2,1)S(1)}, u32[]{:S(2)}, u32[]{:S(2)}) %collective-permute-start.4) | collective-permute-done | bytes 528416 | tf_op jit(solution)/shard_map/ppermute | solution.py:64
  85.5 3.1 %collective-permute-start.8 = (bf16[528,128]{1,0:T(8,128)(2,1)S(1)}, bf16[528,128]{1,0:T(8,128)(2,1)S(1)}, u32[]{:S(2)}, u32[]{:S(2)}) collective-permute-start(bf16[528,128]{1,0:T(8,128)(2,1)S(1)} %get-tuple-element.46), channel_id=1, source_target_pairs={{0,2},{1,3},{2,0},{3,1},{8,10},{9,11},{10,8},{11,9},{16,18},{17,19... | collective-permute-start | bytes 405512 | tf_op jit(solution)/shard_map/ppermute | solution.py:64
  89.3 2.1 %collective-permute-done.8.back_2 = bf16[528,128]{1,0:T(8,128)(2,1)S(1)} collective-permute-done((bf16[528,128]{1,0:T(8,128)(2,1)S(1)}, bf16[528,128]{1,0:T(8,128)(2,1)S(1)}, u32[]{:S(2)}, u32[]{:S(2)}) %collective-permute-start.8) | collective-permute-done | bytes 135200 | tf_op jit(solution)/shard_map/ppermute | solution.py:64
  91.4 1.4 collective-permute-done.9.back_3
  92.9 1.0 collective-permute-start.12
  95.0 9.8 %all-to-all-start.2 = ((bf16[64,64,128]{2,1,0:T(8,128)(2,1)}), bf16[64,64,128]{2,1,0:T(8,128)(2,1)S(1)}, u32[]{:S(2)}, u32[]{:S(2)}) async-start(bf16[64,64,128]{2,1,0:T(8,128)(2,1)} %bitcast.16), calls=%async_computation.2 | async-start | bytes 2097152 | tf_op jit(solution)/shard_map/all_to_all | solution.py:42
  105.5 1.9 %collective-permute-start.14 = (bf16[528,128]{1,0:T(8,128)(2,1)S(1)}, bf16[528,128]{1,0:T(8,128)(2,1)S(1)}, u32[]{:S(2)}, u32[]{:S(2)}) collective-permute-start(bf16[528,128]{1,0:T(8,128)(2,1)S(1)} %sum_four.3.here), channel_id=1, source_target_pairs={{0,2},{1,3},{2,0},{3,1},{8,10},{9,11},{10,8},{11,9},{16,18},{17,19... | collective-permute-start | bytes 405512 | tf_op jit(solution)/shard_map/ppermute | solution.py:64
  107.4 1.5 collective-permute-start.13
  109.2 12.8 %collective-permute-done.14.back_2 = bf16[528,128]{1,0:T(8,128)(2,1)S(1)} collective-permute-done((bf16[528,128]{1,0:T(8,128)(2,1)S(1)}, bf16[528,128]{1,0:T(8,128)(2,1)S(1)}, u32[]{:S(2)}, u32[]{:S(2)}) %collective-permute-start.14) | collective-permute-done | bytes 135200 | tf_op jit(solution)/shard_map/ppermute | solution.py:64
  122.5 1.8 %collective-permute-start.18 = (bf16[2064,128]{1,0:T(8,128)(2,1)S(1)}, bf16[2064,128]{1,0:T(8,128)(2,1)S(1)}, u32[]{:S(2)}, u32[]{:S(2)}) collective-permute-start(bf16[2064,128]{1,0:T(8,128)(2,1)S(1)} %join_four.1.refs_1_), channel_id=1, source_target_pairs={{0,96},{32,0},{64,32},{96,64},{8,104},{40,8},{72,40},{104,72},{16,... | collective-permute-start | bytes 1585160 | tf_op jit(solution)/shard_map/ppermute | solution.py:64
  125.3 10.9 %scatter_rows.1 = f32[8192,128]{1,0:T(8,128)} custom-call(s32[8192]{0:T(1024)S(1)} %bitcast.48, bf16[64,64,128]{2,1,0:T(8,128)(2,1)S(1)} %all-to-all-done.2.arrived_ref), custom_call_target="tpu_custom_call" | custom-call | flops 10000000000 | bytes 10000000 | tf_op jit(solution)/shard_map/scatter_rows/pallas_call | solution.py:367
  136.3 3.7 %collective-permute-done.16.refs_2_ = bf16[2064,128]{1,0:T(8,128)(2,1)} collective-permute-done((bf16[2064,128]{1,0:T(8,128)(2,1)S(1)}, bf16[2064,128]{1,0:T(8,128)(2,1)}, u32[]{:S(2)}, u32[]{:S(2)}) %collective-permute-start.16) | collective-permute-done | bytes 528416 | tf_op jit(solution)/shard_map/ppermute | solution.py:64
  140.0 2.2 %collective-permute-start.19 = (bf16[2064,128]{1,0:T(8,128)(2,1)S(1)}, bf16[2064,128]{1,0:T(8,128)(2,1)S(1)}, u32[]{:S(2)}, u32[]{:S(2)}) collective-permute-start(bf16[2064,128]{1,0:T(8,128)(2,1)S(1)} %join_four.1.refs_1_), channel_id=1, source_target_pairs={{0,4},{4,0},{1,5},{5,1},{2,6},{6,2},{3,7},{7,3},{8,12},{12,8},{9,1... | collective-permute-start | bytes 1585160 | tf_op jit(solution)/shard_map/ppermute | solution.py:38
  142.7 4.1 %finish_own.1 = (f32[2048,512]{1,0:T(8,128)}, f32[512,2048]{1,0:T(8,128)}, f32[16,128]{1,0:T(8,128)S(1)}) custom-call(s32[5]{0:T(128)S(1)} %stack.31.place.refs_0_, bf16[2064,128]{1,0:T(8,128)(2,1)S(1)} %join_four.1.refs_1_, bf16[2064,128]{1,0:T(8,128)(2,1)} %collective-permute-done.16.refs_2_, bf16[2064,128]{1,0:T(8,128)(2,1)S(1)} %collective-permute-done.17.refs_3_, ...), custom_call_target="tpu_custom_call" | custom-call | flops 6000000000 | bytes 10000000 | tf_op jit(solution)/shard_map/finish_own/pallas_call | solution.py:499
  146.9 3.1 %finish_other.1 = (f32[2048,512]{1,0:T(8,128)}, f32[512,2048]{1,0:T(8,128)}, f32[16,128]{1,0:T(8,128)}, f32[4,128]{1,0:T(4,128)}) custom-call(s32[5]{0:T(128)S(1)} %stack.31.place.refs_0_, bf16[2064,128]{1,0:T(8,128)(2,1)S(1)} %collective-permute-done.19.refs_1_, ...), custom_call_target="tpu_custom_call", output_to_operand_aliasing={{0}: (6, {}), {1}: (7, {})} | custom-call | tf_op jit(solution)/shard_map/finish_other/pallas_call | solution.py:512
  (61 shorter events, 11.2 us)
Async XLA Ops:
  1.3 1.5 collective-permute-start
  2.0 2.1 %collective-permute-start.1 = (bf16[512,512]{1,0:T(8,128)(2,1)}, bf16[512,512]{1,0:T(8,128)(2,1)S(1)}, u32[]{:S(2)}, u32[]{:S(2)}) collective-permute-start(bf16[512,512]{1,0:T(8,128)(2,1)} %bitcast.44), channel_id=1, source_target_pairs={{0,4},{4,0},{1,5},{5,1},{2,6},{6,2},{3,7},{7,3},{8,12},{12,8},{9,1... | collective-permute-start | bytes 1572872 | tf_op jit(solution)/shard_map/ppermute | solution.py:38
  51.9 5.1 %collective-permute-start.2 = (bf16[16,4,64,128]{3,2,1,0:T(8,128)(2,1)S(1)}, bf16[16,4,64,128]{3,2,1,0:T(8,128)(2,1)}, u32[]{:S(2)}, u32[]{:S(2)}) collective-permute-start(bf16[16,4,64,128]{3,2,1,0:T(8,128)(2,1)S(1)} %bitcast.40), channel_id=1, source_target_pairs={{0,4},{4,0},{1,5},{5,1},{2,6},{6,2},{3,7},{7,3},{8,12},{12,8},{9,1... | collective-permute-start | bytes 3145736 | tf_op jit(solution)/shard_map/ppermute | solution.py:38
  68.2 3.3 %collective-permute-start.3 = (bf16[1024,512]{1,0:T(8,128)(2,1)S(1)}, bf16[1024,512]{1,0:T(8,128)(2,1)S(1)}, u32[]{:S(2)}, u32[]{:S(2)}) collective-permute-start(bf16[1024,512]{1,0:T(8,128)(2,1)S(1)} %get-tuple-element.37.part_ref), channel_id=1, source_target_pairs={{0,4},{4,0},{1,5},{5,1},{2,6},{6,2},{3,7},{7,3},{8,12},{12,8},{9,1... | collective-permute-start | bytes 3145736 | tf_op jit(solution)/shard_map/ppermute | solution.py:38
  68.7 15.2 %collective-permute-start.4 = (bf16[2064,128]{1,0:T(8,128)(2,1)S(1)}, bf16[2064,128]{1,0:T(8,128)(2,1)S(1)}, u32[]{:S(2)}, u32[]{:S(2)}) collective-permute-start(bf16[2064,128]{1,0:T(8,128)(2,1)S(1)} %get-tuple-element.41), channel_id=1, source_target_pairs={{0,32},{32,64},{64,96},{96,0},{8,40},{40,72},{72,104},{104,8},{16,... | collective-permute-start | bytes 1585160 | tf_op jit(solution)/shard_map/ppermute | solution.py:64
  69.1 14.8 %collective-permute-start.5 = (bf16[2064,128]{1,0:T(8,128)(2,1)S(1)}, bf16[2064,128]{1,0:T(8,128)(2,1)S(1)}, u32[]{:S(2)}, u32[]{:S(2)}) collective-permute-start(bf16[2064,128]{1,0:T(8,128)(2,1)S(1)} %get-tuple-element.42), channel_id=1, source_target_pairs={{0,64},{32,96},{64,0},{96,32},{8,72},{40,104},{72,8},{104,40},{16,... | collective-permute-start | bytes 1585160 | tf_op jit(solution)/shard_map/ppermute | solution.py:64
  70.3 14.2 %collective-permute-start.6 = (bf16[2064,128]{1,0:T(8,128)(2,1)S(1)}, bf16[2064,128]{1,0:T(8,128)(2,1)S(1)}, u32[]{:S(2)}, u32[]{:S(2)}) collective-permute-start(bf16[2064,128]{1,0:T(8,128)(2,1)S(1)} %get-tuple-element.43), channel_id=1, source_target_pairs={{0,96},{32,0},{64,32},{96,64},{8,104},{40,8},{72,40},{104,72},{16,... | collective-permute-start | bytes 1585160 | tf_op jit(solution)/shard_map/ppermute | solution.py:64
  85.4 3.9 %collective-permute-start.7 = (bf16[528,128]{1,0:T(8,128)(2,1)S(1)}, bf16[528,128]{1,0:T(8,128)(2,1)S(1)}, u32[]{:S(2)}, u32[]{:S(2)}) collective-permute-start(bf16[528,128]{1,0:T(8,128)(2,1)S(1)} %get-tuple-element.45), channel_id=1, source_target_pairs={{0,1},{1,2},{2,3},{3,0},{8,9},{9,10},{10,11},{11,8},{16,17},{17,18... | collective-permute-start | bytes 405512 | tf_op jit(solution)/shard_map/ppermute | solution.py:64
  85.5 6.0 %collective-permute-start.8 = (bf16[528,128]{1,0:T(8,128)(2,1)S(1)}, bf16[528,128]{1,0:T(8,128)(2,1)S(1)}, u32[]{:S(2)}, u32[]{:S(2)}) collective-permute-start(bf16[528,128]{1,0:T(8,128)(2,1)S(1)} %get-tuple-element.46), channel_id=1, source_target_pairs={{0,2},{1,3},{2,0},{3,1},{8,10},{9,11},{10,8},{11,9},{16,18},{17,19... | collective-permute-start | bytes 405512 | tf_op jit(solution)/shard_map/ppermute | solution.py:64
  88.6 4.3 %collective-permute-start.9 = (bf16[528,128]{1,0:T(8,128)(2,1)S(1)}, bf16[528,128]{1,0:T(8,128)(2,1)S(1)}, u32[]{:S(2)}, u32[]{:S(2)}) collective-permute-start(bf16[528,128]{1,0:T(8,128)(2,1)S(1)} %get-tuple-element.47), channel_id=1, source_target_pairs={{0,3},{1,0},{2,1},{3,2},{8,11},{9,8},{10,9},{11,10},{16,19},{17,16... | collective-permute-start | bytes 405512 | tf_op jit(solution)/shard_map/ppermute | solution.py:64
  92.9 11.9 %collective-permute-start.12 = (bf16[528,128]{1,0:T(8,128)(2,1)S(1)}, bf16[528,128]{1,0:T(8,128)(2,1)S(1)}, u32[]{:S(2)}, u32[]{:S(2)}) collective-permute-start(bf16[528,128]{1,0:T(8,128)(2,1)S(1)} %sum_four.2.here), channel_id=1, source_target_pairs={{0,24},{8,0},{16,8},{24,16},{1,25},{9,1},{17,9},{25,17},{2,26},{10... | collective-permute-start | bytes 405512 | tf_op jit(solution)/shard_map/ppermute | solution.py:64
  93.9 10.9 %collective-permute-start.11 = (bf16[528,128]{1,0:T(8,128)(2,1)S(1)}, bf16[528,128]{1,0:T(8,128)(2,1)S(1)}, u32[]{:S(2)}, u32[]{:S(2)}) collective-permute-start(bf16[528,128]{1,0:T(8,128)(2,1)S(1)} %sum_four.2.here), channel_id=1, source_target_pairs={{0,16},{8,24},{16,0},{24,8},{1,17},{9,25},{17,1},{25,9},{2,18},{10... | collective-permute-start | bytes 405512 | tf_op jit(solution)/shard_map/ppermute | solution.py:64
  94.8 10.0 %collective-permute-start.10 = (bf16[528,128]{1,0:T(8,128)(2,1)S(1)}, bf16[528,128]{1,0:T(8,128)(2,1)S(1)}, u32[]{:S(2)}, u32[]{:S(2)}) collective-permute-start(bf16[528,128]{1,0:T(8,128)(2,1)S(1)} %sum_four.2.here), channel_id=1, source_target_pairs={{0,8},{8,16},{16,24},{24,0},{1,9},{9,17},{17,25},{25,1},{2,10},{10... | collective-permute-start | bytes 405512 | tf_op jit(solution)/shard_map/ppermute | solution.py:64
  95.0 30.3 %all-to-all-start.2 = ((bf16[64,64,128]{2,1,0:T(8,128)(2,1)}), bf16[64,64,128]{2,1,0:T(8,128)(2,1)S(1)}, u32[]{:S(2)}, u32[]{:S(2)}) async-start(bf16[64,64,128]{2,1,0:T(8,128)(2,1)} %bitcast.16), calls=%async_computation.2 | async-start | bytes 2097152 | tf_op jit(solution)/shard_map/all_to_all | solution.py:42
  104.9 4.3 %collective-permute-start.15 = (bf16[528,128]{1,0:T(8,128)(2,1)S(1)}, bf16[528,128]{1,0:T(8,128)(2,1)S(1)}, u32[]{:S(2)}, u32[]{:S(2)}) collective-permute-start(bf16[528,128]{1,0:T(8,128)(2,1)S(1)} %sum_four.3.here), channel_id=1, source_target_pairs={{0,3},{1,0},{2,1},{3,2},{8,11},{9,8},{10,9},{11,10},{16,19},{17,16... | collective-permute-start | bytes 405512 | tf_op jit(solution)/shard_map/ppermute | solution.py:64
  105.5 16.6 %collective-permute-start.14 = (bf16[528,128]{1,0:T(8,128)(2,1)S(1)}, bf16[528,128]{1,0:T(8,128)(2,1)S(1)}, u32[]{:S(2)}, u32[]{:S(2)}) collective-permute-start(bf16[528,128]{1,0:T(8,128)(2,1)S(1)} %sum_four.3.here), channel_id=1, source_target_pairs={{0,2},{1,3},{2,0},{3,1},{8,10},{9,11},{10,8},{11,9},{16,18},{17,19... | collective-permute-start | bytes 405512 | tf_op jit(solution)/shard_map/ppermute | solution.py:64
  107.4 15.1 %collective-permute-start.13 = (bf16[528,128]{1,0:T(8,128)(2,1)S(1)}, bf16[528,128]{1,0:T(8,128)(2,1)S(1)}, u32[]{:S(2)}, u32[]{:S(2)}) collective-permute-start(bf16[528,128]{1,0:T(8,128)(2,1)S(1)} %sum_four.3.here), channel_id=1, source_target_pairs={{0,1},{1,2},{2,3},{3,0},{8,9},{9,10},{10,11},{11,8},{16,17},{17,18... | collective-permute-start | bytes 405512 | tf_op jit(solution)/shard_map/ppermute | solution.py:64
  122.5 13.8 %collective-permute-start.18 = (bf16[2064,128]{1,0:T(8,128)(2,1)S(1)}, bf16[2064,128]{1,0:T(8,128)(2,1)S(1)}, u32[]{:S(2)}, u32[]{:S(2)}) collective-permute-start(bf16[2064,128]{1,0:T(8,128)(2,1)S(1)} %join_four.1.refs_1_), channel_id=1, source_target_pairs={{0,96},{32,0},{64,32},{96,64},{8,104},{40,8},{72,40},{104,72},{16,... | collective-permute-start | bytes 1585160 | tf_op jit(solution)/shard_map/ppermute | solution.py:64
  124.4 11.9 %collective-permute-start.17 = (bf16[2064,128]{1,0:T(8,128)(2,1)S(1)}, bf16[2064,128]{1,0:T(8,128)(2,1)S(1)}, u32[]{:S(2)}, u32[]{:S(2)}) collective-permute-start(bf16[2064,128]{1,0:T(8,128)(2,1)S(1)} %join_four.1.refs_1_), channel_id=1, source_target_pairs={{0,64},{32,96},{64,0},{96,32},{8,72},{40,104},{72,8},{104,40},{16,... | collective-permute-start | bytes 1585160 | tf_op jit(solution)/shard_map/ppermute | solution.py:64
  125.1 14.9 %collective-permute-start.16 = (bf16[2064,128]{1,0:T(8,128)(2,1)S(1)}, bf16[2064,128]{1,0:T(8,128)(2,1)}, u32[]{:S(2)}, u32[]{:S(2)}) collective-permute-start(bf16[2064,128]{1,0:T(8,128)(2,1)S(1)} %join_four.1.refs_1_), channel_id=1, source_target_pairs={{0,32},{32,64},{64,96},{96,0},{8,40},{40,72},{72,104},{104,8},{16,... | collective-permute-start | bytes 1585160 | tf_op jit(solution)/shard_map/ppermute | solution.py:64
  140.0 6.8 %collective-permute-start.19 = (bf16[2064,128]{1,0:T(8,128)(2,1)S(1)}, bf16[2064,128]{1,0:T(8,128)(2,1)S(1)}, u32[]{:S(2)}, u32[]{:S(2)}) collective-permute-start(bf16[2064,128]{1,0:T(8,128)(2,1)S(1)} %join_four.1.refs_1_), channel_id=1, source_target_pairs={{0,4},{4,0},{1,5},{5,1},{2,6},{6,2},{3,7},{7,3},{8,12},{12,8},{9,1... | collective-permute-start | bytes 1585160 | tf_op jit(solution)/shard_map/ppermute | solution.py:38
  142.2 4.6 %collective-permute-start.20 = (bf16[2064,128]{1,0:T(8,128)(2,1)}, bf16[2064,128]{1,0:T(8,128)(2,1)S(1)}, u32[]{:S(2)}, u32[]{:S(2)}) collective-permute-start(bf16[2064,128]{1,0:T(8,128)(2,1)} %collective-permute-done.16.refs_2_), channel_id=1, source_target_pairs={{0,4},{4,0},{1,5},{5,1},{2,6},{6,2},{3,7},{7,3},{8,12},{12,8},{9,1... | collective-permute-start | bytes 1585160 | tf_op jit(solution)/shard_map/ppermute | solution.py:38
  142.2 4.6 %collective-permute-start.21 = (bf16[2064,128]{1,0:T(8,128)(2,1)S(1)}, bf16[2064,128]{1,0:T(8,128)(2,1)S(1)}, u32[]{:S(2)}, u32[]{:S(2)}) collective-permute-start(bf16[2064,128]{1,0:T(8,128)(2,1)S(1)} %collective-permute-done.17.refs_3_), channel_id=1, source_target_pairs={{0,4},{4,0},{1,5},{5,1},{2,6},{6,2},{3,7},{7,3},{8,12},{12,8},{9,1... | collective-permute-start | bytes 1585160 | tf_op jit(solution)/shard_map/ppermute | solution.py:38
  142.7 4.1 %collective-permute-start.22 = (bf16[2064,128]{1,0:T(8,128)(2,1)S(1)}, bf16[2064,128]{1,0:T(8,128)(2,1)S(1)}, u32[]{:S(2)}, u32[]{:S(2)}) collective-permute-start(bf16[2064,128]{1,0:T(8,128)(2,1)S(1)} %collective-permute-done.18.refs_4_), channel_id=1, source_target_pairs={{0,4},{4,0},{1,5},{5,1},{2,6},{6,2},{3,7},{7,3},{8,12},{12,8},{9,1... | collective-permute-start | bytes 1585160 | tf_op jit(solution)/shard_map/ppermute | solution.py:38
  (4 other events, 100.7 us)

commit v11 on v10

--- a/solution.py
+++ b/solution.py
@@ -402,7 +402,7 @@
         out_specs=[NEAR] * 4,
         out_shape=[jax.ShapeDtypeStruct((N_BLOCK + N_VEC, LANES), bf16)] * 4,
         compiler_params=params(8),
-        cost_estimate=pl.CostEstimate(flops=6 * 10**9, bytes_accessed=10**6, transcendentals=0),
+        cost_estimate=pl.CostEstimate(flops=10 * 10**9, bytes_accessed=10**6, transcendentals=0),
         name="sum_split",
     )(place, *pieces)
 
@@ -419,7 +419,7 @@
         sum_kernel,
         out_shape=jax.ShapeDtypeStruct((N_BLOCK + N_VEC, LANES), bf16),
         compiler_params=params(4),
-        cost_estimate=pl.CostEstimate(flops=6 * 10**9, bytes_accessed=10**6, transcendentals=0),
+        cost_estimate=pl.CostEstimate(flops=10 * 10**9, bytes_accessed=10**6, transcendentals=0),
         name="sum_four",
     )(*pieces)
 
@@ -435,7 +435,7 @@
         join_kernel,
         out_shape=jax.ShapeDtypeStruct((N_RING, LANES), bf16),
         compiler_params=params(4),
-        cost_estimate=pl.CostEstimate(flops=6 * 10**9, bytes_accessed=10**6, transcendentals=0),
+        cost_estimate=pl.CostEstimate(flops=10 * 10**9, bytes_accessed=10**6, transcendentals=0),
         name="join_four",
     )(*pieces)
 

time: 152 us -> 157 us (1.033)
  starting transfers between devices: 31.1 us -> 35.8 us
    all_to_all x1, waiting for transfers between devices: 0.01 us -> 9.06 us  [exchange(): return lax.all_to_all(a, PEERS, split_axis=0, concat_axis=0, tiled=True)]
    ppermute x15, waiting for transfers between devices: 32 us -> 23.3 us  [along(): return lax.ppermute(a, EVERY, pairs)]
    ppermute x8, starting transfers between devices: 6.52 us -> 13 us  [swap(): return lax.ppermute(a, 'core', [(0, 1), (1, 0)])]
    all_to_all x1, starting transfers between devices: 9.84 us -> 5.97 us  [exchange(): return lax.all_to_all(a, PEERS, split_axis=0, concat_axis=0, tiled=True)]
    ppermute x15, starting transfers between devices: 14.8 us -> 16.8 us  [along(): return lax.ppermute(a, EVERY, pairs)]
  transfers between devices with their start and end apart: 24 -> 24, of which waited for: 12 -> 13; matrix products, arithmetic and copies ran while one was open for 1% -> 1% of each run, Pallas kernels for 12% -> 11%
where the time goes in v11:
time: 157 us; the launch traced here: 155 us
  Pallas kernels  41 us (26%)
  blocking collectives  39.8 us (25%)
  starting transfers between devices  35.8 us (23%)
  waiting for transfers between devices  34.7 us (22%)
  local copies, waits for them, and re-layouts  2.12 us (1%)
    all_to_all x2, blocking collectives, exchange(): return lax.all_to_all(a, PEERS, split_axis=0, concat_axis=0, tiled=True)  39.8 us
    ppermute x15, waiting for transfers between devices, along(): return lax.ppermute(a, EVERY, pairs)  23.3 us
    ppermute x15, starting transfers between devices, along(): return lax.ppermute(a, EVERY, pairs)  16.8 us
    ppermute x8, starting transfers between devices, swap(): return lax.ppermute(a, 'core', [(0, 1), (1, 0)])  13 us
    pallas_call x1, Pallas kernels, block(): pl.pallas_call(block_kernel, in_specs=[SCALARS] + [NEAR] * 4 + [FAR] * 2...  11.2 us
    pallas_call x1, Pallas kernels, scatter_rows(): pl.pallas_call(scatter_kernel, in_specs=[SCALARS, NEAR], out_specs=NEAR,...  11 us
    all_to_all x1, waiting for transfers between devices, exchange(): return lax.all_to_all(a, PEERS, split_axis=0, concat_axis=0, tiled=True)  9.06 us
    pallas_call x1, Pallas kernels, gather_rows(): pl.pallas_call(gather_kernel, in_specs=[SCALARS, FAR], out_specs=NEAR, sc...  7.99 us
  transfers between devices with their start and end apart: 24, of which 13 were waited for; matrix products, arithmetic and copies ran while one was open for 1% of the time, Pallas kernels for 11%

profile of v11, /device:TPU:33, one launch (start us, length us, event | category | flops | bytes accessed | tf_op | source)
XLA Modules:
  0.0 154.9 jit_solution(9405918995104207389)
XLA Ops:
  4.1 18.1 %all_to_all.15 = s32[64,1,128]{2,1,0:T(1,128)} all-to-all(s32[64,1,128]{2,1,0:T(1,128)S(1)} %bitcast.53), channel_id=1, replica_groups=mesh['x'=4,'z'=4,'core'=2,'y'=4] {'x','z','y'}, dimensions={0} | all-to-all | bytes 65536 | tf_op jit(solution)/shard_map/all_to_all | solution.py:42
  22.2 8.0 %gather_rows.1 = bf16[64,64,128]{2,1,0:T(8,128)(2,1)} custom-call(s32[8192]{0:T(1024)} %bitcast.47, bf16[8192,128]{1,0:T(8,128)(2,1)} %table_ref.1), custom_call_target="tpu_custom_call" | custom-call | tf_op jit(solution)/shard_map/gather_rows/pallas_call | solution.py:113
  30.3 21.7 %all_to_all.16 = bf16[64,64,128]{2,1,0:T(8,128)(2,1)S(1)} all-to-all(bf16[64,64,128]{2,1,0:T(8,128)(2,1)} %gather_rows.1), channel_id=1, replica_groups=mesh['x'=4,'z'=4,'core'=2,'y'=4] {'x','z','y'}, dimensions={0} | all-to-all | bytes 2097152 | tf_op jit(solution)/shard_map/all_to_all | solution.py:42
  51.9 2.7 %collective-permute-start.2 = (bf16[16,4,64,128]{3,2,1,0:T(8,128)(2,1)S(1)}, bf16[16,4,64,128]{3,2,1,0:T(8,128)(2,1)}, u32[]{:S(2)}, u32[]{:S(2)}) collective-permute-start(bf16[16,4,64,128]{3,2,1,0:T(8,128)(2,1)S(1)} %bitcast.40), channel_id=1, source_target_pairs={{0,4},{4,0},{1,5},{5,1},{2,6},{6,2},{3,7},{7,3},{8,12},{12,8},{9,1... | collective-permute-start | bytes 3145736 | tf_op jit(solution)/shard_map/ppermute | solution.py:38
  55.2 1.9 %collective-permute-done.2.got_other = bf16[16,4,64,128]{3,2,1,0:T(8,128)(2,1)} collective-permute-done((bf16[16,4,64,128]{3,2,1,0:T(8,128)(2,1)S(1)}, bf16[16,4,64,128]{3,2,1,0:T(8,128)(2,1)}, u32[]{:S(2)}, u32[]{:S(2)}) %collective-permute-start.2) | collective-permute-done | bytes 1048608 | tf_op jit(solution)/shard_map/ppermute | solution.py:38
  57.0 11.2 %block.1 = (bf16[1024,512]{1,0:T(8,128)(2,1)S(1)}, bf16[1024,512]{1,0:T(8,128)(2,1)S(1)}, bf16[2064,128]{1,0:T(8,128)(2,1)S(1)}, bf16[2064,128]{1,0:T(8,128)(2,1...) custom-call(s32[5]{0:T(128)S(1)} %stack.31.place.refs_0_, s32[1024,1]{1,0:T(8,128)S(1)} %bitcast.42, ...), custom_call_target="tpu_custom_call" | custom-call | tf_op jit(solution)/shard_map/block/pallas_call | solution.py:263
  71.6 2.6 %pack.1 = bf16[16,4,64,128]{3,2,1,0:T(8,128)(2,1)} custom-call(s32[2,512]{1,0:T(2,128)S(1)} %broadcast_select_fusion.1.slot_ref, bf16[1024,512]{1,0:T(8,128)(2,1)S(1)} %get-tuple-element.37.part_ref, bf16[1024,512]{1,0:T(8,128)(2,1)S(1)} %collective-permute-done.3.other_ref, bf16[1024,512]{1,0:T(8,128)(2,1)S(1)} %get-tuple-element.38.emb_ref, ...), custom_call_target="tpu_custom_call" | custom-call | flops 2000000000 | bytes 10000000 | tf_op jit(solution)/shard_map/pack/pallas_call | solution.py:311
  74.2 9.8 %collective-permute-done.4.back_1 = bf16[2064,128]{1,0:T(8,128)(2,1)S(1)} collective-permute-done((bf16[2064,128]{1,0:T(8,128)(2,1)S(1)}, bf16[2064,128]{1,0:T(8,128)(2,1)S(1)}, u32[]{:S(2)}, u32[]{:S(2)}) %collective-permute-start.4) | collective-permute-done | bytes 528416 | tf_op jit(solution)/shard_map/ppermute | solution.py:64
  85.5 3.1 %collective-permute-start.8 = (bf16[528,128]{1,0:T(8,128)(2,1)S(1)}, bf16[528,128]{1,0:T(8,128)(2,1)S(1)}, u32[]{:S(2)}, u32[]{:S(2)}) collective-permute-start(bf16[528,128]{1,0:T(8,128)(2,1)S(1)} %get-tuple-element.46), channel_id=1, source_target_pairs={{0,2},{1,3},{2,0},{3,1},{8,10},{9,11},{10,8},{11,9},{16,18},{17,19... | collective-permute-start | bytes 405512 | tf_op jit(solution)/shard_map/ppermute | solution.py:64
  89.3 2.1 %collective-permute-done.8.back_2 = bf16[528,128]{1,0:T(8,128)(2,1)S(1)} collective-permute-done((bf16[528,128]{1,0:T(8,128)(2,1)S(1)}, bf16[528,128]{1,0:T(8,128)(2,1)S(1)}, u32[]{:S(2)}, u32[]{:S(2)}) %collective-permute-start.8) | collective-permute-done | bytes 135200 | tf_op jit(solution)/shard_map/ppermute | solution.py:64
  91.4 1.4 collective-permute-done.9.back_3
  95.0 1.9 %collective-permute-done.12.back_3 = bf16[528,128]{1,0:T(8,128)(2,1)S(1)} collective-permute-done((bf16[528,128]{1,0:T(8,128)(2,1)S(1)}, bf16[528,128]{1,0:T(8,128)(2,1)S(1)}, u32[]{:S(2)}, u32[]{:S(2)}) %collective-permute-start.12) | collective-permute-done | bytes 135200 | tf_op jit(solution)/shard_map/ppermute | solution.py:64
  96.9 2.5 %collective-permute-done.11.back_2 = bf16[528,128]{1,0:T(8,128)(2,1)S(1)} collective-permute-done((bf16[528,128]{1,0:T(8,128)(2,1)S(1)}, bf16[528,128]{1,0:T(8,128)(2,1)S(1)}, u32[]{:S(2)}, u32[]{:S(2)}) %collective-permute-start.11) | collective-permute-done | bytes 135200 | tf_op jit(solution)/shard_map/ppermute | solution.py:64
  100.8 1.6 %collective-permute-start.15 = (bf16[528,128]{1,0:T(8,128)(2,1)S(1)}, bf16[528,128]{1,0:T(8,128)(2,1)S(1)}, u32[]{:S(2)}, u32[]{:S(2)}) collective-permute-start(bf16[528,128]{1,0:T(8,128)(2,1)S(1)} %sum_four.3.here), channel_id=1, source_target_pairs={{0,3},{1,0},{2,1},{3,2},{8,11},{9,8},{10,9},{11,10},{16,19},{17,16... | collective-permute-start | bytes 405512 | tf_op jit(solution)/shard_map/ppermute | solution.py:64
  102.4 1.5 collective-permute-start.14
  104.0 2.0 %collective-permute-start.13 = (bf16[528,128]{1,0:T(8,128)(2,1)S(1)}, bf16[528,128]{1,0:T(8,128)(2,1)S(1)}, u32[]{:S(2)}, u32[]{:S(2)}) collective-permute-start(bf16[528,128]{1,0:T(8,128)(2,1)S(1)} %sum_four.3.here), channel_id=1, source_target_pairs={{0,1},{1,2},{2,3},{3,0},{8,9},{9,10},{10,11},{11,8},{16,17},{17,18... | collective-permute-start | bytes 405512 | tf_op jit(solution)/shard_map/ppermute | solution.py:64
  105.9 6.0 %all-to-all-start.2 = ((bf16[64,64,128]{2,1,0:T(8,128)(2,1)}), bf16[64,64,128]{2,1,0:T(8,128)(2,1)S(1)}, u32[]{:S(2)}, u32[]{:S(2)}) async-start(bf16[64,64,128]{2,1,0:T(8,128)(2,1)} %bitcast.16), calls=%async_computation.2 | async-start | bytes 2097152 | tf_op jit(solution)/shard_map/all_to_all | solution.py:42
  112.0 2.5 %collective-permute-start.18 = (bf16[2064,128]{1,0:T(8,128)(2,1)S(1)}, bf16[2064,128]{1,0:T(8,128)(2,1)S(1)}, u32[]{:S(2)}, u32[]{:S(2)}) collective-permute-start(bf16[2064,128]{1,0:T(8,128)(2,1)S(1)} %join_four.1.refs_1_), channel_id=1, source_target_pairs={{0,96},{32,0},{64,32},{96,64},{8,104},{40,8},{72,40},{104,72},{16,... | collective-permute-start | bytes 1585160 | tf_op jit(solution)/shard_map/ppermute | solution.py:64
  115.6 9.1 %all-to-all-done.2.arrived_ref = bf16[64,64,128]{2,1,0:T(8,128)(2,1)S(1)} async-done(((bf16[64,64,128]{2,1,0:T(8,128)(2,1)}), bf16[64,64,128]{2,1,0:T(8,128)(2,1)S(1)}, u32[]{:S(2)}, u32[]{:S(2)}) %all-to-all-start.2) | async-done | bytes 1048608 | tf_op jit(solution)/shard_map/all_to_all | solution.py:42
  124.7 11.0 %scatter_rows.1 = f32[8192,128]{1,0:T(8,128)} custom-call(s32[8192]{0:T(1024)S(1)} %bitcast.48, bf16[64,64,128]{2,1,0:T(8,128)(2,1)S(1)} %all-to-all-done.2.arrived_ref), custom_call_target="tpu_custom_call" | custom-call | flops 10000000000 | bytes 10000000 | tf_op jit(solution)/shard_map/scatter_rows/pallas_call | solution.py:367
  135.6 2.8 %collective-permute-done.16.refs_2_ = bf16[2064,128]{1,0:T(8,128)(2,1)} collective-permute-done((bf16[2064,128]{1,0:T(8,128)(2,1)S(1)}, bf16[2064,128]{1,0:T(8,128)(2,1)}, u32[]{:S(2)}, u32[]{:S(2)}) %collective-permute-start.16) | collective-permute-done | bytes 528416 | tf_op jit(solution)/shard_map/ppermute | solution.py:64
  138.5 8.6 %collective-permute-start.19 = (bf16[2064,128]{1,0:T(8,128)(2,1)S(1)}, bf16[2064,128]{1,0:T(8,128)(2,1)S(1)}, u32[]{:S(2)}, u32[]{:S(2)}) collective-permute-start(bf16[2064,128]{1,0:T(8,128)(2,1)S(1)} %join_four.1.refs_1_), channel_id=1, source_target_pairs={{0,4},{4,0},{1,5},{5,1},{2,6},{6,2},{3,7},{7,3},{8,12},{12,8},{9,1... | collective-permute-start | bytes 1585160 | tf_op jit(solution)/shard_map/ppermute | solution.py:38
  147.7 4.1 %finish_own.1 = (f32[2048,512]{1,0:T(8,128)}, f32[512,2048]{1,0:T(8,128)}, f32[16,128]{1,0:T(8,128)S(1)}) custom-call(s32[5]{0:T(128)S(1)} %stack.31.place.refs_0_, bf16[2064,128]{1,0:T(8,128)(2,1)S(1)} %join_four.1.refs_1_, bf16[2064,128]{1,0:T(8,128)(2,1)} %collective-permute-done.16.refs_2_, bf16[2064,128]{1,0:T(8,128)(2,1)S(1)} %collective-permute-done.17.refs_3_, ...), custom_call_target="tpu_custom_call" | custom-call | flops 6000000000 | bytes 10000000 | tf_op jit(solution)/shard_map/finish_own/pallas_call | solution.py:499
  151.8 3.1 %finish_other.1 = (f32[2048,512]{1,0:T(8,128)}, f32[512,2048]{1,0:T(8,128)}, f32[16,128]{1,0:T(8,128)}, f32[4,128]{1,0:T(4,128)}) custom-call(s32[5]{0:T(128)S(1)} %stack.31.place.refs_0_, bf16[2064,128]{1,0:T(8,128)(2,1)S(1)} %collective-permute-done.19.refs_1_, ...), custom_call_target="tpu_custom_call", output_to_operand_aliasing={{0}: (6, {}), {1}: (7, {})} | custom-call | tf_op jit(solution)/shard_map/finish_other/pallas_call | solution.py:512
  (61 shorter events, 15.0 us)
Async XLA Ops:
  1.3 1.5 collective-permute-start
  2.0 2.1 %collective-permute-start.1 = (bf16[512,512]{1,0:T(8,128)(2,1)}, bf16[512,512]{1,0:T(8,128)(2,1)S(1)}, u32[]{:S(2)}, u32[]{:S(2)}) collective-permute-start(bf16[512,512]{1,0:T(8,128)(2,1)} %bitcast.44), channel_id=1, source_target_pairs={{0,4},{4,0},{1,5},{5,1},{2,6},{6,2},{3,7},{7,3},{8,12},{12,8},{9,1... | collective-permute-start | bytes 1572872 | tf_op jit(solution)/shard_map/ppermute | solution.py:38
  51.9 5.1 %collective-permute-start.2 = (bf16[16,4,64,128]{3,2,1,0:T(8,128)(2,1)S(1)}, bf16[16,4,64,128]{3,2,1,0:T(8,128)(2,1)}, u32[]{:S(2)}, u32[]{:S(2)}) collective-permute-start(bf16[16,4,64,128]{3,2,1,0:T(8,128)(2,1)S(1)} %bitcast.40), channel_id=1, source_target_pairs={{0,4},{4,0},{1,5},{5,1},{2,6},{6,2},{3,7},{7,3},{8,12},{12,8},{9,1... | collective-permute-start | bytes 3145736 | tf_op jit(solution)/shard_map/ppermute | solution.py:38
  68.2 3.3 %collective-permute-start.3 = (bf16[1024,512]{1,0:T(8,128)(2,1)S(1)}, bf16[1024,512]{1,0:T(8,128)(2,1)S(1)}, u32[]{:S(2)}, u32[]{:S(2)}) collective-permute-start(bf16[1024,512]{1,0:T(8,128)(2,1)S(1)} %get-tuple-element.37.part_ref), channel_id=1, source_target_pairs={{0,4},{4,0},{1,5},{5,1},{2,6},{6,2},{3,7},{7,3},{8,12},{12,8},{9,1... | collective-permute-start | bytes 3145736 | tf_op jit(solution)/shard_map/ppermute | solution.py:38
  68.7 15.2 %collective-permute-start.4 = (bf16[2064,128]{1,0:T(8,128)(2,1)S(1)}, bf16[2064,128]{1,0:T(8,128)(2,1)S(1)}, u32[]{:S(2)}, u32[]{:S(2)}) collective-permute-start(bf16[2064,128]{1,0:T(8,128)(2,1)S(1)} %get-tuple-element.41), channel_id=1, source_target_pairs={{0,32},{32,64},{64,96},{96,0},{8,40},{40,72},{72,104},{104,8},{16,... | collective-permute-start | bytes 1585160 | tf_op jit(solution)/shard_map/ppermute | solution.py:64
  69.2 14.8 %collective-permute-start.5 = (bf16[2064,128]{1,0:T(8,128)(2,1)S(1)}, bf16[2064,128]{1,0:T(8,128)(2,1)S(1)}, u32[]{:S(2)}, u32[]{:S(2)}) collective-permute-start(bf16[2064,128]{1,0:T(8,128)(2,1)S(1)} %get-tuple-element.42), channel_id=1, source_target_pairs={{0,64},{32,96},{64,0},{96,32},{8,72},{40,104},{72,8},{104,40},{16,... | collective-permute-start | bytes 1585160 | tf_op jit(solution)/shard_map/ppermute | solution.py:64
  70.3 14.2 %collective-permute-start.6 = (bf16[2064,128]{1,0:T(8,128)(2,1)S(1)}, bf16[2064,128]{1,0:T(8,128)(2,1)S(1)}, u32[]{:S(2)}, u32[]{:S(2)}) collective-permute-start(bf16[2064,128]{1,0:T(8,128)(2,1)S(1)} %get-tuple-element.43), channel_id=1, source_target_pairs={{0,96},{32,0},{64,32},{96,64},{8,104},{40,8},{72,40},{104,72},{16,... | collective-permute-start | bytes 1585160 | tf_op jit(solution)/shard_map/ppermute | solution.py:64
  85.4 3.9 %collective-permute-start.7 = (bf16[528,128]{1,0:T(8,128)(2,1)S(1)}, bf16[528,128]{1,0:T(8,128)(2,1)S(1)}, u32[]{:S(2)}, u32[]{:S(2)}) collective-permute-start(bf16[528,128]{1,0:T(8,128)(2,1)S(1)} %get-tuple-element.45), channel_id=1, source_target_pairs={{0,1},{1,2},{2,3},{3,0},{8,9},{9,10},{10,11},{11,8},{16,17},{17,18... | collective-permute-start | bytes 405512 | tf_op jit(solution)/shard_map/ppermute | solution.py:64
  85.5 6.0 %collective-permute-start.8 = (bf16[528,128]{1,0:T(8,128)(2,1)S(1)}, bf16[528,128]{1,0:T(8,128)(2,1)S(1)}, u32[]{:S(2)}, u32[]{:S(2)}) collective-permute-start(bf16[528,128]{1,0:T(8,128)(2,1)S(1)} %get-tuple-element.46), channel_id=1, source_target_pairs={{0,2},{1,3},{2,0},{3,1},{8,10},{9,11},{10,8},{11,9},{16,18},{17,19... | collective-permute-start | bytes 405512 | tf_op jit(solution)/shard_map/ppermute | solution.py:64
  88.6 4.3 %collective-permute-start.9 = (bf16[528,128]{1,0:T(8,128)(2,1)S(1)}, bf16[528,128]{1,0:T(8,128)(2,1)S(1)}, u32[]{:S(2)}, u32[]{:S(2)}) collective-permute-start(bf16[528,128]{1,0:T(8,128)(2,1)S(1)} %get-tuple-element.47), channel_id=1, source_target_pairs={{0,3},{1,0},{2,1},{3,2},{8,11},{9,8},{10,9},{11,10},{16,19},{17,16... | collective-permute-start | bytes 405512 | tf_op jit(solution)/shard_map/ppermute | solution.py:64
  93.0 3.9 %collective-permute-start.12 = (bf16[528,128]{1,0:T(8,128)(2,1)S(1)}, bf16[528,128]{1,0:T(8,128)(2,1)S(1)}, u32[]{:S(2)}, u32[]{:S(2)}) collective-permute-start(bf16[528,128]{1,0:T(8,128)(2,1)S(1)} %sum_four.2.here), channel_id=1, source_target_pairs={{0,24},{8,0},{16,8},{24,16},{1,25},{9,1},{17,9},{25,17},{2,26},{10... | collective-permute-start | bytes 405512 | tf_op jit(solution)/shard_map/ppermute | solution.py:64
  93.9 5.5 %collective-permute-start.11 = (bf16[528,128]{1,0:T(8,128)(2,1)S(1)}, bf16[528,128]{1,0:T(8,128)(2,1)S(1)}, u32[]{:S(2)}, u32[]{:S(2)}) collective-permute-start(bf16[528,128]{1,0:T(8,128)(2,1)S(1)} %sum_four.2.here), channel_id=1, source_target_pairs={{0,16},{8,24},{16,0},{24,8},{1,17},{9,25},{17,1},{25,9},{2,18},{10... | collective-permute-start | bytes 405512 | tf_op jit(solution)/shard_map/ppermute | solution.py:64
  94.8 5.9 %collective-permute-start.10 = (bf16[528,128]{1,0:T(8,128)(2,1)S(1)}, bf16[528,128]{1,0:T(8,128)(2,1)S(1)}, u32[]{:S(2)}, u32[]{:S(2)}) collective-permute-start(bf16[528,128]{1,0:T(8,128)(2,1)S(1)} %sum_four.2.here), channel_id=1, source_target_pairs={{0,8},{8,16},{16,24},{24,0},{1,9},{9,17},{17,25},{25,1},{2,10},{10... | collective-permute-start | bytes 405512 | tf_op jit(solution)/shard_map/ppermute | solution.py:64
  100.8 11.1 %collective-permute-start.15 = (bf16[528,128]{1,0:T(8,128)(2,1)S(1)}, bf16[528,128]{1,0:T(8,128)(2,1)S(1)}, u32[]{:S(2)}, u32[]{:S(2)}) collective-permute-start(bf16[528,128]{1,0:T(8,128)(2,1)S(1)} %sum_four.3.here), channel_id=1, source_target_pairs={{0,3},{1,0},{2,1},{3,2},{8,11},{9,8},{10,9},{11,10},{16,19},{17,16... | collective-permute-start | bytes 405512 | tf_op jit(solution)/shard_map/ppermute | solution.py:64
  102.4 9.5 %collective-permute-start.14 = (bf16[528,128]{1,0:T(8,128)(2,1)S(1)}, bf16[528,128]{1,0:T(8,128)(2,1)S(1)}, u32[]{:S(2)}, u32[]{:S(2)}) collective-permute-start(bf16[528,128]{1,0:T(8,128)(2,1)S(1)} %sum_four.3.here), channel_id=1, source_target_pairs={{0,2},{1,3},{2,0},{3,1},{8,10},{9,11},{10,8},{11,9},{16,18},{17,19... | collective-permute-start | bytes 405512 | tf_op jit(solution)/shard_map/ppermute | solution.py:64
  104.0 8.0 %collective-permute-start.13 = (bf16[528,128]{1,0:T(8,128)(2,1)S(1)}, bf16[528,128]{1,0:T(8,128)(2,1)S(1)}, u32[]{:S(2)}, u32[]{:S(2)}) collective-permute-start(bf16[528,128]{1,0:T(8,128)(2,1)S(1)} %sum_four.3.here), channel_id=1, source_target_pairs={{0,1},{1,2},{2,3},{3,0},{8,9},{9,10},{10,11},{11,8},{16,17},{17,18... | collective-permute-start | bytes 405512 | tf_op jit(solution)/shard_map/ppermute | solution.py:64
  105.9 18.7 %all-to-all-start.2 = ((bf16[64,64,128]{2,1,0:T(8,128)(2,1)}), bf16[64,64,128]{2,1,0:T(8,128)(2,1)S(1)}, u32[]{:S(2)}, u32[]{:S(2)}) async-start(bf16[64,64,128]{2,1,0:T(8,128)(2,1)} %bitcast.16), calls=%async_computation.2 | async-start | bytes 2097152 | tf_op jit(solution)/shard_map/all_to_all | solution.py:42
  112.0 23.6 %collective-permute-start.18 = (bf16[2064,128]{1,0:T(8,128)(2,1)S(1)}, bf16[2064,128]{1,0:T(8,128)(2,1)S(1)}, u32[]{:S(2)}, u32[]{:S(2)}) collective-permute-start(bf16[2064,128]{1,0:T(8,128)(2,1)S(1)} %join_four.1.refs_1_), channel_id=1, source_target_pairs={{0,96},{32,0},{64,32},{96,64},{8,104},{40,8},{72,40},{104,72},{16,... | collective-permute-start | bytes 1585160 | tf_op jit(solution)/shard_map/ppermute | solution.py:64
  114.5 21.2 %collective-permute-start.17 = (bf16[2064,128]{1,0:T(8,128)(2,1)S(1)}, bf16[2064,128]{1,0:T(8,128)(2,1)S(1)}, u32[]{:S(2)}, u32[]{:S(2)}) collective-permute-start(bf16[2064,128]{1,0:T(8,128)(2,1)S(1)} %join_four.1.refs_1_), channel_id=1, source_target_pairs={{0,64},{32,96},{64,0},{96,32},{8,72},{40,104},{72,8},{104,40},{16,... | collective-permute-start | bytes 1585160 | tf_op jit(solution)/shard_map/ppermute | solution.py:64
  115.0 23.4 %collective-permute-start.16 = (bf16[2064,128]{1,0:T(8,128)(2,1)S(1)}, bf16[2064,128]{1,0:T(8,128)(2,1)}, u32[]{:S(2)}, u32[]{:S(2)}) collective-permute-start(bf16[2064,128]{1,0:T(8,128)(2,1)S(1)} %join_four.1.refs_1_), channel_id=1, source_target_pairs={{0,32},{32,64},{64,96},{96,0},{8,40},{40,72},{72,104},{104,8},{16,... | collective-permute-start | bytes 1585160 | tf_op jit(solution)/shard_map/ppermute | solution.py:64
  138.5 13.3 %collective-permute-start.19 = (bf16[2064,128]{1,0:T(8,128)(2,1)S(1)}, bf16[2064,128]{1,0:T(8,128)(2,1)S(1)}, u32[]{:S(2)}, u32[]{:S(2)}) collective-permute-start(bf16[2064,128]{1,0:T(8,128)(2,1)S(1)} %join_four.1.refs_1_), channel_id=1, source_target_pairs={{0,4},{4,0},{1,5},{5,1},{2,6},{6,2},{3,7},{7,3},{8,12},{12,8},{9,1... | collective-permute-start | bytes 1585160 | tf_op jit(solution)/shard_map/ppermute | solution.py:38
  147.1 4.7 %collective-permute-start.20 = (bf16[2064,128]{1,0:T(8,128)(2,1)}, bf16[2064,128]{1,0:T(8,128)(2,1)S(1)}, u32[]{:S(2)}, u32[]{:S(2)}) collective-permute-start(bf16[2064,128]{1,0:T(8,128)(2,1)} %collective-permute-done.16.refs_2_), channel_id=1, source_target_pairs={{0,4},{4,0},{1,5},{5,1},{2,6},{6,2},{3,7},{7,3},{8,12},{12,8},{9,1... | collective-permute-start | bytes 1585160 | tf_op jit(solution)/shard_map/ppermute | solution.py:38
  147.1 4.6 %collective-permute-start.21 = (bf16[2064,128]{1,0:T(8,128)(2,1)S(1)}, bf16[2064,128]{1,0:T(8,128)(2,1)S(1)}, u32[]{:S(2)}, u32[]{:S(2)}) collective-permute-start(bf16[2064,128]{1,0:T(8,128)(2,1)S(1)} %collective-permute-done.17.refs_3_), channel_id=1, source_target_pairs={{0,4},{4,0},{1,5},{5,1},{2,6},{6,2},{3,7},{7,3},{8,12},{12,8},{9,1... | collective-permute-start | bytes 1585160 | tf_op jit(solution)/shard_map/ppermute | solution.py:38
  147.6 4.2 %collective-permute-start.22 = (bf16[2064,128]{1,0:T(8,128)(2,1)S(1)}, bf16[2064,128]{1,0:T(8,128)(2,1)S(1)}, u32[]{:S(2)}, u32[]{:S(2)}) collective-permute-start(bf16[2064,128]{1,0:T(8,128)(2,1)S(1)} %collective-permute-done.18.refs_4_), channel_id=1, source_target_pairs={{0,4},{4,0},{1,5},{5,1},{2,6},{6,2},{3,7},{7,3},{8,12},{12,8},{9,1... | collective-permute-start | bytes 1585160 | tf_op jit(solution)/shard_map/ppermute | solution.py:38
  (4 other events, 93.1 us)

commit v12 on v10

--- a/solution.py
+++ b/solution.py
@@ -440,11 +440,11 @@
     )(*pieces)
 
 
-def write_pieces(scale, place, a_at, b_at, pieces, out_ref, in_ref, vec_s):
-    for s in range(4):
-
-        @pl.when(pl.program_id(0) == s)
-        def _(ref=pieces[s], s=s):
+def write_pieces(scale, place, a_at, b_at, shifts, pieces, out_ref, in_ref, vec_s):
+    for step, s in enumerate(shifts):
+
+        @pl.when(pl.program_id(0) == step)
+        def _(ref=pieces[step], s=s):
             a = lax.rem(place[a_at] + (4 - s), 4)
             for j in range(4):
                 b = lax.rem(place[b_at] + (4 - j), 4)
@@ -465,13 +465,24 @@
                 vec_s[pl.ds(a * 3 + r, 1), :] = vec[r : r + 1, :]
 
 
+def finish_first_kernel(scale, place, piece, out_ref, in_ref, vec_ref):
+    vec_ref[...] = jnp.zeros_like(vec_ref)
+    write_pieces(scale, place, 1, 2, (0,), [piece], out_ref, in_ref, vec_ref)
+
+
 def finish_own_kernel(scale, place, *refs):
-    write_pieces(scale, place, 1, 2, refs[:4], *refs[4:])
+    vec_before, out_ref, in_ref, vec_ref = refs[3:4] + refs[6:]
+
+    @pl.when(pl.program_id(0) == 0)
+    def _():
+        vec_ref[...] = vec_before[...]
+
+    write_pieces(scale, place, 1, 2, (1, 2, 3), refs[:3], out_ref, in_ref, vec_ref)
 
 
 def finish_other_kernel(scale, place, *refs):
     own_vec, out_ref, in_ref, bias_ref, gain_ref, vec_s = refs[4:5] + refs[7:]
-    write_pieces(scale, place, 3, 4, refs[:4], out_ref, in_ref, vec_s)
+    write_pieces(scale, place, 3, 4, (0, 1, 2, 3), refs[:4], out_ref, in_ref, vec_s)
 
     @pl.when(pl.program_id(0) == 3)
     def _():
@@ -480,50 +491,45 @@
         gain_ref[...] = own_vec[8:12, :] + vec_s[8:12, :]
 
 
-def finish(place, own, other, scale):
-    results = [
-        jax.ShapeDtypeStruct((2 * HALF, D), f32),
-        jax.ShapeDtypeStruct((D, 2 * HALF), f32),
-    ]
-    piece_specs = [whole((N_RING, LANES))] * 4
-
-    def blocks(half_of, a_at):
-        def row_of(s, c):
-            return lax.rem(c[a_at] + 4 - s, 4)
-
-        return [
-            pl.BlockSpec((256, D), lambda s, c: (half_of(c) * 4 + row_of(s, c), 0)),
-            pl.BlockSpec((128, HALF), lambda s, c: (row_of(s, c), half_of(c))),
-        ]
-
-    g_out, g_in, vec = pl.pallas_call(
-        lambda *refs: finish_own_kernel(scale, *refs),
+RESULTS = [
+    jax.ShapeDtypeStruct((2 * HALF, D), f32),
+    jax.ShapeDtypeStruct((D, 2 * HALF), f32),
+]
+VECTORS = [jax.ShapeDtypeStruct((16, LANES), f32), jax.ShapeDtypeStruct((4, LANES), f32)]
+
+
+def finish_part(kernel, name, scale, place, half_of, a_at, first, pieces, before, n_vectors, scratch):
+    n = len(pieces)
+
+    def row_of(s, c):
+        return lax.rem(c[a_at] + 4 - first - s, 4)
+
+    in_specs = [whole((N_RING, LANES))] * n
+    aliases = {}
+    if before:
+        in_specs += [whole((16, LANES))] + [pl.BlockSpec(memory_space=pl.ANY)] * 2
+        aliases = {n + 2: 0, n + 3: 1}
+    return pl.pallas_call(
+        lambda *refs: kernel(scale, *refs),
         grid_spec=pltpu.PrefetchScalarGridSpec(
             num_scalar_prefetch=1,
-            grid=(4,),
-            in_specs=piece_specs,
-            out_specs=blocks(lambda c: c[0], 1) + [whole((16, LANES))],
+            grid=(n,),
+            in_specs=in_specs,
+            out_specs=[
+                pl.BlockSpec((256, D), lambda s, c: (half_of(c) * 4 + row_of(s, c), 0)),
+                pl.BlockSpec((128, HALF), lambda s, c: (row_of(s, c), half_of(c))),
+            ]
+            + [whole(v.shape) for v in VECTORS[:n_vectors]],
+            scratch_shapes=scratch,
         ),
-        out_shape=results + [jax.ShapeDtypeStruct((16, LANES), f32)],
+        out_shape=RESULTS + VECTORS[:n_vectors],
+        input_output_aliases=aliases,
         compiler_params=params(12),
-        cost_estimate=pl.CostEstimate(flops=6 * 10**9, bytes_accessed=10**7, transcendentals=0),
-        name="finish_own",
-    )(place, *own)
-    return pl.pallas_call(
-        lambda *refs: finish_other_kernel(scale, *refs),
-        grid_spec=pltpu.PrefetchScalarGridSpec(
-            num_scalar_prefetch=1,
-            grid=(4,),
-            in_specs=piece_specs + [whole((16, LANES))] + [pl.BlockSpec(memory_space=pl.ANY)] * 2,
-            out_specs=blocks(lambda c: 1 - c[0], 3) + [whole((16, LANES)), whole((4, LANES))],
-            scratch_shapes=[pltpu.VMEM((16, LANES), f32)],
+        cost_estimate=pl.CostEstimate(
+            flops=n * 15 * 10**8, bytes_accessed=n * 10**6, transcendentals=0
         ),
-        out_shape=results
-        + [jax.ShapeDtypeStruct((16, LANES), f32), jax.ShapeDtypeStruct((4, LANES), f32)],
-        input_output_aliases={6: 0, 7: 1},
-        compiler_params=params(12),
-        name="finish_other",
-    )(place, *other, vec, g_out, g_in)
+        name=name,
+    )(place, *pieces, *before)
 
 
 def local(table, item_ids, cotangent, norm_gain, w_in, bias_in, w_out):
@@ -593,10 +599,31 @@
     joined = join_four([total] + [along(1, total, s) for s in (1, 2, 3)])
     pieces = [joined] + [along(0, joined, s) for s in (1, 2, 3)]
     table_grad = scatter_rows(asked, arrived)
-    *late, table_grad = lax.optimization_barrier((*pieces, table_grad))
-    others = [swap(p) for p in late]
     scale = 1.0 / math.sqrt(TOK * N_PEERS * N_CORE)
-    g_out, g_in, g_bias, g_gain = finish(place, late, others, scale)
+    other_first = swap(joined)
+    g_out, g_in, vec = finish_part(
+        finish_first_kernel, "finish_first", scale, place, lambda c: c[0], 1, 0, [joined], (), 1, []
+    )
+    *late, table_grad, g_out, g_in, vec = lax.optimization_barrier(
+        (*pieces[1:], table_grad, g_out, g_in, vec)
+    )
+    others = [other_first] + [swap(p) for p in late]
+    g_out, g_in, vec = finish_part(
+        finish_own_kernel, "finish_own", scale, place, lambda c: c[0], 1, 1, late, (vec, g_out, g_in), 1, []
+    )
+    g_out, g_in, g_bias, g_gain = finish_part(
+        finish_other_kernel,
+        "finish_other",
+        scale,
+        place,
+        lambda c: 1 - c[0],
+        3,
+        0,
+        others,
+        (vec, g_out, g_in),
+        2,
+        [pltpu.VMEM((16, LANES), f32)],
+    )
     return (table_grad, g_in, g_bias.reshape(-1), g_out, g_gain.reshape(-1))
 
 

time: 152 us -> 151 us (level)
  waiting for transfers between devices: 34.3 us -> 31.4 us
    ppermute x15, waiting for transfers between devices: 32 us -> 29.1 us  [along(): return lax.ppermute(a, EVERY, pairs)]
    ppermute x15, starting transfers between devices: 14.8 us -> 16.7 us  [along(): return lax.ppermute(a, EVERY, pairs)]
    pallas_call x2 -> x3, Pallas kernels: 7.21 us -> 8.61 us  [finish_part(): pl.pallas_call(lambda *refs: kernel(scale, *refs), grid_spec=pltpu.Prefet...]
  transfers between devices with their start and end apart: 24 -> 24, of which waited for: 12 -> 11; matrix products, arithmetic and copies ran while one was open for 1% -> 1% of each run, Pallas kernels for 12% -> 13%
where the time goes in v12:
time: 151 us; the launch traced here: 149 us
  Pallas kernels  42.4 us (28%)
  blocking collectives  39.5 us (26%)
  starting transfers between devices  32.1 us (21%)
  waiting for transfers between devices  31.4 us (21%)
  local copies, waits for them, and re-layouts  2.12 us (1%)
    all_to_all x2, blocking collectives, exchange(): return lax.all_to_all(a, PEERS, split_axis=0, concat_axis=0, tiled=True)  39.5 us
    ppermute x15, waiting for transfers between devices, along(): return lax.ppermute(a, EVERY, pairs)  29.1 us
    ppermute x15, starting transfers between devices, along(): return lax.ppermute(a, EVERY, pairs)  16.7 us
    pallas_call x1, Pallas kernels, block(): pl.pallas_call(block_kernel, in_specs=[SCALARS] + [NEAR] * 4 + [FAR] * 2...  11.2 us
    pallas_call x1, Pallas kernels, scatter_rows(): pl.pallas_call(scatter_kernel, in_specs=[SCALARS, NEAR], out_specs=NEAR,...  11 us
    all_to_all x1, starting transfers between devices, exchange(): return lax.all_to_all(a, PEERS, split_axis=0, concat_axis=0, tiled=True)  8.74 us
    pallas_call x3, Pallas kernels, finish_part(): pl.pallas_call(lambda *refs: kernel(scale, *refs), grid_spec=pltpu.Prefet...  8.61 us
    pallas_call x1, Pallas kernels, gather_rows(): pl.pallas_call(gather_kernel, in_specs=[SCALARS, FAR], out_specs=NEAR, sc...  7.99 us
  transfers between devices with their start and end apart: 24, of which 11 were waited for; matrix products, arithmetic and copies ran while one was open for 1% of the time, Pallas kernels for 13%

profile of v12, /device:TPU:33, one launch (start us, length us, event | category | flops | bytes accessed | tf_op | source)
XLA Modules:
  0.0 149.2 jit_solution(9346490483274092785)
XLA Ops:
  4.1 18.3 %all_to_all.15 = s32[64,1,128]{2,1,0:T(1,128)} all-to-all(s32[64,1,128]{2,1,0:T(1,128)S(1)} %bitcast.53), channel_id=1, replica_groups=mesh['x'=4,'z'=4,'core'=2,'y'=4] {'x','z','y'}, dimensions={0} | all-to-all | bytes 65536 | tf_op jit(solution)/shard_map/all_to_all | solution.py:42
  22.4 8.0 %gather_rows.1 = bf16[64,64,128]{2,1,0:T(8,128)(2,1)} custom-call(s32[8192]{0:T(1024)} %bitcast.47, bf16[8192,128]{1,0:T(8,128)(2,1)} %table_ref.1), custom_call_target="tpu_custom_call" | custom-call | tf_op jit(solution)/shard_map/gather_rows/pallas_call | solution.py:113
  30.4 21.2 %all_to_all.16 = bf16[64,64,128]{2,1,0:T(8,128)(2,1)S(1)} all-to-all(bf16[64,64,128]{2,1,0:T(8,128)(2,1)} %gather_rows.1), channel_id=1, replica_groups=mesh['x'=4,'z'=4,'core'=2,'y'=4] {'x','z','y'}, dimensions={0} | all-to-all | bytes 2097152 | tf_op jit(solution)/shard_map/all_to_all | solution.py:42
  51.6 2.8 %collective-permute-start.2 = (bf16[16,4,64,128]{3,2,1,0:T(8,128)(2,1)S(1)}, bf16[16,4,64,128]{3,2,1,0:T(8,128)(2,1)}, u32[]{:S(2)}, u32[]{:S(2)}) collective-permute-start(bf16[16,4,64,128]{3,2,1,0:T(8,128)(2,1)S(1)} %bitcast.40), channel_id=1, source_target_pairs={{0,4},{4,0},{1,5},{5,1},{2,6},{6,2},{3,7},{7,3},{8,12},{12,8},{9,1... | collective-permute-start | bytes 3145736 | tf_op jit(solution)/shard_map/ppermute | solution.py:38
  55.0 1.9 %collective-permute-done.2.got_other = bf16[16,4,64,128]{3,2,1,0:T(8,128)(2,1)} collective-permute-done((bf16[16,4,64,128]{3,2,1,0:T(8,128)(2,1)S(1)}, bf16[16,4,64,128]{3,2,1,0:T(8,128)(2,1)}, u32[]{:S(2)}, u32[]{:S(2)}) %collective-permute-start.2) | collective-permute-done | bytes 1048608 | tf_op jit(solution)/shard_map/ppermute | solution.py:38
  56.9 11.2 %block.1 = (bf16[1024,512]{1,0:T(8,128)(2,1)S(1)}, bf16[1024,512]{1,0:T(8,128)(2,1)S(1)}, bf16[2064,128]{1,0:T(8,128)(2,1)S(1)}, bf16[2064,128]{1,0:T(8,128)(2,1...) custom-call(s32[5]{0:T(128)S(1)} %stack.31.place.refs_0_, s32[1024,1]{1,0:T(8,128)S(1)} %bitcast.42, ...), custom_call_target="tpu_custom_call" | custom-call | tf_op jit(solution)/shard_map/block/pallas_call | solution.py:263
  71.4 2.6 %pack.1 = bf16[16,4,64,128]{3,2,1,0:T(8,128)(2,1)} custom-call(s32[2,512]{1,0:T(2,128)S(1)} %broadcast_select_fusion.1.slot_ref, bf16[1024,512]{1,0:T(8,128)(2,1)S(1)} %get-tuple-element.42.part_ref, bf16[1024,512]{1,0:T(8,128)(2,1)S(1)} %collective-permute-done.3.other_ref, bf16[1024,512]{1,0:T(8,128)(2,1)S(1)} %get-tuple-element.43.emb_ref, ...), custom_call_target="tpu_custom_call" | custom-call | flops 2000000000 | bytes 10000000 | tf_op jit(solution)/shard_map/pack/pallas_call | solution.py:311
  74.1 9.8 %collective-permute-done.4.back_1 = bf16[2064,128]{1,0:T(8,128)(2,1)S(1)} collective-permute-done((bf16[2064,128]{1,0:T(8,128)(2,1)S(1)}, bf16[2064,128]{1,0:T(8,128)(2,1)S(1)}, u32[]{:S(2)}, u32[]{:S(2)}) %collective-permute-start.4) | collective-permute-done | bytes 528416 | tf_op jit(solution)/shard_map/ppermute | solution.py:64
  85.4 3.1 %collective-permute-start.8 = (bf16[528,128]{1,0:T(8,128)(2,1)S(1)}, bf16[528,128]{1,0:T(8,128)(2,1)S(1)}, u32[]{:S(2)}, u32[]{:S(2)}) collective-permute-start(bf16[528,128]{1,0:T(8,128)(2,1)S(1)} %get-tuple-element.51), channel_id=1, source_target_pairs={{0,2},{1,3},{2,0},{3,1},{8,10},{9,11},{10,8},{11,9},{16,18},{17,19... | collective-permute-start | bytes 405512 | tf_op jit(solution)/shard_map/ppermute | solution.py:64
  89.2 2.1 %collective-permute-done.8.back_2 = bf16[528,128]{1,0:T(8,128)(2,1)S(1)} collective-permute-done((bf16[528,128]{1,0:T(8,128)(2,1)S(1)}, bf16[528,128]{1,0:T(8,128)(2,1)S(1)}, u32[]{:S(2)}, u32[]{:S(2)}) %collective-permute-start.8) | collective-permute-done | bytes 135200 | tf_op jit(solution)/shard_map/ppermute | solution.py:64
  91.3 1.4 collective-permute-done.9.back_3
  93.0 2.0 %collective-permute-start.11 = (bf16[528,128]{1,0:T(8,128)(2,1)S(1)}, bf16[528,128]{1,0:T(8,128)(2,1)S(1)}, u32[]{:S(2)}, u32[]{:S(2)}) collective-permute-start(bf16[528,128]{1,0:T(8,128)(2,1)S(1)} %sum_four.2.here), channel_id=1, source_target_pairs={{0,16},{8,24},{16,0},{24,8},{1,17},{9,25},{17,1},{25,9},{2,18},{10... | collective-permute-start | bytes 405512 | tf_op jit(solution)/shard_map/ppermute | solution.py:64
  96.0 8.7 %all-to-all-start.2 = ((bf16[64,64,128]{2,1,0:T(8,128)(2,1)}), bf16[64,64,128]{2,1,0:T(8,128)(2,1)S(1)}, u32[]{:S(2)}, u32[]{:S(2)}) async-start(bf16[64,64,128]{2,1,0:T(8,128)(2,1)} %bitcast.16), calls=%async_computation.2 | async-start | bytes 2097152 | tf_op jit(solution)/shard_map/all_to_all | solution.py:42
  104.8 1.3 collective-permute-start.13
  107.1 1.6 %collective-permute-start.15 = (bf16[528,128]{1,0:T(8,128)(2,1)S(1)}, bf16[528,128]{1,0:T(8,128)(2,1)S(1)}, u32[]{:S(2)}, u32[]{:S(2)}) collective-permute-start(bf16[528,128]{1,0:T(8,128)(2,1)S(1)} %sum_four.3.here), channel_id=1, source_target_pairs={{0,3},{1,0},{2,1},{3,2},{8,11},{9,8},{10,9},{11,10},{16,19},{17,16... | collective-permute-start | bytes 405512 | tf_op jit(solution)/shard_map/ppermute | solution.py:64
  109.7 7.7 %collective-permute-done.14.back_2 = bf16[528,128]{1,0:T(8,128)(2,1)S(1)} collective-permute-done((bf16[528,128]{1,0:T(8,128)(2,1)S(1)}, bf16[528,128]{1,0:T(8,128)(2,1)S(1)}, u32[]{:S(2)}, u32[]{:S(2)}) %collective-permute-start.14) | collective-permute-done | bytes 135200 | tf_op jit(solution)/shard_map/ppermute | solution.py:64
  117.3 5.8 %collective-permute-done.15.back_3 = bf16[528,128]{1,0:T(8,128)(2,1)S(1)} collective-permute-done((bf16[528,128]{1,0:T(8,128)(2,1)S(1)}, bf16[528,128]{1,0:T(8,128)(2,1)S(1)}, u32[]{:S(2)}, u32[]{:S(2)}) %collective-permute-start.15) | collective-permute-done | bytes 135200 | tf_op jit(solution)/shard_map/ppermute | solution.py:64
  123.7 1.9 %collective-permute-start.17 = (bf16[2064,128]{1,0:T(8,128)(2,1)S(1)}, bf16[2064,128]{1,0:T(8,128)(2,1)}, u32[]{:S(2)}, u32[]{:S(2)}) collective-permute-start(bf16[2064,128]{1,0:T(8,128)(2,1)S(1)} %join_four.1.refs_1_), channel_id=1, source_target_pairs={{0,64},{32,96},{64,0},{96,32},{8,72},{40,104},{72,8},{104,40},{16,... | collective-permute-start | bytes 1585160 | tf_op jit(solution)/shard_map/ppermute | solution.py:64
  125.6 1.4 collective-permute-start.18
  126.9 1.9 %collective-permute-start.19 = (bf16[2064,128]{1,0:T(8,128)(2,1)S(1)}, bf16[2064,128]{1,0:T(8,128)(2,1)S(1)}, u32[]{:S(2)}, u32[]{:S(2)}) collective-permute-start(bf16[2064,128]{1,0:T(8,128)(2,1)S(1)} %join_four.1.refs_1_), channel_id=1, source_target_pairs={{0,4},{4,0},{1,5},{5,1},{2,6},{6,2},{3,7},{7,3},{8,12},{12,8},{9,1... | collective-permute-start | bytes 1585160 | tf_op jit(solution)/shard_map/ppermute | solution.py:38
  128.9 1.6 %finish_first.1 = (f32[2048,512]{1,0:T(8,128)}, f32[512,2048]{1,0:T(8,128)}, f32[16,128]{1,0:T(8,128)S(1)}) custom-call(s32[5]{0:T(128)S(1)} %stack.31.place.refs_0_, bf16[2064,128]{1,0:T(8,128)(2,1)S(1)} %join_four.1.refs_1_), custom_call_target="tpu_custom_call" | custom-call | flops 1500000000 | bytes 1000000 | tf_op jit(solution)/shard_map/finish_first/pallas_call | solution.py:512
  130.5 11.0 %scatter_rows.1 = f32[8192,128]{1,0:T(8,128)} custom-call(s32[8192]{0:T(1024)S(1)} %bitcast.48, bf16[64,64,128]{2,1,0:T(8,128)(2,1)S(1)} %all-to-all-done.2.arrived_ref), custom_call_target="tpu_custom_call" | custom-call | flops 10000000000 | bytes 10000000 | tf_op jit(solution)/shard_map/scatter_rows/pallas_call | solution.py:367
  142.1 3.9 %finish_own.1 = (f32[2048,512]{1,0:T(8,128)}, f32[512,2048]{1,0:T(8,128)}, f32[16,128]{1,0:T(8,128)S(1)}) custom-call(s32[5]{0:T(128)S(1)} %stack.31.place.refs_0_, bf16[2064,128]{1,0:T(8,128)(2,1)S(1)} %collective-permute-done.16.refs_1_, bf16[2064,128]{1,0:T(8,128)(2,1)} %collective-permute-done.17.refs_2_, ...), custom_call_target="tpu_custom_call", output_to_operand_aliasing={{0}: (5, {}), {1}: (6, {})} | custom-call | flops 4499999744 | bytes 3000000 | tf_op jit(solution)/shard_map/finish_own/pallas_call | solution.py:512
  146.1 3.1 %finish_other.1 = (f32[2048,512]{1,0:T(8,128)}, f32[512,2048]{1,0:T(8,128)}, f32[16,128]{1,0:T(8,128)}, f32[4,128]{1,0:T(4,128)}) custom-call(s32[5]{0:T(128)S(1)} %stack.31.place.refs_0_, bf16[2064,128]{1,0:T(8,128)(2,1)S(1)} %collective-permute-done.19.refs_1_, ...), custom_call_target="tpu_custom_call", output_to_operand_aliasing={{0}: (6, {}), {1}: (7, {})} | custom-call | flops 6000000000 | bytes 4000000 | tf_op jit(solution)/shard_map/finish_other/pallas_call | solution.py:512
  (62 shorter events, 14.0 us)
Async XLA Ops:
  1.3 1.5 %collective-permute-start = (s32[512]{0:T(512)S(1)}, s32[512]{0:T(512)S(1)}, u32[]{:S(2)}, u32[]{:S(2)}) collective-permute-start(s32[512]{0:T(512)S(1)} %bitcast.61), channel_id=1, source_target_pairs={{0,4},{4,0},{1,5},{5,1},{2,6},{6,2},{3,7},{7,3},{8,12},{12,8},{9,1... | collective-permute-start | bytes 6152 | tf_op jit(solution)/shard_map/ppermute | solution.py:38
  2.0 2.1 %collective-permute-start.1 = (bf16[512,512]{1,0:T(8,128)(2,1)}, bf16[512,512]{1,0:T(8,128)(2,1)S(1)}, u32[]{:S(2)}, u32[]{:S(2)}) collective-permute-start(bf16[512,512]{1,0:T(8,128)(2,1)} %bitcast.44), channel_id=1, source_target_pairs={{0,4},{4,0},{1,5},{5,1},{2,6},{6,2},{3,7},{7,3},{8,12},{12,8},{9,1... | collective-permute-start | bytes 1572872 | tf_op jit(solution)/shard_map/ppermute | solution.py:38
  51.6 5.3 %collective-permute-start.2 = (bf16[16,4,64,128]{3,2,1,0:T(8,128)(2,1)S(1)}, bf16[16,4,64,128]{3,2,1,0:T(8,128)(2,1)}, u32[]{:S(2)}, u32[]{:S(2)}) collective-permute-start(bf16[16,4,64,128]{3,2,1,0:T(8,128)(2,1)S(1)} %bitcast.40), channel_id=1, source_target_pairs={{0,4},{4,0},{1,5},{5,1},{2,6},{6,2},{3,7},{7,3},{8,12},{12,8},{9,1... | collective-permute-start | bytes 3145736 | tf_op jit(solution)/shard_map/ppermute | solution.py:38
  68.1 3.3 %collective-permute-start.3 = (bf16[1024,512]{1,0:T(8,128)(2,1)S(1)}, bf16[1024,512]{1,0:T(8,128)(2,1)S(1)}, u32[]{:S(2)}, u32[]{:S(2)}) collective-permute-start(bf16[1024,512]{1,0:T(8,128)(2,1)S(1)} %get-tuple-element.42.part_ref), channel_id=1, source_target_pairs={{0,4},{4,0},{1,5},{5,1},{2,6},{6,2},{3,7},{7,3},{8,12},{12,8},{9,1... | collective-permute-start | bytes 3145736 | tf_op jit(solution)/shard_map/ppermute | solution.py:38
  68.6 15.2 %collective-permute-start.4 = (bf16[2064,128]{1,0:T(8,128)(2,1)S(1)}, bf16[2064,128]{1,0:T(8,128)(2,1)S(1)}, u32[]{:S(2)}, u32[]{:S(2)}) collective-permute-start(bf16[2064,128]{1,0:T(8,128)(2,1)S(1)} %get-tuple-element.46), channel_id=1, source_target_pairs={{0,32},{32,64},{64,96},{96,0},{8,40},{40,72},{72,104},{104,8},{16,... | collective-permute-start | bytes 1585160 | tf_op jit(solution)/shard_map/ppermute | solution.py:64
  69.0 14.8 %collective-permute-start.5 = (bf16[2064,128]{1,0:T(8,128)(2,1)S(1)}, bf16[2064,128]{1,0:T(8,128)(2,1)S(1)}, u32[]{:S(2)}, u32[]{:S(2)}) collective-permute-start(bf16[2064,128]{1,0:T(8,128)(2,1)S(1)} %get-tuple-element.47), channel_id=1, source_target_pairs={{0,64},{32,96},{64,0},{96,32},{8,72},{40,104},{72,8},{104,40},{16,... | collective-permute-start | bytes 1585160 | tf_op jit(solution)/shard_map/ppermute | solution.py:64
  70.2 14.3 %collective-permute-start.6 = (bf16[2064,128]{1,0:T(8,128)(2,1)S(1)}, bf16[2064,128]{1,0:T(8,128)(2,1)S(1)}, u32[]{:S(2)}, u32[]{:S(2)}) collective-permute-start(bf16[2064,128]{1,0:T(8,128)(2,1)S(1)} %get-tuple-element.48), channel_id=1, source_target_pairs={{0,96},{32,0},{64,32},{96,64},{8,104},{40,8},{72,40},{104,72},{16,... | collective-permute-start | bytes 1585160 | tf_op jit(solution)/shard_map/ppermute | solution.py:64
  85.3 3.9 %collective-permute-start.7 = (bf16[528,128]{1,0:T(8,128)(2,1)S(1)}, bf16[528,128]{1,0:T(8,128)(2,1)S(1)}, u32[]{:S(2)}, u32[]{:S(2)}) collective-permute-start(bf16[528,128]{1,0:T(8,128)(2,1)S(1)} %get-tuple-element.50), channel_id=1, source_target_pairs={{0,1},{1,2},{2,3},{3,0},{8,9},{9,10},{10,11},{11,8},{16,17},{17,18... | collective-permute-start | bytes 405512 | tf_op jit(solution)/shard_map/ppermute | solution.py:64
  85.4 6.0 %collective-permute-start.8 = (bf16[528,128]{1,0:T(8,128)(2,1)S(1)}, bf16[528,128]{1,0:T(8,128)(2,1)S(1)}, u32[]{:S(2)}, u32[]{:S(2)}) collective-permute-start(bf16[528,128]{1,0:T(8,128)(2,1)S(1)} %get-tuple-element.51), channel_id=1, source_target_pairs={{0,2},{1,3},{2,0},{3,1},{8,10},{9,11},{10,8},{11,9},{16,18},{17,19... | collective-permute-start | bytes 405512 | tf_op jit(solution)/shard_map/ppermute | solution.py:64
  88.5 4.3 %collective-permute-start.9 = (bf16[528,128]{1,0:T(8,128)(2,1)S(1)}, bf16[528,128]{1,0:T(8,128)(2,1)S(1)}, u32[]{:S(2)}, u32[]{:S(2)}) collective-permute-start(bf16[528,128]{1,0:T(8,128)(2,1)S(1)} %get-tuple-element.52), channel_id=1, source_target_pairs={{0,3},{1,0},{2,1},{3,2},{8,11},{9,8},{10,9},{11,10},{16,19},{17,16... | collective-permute-start | bytes 405512 | tf_op jit(solution)/shard_map/ppermute | solution.py:64
  92.9 11.9 %collective-permute-start.10 = (bf16[528,128]{1,0:T(8,128)(2,1)S(1)}, bf16[528,128]{1,0:T(8,128)(2,1)S(1)}, u32[]{:S(2)}, u32[]{:S(2)}) collective-permute-start(bf16[528,128]{1,0:T(8,128)(2,1)S(1)} %sum_four.2.here), channel_id=1, source_target_pairs={{0,8},{8,16},{16,24},{24,0},{1,9},{9,17},{17,25},{25,1},{2,10},{10... | collective-permute-start | bytes 405512 | tf_op jit(solution)/shard_map/ppermute | solution.py:64
  93.0 11.8 %collective-permute-start.11 = (bf16[528,128]{1,0:T(8,128)(2,1)S(1)}, bf16[528,128]{1,0:T(8,128)(2,1)S(1)}, u32[]{:S(2)}, u32[]{:S(2)}) collective-permute-start(bf16[528,128]{1,0:T(8,128)(2,1)S(1)} %sum_four.2.here), channel_id=1, source_target_pairs={{0,16},{8,24},{16,0},{24,8},{1,17},{9,25},{17,1},{25,9},{2,18},{10... | collective-permute-start | bytes 405512 | tf_op jit(solution)/shard_map/ppermute | solution.py:64
  95.0 9.8 %collective-permute-start.12 = (bf16[528,128]{1,0:T(8,128)(2,1)S(1)}, bf16[528,128]{1,0:T(8,128)(2,1)S(1)}, u32[]{:S(2)}, u32[]{:S(2)}) collective-permute-start(bf16[528,128]{1,0:T(8,128)(2,1)S(1)} %sum_four.2.here), channel_id=1, source_target_pairs={{0,24},{8,0},{16,8},{24,16},{1,25},{9,1},{17,9},{25,17},{2,26},{10... | collective-permute-start | bytes 405512 | tf_op jit(solution)/shard_map/ppermute | solution.py:64
  96.0 34.5 %all-to-all-start.2 = ((bf16[64,64,128]{2,1,0:T(8,128)(2,1)}), bf16[64,64,128]{2,1,0:T(8,128)(2,1)S(1)}, u32[]{:S(2)}, u32[]{:S(2)}) async-start(bf16[64,64,128]{2,1,0:T(8,128)(2,1)} %bitcast.16), calls=%async_computation.2 | async-start | bytes 2097152 | tf_op jit(solution)/shard_map/all_to_all | solution.py:42
  104.8 4.8 %collective-permute-start.13 = (bf16[528,128]{1,0:T(8,128)(2,1)S(1)}, bf16[528,128]{1,0:T(8,128)(2,1)S(1)}, u32[]{:S(2)}, u32[]{:S(2)}) collective-permute-start(bf16[528,128]{1,0:T(8,128)(2,1)S(1)} %sum_four.3.here), channel_id=1, source_target_pairs={{0,1},{1,2},{2,3},{3,0},{8,9},{9,10},{10,11},{11,8},{16,17},{17,18... | collective-permute-start | bytes 405512 | tf_op jit(solution)/shard_map/ppermute | solution.py:64
  106.1 11.2 %collective-permute-start.14 = (bf16[528,128]{1,0:T(8,128)(2,1)S(1)}, bf16[528,128]{1,0:T(8,128)(2,1)S(1)}, u32[]{:S(2)}, u32[]{:S(2)}) collective-permute-start(bf16[528,128]{1,0:T(8,128)(2,1)S(1)} %sum_four.3.here), channel_id=1, source_target_pairs={{0,2},{1,3},{2,0},{3,1},{8,10},{9,11},{10,8},{11,9},{16,18},{17,19... | collective-permute-start | bytes 405512 | tf_op jit(solution)/shard_map/ppermute | solution.py:64
  107.1 16.0 %collective-permute-start.15 = (bf16[528,128]{1,0:T(8,128)(2,1)S(1)}, bf16[528,128]{1,0:T(8,128)(2,1)S(1)}, u32[]{:S(2)}, u32[]{:S(2)}) collective-permute-start(bf16[528,128]{1,0:T(8,128)(2,1)S(1)} %sum_four.3.here), channel_id=1, source_target_pairs={{0,3},{1,0},{2,1},{3,2},{8,11},{9,8},{10,9},{11,10},{16,19},{17,16... | collective-permute-start | bytes 405512 | tf_op jit(solution)/shard_map/ppermute | solution.py:64
  123.2 18.2 %collective-permute-start.16 = (bf16[2064,128]{1,0:T(8,128)(2,1)S(1)}, bf16[2064,128]{1,0:T(8,128)(2,1)S(1)}, u32[]{:S(2)}, u32[]{:S(2)}) collective-permute-start(bf16[2064,128]{1,0:T(8,128)(2,1)S(1)} %join_four.1.refs_1_), channel_id=1, source_target_pairs={{0,32},{32,64},{64,96},{96,0},{8,40},{40,72},{72,104},{104,8},{16,... | collective-permute-start | bytes 1585160 | tf_op jit(solution)/shard_map/ppermute | solution.py:64
  123.7 17.7 %collective-permute-start.17 = (bf16[2064,128]{1,0:T(8,128)(2,1)S(1)}, bf16[2064,128]{1,0:T(8,128)(2,1)}, u32[]{:S(2)}, u32[]{:S(2)}) collective-permute-start(bf16[2064,128]{1,0:T(8,128)(2,1)S(1)} %join_four.1.refs_1_), channel_id=1, source_target_pairs={{0,64},{32,96},{64,0},{96,32},{8,72},{40,104},{72,8},{104,40},{16,... | collective-permute-start | bytes 1585160 | tf_op jit(solution)/shard_map/ppermute | solution.py:64
  125.6 15.9 %collective-permute-start.18 = (bf16[2064,128]{1,0:T(8,128)(2,1)S(1)}, bf16[2064,128]{1,0:T(8,128)(2,1)}, u32[]{:S(2)}, u32[]{:S(2)}) collective-permute-start(bf16[2064,128]{1,0:T(8,128)(2,1)S(1)} %join_four.1.refs_1_), channel_id=1, source_target_pairs={{0,96},{32,0},{64,32},{96,64},{8,104},{40,8},{72,40},{104,72},{16,... | collective-permute-start | bytes 1585160 | tf_op jit(solution)/shard_map/ppermute | solution.py:64
  126.9 19.1 %collective-permute-start.19 = (bf16[2064,128]{1,0:T(8,128)(2,1)S(1)}, bf16[2064,128]{1,0:T(8,128)(2,1)S(1)}, u32[]{:S(2)}, u32[]{:S(2)}) collective-permute-start(bf16[2064,128]{1,0:T(8,128)(2,1)S(1)} %join_four.1.refs_1_), channel_id=1, source_target_pairs={{0,4},{4,0},{1,5},{5,1},{2,6},{6,2},{3,7},{7,3},{8,12},{12,8},{9,1... | collective-permute-start | bytes 1585160 | tf_op jit(solution)/shard_map/ppermute | solution.py:38
  141.5 4.6 %collective-permute-start.20 = (bf16[2064,128]{1,0:T(8,128)(2,1)S(1)}, bf16[2064,128]{1,0:T(8,128)(2,1)S(1)}, u32[]{:S(2)}, u32[]{:S(2)}) collective-permute-start(bf16[2064,128]{1,0:T(8,128)(2,1)S(1)} %collective-permute-done.16.refs_1_), channel_id=1, source_target_pairs={{0,4},{4,0},{1,5},{5,1},{2,6},{6,2},{3,7},{7,3},{8,12},{12,8},{9,1... | collective-permute-start | bytes 1585160 | tf_op jit(solution)/shard_map/ppermute | solution.py:38
  141.6 4.5 %collective-permute-start.21 = (bf16[2064,128]{1,0:T(8,128)(2,1)}, bf16[2064,128]{1,0:T(8,128)(2,1)S(1)}, u32[]{:S(2)}, u32[]{:S(2)}) collective-permute-start(bf16[2064,128]{1,0:T(8,128)(2,1)} %collective-permute-done.17.refs_2_), channel_id=1, source_target_pairs={{0,4},{4,0},{1,5},{5,1},{2,6},{6,2},{3,7},{7,3},{8,12},{12,8},{9,1... | collective-permute-start | bytes 1585160 | tf_op jit(solution)/shard_map/ppermute | solution.py:38
  142.0 4.0 %collective-permute-start.22 = (bf16[2064,128]{1,0:T(8,128)(2,1)}, bf16[2064,128]{1,0:T(8,128)(2,1)S(1)}, u32[]{:S(2)}, u32[]{:S(2)}) collective-permute-start(bf16[2064,128]{1,0:T(8,128)(2,1)} %collective-permute-done.18.refs_3_), channel_id=1, source_target_pairs={{0,4},{4,0},{1,5},{5,1},{2,6},{6,2},{3,7},{7,3},{8,12},{12,8},{9,1... | collective-permute-start | bytes 1585160 | tf_op jit(solution)/shard_map/ppermute | solution.py:38
  (4 other events, 86.7 us)

commit v13 on v12

--- a/solution.py
+++ b/solution.py
@@ -321,7 +321,7 @@
 SCATTER_MIB = 48
 
 
-def scatter_kernel(asked, arrived_ref, out_ref, grads, *accs):
+def scatter_kernel(asked, arrived_ref, far_ref, sems, grads, out_ref, *accs):
     zero = jnp.zeros((512, LANES), f32)
 
     def clear(i, carry):
@@ -358,18 +358,26 @@
         for acc in accs:
             total = total + acc[rows, :]
         out_ref[rows, :] = total
+        pltpu.make_async_copy(out_ref.at[rows], far_ref.at[rows], sems.at[i]).start()
         return carry
 
     lax.fori_loop(0, ROWS // 512, merge, 0)
+
+    def finished(i, carry):
+        rows = pl.ds(pl.multiple_of(i * 512, 512), 512)
+        pltpu.make_async_copy(out_ref.at[rows], far_ref.at[rows], sems.at[i]).wait()
+        return carry
+
+    lax.fori_loop(0, ROWS // 512, finished, 0)
 
 
 def scatter_rows(asked, arrived):
     return pl.pallas_call(
         scatter_kernel,
         in_specs=[SCALARS, NEAR],
-        out_specs=NEAR,
-        scratch_shapes=[pltpu.VMEM((N_REQ, LANES), f32)]
-        + [pltpu.VMEM((ROWS, LANES), f32)] * (N_ACC - 1),
+        out_specs=FAR,
+        scratch_shapes=[pltpu.SemaphoreType.DMA((ROWS // 512,)), pltpu.VMEM((N_REQ, LANES), f32)]
+        + [pltpu.VMEM((ROWS, LANES), f32)] * N_ACC,
         out_shape=jax.ShapeDtypeStruct((ROWS, LANES), f32),
         compiler_params=params(SCATTER_MIB),
         cost_estimate=pl.CostEstimate(flops=10**10, bytes_accessed=10**7, transcendentals=0),

time: 151 us -> 151 us (level)
  transfers between devices with their start and end apart: 24 -> 24, of which waited for: 11 -> 11; matrix products, arithmetic and copies ran while one was open for 1% -> 1% of each run, Pallas kernels for 13% -> 12%
where the time goes in v13:
time: 151 us; the launch traced here: 149 us
  Pallas kernels  41.3 us (27%)
  blocking collectives  39.5 us (26%)
  starting transfers between devices  33.3 us (22%)
  waiting for transfers between devices  31.4 us (21%)
  local copies, waits for them, and re-layouts  2.12 us (1%)
    all_to_all x2, blocking collectives, exchange(): return lax.all_to_all(a, PEERS, split_axis=0, concat_axis=0, tiled=True)  39.5 us
    ppermute x15, waiting for transfers between devices, along(): return lax.ppermute(a, EVERY, pairs)  29.1 us
    ppermute x15, starting transfers between devices, along(): return lax.ppermute(a, EVERY, pairs)  16.9 us
    pallas_call x1, Pallas kernels, block(): pl.pallas_call(block_kernel, in_specs=[SCALARS] + [NEAR] * 4 + [FAR] * 2...  11.2 us
    pallas_call x1, Pallas kernels, scatter_rows(): pl.pallas_call(scatter_kernel, in_specs=[SCALARS, NEAR], out_specs=FAR, s...  9.79 us
    all_to_all x1, starting transfers between devices, exchange(): return lax.all_to_all(a, PEERS, split_axis=0, concat_axis=0, tiled=True)  8.74 us
    pallas_call x3, Pallas kernels, finish_part(): pl.pallas_call(lambda *refs: kernel(scale, *refs), grid_spec=pltpu.Prefet...  8.61 us
    pallas_call x1, Pallas kernels, gather_rows(): pl.pallas_call(gather_kernel, in_specs=[SCALARS, FAR], out_specs=NEAR, sc...  7.99 us
  transfers between devices with their start and end apart: 24, of which 11 were waited for; matrix products, arithmetic and copies ran while one was open for 1% of the time, Pallas kernels for 12%

profile of v13, /device:TPU:33, one launch (start us, length us, event | category | flops | bytes accessed | tf_op | source)
XLA Modules:
  0.0 149.1 jit_solution(5967896818343117035)
XLA Ops:
  4.1 18.3 %all_to_all.15 = s32[64,1,128]{2,1,0:T(1,128)} all-to-all(s32[64,1,128]{2,1,0:T(1,128)S(1)} %bitcast.53), channel_id=1, replica_groups=mesh['x'=4,'z'=4,'core'=2,'y'=4] {'x','z','y'}, dimensions={0} | all-to-all | bytes 65536 | tf_op jit(solution)/shard_map/all_to_all | solution.py:42
  22.4 8.0 %gather_rows.1 = bf16[64,64,128]{2,1,0:T(8,128)(2,1)} custom-call(s32[8192]{0:T(1024)} %bitcast.47, bf16[8192,128]{1,0:T(8,128)(2,1)} %table_ref.1), custom_call_target="tpu_custom_call" | custom-call | tf_op jit(solution)/shard_map/gather_rows/pallas_call | solution.py:113
  30.4 21.2 %all_to_all.16 = bf16[64,64,128]{2,1,0:T(8,128)(2,1)S(1)} all-to-all(bf16[64,64,128]{2,1,0:T(8,128)(2,1)} %gather_rows.1), channel_id=1, replica_groups=mesh['x'=4,'z'=4,'core'=2,'y'=4] {'x','z','y'}, dimensions={0} | all-to-all | bytes 2097152 | tf_op jit(solution)/shard_map/all_to_all | solution.py:42
  51.6 2.8 %collective-permute-start.2 = (bf16[16,4,64,128]{3,2,1,0:T(8,128)(2,1)S(1)}, bf16[16,4,64,128]{3,2,1,0:T(8,128)(2,1)}, u32[]{:S(2)}, u32[]{:S(2)}) collective-permute-start(bf16[16,4,64,128]{3,2,1,0:T(8,128)(2,1)S(1)} %bitcast.40), channel_id=1, source_target_pairs={{0,4},{4,0},{1,5},{5,1},{2,6},{6,2},{3,7},{7,3},{8,12},{12,8},{9,1... | collective-permute-start | bytes 3145736 | tf_op jit(solution)/shard_map/ppermute | solution.py:38
  55.0 1.9 %collective-permute-done.2.got_other = bf16[16,4,64,128]{3,2,1,0:T(8,128)(2,1)} collective-permute-done((bf16[16,4,64,128]{3,2,1,0:T(8,128)(2,1)S(1)}, bf16[16,4,64,128]{3,2,1,0:T(8,128)(2,1)}, u32[]{:S(2)}, u32[]{:S(2)}) %collective-permute-start.2) | collective-permute-done | bytes 1048608 | tf_op jit(solution)/shard_map/ppermute | solution.py:38
  56.9 11.2 %block.1 = (bf16[1024,512]{1,0:T(8,128)(2,1)S(1)}, bf16[1024,512]{1,0:T(8,128)(2,1)S(1)}, bf16[2064,128]{1,0:T(8,128)(2,1)S(1)}, bf16[2064,128]{1,0:T(8,128)(2,1...) custom-call(s32[5]{0:T(128)S(1)} %stack.31.place.refs_0_, s32[1024,1]{1,0:T(8,128)S(1)} %bitcast.42, ...), custom_call_target="tpu_custom_call" | custom-call | tf_op jit(solution)/shard_map/block/pallas_call | solution.py:263
  71.4 2.6 %pack.1 = bf16[16,4,64,128]{3,2,1,0:T(8,128)(2,1)} custom-call(s32[2,512]{1,0:T(2,128)S(1)} %broadcast_select_fusion.1.slot_ref, bf16[1024,512]{1,0:T(8,128)(2,1)S(1)} %get-tuple-element.42.part_ref, bf16[1024,512]{1,0:T(8,128)(2,1)S(1)} %collective-permute-done.3.other_ref, bf16[1024,512]{1,0:T(8,128)(2,1)S(1)} %get-tuple-element.43.emb_ref, ...), custom_call_target="tpu_custom_call" | custom-call | flops 2000000000 | bytes 10000000 | tf_op jit(solution)/shard_map/pack/pallas_call | solution.py:311
  74.1 9.7 %collective-permute-done.4.back_1 = bf16[2064,128]{1,0:T(8,128)(2,1)S(1)} collective-permute-done((bf16[2064,128]{1,0:T(8,128)(2,1)S(1)}, bf16[2064,128]{1,0:T(8,128)(2,1)S(1)}, u32[]{:S(2)}, u32[]{:S(2)}) %collective-permute-start.4) | collective-permute-done | bytes 528416 | tf_op jit(solution)/shard_map/ppermute | solution.py:64
  85.3 3.1 %collective-permute-start.8 = (bf16[528,128]{1,0:T(8,128)(2,1)S(1)}, bf16[528,128]{1,0:T(8,128)(2,1)S(1)}, u32[]{:S(2)}, u32[]{:S(2)}) collective-permute-start(bf16[528,128]{1,0:T(8,128)(2,1)S(1)} %get-tuple-element.51), channel_id=1, source_target_pairs={{0,2},{1,3},{2,0},{3,1},{8,10},{9,11},{10,8},{11,9},{16,18},{17,19... | collective-permute-start | bytes 405512 | tf_op jit(solution)/shard_map/ppermute | solution.py:64
  89.2 2.1 %collective-permute-done.8.back_2 = bf16[528,128]{1,0:T(8,128)(2,1)S(1)} collective-permute-done((bf16[528,128]{1,0:T(8,128)(2,1)S(1)}, bf16[528,128]{1,0:T(8,128)(2,1)S(1)}, u32[]{:S(2)}, u32[]{:S(2)}) %collective-permute-start.8) | collective-permute-done | bytes 135200 | tf_op jit(solution)/shard_map/ppermute | solution.py:64
  91.3 1.4 collective-permute-done.9.back_3
  92.9 2.0 %collective-permute-start.11 = (bf16[528,128]{1,0:T(8,128)(2,1)S(1)}, bf16[528,128]{1,0:T(8,128)(2,1)S(1)}, u32[]{:S(2)}, u32[]{:S(2)}) collective-permute-start(bf16[528,128]{1,0:T(8,128)(2,1)S(1)} %sum_four.2.here), channel_id=1, source_target_pairs={{0,16},{8,24},{16,0},{24,8},{1,17},{9,25},{17,1},{25,9},{2,18},{10... | collective-permute-start | bytes 405512 | tf_op jit(solution)/shard_map/ppermute | solution.py:64
  96.0 8.7 %all-to-all-start.2 = ((bf16[64,64,128]{2,1,0:T(8,128)(2,1)}), bf16[64,64,128]{2,1,0:T(8,128)(2,1)S(1)}, u32[]{:S(2)}, u32[]{:S(2)}) async-start(bf16[64,64,128]{2,1,0:T(8,128)(2,1)} %bitcast.16), calls=%async_computation.2 | async-start | bytes 2097152 | tf_op jit(solution)/shard_map/all_to_all | solution.py:42
  104.8 1.3 collective-permute-start.13
  107.2 1.6 %collective-permute-start.15 = (bf16[528,128]{1,0:T(8,128)(2,1)S(1)}, bf16[528,128]{1,0:T(8,128)(2,1)S(1)}, u32[]{:S(2)}, u32[]{:S(2)}) collective-permute-start(bf16[528,128]{1,0:T(8,128)(2,1)S(1)} %sum_four.3.here), channel_id=1, source_target_pairs={{0,3},{1,0},{2,1},{3,2},{8,11},{9,8},{10,9},{11,10},{16,19},{17,16... | collective-permute-start | bytes 405512 | tf_op jit(solution)/shard_map/ppermute | solution.py:64
  109.7 7.7 %collective-permute-done.14.back_2 = bf16[528,128]{1,0:T(8,128)(2,1)S(1)} collective-permute-done((bf16[528,128]{1,0:T(8,128)(2,1)S(1)}, bf16[528,128]{1,0:T(8,128)(2,1)S(1)}, u32[]{:S(2)}, u32[]{:S(2)}) %collective-permute-start.14) | collective-permute-done | bytes 135200 | tf_op jit(solution)/shard_map/ppermute | solution.py:64
  117.3 5.8 %collective-permute-done.15.back_3 = bf16[528,128]{1,0:T(8,128)(2,1)S(1)} collective-permute-done((bf16[528,128]{1,0:T(8,128)(2,1)S(1)}, bf16[528,128]{1,0:T(8,128)(2,1)S(1)}, u32[]{:S(2)}, u32[]{:S(2)}) %collective-permute-start.15) | collective-permute-done | bytes 135200 | tf_op jit(solution)/shard_map/ppermute | solution.py:64
  123.7 1.9 %collective-permute-start.17 = (bf16[2064,128]{1,0:T(8,128)(2,1)S(1)}, bf16[2064,128]{1,0:T(8,128)(2,1)}, u32[]{:S(2)}, u32[]{:S(2)}) collective-permute-start(bf16[2064,128]{1,0:T(8,128)(2,1)S(1)} %join_four.1.refs_1_), channel_id=1, source_target_pairs={{0,64},{32,96},{64,0},{96,32},{8,72},{40,104},{72,8},{104,40},{16,... | collective-permute-start | bytes 1585160 | tf_op jit(solution)/shard_map/ppermute | solution.py:64
  125.6 1.4 collective-permute-start.18
  126.9 1.9 %collective-permute-start.19 = (bf16[2064,128]{1,0:T(8,128)(2,1)S(1)}, bf16[2064,128]{1,0:T(8,128)(2,1)S(1)}, u32[]{:S(2)}, u32[]{:S(2)}) collective-permute-start(bf16[2064,128]{1,0:T(8,128)(2,1)S(1)} %join_four.1.refs_1_), channel_id=1, source_target_pairs={{0,4},{4,0},{1,5},{5,1},{2,6},{6,2},{3,7},{7,3},{8,12},{12,8},{9,1... | collective-permute-start | bytes 1585160 | tf_op jit(solution)/shard_map/ppermute | solution.py:38
  128.9 1.6 %finish_first.1 = (f32[2048,512]{1,0:T(8,128)}, f32[512,2048]{1,0:T(8,128)}, f32[16,128]{1,0:T(8,128)S(1)}) custom-call(s32[5]{0:T(128)S(1)} %stack.31.place.refs_0_, bf16[2064,128]{1,0:T(8,128)(2,1)S(1)} %join_four.1.refs_1_), custom_call_target="tpu_custom_call" | custom-call | flops 1500000000 | bytes 1000000 | tf_op jit(solution)/shard_map/finish_first/pallas_call | solution.py:520
  130.5 9.8 %scatter_rows.1 = f32[8192,128]{1,0:T(8,128)} custom-call(s32[8192]{0:T(1024)S(1)} %bitcast.48, bf16[64,64,128]{2,1,0:T(8,128)(2,1)S(1)} %all-to-all-done.2.arrived_ref), custom_call_target="tpu_custom_call" | custom-call | flops 10000000000 | bytes 10000000 | tf_op jit(solution)/shard_map/scatter_rows/pallas_call | solution.py:375
  142.1 3.9 %finish_own.1 = (f32[2048,512]{1,0:T(8,128)}, f32[512,2048]{1,0:T(8,128)}, f32[16,128]{1,0:T(8,128)S(1)}) custom-call(s32[5]{0:T(128)S(1)} %stack.31.place.refs_0_, bf16[2064,128]{1,0:T(8,128)(2,1)S(1)} %collective-permute-done.16.refs_1_, bf16[2064,128]{1,0:T(8,128)(2,1)} %collective-permute-done.17.refs_2_, ...), custom_call_target="tpu_custom_call", output_to_operand_aliasing={{0}: (5, {}), {1}: (6, {})} | custom-call | flops 4499999744 | bytes 3000000 | tf_op jit(solution)/shard_map/finish_own/pallas_call | solution.py:520
  146.0 3.1 %finish_other.1 = (f32[2048,512]{1,0:T(8,128)}, f32[512,2048]{1,0:T(8,128)}, f32[16,128]{1,0:T(8,128)}, f32[4,128]{1,0:T(4,128)}) custom-call(s32[5]{0:T(128)S(1)} %stack.31.place.refs_0_, bf16[2064,128]{1,0:T(8,128)(2,1)S(1)} %collective-permute-done.19.refs_1_, ...), custom_call_target="tpu_custom_call", output_to_operand_aliasing={{0}: (6, {}), {1}: (7, {})} | custom-call | flops 6000000000 | bytes 4000000 | tf_op jit(solution)/shard_map/finish_other/pallas_call | solution.py:520
  (62 shorter events, 15.1 us)
Async XLA Ops:
  1.3 1.5 %collective-permute-start = (s32[512]{0:T(512)S(1)}, s32[512]{0:T(512)S(1)}, u32[]{:S(2)}, u32[]{:S(2)}) collective-permute-start(s32[512]{0:T(512)S(1)} %bitcast.61), channel_id=1, source_target_pairs={{0,4},{4,0},{1,5},{5,1},{2,6},{6,2},{3,7},{7,3},{8,12},{12,8},{9,1... | collective-permute-start | bytes 6152 | tf_op jit(solution)/shard_map/ppermute | solution.py:38
  2.0 2.1 %collective-permute-start.1 = (bf16[512,512]{1,0:T(8,128)(2,1)}, bf16[512,512]{1,0:T(8,128)(2,1)S(1)}, u32[]{:S(2)}, u32[]{:S(2)}) collective-permute-start(bf16[512,512]{1,0:T(8,128)(2,1)} %bitcast.44), channel_id=1, source_target_pairs={{0,4},{4,0},{1,5},{5,1},{2,6},{6,2},{3,7},{7,3},{8,12},{12,8},{9,1... | collective-permute-start | bytes 1572872 | tf_op jit(solution)/shard_map/ppermute | solution.py:38
  51.6 5.3 %collective-permute-start.2 = (bf16[16,4,64,128]{3,2,1,0:T(8,128)(2,1)S(1)}, bf16[16,4,64,128]{3,2,1,0:T(8,128)(2,1)}, u32[]{:S(2)}, u32[]{:S(2)}) collective-permute-start(bf16[16,4,64,128]{3,2,1,0:T(8,128)(2,1)S(1)} %bitcast.40), channel_id=1, source_target_pairs={{0,4},{4,0},{1,5},{5,1},{2,6},{6,2},{3,7},{7,3},{8,12},{12,8},{9,1... | collective-permute-start | bytes 3145736 | tf_op jit(solution)/shard_map/ppermute | solution.py:38
  68.1 3.3 %collective-permute-start.3 = (bf16[1024,512]{1,0:T(8,128)(2,1)S(1)}, bf16[1024,512]{1,0:T(8,128)(2,1)S(1)}, u32[]{:S(2)}, u32[]{:S(2)}) collective-permute-start(bf16[1024,512]{1,0:T(8,128)(2,1)S(1)} %get-tuple-element.42.part_ref), channel_id=1, source_target_pairs={{0,4},{4,0},{1,5},{5,1},{2,6},{6,2},{3,7},{7,3},{8,12},{12,8},{9,1... | collective-permute-start | bytes 3145736 | tf_op jit(solution)/shard_map/ppermute | solution.py:38
  68.6 15.2 %collective-permute-start.4 = (bf16[2064,128]{1,0:T(8,128)(2,1)S(1)}, bf16[2064,128]{1,0:T(8,128)(2,1)S(1)}, u32[]{:S(2)}, u32[]{:S(2)}) collective-permute-start(bf16[2064,128]{1,0:T(8,128)(2,1)S(1)} %get-tuple-element.46), channel_id=1, source_target_pairs={{0,32},{32,64},{64,96},{96,0},{8,40},{40,72},{72,104},{104,8},{16,... | collective-permute-start | bytes 1585160 | tf_op jit(solution)/shard_map/ppermute | solution.py:64
  69.0 14.8 %collective-permute-start.5 = (bf16[2064,128]{1,0:T(8,128)(2,1)S(1)}, bf16[2064,128]{1,0:T(8,128)(2,1)S(1)}, u32[]{:S(2)}, u32[]{:S(2)}) collective-permute-start(bf16[2064,128]{1,0:T(8,128)(2,1)S(1)} %get-tuple-element.47), channel_id=1, source_target_pairs={{0,64},{32,96},{64,0},{96,32},{8,72},{40,104},{72,8},{104,40},{16,... | collective-permute-start | bytes 1585160 | tf_op jit(solution)/shard_map/ppermute | solution.py:64
  70.2 14.2 %collective-permute-start.6 = (bf16[2064,128]{1,0:T(8,128)(2,1)S(1)}, bf16[2064,128]{1,0:T(8,128)(2,1)S(1)}, u32[]{:S(2)}, u32[]{:S(2)}) collective-permute-start(bf16[2064,128]{1,0:T(8,128)(2,1)S(1)} %get-tuple-element.48), channel_id=1, source_target_pairs={{0,96},{32,0},{64,32},{96,64},{8,104},{40,8},{72,40},{104,72},{16,... | collective-permute-start | bytes 1585160 | tf_op jit(solution)/shard_map/ppermute | solution.py:64
  85.3 3.9 %collective-permute-start.7 = (bf16[528,128]{1,0:T(8,128)(2,1)S(1)}, bf16[528,128]{1,0:T(8,128)(2,1)S(1)}, u32[]{:S(2)}, u32[]{:S(2)}) collective-permute-start(bf16[528,128]{1,0:T(8,128)(2,1)S(1)} %get-tuple-element.50), channel_id=1, source_target_pairs={{0,1},{1,2},{2,3},{3,0},{8,9},{9,10},{10,11},{11,8},{16,17},{17,18... | collective-permute-start | bytes 405512 | tf_op jit(solution)/shard_map/ppermute | solution.py:64
  85.3 6.0 %collective-permute-start.8 = (bf16[528,128]{1,0:T(8,128)(2,1)S(1)}, bf16[528,128]{1,0:T(8,128)(2,1)S(1)}, u32[]{:S(2)}, u32[]{:S(2)}) collective-permute-start(bf16[528,128]{1,0:T(8,128)(2,1)S(1)} %get-tuple-element.51), channel_id=1, source_target_pairs={{0,2},{1,3},{2,0},{3,1},{8,10},{9,11},{10,8},{11,9},{16,18},{17,19... | collective-permute-start | bytes 405512 | tf_op jit(solution)/shard_map/ppermute | solution.py:64
  88.4 4.3 %collective-permute-start.9 = (bf16[528,128]{1,0:T(8,128)(2,1)S(1)}, bf16[528,128]{1,0:T(8,128)(2,1)S(1)}, u32[]{:S(2)}, u32[]{:S(2)}) collective-permute-start(bf16[528,128]{1,0:T(8,128)(2,1)S(1)} %get-tuple-element.52), channel_id=1, source_target_pairs={{0,3},{1,0},{2,1},{3,2},{8,11},{9,8},{10,9},{11,10},{16,19},{17,16... | collective-permute-start | bytes 405512 | tf_op jit(solution)/shard_map/ppermute | solution.py:64
  92.8 11.9 %collective-permute-start.10 = (bf16[528,128]{1,0:T(8,128)(2,1)S(1)}, bf16[528,128]{1,0:T(8,128)(2,1)S(1)}, u32[]{:S(2)}, u32[]{:S(2)}) collective-permute-start(bf16[528,128]{1,0:T(8,128)(2,1)S(1)} %sum_four.2.here), channel_id=1, source_target_pairs={{0,8},{8,16},{16,24},{24,0},{1,9},{9,17},{17,25},{25,1},{2,10},{10... | collective-permute-start | bytes 405512 | tf_op jit(solution)/shard_map/ppermute | solution.py:64
  92.9 11.8 %collective-permute-start.11 = (bf16[528,128]{1,0:T(8,128)(2,1)S(1)}, bf16[528,128]{1,0:T(8,128)(2,1)S(1)}, u32[]{:S(2)}, u32[]{:S(2)}) collective-permute-start(bf16[528,128]{1,0:T(8,128)(2,1)S(1)} %sum_four.2.here), channel_id=1, source_target_pairs={{0,16},{8,24},{16,0},{24,8},{1,17},{9,25},{17,1},{25,9},{2,18},{10... | collective-permute-start | bytes 405512 | tf_op jit(solution)/shard_map/ppermute | solution.py:64
  95.0 9.8 %collective-permute-start.12 = (bf16[528,128]{1,0:T(8,128)(2,1)S(1)}, bf16[528,128]{1,0:T(8,128)(2,1)S(1)}, u32[]{:S(2)}, u32[]{:S(2)}) collective-permute-start(bf16[528,128]{1,0:T(8,128)(2,1)S(1)} %sum_four.2.here), channel_id=1, source_target_pairs={{0,24},{8,0},{16,8},{24,16},{1,25},{9,1},{17,9},{25,17},{2,26},{10... | collective-permute-start | bytes 405512 | tf_op jit(solution)/shard_map/ppermute | solution.py:64
  96.0 34.5 %all-to-all-start.2 = ((bf16[64,64,128]{2,1,0:T(8,128)(2,1)}), bf16[64,64,128]{2,1,0:T(8,128)(2,1)S(1)}, u32[]{:S(2)}, u32[]{:S(2)}) async-start(bf16[64,64,128]{2,1,0:T(8,128)(2,1)} %bitcast.16), calls=%async_computation.2 | async-start | bytes 2097152 | tf_op jit(solution)/shard_map/all_to_all | solution.py:42
  104.8 4.8 %collective-permute-start.13 = (bf16[528,128]{1,0:T(8,128)(2,1)S(1)}, bf16[528,128]{1,0:T(8,128)(2,1)S(1)}, u32[]{:S(2)}, u32[]{:S(2)}) collective-permute-start(bf16[528,128]{1,0:T(8,128)(2,1)S(1)} %sum_four.3.here), channel_id=1, source_target_pairs={{0,1},{1,2},{2,3},{3,0},{8,9},{9,10},{10,11},{11,8},{16,17},{17,18... | collective-permute-start | bytes 405512 | tf_op jit(solution)/shard_map/ppermute | solution.py:64
  106.1 11.2 %collective-permute-start.14 = (bf16[528,128]{1,0:T(8,128)(2,1)S(1)}, bf16[528,128]{1,0:T(8,128)(2,1)S(1)}, u32[]{:S(2)}, u32[]{:S(2)}) collective-permute-start(bf16[528,128]{1,0:T(8,128)(2,1)S(1)} %sum_four.3.here), channel_id=1, source_target_pairs={{0,2},{1,3},{2,0},{3,1},{8,10},{9,11},{10,8},{11,9},{16,18},{17,19... | collective-permute-start | bytes 405512 | tf_op jit(solution)/shard_map/ppermute | solution.py:64
  107.2 16.0 %collective-permute-start.15 = (bf16[528,128]{1,0:T(8,128)(2,1)S(1)}, bf16[528,128]{1,0:T(8,128)(2,1)S(1)}, u32[]{:S(2)}, u32[]{:S(2)}) collective-permute-start(bf16[528,128]{1,0:T(8,128)(2,1)S(1)} %sum_four.3.here), channel_id=1, source_target_pairs={{0,3},{1,0},{2,1},{3,2},{8,11},{9,8},{10,9},{11,10},{16,19},{17,16... | collective-permute-start | bytes 405512 | tf_op jit(solution)/shard_map/ppermute | solution.py:64
  123.2 17.1 %collective-permute-start.16 = (bf16[2064,128]{1,0:T(8,128)(2,1)S(1)}, bf16[2064,128]{1,0:T(8,128)(2,1)S(1)}, u32[]{:S(2)}, u32[]{:S(2)}) collective-permute-start(bf16[2064,128]{1,0:T(8,128)(2,1)S(1)} %join_four.1.refs_1_), channel_id=1, source_target_pairs={{0,32},{32,64},{64,96},{96,0},{8,40},{40,72},{72,104},{104,8},{16,... | collective-permute-start | bytes 1585160 | tf_op jit(solution)/shard_map/ppermute | solution.py:64
  123.7 16.6 %collective-permute-start.17 = (bf16[2064,128]{1,0:T(8,128)(2,1)S(1)}, bf16[2064,128]{1,0:T(8,128)(2,1)}, u32[]{:S(2)}, u32[]{:S(2)}) collective-permute-start(bf16[2064,128]{1,0:T(8,128)(2,1)S(1)} %join_four.1.refs_1_), channel_id=1, source_target_pairs={{0,64},{32,96},{64,0},{96,32},{8,72},{40,104},{72,8},{104,40},{16,... | collective-permute-start | bytes 1585160 | tf_op jit(solution)/shard_map/ppermute | solution.py:64
  125.6 14.7 %collective-permute-start.18 = (bf16[2064,128]{1,0:T(8,128)(2,1)S(1)}, bf16[2064,128]{1,0:T(8,128)(2,1)}, u32[]{:S(2)}, u32[]{:S(2)}) collective-permute-start(bf16[2064,128]{1,0:T(8,128)(2,1)S(1)} %join_four.1.refs_1_), channel_id=1, source_target_pairs={{0,96},{32,0},{64,32},{96,64},{8,104},{40,8},{72,40},{104,72},{16,... | collective-permute-start | bytes 1585160 | tf_op jit(solution)/shard_map/ppermute | solution.py:64
  126.9 19.1 %collective-permute-start.19 = (bf16[2064,128]{1,0:T(8,128)(2,1)S(1)}, bf16[2064,128]{1,0:T(8,128)(2,1)S(1)}, u32[]{:S(2)}, u32[]{:S(2)}) collective-permute-start(bf16[2064,128]{1,0:T(8,128)(2,1)S(1)} %join_four.1.refs_1_), channel_id=1, source_target_pairs={{0,4},{4,0},{1,5},{5,1},{2,6},{6,2},{3,7},{7,3},{8,12},{12,8},{9,1... | collective-permute-start | bytes 1585160 | tf_op jit(solution)/shard_map/ppermute | solution.py:38
  140.3 5.7 %collective-permute-start.20 = (bf16[2064,128]{1,0:T(8,128)(2,1)S(1)}, bf16[2064,128]{1,0:T(8,128)(2,1)S(1)}, u32[]{:S(2)}, u32[]{:S(2)}) collective-permute-start(bf16[2064,128]{1,0:T(8,128)(2,1)S(1)} %collective-permute-done.16.refs_1_), channel_id=1, source_target_pairs={{0,4},{4,0},{1,5},{5,1},{2,6},{6,2},{3,7},{7,3},{8,12},{12,8},{9,1... | collective-permute-start | bytes 1585160 | tf_op jit(solution)/shard_map/ppermute | solution.py:38
  141.6 4.4 %collective-permute-start.21 = (bf16[2064,128]{1,0:T(8,128)(2,1)}, bf16[2064,128]{1,0:T(8,128)(2,1)S(1)}, u32[]{:S(2)}, u32[]{:S(2)}) collective-permute-start(bf16[2064,128]{1,0:T(8,128)(2,1)} %collective-permute-done.17.refs_2_), channel_id=1, source_target_pairs={{0,4},{4,0},{1,5},{5,1},{2,6},{6,2},{3,7},{7,3},{8,12},{12,8},{9,1... | collective-permute-start | bytes 1585160 | tf_op jit(solution)/shard_map/ppermute | solution.py:38
  141.6 4.5 %collective-permute-start.22 = (bf16[2064,128]{1,0:T(8,128)(2,1)}, bf16[2064,128]{1,0:T(8,128)(2,1)S(1)}, u32[]{:S(2)}, u32[]{:S(2)}) collective-permute-start(bf16[2064,128]{1,0:T(8,128)(2,1)} %collective-permute-done.18.refs_3_), channel_id=1, source_target_pairs={{0,4},{4,0},{1,5},{5,1},{2,6},{6,2},{3,7},{7,3},{8,12},{12,8},{9,1... | collective-permute-start | bytes 1585160 | tf_op jit(solution)/shard_map/ppermute | solution.py:38
  (4 other events, 86.7 us)
